TPU v7x, 128 devices: a whole 4x4x4 slice. The times are simulated.
128 devices in a mesh: tm: 4 (over x), grid: 32 (over y, z, core).
Axes of the slice: x: 4, y: 4, z: 4, core: 2. Of those that a mesh axis runs over, the one named last changes fastest.
Arguments:
- clocked_seawarmth: bfloat16 [4096, 98304], P(('tm', 'grid')), may hold values from -12 to 12
- clocked_precipitation: bfloat16 [4096, 98304], P(('tm', 'grid')), may hold values from -12 to 12
- fading_weights: float32 [2, 4096], P(None, 'tm'), may hold values from 0.4 to 1, as said below
- starting_average: float32 [2, 98304], P(None, 'grid'), may hold values from -6 to 6
- warmth_random_operator: bfloat16 [98304, 256], P('grid'), may hold values from -0.01953125 to 0.01953125
- wetness_random_operator: bfloat16 [98304, 256], P('grid'), may hold values from -0.01953125 to 0.01953125
Outputs:
- warmth_summary: float32 [256, 98304], P('tm', 'grid')
- wetness_summary: float32 [256, 98304], P('tm', 'grid')
- kernel_middle: float32 [256, 256], replicated
Inputs may be any that keep to these rules, and one draw needn't show every extreme that they name: `fading_weights`: each factor lies below one.
All inputs are finite; a program needn't handle non-finite values.
Results may differ from a plain program's by a relative error of at most 0.0085.
Values may be sent and summed in bfloat16 or wider, within the bound.
No kernel may reach another device: no remote copies, remote signals or barrier semaphores. Data moves between devices by JAX's collectives and lax.ppermute only.
A program may use at most 192 MiB of HBM per device.

v0:
```python
import jax
import jax.numpy as jnp
from jax import lax
from jax.sharding import PartitionSpec as P

BLK = 128


def split_up(x, dim, peers):
    dims = x.shape
    parts = x.reshape(*dims[:dim], peers, dims[dim] // peers, *dims[dim + 1 :])
    return jnp.moveaxis(parts, dim, 0)


def edges_of(length, count):
    unit = 8 if length >= 8 * count else 1
    return [length // unit * k // count * unit for k in range(1, count)]


def joined_along(parts, dim):
    dims = list(parts.shape[1:])
    dims[dim] *= parts.shape[0]
    return jnp.moveaxis(parts, 0, dim).reshape(dims)


def cut_exchange(x, axis, pieces, split_dim, concat_dim):
    parts = split_up(x, split_dim, lax.axis_size(axis))
    cut = max(range(1, max(2, parts.ndim - 1)), key=lambda d: parts.shape[d])
    outs = []
    for section in jnp.split(parts, edges_of(parts.shape[cut], pieces), axis=cut):
        if section.size:
            outs.append(lax.all_to_all(section, axis, split_axis=0, concat_axis=0, tiled=True))
    return joined_along(jnp.concatenate(outs, axis=cut), concat_dim)


def from_everyone(x, axis):
    copies = jnp.broadcast_to(x, (lax.axis_size(axis), *x.shape))
    return lax.all_to_all(copies, axis, split_axis=0, concat_axis=0, tiled=True)


def gathered_once(x, axis):
    leaves = jax.tree.leaves(x)
    turns = sorted(range(len(leaves)), key=lambda k: -leaves[k].size)
    width = (1, *leaves[turns[0]].shape)[-1]
    lines = [
        jnp.pad(leaves[k].reshape(-1), (0, -leaves[k].size % width)).reshape(-1, width)
        for k in turns
    ]
    both, at, found = (from_everyone(jnp.concatenate(lines), axis), 0, {})
    for k, line in zip(turns, lines):
        section = both[:, at : at + len(line)].reshape(len(both), -1)
        found[k] = section[:, : leaves[k].size].reshape(-1, *leaves[k].shape)
        at += len(line)
    numbers = iter(range(len(leaves)))
    return jax.tree.map(lambda _: found[next(numbers)], x)


def combined_pairwise(pieces, combine):
    while len(jax.tree.leaves(pieces)[0]) > 1:
        pieces = jax.vmap(combine)(
            *(jax.tree.map(lambda part: part[side::2], pieces) for side in (0, 1))
        )
    return jax.tree.map(lambda part: part[0], pieces)


def carried_in(x, axis, combine, identity):
    peers, index = (lax.axis_size(axis), lax.axis_index(axis))
    passed = jnp.arange(peers) < index

    def kept(part, zero, own):
        part = jnp.where(
            passed.reshape(-1, *(1 for _ in own.shape)), part, jnp.asarray(zero, own.dtype)
        )
        return part

    pieces = gathered_once(x, axis)
    return combined_pairwise(jax.tree.map(kept, pieces, identity, x), combine)


def of_everyone(x, axis):
    return from_everyone(x, axis).sum(axis=0)


def compose(earlier, later):
    gain_early, offset_early = earlier
    gain_late, offset_late = later
    return (gain_early * gain_late, gain_late[:, None] * offset_early + offset_late)


def reduce_line_couples(left, right):
    return lax.dot_general(
        left, right, (((0,), (0,)), ((), ())), preferred_element_type=jnp.float32
    )


def split_three(weights):
    high_part = weights.astype(jnp.bfloat16)
    rest_one = weights - high_part.astype(jnp.float32)
    middle_part = rest_one.astype(jnp.bfloat16)
    rest_two = rest_one - middle_part.astype(jnp.float32)
    return (high_part, middle_part, rest_two.astype(jnp.bfloat16))


def per_device(
    clocked_seawarmth,
    clocked_precipitation,
    fading_weights,
    starting_average,
    warmth_random_operator,
    wetness_random_operator,
):
    piled_quantities = jnp.stack([clocked_seawarmth, clocked_precipitation])
    fields = cut_exchange(piled_quantities, "grid", 2, 2, 1)
    hour_count = fields.shape[1]
    tile_width = fields.shape[2]
    block_count = hour_count // BLK
    decay_blocks = fading_weights.reshape(2, block_count, BLK)
    log_decay = jnp.log(decay_blocks)
    inclusive = jnp.cumsum(log_decay, axis=2)
    exclusive = inclusive - log_decay
    row_index = lax.broadcasted_iota(jnp.int32, (BLK, BLK), 0)
    col_index = lax.broadcasted_iota(jnp.int32, (BLK, BLK), 1)
    strictly = row_index > col_index
    spread = exclusive[..., :, None] - inclusive[..., None, :]
    within = (
        jnp.where(strictly, jnp.exp(jnp.minimum(spread, 0.0)), 0.0)
        * (1.0 - decay_blocks)[..., None, :]
    )
    to_end = jnp.exp(inclusive[..., -1:] - inclusive) * (1.0 - decay_blocks)
    block_gain = jnp.exp(inclusive[..., -1])
    field_blocks = fields.reshape(2, block_count, BLK, tile_width)
    inside = jnp.zeros((2, block_count, BLK, tile_width), jnp.float32)
    for within_part in split_three(within):
        inside = inside + jnp.einsum(
            "fbij,fbjp->fbip", within_part, field_blocks, preferred_element_type=jnp.float32
        )
    block_end = jnp.zeros((2, block_count, tile_width), jnp.float32)
    for to_end_part in split_three(to_end):
        block_end = block_end + jnp.einsum(
            "fbj,fbjp->fbp", to_end_part, field_blocks, preferred_element_type=jnp.float32
        )

    def fold(running, single_tick_feed):
        gain_step, end_step = single_tick_feed
        gain_now, offset_now = running
        return (
            (gain_now * gain_step, gain_step[:, None] * offset_now + end_step),
            (gain_now, offset_now),
        )

    ones_pair = jnp.ones((2,), jnp.float32)
    zero_state = jnp.zeros((2, tile_width), jnp.float32)
    device_state, entering = lax.scan(
        fold, (ones_pair, zero_state), (jnp.transpose(block_gain), jnp.moveaxis(block_end, 1, 0))
    )
    enter_gain, enter_offset = entering
    prior_gain, prior_offset = carried_in(device_state, "tm", compose, (ones_pair, zero_state))
    start_mean = prior_gain[:, None] * starting_average + prior_offset
    block_mean = jnp.moveaxis(enter_offset + enter_gain[..., None] * start_mean[None], 0, 1)
    previous = inside + jnp.exp(exclusive)[..., None] * block_mean[:, :, None, :]
    departure_amount = (
        (field_blocks.astype(jnp.float32) - previous)
        .astype(jnp.bfloat16)
        .reshape(2, hour_count, tile_width)
    )
    partials = jnp.stack(
        [
            jnp.dot(
                departure_amount[0], warmth_random_operator, preferred_element_type=jnp.float32
            ),
            jnp.dot(
                departure_amount[1], wetness_random_operator, preferred_element_type=jnp.float32
            ),
        ]
    )
    compressed_lines = lax.psum(partials, "grid").astype(jnp.bfloat16)
    divisor_magnitude = (hour_count * lax.axis_size("tm")) ** (-0.5)
    warmth_lanes = compressed_lines[0]
    wetness_lanes = compressed_lines[1]
    onto_warmth = reduce_line_couples(wetness_lanes, departure_amount[0])
    onto_wetness = reduce_line_couples(warmth_lanes, departure_amount[1])
    accumulated_aggregate = lax.psum_scatter(
        jnp.stack([onto_warmth, onto_wetness], axis=1), "tm", scatter_dimension=0, tiled=True
    )
    warmth_summary = accumulated_aggregate[:, 0] * divisor_magnitude
    wetness_summary = accumulated_aggregate[:, 1] * divisor_magnitude
    cross_part = reduce_line_couples(compressed_lines[0], compressed_lines[1])
    kernel_middle = of_everyone(cross_part, "tm") * divisor_magnitude
    return (warmth_summary, wetness_summary, kernel_middle)


def solution(mesh):
    return jax.shard_map(
        per_device,
        mesh=mesh,
        in_specs=(
            P(("tm", "grid"), None),
            P(("tm", "grid"), None),
            P(None, "tm"),
            P(None, "grid"),
            P("grid", None),
            P("grid", None),
        ),
        out_specs=(P("tm", "grid"), P("tm", "grid"), P()),
        check_vma=False,
    )
```

profile of v0, /device:TPU:1, one launch (start us, length us, event | category | flops | bytes accessed | tf_op | source)
XLA Modules:
  0.0 562.5 jit_solution(8880140532888412898)
XLA Ops:
  7.2 6.4 %copy.38 = bf16[4,8,32,3072]{3,2,1,0:T(8,128)(2,1)S(1)} copy(bf16[4,8,32,3072]{3,1,2,0:T(8,128)(2,1)} %bitcast.111) | data formatting | bytes 12582912
  13.5 6.2 %copy.39 = bf16[4,8,32,3072]{3,2,1,0:T(8,128)(2,1)S(1)} copy(bf16[4,8,32,3072]{3,1,2,0:T(8,128)(2,1)} %bitcast.112) | data formatting | bytes 12582912
  21.0 3.7 fusion.41
  24.8 6.0 %copy.25 = bf16[32,2,16,3072]{3,2,1,0:T(8,128)(2,1)} copy(bf16[32,2,16,3072]{3,0,2,1:T(8,128)(2,1)S(1)} %get-tuple-element.129) | data formatting | bytes 12582912 | tf_op jit(solution)/shard_map/split | solution.py:30
  30.8 10.1 %all-to-all-start = ((bf16[32,2,16,3072]{3,2,1,0:T(8,128)(2,1)}), bf16[32,2,16,3072]{3,2,1,0:T(8,128)(2,1)}, u32[]{:S(2)}, u32[]{:S(2)}) async-start(bf16[32,2,16,3072]{3,2,1,0:T(8,128)(2,1)} %copy.25), calls=%async_computation | async-start | bytes 12582912 | tf_op jit(solution)/shard_map/all_to_all | solution.py:32
  40.9 8.8 %copy.26 = bf16[32,2,16,3072]{3,2,1,0:T(8,128)(2,1)} copy(bf16[32,2,16,3072]{3,0,2,1:T(8,128)(2,1)} %get-tuple-element.130) | data formatting | bytes 12582912 | tf_op jit(solution)/shard_map/split | solution.py:30
  49.8 68.5 %all-to-all-done = bf16[32,2,16,3072]{3,2,1,0:T(8,128)(2,1)} async-done(((bf16[32,2,16,3072]{3,2,1,0:T(8,128)(2,1)}), bf16[32,2,16,3072]{3,2,1,0:T(8,128)(2,1)}, u32[]{:S(2)}, u32[]{:S(2)}) %all-to-all-start) | async-done | bytes 6291488 | tf_op jit(solution)/shard_map/all_to_all | solution.py:32
  118.2 14.7 %all-to-all-start.1 = ((bf16[32,2,16,3072]{3,2,1,0:T(8,128)(2,1)}), bf16[32,2,16,3072]{3,2,1,0:T(8,128)(2,1)}, u32[]{:S(2)}, u32[]{:S(2)}) async-start(bf16[32,2,16,3072]{3,2,1,0:T(8,128)(2,1)} %copy.26), calls=%async_computation.1 | async-start | bytes 12582912 | tf_op jit(solution)/shard_map/all_to_all | solution.py:32
  134.0 76.7 %all-to-all-done.1 = bf16[32,2,16,3072]{3,2,1,0:T(8,128)(2,1)} async-done(((bf16[32,2,16,3072]{3,2,1,0:T(8,128)(2,1)}), bf16[32,2,16,3072]{3,2,1,0:T(8,128)(2,1)}, u32[]{:S(2)}, u32[]{:S(2)}) %all-to-all-start.1) | async-done | bytes 6291488 | tf_op jit(solution)/shard_map/all_to_all | solution.py:32
  210.7 6.4 %maximum_bitcast_fusion.1 = bf16[2,32,32,3072]{3,2,0,1:T(8,128)(2,1)S(1)} fusion(bf16[32,2,16,3072]{3,2,1,0:T(8,128)(2,1)} %all-to-all-done.1, bf16[32,2,16,3072]{3,2,1,0:T(8,128)(2,1)} %all-to-all-done), kind=kLoop, calls=%fused_computation.10 | loop fusion | flops 25165824 | bytes 25165824 | tf_op jit(solution)/shard_map/transpose | solution.py:23
  217.1 5.6 copy.27
  222.7 6.3 %fusion.3 = f32[8,2,1,3072]{3,2,1,0:T(1,128)S(1)} fusion(bf16[2,8,128,3072]{3,2,1,0:T(8,128)(2,1)} %bitcast.99, bf16[2,8,128,1]{2,1,0,3:T(8,128)(2,1)S(1)} %get-tuple-element.134), kind=kOutput, calls=%fused_computation.11 | convolution fusion | flops 12582912 | bytes 12783616 | tf_op jit(solution)/shard_map/fbj,fbjp->fbp/dot_general | solution.py:139
  229.0 6.3 %fusion.7 = f32[8,2,1,3072]{3,2,1,0:T(1,128)S(1)} fusion(bf16[2,8,128,3072]{3,2,1,0:T(8,128)(2,1)} %bitcast.100, bf16[2,8,128,1]{2,1,0,3:T(8,128)(2,1)S(1)} %get-tuple-element.124), kind=kOutput, calls=%fused_computation.15 | convolution fusion | flops 12582912 | bytes 12783616 | tf_op jit(solution)/shard_map/fbj,fbjp->fbp/dot_general | solution.py:139
  235.3 6.3 %fusion.5 = f32[8,2,1,3072]{3,2,1,0:T(1,128)S(1)} fusion(bf16[2,8,128,3072]{3,2,1,0:T(8,128)(2,1)} %bitcast.101, bf16[2,8,128,1]{2,1,0,3:T(8,128)(2,1)S(1)} %get-tuple-element.133), kind=kOutput, calls=%fused_computation.13 | convolution fusion | flops 12582912 | bytes 12783616 | tf_op jit(solution)/shard_map/fbj,fbjp->fbp/dot_general | solution.py:139
  244.1 4.0 all-to-all-start.2
  248.3 16.4 %fusion.23 = f32[2,8,128,3072]{3,2,1,0:T(8,128)} fusion(bf16[2,8,128,3072]{3,2,1,0:T(8,128)(2,1)} %bitcast.102, f32[2,8,128]{2,1,0:T(8,128)S(1)} %get-tuple-element.141, f32[2,8,128]{2,1,0:T(8,128)S(1)} %reduce_window_sum.11, f32[2,8,128]{2,1,0:T(8,128)S(1)} %get-tuple-element.136, pred[128,128]{1,0:T(8,128)(4,1)S(1)} %iota_compare_fusion), kind=kOutput, calls=%fused_computation.41 | convolution fusion | flops 1612709888 | bytes 37789696 | tf_op jit(solution)/shard_map/fbij,fbjp->fbip/dot_general | solution.py:134
  264.7 16.4 %fusion.20 = f32[2,8,128,3072]{3,2,1,0:T(8,128)} fusion(bf16[2,8,128,3072]{3,2,1,0:T(8,128)(2,1)} %bitcast.103, f32[2,8,128]{2,1,0:T(8,128)S(1)} %get-tuple-element.141, f32[2,8,128]{2,1,0:T(8,128)S(1)} %reduce_window_sum.11, f32[2,8,128]{2,1,0:T(8,128)S(1)} %get-tuple-element.136, pred[128,128]{1,0:T(8,128)(4,1)S(1)} %iota_compare_fusion), kind=kOutput, calls=%fused_computation.40 | convolution fusion | flops 1611923456 | bytes 37789696 | tf_op jit(solution)/shard_map/fbij,fbjp->fbip/dot_general | solution.py:134
  281.9 30.8 %subtract_convert_fusion = bf16[2,8,128,3072]{3,2,1,0:T(8,128)(2,1)} fusion(f32[2,8,128,3072]{3,2,1,0:T(8,128)} %fusion.20, f32[2,8,128,3072]{3,2,1,0:T(8,128)} %fusion.23, bf16[2,8,128,3072]{3,2,1,0:T(8,128)(2,1)} %bitcast.104, f32[2,8,3072]{2,1,0:T(8,128)S(1)} %copy.29, f32[2,8,128]{2,1,0:T(8,128)S(1)} %get-tuple-element.135, ...), kind=kOutput, calls=%fused_computation.8 | convolution fusion | flops 1657536512 | bytes 75743232 | tf_op jit(solution)/shard_map/fbij,fbjp->fbip/dot_general | solution.py:134
  312.6 5.6 fusion.40
  324.3 146.5 %all-reduce.2 = bf16[2,1024,256]{2,1,0:T(8,128)(2,1)S(1)} all-reduce(f32[2,1024,256]{2,1,0:T(8,128)} %pad_maximum_fusion.1), channel_id=1, replica_groups=mesh['tm'=4,'grid'=32] {'grid'}, use_global_device_ids=true, to_apply=%region_3.4 | all-reduce | flops 524288 | bytes 3145728 | tf_op jit(solution)/shard_map/psum | solution.py:176
  470.8 4.8 convolution_bitcast_fusion
  477.5 3.1 pad_maximum_fusion
  481.0 14.5 %all_to_all.20 = f32[4,256,256]{2,1,0:T(8,128)S(1)} all-to-all(f32[4,256,256]{2,1,0:T(8,128)S(1)} %broadcast_in_dim.68), channel_id=1, replica_groups=mesh['tm'=4,'grid'=32] {'tm'}, dimensions={0} | all-to-all | bytes 2097152 | tf_op jit(solution)/shard_map/all_to_all | solution.py:38
  496.3 56.4 %reduce-scatter.2.cloned.1.call-done = f32[64,2,3072]{2,0,1:T(8,128)} async-done(((f32[256,2,3072]{2,0,1:T(8,128)}), f32[64,2,3072]{2,0,1:T(8,128)}) %reduce-scatter.2.cloned.1.call-update) | async-done | bytes 1572880 | tf_op jit(solution)/shard_map/reduce_scatter | solution.py:182
  (90 shorter events, 18.6 us)
Async XLA Ops:
  7.2 311.1 %copy-start = (bf16[3072,256]{1,0:T(8,128)(2,1)S(1)}, bf16[3072,256]{1,0:T(8,128)(2,1)}, u32[]{:S(2)}) copy-start(bf16[3072,256]{1,0:T(8,128)(2,1)} %param.13) | copy-start | bytes 4718596
  30.8 87.4 %all-to-all-start = ((bf16[32,2,16,3072]{3,2,1,0:T(8,128)(2,1)}), bf16[32,2,16,3072]{3,2,1,0:T(8,128)(2,1)}, u32[]{:S(2)}, u32[]{:S(2)}) async-start(bf16[32,2,16,3072]{3,2,1,0:T(8,128)(2,1)} %copy.25), calls=%async_computation | async-start | bytes 12582912 | tf_op jit(solution)/shard_map/all_to_all | solution.py:32
  49.7 83.2 %copy-start.5 = (f32[2,1024]{1,0:T(2,128)S(1)}, f32[2,1024]{1,0:T(2,128)}, u32[]{:S(2)}) copy-start(f32[2,1024]{1,0:T(2,128)} %param.10) | copy-start | bytes 24580
  118.2 92.5 %all-to-all-start.1 = ((bf16[32,2,16,3072]{3,2,1,0:T(8,128)(2,1)}), bf16[32,2,16,3072]{3,2,1,0:T(8,128)(2,1)}, u32[]{:S(2)}, u32[]{:S(2)}) async-start(bf16[32,2,16,3072]{3,2,1,0:T(8,128)(2,1)} %copy.26), calls=%async_computation.1 | async-start | bytes 12582912 | tf_op jit(solution)/shard_map/all_to_all | solution.py:32
  244.1 37.0 %all-to-all-start.2 = ((f32[4,3,3072]{2,1,0:T(4,128)}), f32[4,3,3072]{2,1,0:T(4,128)S(1)}, u32[]{:S(2)}, u32[]{:S(2)}) async-start(f32[4,3,3072]{2,1,0:T(4,128)} %broadcast_in_dim.64), calls=%async_computation.2 | async-start | bytes 393216 | tf_op jit(solution)/shard_map/all_to_all | solution.py:38
  248.1 304.6 %reduce-scatter.2.cloned.1.call-start = ((), (), s32[]{:S(2)}) async-start(), calls=%async_computation.5 | async-start | bytes 7864320 | tf_op jit(solution)/shard_map/reduce_scatter | solution.py:182
  264.7 16.8 %copy-start.4 = (f32[2,3072]{1,0:T(2,128)S(1)}, f32[2,3072]{1,0:T(2,128)}, u32[]{:S(2)}) copy-start(f32[2,3072]{1,0:T(2,128)} %param.11) | copy-start | bytes 73732
  318.2 4.4 copy-start.1
  318.3 4.6 copy-start.3
  318.3 2.6 copy-start.6
  470.8 4.8 copy-start.2
Sparse Core Ops, SparseCore 0:
  480.7 72.0 reduce-scatter.1
where the time goes:
time: 572 us; the launch traced here: 563 us
  waiting for transfers between devices  202 us (35%)
  blocking collectives  161 us (28%)
  matrix products  93 us (16%)
  local copies, waits for them, and re-layouts  44.9 us (8%)
  starting transfers between devices  29 us (5%)
  other arithmetic  18.1 us (3%)
  between operations  14.6 us (3%)
    psum x1, blocking collectives, per_device(): compressed_lines = lax.psum(partials, 'grid').astype(jnp.bfloat16)  147 us
    all_to_all x2, waiting for transfers between devices, cut_exchange(): lax.all_to_all(section, axis, split_axis=0, concat_axis=0, tiled=True)  145 us
    dot_general x3, matrix products, per_device(): jnp.einsum('fbij,fbjp->fbip', within_part, field_blocks, preferred_elemen...  63.5 us
    reduce_scatter x1, waiting for transfers between devices, per_device(): lax.psum_scatter(jnp.stack([onto_warmth, onto_wetness], axis=1), 'tm', sc...  56.4 us
    all_to_all x2, starting transfers between devices, cut_exchange(): lax.all_to_all(section, axis, split_axis=0, concat_axis=0, tiled=True)  24.8 us
    dot_general x3, matrix products, per_device(): jnp.einsum('fbj,fbjp->fbp', to_end_part, field_blocks, preferred_element_...  18.9 us
    split x3, local copies, waits for them, and re-layouts, cut_exchange(): jnp.split(parts, edges_of(parts.shape[cut], pieces), axis=cut)  18.6 us
    all_to_all x1, blocking collectives, from_everyone(): return lax.all_to_all(copies, axis, split_axis=0, concat_axis=0, tiled=True)  14.5 us
  transfers between devices with their start and end apart: 4, of which 3 were waited for; matrix products, arithmetic and copies ran while one was open for 8% of the time, Pallas kernels for 0%

commit v1 on v0

v1 whole, which is shorter than its diff:
```python
import jax
import jax.numpy as jnp
from jax import lax
from jax.experimental import pallas as pl
from jax.experimental.pallas import tpu as pltpu
from jax.sharding import PartitionSpec as P

BLK = 256
NCHUNK = 512
Y, Z, C = 4, 4, 2
F32, BF16 = jnp.float32, jnp.bfloat16
HIGHEST = lax.Precision.HIGHEST


def decay_blocks(fading):
    nb = fading.shape[1] // BLK
    a = fading.reshape(2, nb, BLK)
    log_a = jnp.log(a)
    inclusive = jnp.cumsum(log_a, axis=2)
    before = jnp.concatenate([jnp.zeros((2, nb, 1), F32), inclusive, jnp.zeros((2, nb, 7), F32)], axis=2)
    rows, cols = BLK + 8, BLK + 128
    r = lax.broadcasted_iota(jnp.int32, (rows, cols), 0)
    c = lax.broadcasted_iota(jnp.int32, (rows, cols), 1)
    pad = lambda v: jnp.pad(v, ((0, 0), (0, 0), (0, 128)))
    spread = before[..., :, None] - pad(inclusive)[..., None, :]
    gain = pad(1.0 - a)[..., None, :]
    gain = jnp.where(c == BLK, 1.0, gain)
    weight = jnp.exp(jnp.minimum(spread, 0.0)) * gain
    weight = jnp.where((c < jnp.minimum(r, BLK)) | (c == BLK), weight, 0.0)
    sign = jnp.where((r < BLK) == (c < BLK), -1.0, 1.0)
    block = jnp.where(r == c, jnp.where(r < BLK, 1.0, sign * weight), sign * weight)
    block = jnp.where(r <= BLK, block, 0.0)
    total = inclusive[..., -1]
    ahead = jnp.cumsum(total, axis=1) - total
    since_start = jnp.exp(ahead[..., None] + before[..., :BLK]).reshape(2, nb * BLK)
    behind = jnp.cumsum(total[:, ::-1], axis=1)[:, ::-1] - total
    to_end = jnp.exp(behind[..., None] + inclusive[..., -1:] - inclusive) * (1.0 - a)
    return block, since_start, to_end.reshape(2, nb * BLK), jnp.exp(total.sum(axis=1))


def forward_kernel(x_ref, op_ref, block_ref, p_ref, end_ref, state):
    b = pl.program_id(0)

    @pl.when(b == 0)
    def _():
        state[...] = jnp.zeros_like(state)

    y = jnp.dot(x_ref[...], op_ref[...], preferred_element_type=F32)
    out = jnp.dot(block_ref[0, :, :BLK], y, precision=HIGHEST, preferred_element_type=F32)
    out = out - block_ref[0, :, BLK : BLK + 1] * state[0:1, :]
    p_ref[...] = out[:BLK]
    state[...] = out[BLK:]
    end_ref[...] = out[BLK:]


def forward(x, operator, block):
    hours, width = x.shape
    rank = operator.shape[1]
    nb = hours // BLK
    return pl.pallas_call(
        forward_kernel,
        grid=(nb,),
        in_specs=[
            pl.BlockSpec((BLK, width), lambda b: (b, 0)),
            pl.BlockSpec((width, rank), lambda b: (0, 0)),
            pl.BlockSpec((1, BLK + 8, BLK + 128), lambda b: (b, 0, 0)),
        ],
        out_specs=[
            pl.BlockSpec((BLK, rank), lambda b: (b, 0)),
            pl.BlockSpec((8, rank), lambda b: (0, 0)),
        ],
        out_shape=[
            jax.ShapeDtypeStruct((hours, rank), F32),
            jax.ShapeDtypeStruct((8, rank), F32),
        ],
        scratch_shapes=[pltpu.VMEM((8, rank), F32)],
        compiler_params=pltpu.CompilerParams(vmem_limit_bytes=24 << 20),
        cost_estimate=pl.CostEstimate(
            flops=2 * hours * width * rank, bytes_accessed=2 * hours * width, transcendentals=0
        ),
        name="forward",
    )(x, operator, block)


def backward_kernel(q_ref, block_ref, x_ref, enter_ref, w_ref, z_high, z_low, carried):
    @pl.when(pl.program_id(0) == 0)
    def _():
        nb = block_ref.shape[0]
        reverse = jnp.zeros((q_ref.shape[1], 1), F32)
        for b in reversed(range(nb)):
            q = q_ref[b * BLK : (b + 1) * BLK, :].astype(F32)
            out = jnp.dot(q.T, block_ref[b, :BLK, :], precision=HIGHEST, preferred_element_type=F32)
            out = out - reverse * block_ref[b, BLK : BLK + 1, :]
            z = out[:, :BLK]
            high = z.astype(BF16)
            z_high[:, b * BLK : (b + 1) * BLK] = high
            z_low[:, b * BLK : (b + 1) * BLK] = (z - high.astype(F32)).astype(BF16)
            reverse = out[:, BLK : BLK + 1]
        carried[...] = jnp.broadcast_to(reverse, carried.shape)

    x = x_ref[...]
    w = jnp.dot(z_high[...], x, preferred_element_type=F32)
    w = w + jnp.dot(z_low[...], x, preferred_element_type=F32)
    w = w - carried[:, 0:1] * enter_ref[0:1, :]
    w_ref[...] = w.astype(w_ref.dtype)


def backward(q, block, x, enter):
    hours, width = x.shape
    rank = q.shape[1]
    nb = hours // BLK
    return pl.pallas_call(
        backward_kernel,
        grid=(width // NCHUNK,),
        in_specs=[
            pl.BlockSpec((hours, rank), lambda n: (0, 0)),
            pl.BlockSpec((nb, BLK + 8, BLK + 128), lambda n: (0, 0, 0)),
            pl.BlockSpec((hours, NCHUNK), lambda n: (0, n)),
            pl.BlockSpec((8, NCHUNK), lambda n: (0, n)),
        ],
        out_specs=pl.BlockSpec((rank, NCHUNK), lambda n: (0, n)),
        out_shape=jax.ShapeDtypeStruct((rank, width), BF16),
        scratch_shapes=[
            pltpu.VMEM((rank, hours), BF16),
            pltpu.VMEM((rank, hours), BF16),
            pltpu.VMEM((rank, 128), F32),
        ],
        compiler_params=pltpu.CompilerParams(vmem_limit_bytes=24 << 20),
        cost_estimate=pl.CostEstimate(
            flops=4 * hours * width * rank, bytes_accessed=2 * hours * width, transcendentals=0
        ),
        name="backward",
    )(q, block, x, enter)


def middle_kernel(left_ref, right_ref, out_ref):
    out = jnp.dot(left_ref[...].astype(F32).T.astype(BF16), right_ref[...], preferred_element_type=F32)
    out_ref[...] = out.astype(out_ref.dtype)


def cross(left, right):
    rank = left.shape[1]
    return pl.pallas_call(
        middle_kernel,
        out_shape=jax.ShapeDtypeStruct((rank, rank), BF16),
        in_specs=[pl.BlockSpec(memory_space=pltpu.VMEM)] * 2,
        out_specs=pl.BlockSpec(memory_space=pltpu.VMEM),
        compiler_params=pltpu.CompilerParams(vmem_limit_bytes=8 << 20),
        cost_estimate=pl.CostEstimate(flops=2 * left.size * rank, bytes_accessed=4 * left.size, transcendentals=0),
        name="cross",
    )(left, right)


def all_to_all(x, axis, groups=None):
    return lax.all_to_all(x, axis, split_axis=0, concat_axis=0, tiled=True, axis_index_groups=groups)


def pick(x, i):
    return lax.dynamic_index_in_dim(x, i, 0, keepdims=False)


def shifted(x, by):
    n = lax.axis_size("tm")
    return lax.ppermute(x, "tm", [(i, (i + by) % n) for i in range(n)])


def entering(end, gain, start):
    message = jnp.concatenate([end[None], jnp.broadcast_to(gain, (1, end.shape[0])), jnp.zeros((6, end.shape[0]), F32)])
    i = lax.axis_index("tm")
    total, so_far = jnp.zeros_like(end), jnp.ones_like(end)
    for d in range(1, lax.axis_size("tm")):
        got = shifted(message, d)
        total = total + jnp.where(i >= d, so_far * got[0], 0.0)
        so_far = so_far * jnp.where(i >= d, got[1], 1.0)
    return total + so_far * start


def grid_place():
    g = lax.axis_index("grid")
    return g // (Z * C), (g // C) % Z, g % C


def along(x, dim, by):
    def moved(g):
        y, z, c = g // (Z * C), (g // C) % Z, g % C
        y, z, c = ((y + by) % Y, z, c) if dim == "y" else (y, (z + by) % Z, c) if dim == "z" else (y, z, 1 - c)
        return (y * Z + z) * C + c

    return lax.ppermute(x, "grid", [(g, moved(g)) for g in range(Y * Z * C)])


def scattered(x, dim, me, n):
    out = pick(x, me)
    for by in range(1, n):
        out = out + along(pick(x, (me + by) % n), dim, by)
    return out


def gathered(x, dim, me, n):
    out = jnp.zeros((n, *x.shape), x.dtype)
    out = lax.dynamic_update_index_in_dim(out, x, me, 0)
    for by in range(1, n):
        out = lax.dynamic_update_index_in_dim(out, along(x, dim, by), (me + n - by) % n, 0)
    return out


def summed_by_permutes(p):
    y, z, c = grid_place()
    hours, rank = p.shape
    rows = hours // (Y * Z * C)
    p = scattered(p.reshape(C, Y * Z * rows, rank), "core", c, C)
    p = scattered(p.reshape(Y, Z * rows, rank), "y", y, Y)
    p = scattered(p.reshape(Z, rows, rank), "z", z, Z)
    q = gathered(p.astype(BF16), "z", z, Z).reshape(Z * rows, rank)
    q = gathered(q, "y", y, Y).reshape(Y * Z * rows, rank)
    return gathered(q, "core", c, C).reshape(hours, rank)


def summed_by_all_to_all(p, *held):
    _, _, c = grid_place()
    hours, rank = p.shape
    n = Y * Z
    rows = hours // (n * C)
    groups = [[k * C + core for k in range(n)] for core in range(C)]
    p = scattered(p.reshape(C, n * rows, rank), "core", c, C).astype(BF16)
    p, *held = lax.optimization_barrier((p, *held))
    p = all_to_all(p.reshape(n, rows, rank), "grid", groups)
    q = p.astype(F32).sum(axis=0).astype(BF16)
    q = all_to_all(jnp.broadcast_to(q, (n, rows, rank)), "grid", groups)
    q = gathered(q.reshape(n * rows, rank), "core", c, C).reshape(hours, rank)
    return q, *held


def summed_over_hours(w):
    n = lax.axis_size("tm")
    rank, width = w.shape
    w = w.reshape(n, rank // n, width)
    i, half = lax.axis_index("tm"), width // 2
    own, ahead, far, back = (pick(w, (i + k) % n) for k in range(n))
    add = lambda a, b: a.astype(F32) + b.astype(F32)
    up = shifted(far[:, :half], 1)
    down = shifted(far[:, half:], n - 1)
    from_below = shifted(ahead[:, half:], 1)
    from_above = shifted(back[:, :half], n - 1)
    up = shifted(add(up, ahead[:, :half]).astype(BF16), 1)
    down = shifted(add(down, back[:, half:]).astype(BF16), n - 1)
    left = add(own[:, :half], from_above) + up.astype(F32)
    right = add(own[:, half:], from_below) + down.astype(F32)
    return jnp.concatenate([left, right], axis=1)


def per_device(x0, x1, fading, starting, operator0, operator1):
    grid = lax.axis_size("grid")
    rows, points = x0.shape
    width, hours = points // grid, rows * grid
    scale = (hours * lax.axis_size("tm")) ** -0.5

    def tile(x):
        x = x.reshape(rows, grid, width).transpose(1, 0, 2)
        return all_to_all(x, "grid").reshape(hours, width)

    block, since_start, to_end, gain = decay_blocks(fading)
    operators = (operator0, operator1)

    def start_projection(f):
        s = starting[f]
        parts = []
        for _ in range(3):
            part = s.astype(BF16)
            parts.append(part)
            s = s - part.astype(F32)
        return jnp.dot(jnp.stack(parts), operators[f], preferred_element_type=F32).sum(axis=0)

    def partial_projection(f, x):
        p, end = forward(x, operators[f], block[f])
        enter = entering(end[0], gain[f], start_projection(f))
        return p - since_start[f][:, None] * enter[None]

    def entering_mean(f, x):
        end = (x.astype(F32) * to_end[f][:, None]).sum(axis=0)
        enter = entering(end, gain[f], starting[f])
        return jnp.broadcast_to(enter[None], (8, width))

    t0 = tile(x0)
    t1 = tile(x1)
    p0 = partial_projection(0, t0)
    q0 = summed_by_permutes(p0)
    mean0 = entering_mean(0, t0)
    t1, q0, mean0 = lax.optimization_barrier((t1, q0, mean0))
    p1 = partial_projection(1, t1)
    q1, t1 = summed_by_all_to_all(p1, t1)
    mean1 = entering_mean(1, t1)
    w1 = backward(q0, block[1], t1, mean1)
    wetness = summed_over_hours(w1) * scale
    sent = cross(q0, q1)
    middle = sent.astype(F32)
    for d in range(1, lax.axis_size("tm")):
        middle = middle + shifted(sent, d).astype(F32)
    w0 = backward(q1, block[0], t0, mean0)
    warmth = summed_over_hours(w0) * scale
    return warmth, wetness, middle * scale


def solution(mesh):
    return jax.shard_map(
        per_device,
        mesh=mesh,
        in_specs=(
            P(("tm", "grid"), None),
            P(("tm", "grid"), None),
            P(None, "tm"),
            P(None, "grid"),
            P("grid", None),
            P("grid", None),
        ),
        out_specs=(P("tm", "grid"), P("tm", "grid"), P()),
        check_vma=False,
    )
```

time: 572 us -> 340 us (0.59); the launches traced: 563 us -> 337 us
  blocking collectives: 161 us -> 0 us
  matrix products: 93 us -> 0.66 us
  starting transfers between devices: 29 us -> 102 us
  waiting for transfers between devices: 202 us -> 144 us
  Pallas kernels: 0 us -> 31.7 us
  local copies, waits for them, and re-layouts: 44.9 us -> 29.2 us
  between operations: 14.6 us -> 1.3 us
  other arithmetic: 18.1 us -> 28.5 us
    psum x1 -> x0, blocking collectives: 147 us -> none  [per_device(): compressed_lines = lax.psum(partials, 'grid').astype(jnp.bfloat16)]
    dot_general x11 -> x2, matrix products: 93 us -> 0.66 us  [start_projection(): jnp.dot(jnp.stack(parts), operators[f], preferred_element_type=F32)]
    all_to_all x3 -> x4, waiting for transfers between devices: 145 us -> 63.5 us  [all_to_all(): lax.all_to_all(x, axis, split_axis=0, concat_axis=0, tiled=True, axis_ind...]
    ppermute x0 -> x43, waiting for transfers between devices: none -> 80.7 us  [the longest x16 57.1 us: along(): return lax.ppermute(x, 'grid', [(g, moved(g)) for g in range(Y * Z * C)])]
    ppermute x0 -> x43, starting transfers between devices: none -> 67.7 us  [the longest x16 37.5 us: along(): return lax.ppermute(x, 'grid', [(g, moved(g)) for g in range(Y * Z * C)])]
    reduce_scatter x1 -> x0, waiting for transfers between devices: 56.4 us -> none  [per_device(): lax.psum_scatter(jnp.stack([onto_warmth, onto_wetness], axis=1), 'tm', sc...]
    pallas_call x0 -> x5, Pallas kernels: none -> 31.7 us  [the longest x2 17.6 us: backward(): pl.pallas_call(backward_kernel, grid=(width // NCHUNK,), in_specs=[pl.Blo...]
    split x3 -> x0, local copies, waits for them, and re-layouts: 18.6 us -> none  [cut_exchange(): jnp.split(parts, edges_of(parts.shape[cut], pieces), axis=cut)]
  transfers between devices with their start and end apart: 4 -> 47, of which waited for: 3 -> 23; matrix products, arithmetic and copies ran while one was open for 8% -> 11% of each run, Pallas kernels for 0% -> 5%
where the time goes in v1:
time: 340 us; the launch traced here: 337 us
  waiting for transfers between devices  144 us (42%)
  starting transfers between devices  102 us (30%)
  Pallas kernels  31.7 us (9%)
  local copies, waits for them, and re-layouts  29.2 us (9%)
  other arithmetic  28.5 us (8%)
    all_to_all x4, waiting for transfers between devices, all_to_all(): lax.all_to_all(x, axis, split_axis=0, concat_axis=0, tiled=True, axis_ind...  63.5 us
    ppermute x16, waiting for transfers between devices, along(): return lax.ppermute(x, 'grid', [(g, moved(g)) for g in range(Y * Z * C)])  57.1 us
    ppermute x16, starting transfers between devices, along(): return lax.ppermute(x, 'grid', [(g, moved(g)) for g in range(Y * Z * C)])  37.5 us
    all_to_all x4, starting transfers between devices, all_to_all(): lax.all_to_all(x, axis, split_axis=0, concat_axis=0, tiled=True, axis_ind...  34 us
    ppermute x27, starting transfers between devices, shifted(): return lax.ppermute(x, 'tm', [(i, (i + by) % n) for i in range(n)])  30.3 us
    ppermute x27, waiting for transfers between devices, shifted(): return lax.ppermute(x, 'tm', [(i, (i + by) % n) for i in range(n)])  23.6 us
    pallas_call x2, Pallas kernels, backward(): pl.pallas_call(backward_kernel, grid=(width // NCHUNK,), in_specs=[pl.Blo...  17.6 us
    pallas_call x2, Pallas kernels, forward(): pl.pallas_call(forward_kernel, grid=(nb,), in_specs=[pl.BlockSpec((BLK, w...  13.8 us
  transfers between devices with their start and end apart: 47, of which 23 were waited for; matrix products, arithmetic and copies ran while one was open for 11% of the time, Pallas kernels for 5%

profile of v1, /device:TPU:1, one launch (start us, length us, event | category | flops | bytes accessed | tf_op | source)
XLA Modules:
  0.0 337.5 jit_solution(11956500830830308779)
XLA Ops:
  0.6 6.1 %copy.23 = bf16[4,32,8,3072]{3,2,0,1:T(8,128)(2,1)} copy(bf16[4,32,8,3072]{3,2,1,0:T(8,128)(2,1)} %bitcast.153) | data formatting | bytes 12582912 | tf_op jit(solution)/shard_map/reshape | solution.py:259
  6.7 9.6 %all-to-all-start.1 = ((bf16[32,32,3072]{2,1,0:T(8,128)(2,1)}), bf16[32,32,3072]{2,1,0:T(8,128)(2,1)}, u32[]{:S(2)}, u32[]{:S(2)}) async-start(bf16[32,32,3072]{2,1,0:T(8,128)(2,1)} %bitcast.152), calls=%async_computation.1 | async-start | bytes 12582912 | tf_op jit(solution)/shard_map/all_to_all | solution.py:155
  16.4 6.0 %copy.24 = bf16[4,32,8,3072]{3,2,0,1:T(8,128)(2,1)} copy(bf16[4,32,8,3072]{3,2,1,0:T(8,128)(2,1)} %bitcast.154) | data formatting | bytes 12582912 | tf_op jit(solution)/shard_map/reshape | solution.py:259
  32.2 61.5 %all-to-all-done.1 = bf16[32,32,3072]{2,1,0:T(8,128)(2,1)} async-done(((bf16[32,32,3072]{2,1,0:T(8,128)(2,1)}), bf16[32,32,3072]{2,1,0:T(8,128)(2,1)}, u32[]{:S(2)}, u32[]{:S(2)}) %all-to-all-start.1) | async-done | bytes 6291488 | tf_op jit(solution)/shard_map/all_to_all | solution.py:155
  93.7 14.7 %all-to-all-start = ((bf16[32,32,3072]{2,1,0:T(8,128)(2,1)}), bf16[32,32,3072]{2,1,0:T(8,128)(2,1)}, u32[]{:S(2)}, u32[]{:S(2)}) async-start(bf16[32,32,3072]{2,1,0:T(8,128)(2,1)} %bitcast.151), calls=%async_computation | async-start | bytes 12582912 | tf_op jit(solution)/shard_map/all_to_all | solution.py:155
  108.4 5.2 %multiply_reduce_fusion.1 = f32[3072]{0:T(1024)S(1)} fusion(bf16[32,32,3072]{2,1,0:T(8,128)(2,1)} %all-to-all-done.1, f32[32,32]{1,0:T(8,128)S(1)} %mul.179), kind=kLoop, calls=%fused_computation.1 | loop fusion | flops 9434112 | bytes 6307840 | tf_op jit(solution)/shard_map/reduce_sum | solution.py:280
  117.4 6.9 %forward.2 = (f32[1024,256]{1,0:T(8,128)S(1)}, f32[8,256]{1,0:T(8,128)S(1)}) custom-call(bf16[1024,3072]{1,0:T(8,128)(2,1)} %bitcast.3.x_ref, bf16[3072,256]{1,0:T(8,128)(2,1)S(1)} %copy-done, f32[4,264,384]{2,1,0:T(8,128)S(1)} %get-tuple-element.24.block_ref), custom_call_target="tpu_custom_call" | custom-call | flops 1610612736 | bytes 6291456 | tf_op jit(solution)/shard_map/forward/pallas_call | solution.py:60
  141.0 2.7 collective-permute-start.6
  144.8 43.7 %collective-permute-done.6 = f32[128,256]{1,0:T(8,128)S(1)} collective-permute-done((f32[128,256]{1,0:T(8,128)}, f32[128,256]{1,0:T(8,128)S(1)}, u32[]{:S(2)}, u32[]{:S(2)}) %collective-permute-start.6) | collective-permute-done | bytes 131104 | tf_op jit(solution)/shard_map/ppermute | solution.py:189
  191.4 12.1 %collective-permute-start.8 = (f32[32,256]{1,0:T(8,128)}, f32[32,256]{1,0:T(8,128)S(1)}, u32[]{:S(2)}, u32[]{:S(2)}) collective-permute-start(f32[32,256]{1,0:T(8,128)} %get-tuple-element.46), channel_id=1, source_target_pairs={{0,4},{1,5},{2,6},{3,7},{4,0},{5,1},{6,2},{7,3},{8,12},{9,13},{10,... | collective-permute-start | bytes 98312 | tf_op jit(solution)/shard_map/ppermute | solution.py:189
  212.1 4.3 %collective-permute-start.14 = (bf16[128,256]{1,0:T(8,128)(2,1)S(1)}, bf16[128,256]{1,0:T(8,128)(2,1)S(1)}, u32[]{:S(2)}, u32[]{:S(2)}) collective-permute-start(bf16[128,256]{1,0:T(8,128)(2,1)S(1)} %bitcast.167), channel_id=1, source_target_pairs={{0,16},{1,17},{2,18},{3,19},{4,20},{5,21},{6,22},{7,23},{8,24},{9,... | collective-permute-start | bytes 196616 | tf_op jit(solution)/shard_map/ppermute | solution.py:189
  219.5 5.9 %collective-permute-start.16 = (bf16[512,256]{1,0:T(8,128)(2,1)S(1)}, bf16[512,256]{1,0:T(8,128)(2,1)S(1)}, u32[]{:S(2)}, u32[]{:S(2)}) collective-permute-start(bf16[512,256]{1,0:T(8,128)(2,1)S(1)} %bitcast.162), channel_id=1, source_target_pairs={{0,1},{1,0},{2,3},{3,2},{4,5},{5,4},{6,7},{7,6},{8,9},{9,8},{10,11... | collective-permute-start | bytes 786440 | tf_op jit(solution)/shard_map/ppermute | solution.py:189
  229.8 6.9 %forward.3 = (f32[1024,256]{1,0:T(8,128)S(1)}, f32[8,256]{1,0:T(8,128)S(1)}) custom-call(bf16[1024,3072]{1,0:T(8,128)(2,1)} %bitcast.1.x_ref, bf16[3072,256]{1,0:T(8,128)(2,1)S(1)} %copy-done.1, f32[4,264,384]{2,1,0:T(8,128)S(1)} %get-tuple-element.23.block_ref), custom_call_target="tpu_custom_call" | custom-call | flops 1610612736 | bytes 6291456 | tf_op jit(solution)/shard_map/forward/pallas_call | solution.py:60
  247.9 5.1 %multiply_reduce_fusion = f32[3072]{0:T(1024)S(1)} fusion(bf16[1024,3072]{1,0:T(8,128)(2,1)} %bitcast.1.x_ref, f32[1024]{0:T(1024)S(1)} %bitcast.176), kind=kLoop, calls=%fused_computation | loop fusion | flops 9434112 | bytes 6307840 | tf_op jit(solution)/shard_map/reduce_sum | solution.py:280
  255.3 4.7 %all-to-all-start.2 = ((bf16[16,32,256]{2,1,0:T(8,128)(2,1)}), bf16[16,32,256]{2,1,0:T(8,128)(2,1)}, u32[]{:S(2)}, u32[]{:S(2)}) async-start(bf16[16,32,256]{2,1,0:T(8,128)(2,1)} %bitcast.161), calls=%async_computation.2 | async-start | bytes 524288 | tf_op jit(solution)/shard_map/all_to_all | solution.py:155
  263.9 8.8 %backward.3 = bf16[256,3072]{1,0:T(8,128)(2,1)S(1)} custom-call(bf16[1024,256]{1,0:T(8,128)(2,1)S(1)} %bitcast.147, f32[4,264,384]{2,1,0:T(8,128)S(1)} %get-tuple-element.23.block_ref, bf16[1024,3072]{1,0:T(8,128)(2,1)} %bitcast.1.x_ref, f32[8,3072]{1,0:T(8,128)S(1)} %broadcast_in_dim.213.enter_ref), custom_call_target="tpu_custom_call" | custom-call | flops 3221225472 | bytes 6291456 | tf_op jit(solution)/shard_map/backward/pallas_call | solution.py:112
  273.6 2.7 collective-permute-start.34
  279.6 5.0 %all-to-all-start.3 = ((bf16[16,32,256]{2,1,0:T(8,128)(2,1)}), bf16[16,32,256]{2,1,0:T(8,128)(2,1)}, u32[]{:S(2)}, u32[]{:S(2)}) async-start(bf16[16,32,256]{2,1,0:T(8,128)(2,1)} %broadcast_in_dim.207), calls=%async_computation.3 | async-start | bytes 524288 | tf_op jit(solution)/shard_map/all_to_all | solution.py:155
  287.3 2.7 collective-permute-start.39
  292.0 4.3 %collective-permute-start.24 = (bf16[512,256]{1,0:T(8,128)(2,1)}, bf16[512,256]{1,0:T(8,128)(2,1)S(1)}, u32[]{:S(2)}, u32[]{:S(2)}) collective-permute-start(bf16[512,256]{1,0:T(8,128)(2,1)} %bitcast.50), channel_id=1, source_target_pairs={{0,1},{1,0},{2,3},{3,2},{4,5},{5,4},{6,7},{7,6},{8,9},{9,8},{10,11... | collective-permute-start | bytes 786440 | tf_op jit(solution)/shard_map/ppermute | solution.py:189
  298.5 8.8 %backward.2 = bf16[256,3072]{1,0:T(8,128)(2,1)S(1)} custom-call(bf16[1024,256]{1,0:T(8,128)(2,1)S(1)} %bitcast.145, f32[4,264,384]{2,1,0:T(8,128)S(1)} %get-tuple-element.24.block_ref, bf16[1024,3072]{1,0:T(8,128)(2,1)} %bitcast.3.x_ref, f32[8,3072]{1,0:T(8,128)S(1)} %broadcast_in_dim.205.enter_ref), custom_call_target="tpu_custom_call" | custom-call | flops 3221225472 | bytes 6291456 | tf_op jit(solution)/shard_map/backward/pallas_call | solution.py:112
  308.9 2.7 collective-permute-start.42
  315.2 9.9 %collective-permute-done.29 = bf16[64,1536]{1,0:T(8,128)(2,1)S(1)} collective-permute-done((bf16[64,1536]{1,0:T(8,128)(2,1)S(1)}, bf16[64,1536]{1,0:T(8,128)(2,1)S(1)}, u32[]{:S(2)}, u32[]{:S(2)}) %collective-permute-start.29) | collective-permute-done | bytes 196640 | tf_op jit(solution)/shard_map/ppermute | solution.py:164
  332.2 4.2 %collective-permute-done.27 = bf16[64,1536]{1,0:T(8,128)(2,1)S(1)} collective-permute-done((bf16[64,1536]{1,0:T(8,128)(2,1)S(1)}, bf16[64,1536]{1,0:T(8,128)(2,1)S(1)}, u32[]{:S(2)}, u32[]{:S(2)}) %collective-permute-start.27) | collective-permute-done | bytes 196640 | tf_op jit(solution)/shard_map/ppermute | solution.py:164
  (209 shorter events, 91.5 us)
Async XLA Ops:
  6.7 86.9 %all-to-all-start.1 = ((bf16[32,32,3072]{2,1,0:T(8,128)(2,1)}), bf16[32,32,3072]{2,1,0:T(8,128)(2,1)}, u32[]{:S(2)}, u32[]{:S(2)}) async-start(bf16[32,32,3072]{2,1,0:T(8,128)(2,1)} %bitcast.152), calls=%async_computation.1 | async-start | bytes 12582912 | tf_op jit(solution)/shard_map/all_to_all | solution.py:155
  93.7 134.0 %all-to-all-start = ((bf16[32,32,3072]{2,1,0:T(8,128)(2,1)}), bf16[32,32,3072]{2,1,0:T(8,128)(2,1)}, u32[]{:S(2)}, u32[]{:S(2)}) async-start(bf16[32,32,3072]{2,1,0:T(8,128)(2,1)} %bitcast.151), calls=%async_computation | async-start | bytes 12582912 | tf_op jit(solution)/shard_map/all_to_all | solution.py:155
  113.7 14.0 %collective-permute-start.19 = (f32[8,3072]{1,0:T(8,128)S(1)}, f32[8,3072]{1,0:T(8,128)S(1)}, u32[]{:S(2)}, u32[]{:S(2)}) collective-permute-start(f32[8,3072]{1,0:T(8,128)S(1)} %maximum_maximum_fusion), channel_id=1, source_target_pairs={{0,96},{32,0},{64,32},{96,64},{1,97},{33,1},{65,33},{97,65},{2,98}... | collective-permute-start | bytes 294920 | tf_op jit(solution)/shard_map/ppermute | solution.py:164
  116.3 11.5 %collective-permute-start.18 = (f32[8,3072]{1,0:T(8,128)S(1)}, f32[8,3072]{1,0:T(8,128)S(1)}, u32[]{:S(2)}, u32[]{:S(2)}) collective-permute-start(f32[8,3072]{1,0:T(8,128)S(1)} %maximum_maximum_fusion), channel_id=1, source_target_pairs={{0,64},{32,96},{64,0},{96,32},{1,65},{33,97},{65,1},{97,33},{2,66}... | collective-permute-start | bytes 294920 | tf_op jit(solution)/shard_map/ppermute | solution.py:164
  116.8 10.9 %collective-permute-start.17 = (f32[8,3072]{1,0:T(8,128)S(1)}, f32[8,3072]{1,0:T(8,128)S(1)}, u32[]{:S(2)}, u32[]{:S(2)}) collective-permute-start(f32[8,3072]{1,0:T(8,128)S(1)} %maximum_maximum_fusion), channel_id=1, source_target_pairs={{0,32},{32,64},{64,96},{96,0},{1,33},{33,65},{65,97},{97,1},{2,34}... | collective-permute-start | bytes 294920 | tf_op jit(solution)/shard_map/ppermute | solution.py:164
  141.0 47.5 %collective-permute-start.6 = (f32[128,256]{1,0:T(8,128)}, f32[128,256]{1,0:T(8,128)S(1)}, u32[]{:S(2)}, u32[]{:S(2)}) collective-permute-start(f32[128,256]{1,0:T(8,128)} %get-tuple-element.34), channel_id=1, source_target_pairs={{0,24},{1,25},{2,26},{3,27},{4,28},{5,29},{6,30},{7,31},{8,0},{9,1... | collective-permute-start | bytes 393224 | tf_op jit(solution)/shard_map/ppermute | solution.py:189
  143.7 45.3 %collective-permute-start.5 = (f32[128,256]{1,0:T(8,128)}, f32[128,256]{1,0:T(8,128)}, u32[]{:S(2)}, u32[]{:S(2)}) collective-permute-start(f32[128,256]{1,0:T(8,128)} %get-tuple-element.35), channel_id=1, source_target_pairs={{0,16},{1,17},{2,18},{3,19},{4,20},{5,21},{6,22},{7,23},{8,24},{9,... | collective-permute-start | bytes 393224 | tf_op jit(solution)/shard_map/ppermute | solution.py:189
  144.2 45.4 %collective-permute-start.4 = (f32[128,256]{1,0:T(8,128)S(1)}, f32[128,256]{1,0:T(8,128)}, u32[]{:S(2)}, u32[]{:S(2)}) collective-permute-start(f32[128,256]{1,0:T(8,128)S(1)} %get-tuple-element.33), channel_id=1, source_target_pairs={{0,8},{1,9},{2,10},{3,11},{4,12},{5,13},{6,14},{7,15},{8,16},{9,17... | collective-permute-start | bytes 393224 | tf_op jit(solution)/shard_map/ppermute | solution.py:189
  191.4 12.1 %collective-permute-start.9 = (f32[32,256]{1,0:T(8,128)}, f32[32,256]{1,0:T(8,128)S(1)}, u32[]{:S(2)}, u32[]{:S(2)}) collective-permute-start(f32[32,256]{1,0:T(8,128)} %get-tuple-element.45), channel_id=1, source_target_pairs={{0,6},{1,7},{2,0},{3,1},{4,2},{5,3},{6,4},{7,5},{8,14},{9,15},{10,... | collective-permute-start | bytes 98312 | tf_op jit(solution)/shard_map/ppermute | solution.py:189
  191.4 13.6 %collective-permute-start.8 = (f32[32,256]{1,0:T(8,128)}, f32[32,256]{1,0:T(8,128)S(1)}, u32[]{:S(2)}, u32[]{:S(2)}) collective-permute-start(f32[32,256]{1,0:T(8,128)} %get-tuple-element.46), channel_id=1, source_target_pairs={{0,4},{1,5},{2,6},{3,7},{4,0},{5,1},{6,2},{7,3},{8,12},{9,13},{10,... | collective-permute-start | bytes 98312 | tf_op jit(solution)/shard_map/ppermute | solution.py:189
  255.3 22.6 %all-to-all-start.2 = ((bf16[16,32,256]{2,1,0:T(8,128)(2,1)}), bf16[16,32,256]{2,1,0:T(8,128)(2,1)}, u32[]{:S(2)}, u32[]{:S(2)}) async-start(bf16[16,32,256]{2,1,0:T(8,128)(2,1)} %bitcast.161), calls=%async_computation.2 | async-start | bytes 524288 | tf_op jit(solution)/shard_map/all_to_all | solution.py:155
  273.6 11.0 %collective-permute-start.35 = (bf16[64,1536]{1,0:T(8,128)(2,1)}, bf16[64,1536]{1,0:T(8,128)(2,1)}, u32[]{:S(2)}, u32[]{:S(2)}) collective-permute-start(bf16[64,1536]{1,0:T(8,128)(2,1)} %get-tuple-element.38), channel_id=1, source_target_pairs={{0,32},{32,64},{64,96},{96,0},{1,33},{33,65},{65,97},{97,1},{2,34}... | collective-permute-start | bytes 589832 | tf_op jit(solution)/shard_map/ppermute | solution.py:164
  273.6 22.7 %collective-permute-start.34 = (bf16[64,1536]{1,0:T(8,128)(2,1)S(1)}, bf16[64,1536]{1,0:T(8,128)(2,1)}, u32[]{:S(2)}, u32[]{:S(2)}) collective-permute-start(bf16[64,1536]{1,0:T(8,128)(2,1)S(1)} %slice.278), channel_id=1, source_target_pairs={{0,96},{32,0},{64,32},{96,64},{1,97},{33,1},{65,33},{97,65},{2,98}... | collective-permute-start | bytes 589832 | tf_op jit(solution)/shard_map/ppermute | solution.py:164
  276.3 10.0 %collective-permute-start.38 = (bf16[64,1536]{1,0:T(8,128)(2,1)S(1)}, bf16[64,1536]{1,0:T(8,128)(2,1)}, u32[]{:S(2)}, u32[]{:S(2)}) collective-permute-start(bf16[64,1536]{1,0:T(8,128)(2,1)S(1)} %get-tuple-element.39), channel_id=1, source_target_pairs={{0,96},{32,0},{64,32},{96,64},{1,97},{33,1},{65,33},{97,65},{2,98}... | collective-permute-start | bytes 589832 | tf_op jit(solution)/shard_map/ppermute | solution.py:164
  276.4 19.9 %collective-permute-start.37 = (bf16[64,1536]{1,0:T(8,128)(2,1)S(1)}, bf16[64,1536]{1,0:T(8,128)(2,1)}, u32[]{:S(2)}, u32[]{:S(2)}) collective-permute-start(bf16[64,1536]{1,0:T(8,128)(2,1)S(1)} %slice.282), channel_id=1, source_target_pairs={{0,32},{32,64},{64,96},{96,0},{1,33},{33,65},{65,97},{97,1},{2,34}... | collective-permute-start | bytes 589832 | tf_op jit(solution)/shard_map/ppermute | solution.py:164
  279.6 12.4 %all-to-all-start.3 = ((bf16[16,32,256]{2,1,0:T(8,128)(2,1)}), bf16[16,32,256]{2,1,0:T(8,128)(2,1)}, u32[]{:S(2)}, u32[]{:S(2)}) async-start(bf16[16,32,256]{2,1,0:T(8,128)(2,1)} %broadcast_in_dim.207), calls=%async_computation.3 | async-start | bytes 524288 | tf_op jit(solution)/shard_map/all_to_all | solution.py:155
  286.3 10.0 %collective-permute-start.36 = (bf16[64,1536]{1,0:T(8,128)(2,1)}, bf16[64,1536]{1,0:T(8,128)(2,1)S(1)}, u32[]{:S(2)}, u32[]{:S(2)}) collective-permute-start(bf16[64,1536]{1,0:T(8,128)(2,1)} %add_convert_fusion.1), channel_id=1, source_target_pairs={{0,32},{32,64},{64,96},{96,0},{1,33},{33,65},{65,97},{97,1},{2,34}... | collective-permute-start | bytes 589832 | tf_op jit(solution)/shard_map/ppermute | solution.py:164
  308.9 17.7 %collective-permute-start.42 = (bf16[256,256]{1,0:T(8,128)(2,1)S(1)}, bf16[256,256]{1,0:T(8,128)(2,1)S(1)}, u32[]{:S(2)}, u32[]{:S(2)}) collective-permute-start(bf16[256,256]{1,0:T(8,128)(2,1)S(1)} %cross.1), channel_id=1, source_target_pairs={{0,96},{32,0},{64,32},{96,64},{1,97},{33,1},{65,33},{97,65},{2,98}... | collective-permute-start | bytes 393224 | tf_op jit(solution)/shard_map/ppermute | solution.py:164
  311.7 15.1 %collective-permute-start.41 = (bf16[256,256]{1,0:T(8,128)(2,1)S(1)}, bf16[256,256]{1,0:T(8,128)(2,1)S(1)}, u32[]{:S(2)}, u32[]{:S(2)}) collective-permute-start(bf16[256,256]{1,0:T(8,128)(2,1)S(1)} %cross.1), channel_id=1, source_target_pairs={{0,64},{32,96},{64,0},{96,32},{1,65},{33,97},{65,1},{97,33},{2,66}... | collective-permute-start | bytes 393224 | tf_op jit(solution)/shard_map/ppermute | solution.py:164
  312.2 17.2 %collective-permute-start.40 = (bf16[256,256]{1,0:T(8,128)(2,1)S(1)}, bf16[256,256]{1,0:T(8,128)(2,1)S(1)}, u32[]{:S(2)}, u32[]{:S(2)}) collective-permute-start(bf16[256,256]{1,0:T(8,128)(2,1)S(1)} %cross.1), channel_id=1, source_target_pairs={{0,32},{32,64},{64,96},{96,0},{1,33},{33,65},{65,97},{97,1},{2,34}... | collective-permute-start | bytes 393224 | tf_op jit(solution)/shard_map/ppermute | solution.py:164
  312.8 17.4 %collective-permute-start.25 = (bf16[64,1536]{1,0:T(8,128)(2,1)S(1)}, bf16[64,1536]{1,0:T(8,128)(2,1)S(1)}, u32[]{:S(2)}, u32[]{:S(2)}) collective-permute-start(bf16[64,1536]{1,0:T(8,128)(2,1)S(1)} %slice.263), channel_id=1, source_target_pairs={{0,96},{32,0},{64,32},{96,64},{1,97},{33,1},{65,33},{97,65},{2,98}... | collective-permute-start | bytes 589832 | tf_op jit(solution)/shard_map/ppermute | solution.py:164
  315.0 10.1 %collective-permute-start.29 = (bf16[64,1536]{1,0:T(8,128)(2,1)S(1)}, bf16[64,1536]{1,0:T(8,128)(2,1)S(1)}, u32[]{:S(2)}, u32[]{:S(2)}) collective-permute-start(bf16[64,1536]{1,0:T(8,128)(2,1)S(1)} %get-tuple-element.43), channel_id=1, source_target_pairs={{0,96},{32,0},{64,32},{96,64},{1,97},{33,1},{65,33},{97,65},{2,98}... | collective-permute-start | bytes 589832 | tf_op jit(solution)/shard_map/ppermute | solution.py:164
  326.6 9.7 %collective-permute-start.27 = (bf16[64,1536]{1,0:T(8,128)(2,1)S(1)}, bf16[64,1536]{1,0:T(8,128)(2,1)S(1)}, u32[]{:S(2)}, u32[]{:S(2)}) collective-permute-start(bf16[64,1536]{1,0:T(8,128)(2,1)S(1)} %add_convert_fusion.3), channel_id=1, source_target_pairs={{0,32},{32,64},{64,96},{96,0},{1,33},{33,65},{65,97},{97,1},{2,34}... | collective-permute-start | bytes 589832 | tf_op jit(solution)/shard_map/ppermute | solution.py:164
  326.7 9.6 %collective-permute-start.30 = (bf16[64,1536]{1,0:T(8,128)(2,1)S(1)}, bf16[64,1536]{1,0:T(8,128)(2,1)S(1)}, u32[]{:S(2)}, u32[]{:S(2)}) collective-permute-start(bf16[64,1536]{1,0:T(8,128)(2,1)S(1)} %add_convert_fusion.2), channel_id=1, source_target_pairs={{0,96},{32,0},{64,32},{96,64},{1,97},{33,1},{65,33},{97,65},{2,98}... | collective-permute-start | bytes 589832 | tf_op jit(solution)/shard_map/ppermute | solution.py:164
  (36 other events, 266.4 us)

commit v2 on v1

v2 whole, which is shorter than its diff:
```python
import jax
import jax.numpy as jnp
from jax import lax
from jax.experimental import pallas as pl
from jax.experimental.pallas import tpu as pltpu
from jax.sharding import PartitionSpec as P


BLK = 256
NCHUNK = 512
Y, Z, C = 4, 4, 2
F32, BF16 = jnp.float32, jnp.bfloat16
HIGHEST = lax.Precision.HIGHEST


def decay_blocks(fading):
    nb = fading.shape[1] // BLK
    a = fading.reshape(2, nb, BLK)
    log_a = jnp.log(a)
    inclusive = jnp.cumsum(log_a, axis=2)
    before = jnp.concatenate([jnp.zeros((2, nb, 1), F32), inclusive, jnp.zeros((2, nb, 7), F32)], axis=2)
    rows, cols = BLK + 8, BLK + 128
    r = lax.broadcasted_iota(jnp.int32, (rows, cols), 0)
    c = lax.broadcasted_iota(jnp.int32, (rows, cols), 1)
    pad = lambda v: jnp.pad(v, ((0, 0), (0, 0), (0, 128)))
    spread = before[..., :, None] - pad(inclusive)[..., None, :]
    gain = pad(1.0 - a)[..., None, :]
    gain = jnp.where(c == BLK, 1.0, gain)
    weight = jnp.exp(jnp.minimum(spread, 0.0)) * gain
    weight = jnp.where((c < jnp.minimum(r, BLK)) | (c == BLK), weight, 0.0)
    sign = jnp.where((r < BLK) == (c < BLK), -1.0, 1.0)
    block = jnp.where(r == c, jnp.where(r < BLK, 1.0, sign * weight), sign * weight)
    block = jnp.where(r <= BLK, block, 0.0)
    total = inclusive[..., -1]
    ahead = jnp.cumsum(total, axis=1) - total
    since_start = jnp.exp(ahead[..., None] + before[..., :BLK]).reshape(2, nb * BLK)
    behind = jnp.cumsum(total[:, ::-1], axis=1)[:, ::-1] - total
    to_end = jnp.exp(behind[..., None] + inclusive[..., -1:] - inclusive) * (1.0 - a)
    return block, since_start, to_end.reshape(2, nb * BLK), jnp.exp(total.sum(axis=1))


def pack_kernel(x0_ref, x1_ref, out_ref):
    out_ref[0, 0] = x0_ref[...]
    out_ref[0, 1] = x1_ref[...]


def pack(x0, x1, n):
    rows, points = x0.shape
    width = points // n
    return pl.pallas_call(
        pack_kernel,
        grid=(n,),
        in_specs=[pl.BlockSpec((rows, width), lambda i: (0, i))] * 2,
        out_specs=pl.BlockSpec((1, 2, rows, width), lambda i: (i, 0, 0, 0)),
        out_shape=jax.ShapeDtypeStruct((n, 2, rows, width), x0.dtype),
        compiler_params=pltpu.CompilerParams(vmem_limit_bytes=16 << 20),
        cost_estimate=pl.CostEstimate(flops=0, bytes_accessed=8 * x0.size, transcendentals=0),
        name="pack",
    )(x0, x1)


def forward_kernel(x_ref, op_ref, block_ref, p_ref, end_ref, state):
    b = pl.program_id(1)

    @pl.when(b == 0)
    def _():
        state[...] = jnp.zeros_like(state)

    x = x_ref[:, 0].reshape(BLK, x_ref.shape[3])
    y = jnp.dot(x, op_ref[0], preferred_element_type=F32)
    out = jnp.dot(block_ref[0, 0, :, :BLK], y, precision=HIGHEST, preferred_element_type=F32)
    out = out - block_ref[0, 0, :, BLK : BLK + 1] * state[0:1, :]
    p_ref[0] = out[:BLK]
    state[...] = out[BLK:]
    end_ref[0] = out[BLK:]


def forward(x, operators, block):
    n, _, rows, width = x.shape
    rank = operators.shape[2]
    hours = n * rows
    nb, per = hours // BLK, BLK // rows
    return pl.pallas_call(
        forward_kernel,
        grid=(2, nb),
        in_specs=[
            pl.BlockSpec((per, 1, rows, width), lambda f, b: (b, f, 0, 0)),
            pl.BlockSpec((1, width, rank), lambda f, b: (f, 0, 0)),
            pl.BlockSpec((1, 1, BLK + 8, BLK + 128), lambda f, b: (f, b, 0, 0)),
        ],
        out_specs=[
            pl.BlockSpec((1, BLK, rank), lambda f, b: (f, b, 0)),
            pl.BlockSpec((1, 8, rank), lambda f, b: (f, 0, 0)),
        ],
        out_shape=[
            jax.ShapeDtypeStruct((2, hours, rank), F32),
            jax.ShapeDtypeStruct((2, 8, rank), F32),
        ],
        scratch_shapes=[pltpu.VMEM((8, rank), F32)],
        compiler_params=pltpu.CompilerParams(vmem_limit_bytes=24 << 20),
        cost_estimate=pl.CostEstimate(
            flops=4 * hours * width * rank, bytes_accessed=4 * hours * width, transcendentals=0
        ),
        name="forward",
    )(x, operators, block)


def backward_kernel(q_ref, block_ref, x_ref, enter_ref, w_ref, z_high, z_low, carried):
    @pl.when(pl.program_id(0) == 0)
    def _():
        nb = block_ref.shape[1]
        reverse = jnp.zeros((q_ref.shape[2], 1), F32)
        for b in reversed(range(nb)):
            q = q_ref[0, b * BLK : (b + 1) * BLK, :].astype(F32)
            out = jnp.dot(q.T, block_ref[0, b, :BLK, :], precision=HIGHEST, preferred_element_type=F32)
            out = out - reverse * block_ref[0, b, BLK : BLK + 1, :]
            z = out[:, :BLK]
            high = z.astype(BF16)
            z_high[:, b * BLK : (b + 1) * BLK] = high
            z_low[:, b * BLK : (b + 1) * BLK] = (z - high.astype(F32)).astype(BF16)
            reverse = out[:, BLK : BLK + 1]
        carried[...] = jnp.broadcast_to(reverse, carried.shape)

    x = x_ref[:, 0].reshape(z_high.shape[1], x_ref.shape[3])
    w = jnp.dot(z_high[...], x, preferred_element_type=F32)
    w = w + jnp.dot(z_low[...], x, preferred_element_type=F32)
    w = w - carried[:, 0:1] * enter_ref[0, 0:1, :]
    w_ref[...] = w.astype(w_ref.dtype)


def backward(f, q, block, x, enter):
    n, _, rows, width = x.shape
    hours, rank = q.shape[1:]
    nb = hours // BLK
    return pl.pallas_call(
        backward_kernel,
        grid=(width // NCHUNK,),
        in_specs=[
            pl.BlockSpec((1, hours, rank), lambda i: (1 - f, 0, 0)),
            pl.BlockSpec((1, nb, BLK + 8, BLK + 128), lambda i: (f, 0, 0, 0)),
            pl.BlockSpec((n, 1, rows, NCHUNK), lambda i: (0, f, 0, i)),
            pl.BlockSpec((1, 8, NCHUNK), lambda i: (f, 0, i)),
        ],
        out_specs=pl.BlockSpec((rank, NCHUNK), lambda i: (0, i)),
        out_shape=jax.ShapeDtypeStruct((rank, width), BF16),
        scratch_shapes=[
            pltpu.VMEM((rank, hours), BF16),
            pltpu.VMEM((rank, hours), BF16),
            pltpu.VMEM((rank, 128), F32),
        ],
        compiler_params=pltpu.CompilerParams(vmem_limit_bytes=24 << 20),
        cost_estimate=pl.CostEstimate(
            flops=4 * hours * width * rank, bytes_accessed=2 * hours * width, transcendentals=0
        ),
        name="backward",
    )(q, block, x, enter)


def middle_kernel(q_ref, out_ref):
    left = q_ref[0].astype(F32).T.astype(BF16)
    out_ref[...] = jnp.dot(left, q_ref[1], preferred_element_type=F32)


def cross(q):
    _, hours, rank = q.shape
    return pl.pallas_call(
        middle_kernel,
        out_shape=jax.ShapeDtypeStruct((rank, rank), F32),
        in_specs=[pl.BlockSpec(memory_space=pltpu.VMEM)],
        out_specs=pl.BlockSpec(memory_space=pltpu.VMEM),
        compiler_params=pltpu.CompilerParams(vmem_limit_bytes=8 << 20),
        cost_estimate=pl.CostEstimate(flops=2 * hours * rank * rank, bytes_accessed=2 * q.size, transcendentals=0),
        name="cross",
    )(q)


def all_to_all(x, axis, groups=None):
    return lax.all_to_all(x, axis, split_axis=0, concat_axis=0, tiled=True, axis_index_groups=groups)


def pick(x, i):
    return lax.dynamic_index_in_dim(x, i, 0, keepdims=False)


def shifted(x, by):
    n = lax.axis_size("tm")
    return lax.ppermute(x, "tm", [(i, (i + by) % n) for i in range(n)])


def entering(end, gain, start):
    message = jnp.concatenate([end, jnp.broadcast_to(gain[:, None], end.shape), jnp.zeros((4, end.shape[1]), F32)])
    i = lax.axis_index("tm")
    total, so_far = jnp.zeros_like(end), jnp.ones_like(end)
    for d in range(1, lax.axis_size("tm")):
        got = shifted(message, d)
        total = total + jnp.where(i >= d, so_far * got[:2], 0.0)
        so_far = so_far * jnp.where(i >= d, got[2:4], 1.0)
    return total + so_far * start


def across(x):
    return lax.ppermute(x, "grid", [(g, g ^ 1) for g in range(Y * Z * C)])


def summed_over_grid(p, *held):
    core = lax.axis_index("grid") % C
    _, hours, rank = p.shape
    n = Y * Z
    rows = hours // (n * C)
    groups = [[k * C + c for k in range(n)] for c in range(C)]
    p = p.reshape(2, C, n * rows, rank)
    own = lax.dynamic_index_in_dim(p, core, 1, keepdims=False)
    other = lax.dynamic_index_in_dim(p, 1 - core, 1, keepdims=False)
    p = (own + across(other)).astype(BF16).reshape(2, n, rows, rank)
    p, *held = lax.optimization_barrier((p.transpose(1, 0, 2, 3), *held))
    p = all_to_all(p, "grid", groups)
    q = p.astype(F32).sum(axis=0).astype(BF16)
    q = all_to_all(jnp.broadcast_to(q, p.shape), "grid", groups)
    q = q.transpose(1, 0, 2, 3).reshape(2, n * rows, rank)
    other = across(q)
    first = core == 0
    low, high = jnp.where(first, q, other), jnp.where(first, other, q)
    q = jnp.stack([low, high], axis=1).reshape(2, hours, rank)
    return q, *held


def summed_over_hours(w):
    n = lax.axis_size("tm")
    rank, width = w.shape
    w = w.reshape(n, rank // n, width)
    i, half = lax.axis_index("tm"), width // 2
    own, ahead, far, back = (pick(w, (i + k) % n) for k in range(n))
    add = lambda a, b: a.astype(F32) + b.astype(F32)
    up = shifted(far[:, :half], 1)
    down = shifted(far[:, half:], n - 1)
    from_below = shifted(ahead[:, half:], 1)
    from_above = shifted(back[:, :half], n - 1)
    up = shifted(add(up, ahead[:, :half]).astype(BF16), 1)
    down = shifted(add(down, back[:, half:]).astype(BF16), n - 1)
    left = add(own[:, :half], from_above) + up.astype(F32)
    right = add(own[:, half:], from_below) + down.astype(F32)
    return jnp.concatenate([left, right], axis=1)


def per_device(x0, x1, fading, starting, operator0, operator1):
    grid = lax.axis_size("grid")
    rows, points = x0.shape
    width, hours = points // grid, rows * grid
    scale = (hours * lax.axis_size("tm")) ** -0.5
    x = all_to_all(pack(x0, x1, grid), "grid")
    block, since_start, to_end, gain = decay_blocks(fading)
    operators = jnp.stack([operator0, operator1])
    start = []
    for f in range(2):
        rest, parts = starting[f], []
        for _ in range(3):
            parts.append(rest.astype(BF16))
            rest = rest - parts[-1].astype(F32)
        start.append(jnp.dot(jnp.stack(parts), operators[f], preferred_element_type=F32).sum(axis=0))
    start = jnp.stack(start)
    p, end = forward(x, operators, block)
    p = p - since_start[:, :, None] * entering(end[:, 0], gain, start)[:, None]
    q, x = summed_over_grid(p, x)
    weight = to_end.reshape(2, grid, rows).transpose(1, 0, 2)[..., None]
    mean = entering((x.astype(F32) * weight).sum(axis=(0, 2)), gain, starting)
    mean = jnp.broadcast_to(mean[:, None], (2, 8, width))
    w1 = backward(1, q, block, x, mean)
    wetness = summed_over_hours(w1) * scale
    core = lax.axis_index("grid") % C
    halves = cross(q).reshape(C, -1, q.shape[2])
    sent = pick(halves, core).astype(BF16)
    half = sent.astype(F32)
    for d in range(1, lax.axis_size("tm")):
        half = half + shifted(sent, d).astype(F32)
    other = across(half)
    middle = jnp.concatenate([jnp.where(core == 0, half, other), jnp.where(core == 0, other, half)])
    w0 = backward(0, q, block, x, mean)
    warmth = summed_over_hours(w0) * scale
    return warmth, wetness, middle * scale


def solution(mesh):
    return jax.shard_map(
        per_device,
        mesh=mesh,
        in_specs=(
            P(("tm", "grid"), None),
            P(("tm", "grid"), None),
            P(None, "tm"),
            P(None, "grid"),
            P("grid", None),
            P("grid", None),
        ),
        out_specs=(P("tm", "grid"), P("tm", "grid"), P()),
        check_vma=False,
    )
```

time: 340 us -> 350 us (1.029)
  waiting for transfers between devices: 144 us -> 202 us
  starting transfers between devices: 102 us -> 66.2 us
  local copies, waits for them, and re-layouts: 29.2 us -> 20.1 us
  other arithmetic: 28.5 us -> 24.7 us
    all_to_all x4 -> x3, waiting for transfers between devices: 63.5 us -> 176 us  [all_to_all(): lax.all_to_all(x, axis, split_axis=0, concat_axis=0, tiled=True, axis_ind...]
    ppermute x16 -> x3, waiting for transfers between devices: 57.1 us -> 2.59 us  [across(): return lax.ppermute(x, 'grid', [(g, g ^ 1) for g in range(Y * Z * C)])]
    ppermute x16 -> x3, starting transfers between devices: 37.5 us -> 8.94 us  [across(): return lax.ppermute(x, 'grid', [(g, g ^ 1) for g in range(Y * Z * C)])]
    ppermute x27 -> x21, starting transfers between devices: 30.3 us -> 17.9 us  [shifted(): return lax.ppermute(x, 'tm', [(i, (i + by) % n) for i in range(n)])]
    reshape x2 -> x0, local copies, waits for them, and re-layouts: 12.1 us -> none  [tile(): x = x.reshape(rows, grid, width).transpose(1, 0, 2)]
    unnamed x32 -> x25, local copies, waits for them, and re-layouts: 7.5 us -> 14.7 us
    all_to_all x4 -> x3, starting transfers between devices: 34 us -> 39.4 us  [all_to_all(): lax.all_to_all(x, axis, split_axis=0, concat_axis=0, tiled=True, axis_ind...]
    reduce_sum x3 -> x2, other arithmetic: 11.3 us -> 9.66 us  [the longest x1 8.54 us: per_device(): mean = entering((x.astype(F32) * weight).sum(axis=(0, 2)), gain, starting)]
  transfers between devices with their start and end apart: 47 -> 27, of which waited for: 23 -> 14; matrix products, arithmetic and copies ran while one was open for 11% -> 6% of each run, Pallas kernels for 5% -> 0%
where the time goes in v2:
time: 350 us; the launch traced here: 348 us
  waiting for transfers between devices  202 us (58%)
  starting transfers between devices  66.2 us (19%)
  Pallas kernels  33 us (9%)
  other arithmetic  24.7 us (7%)
  local copies, waits for them, and re-layouts  20.1 us (6%)
    all_to_all x3, waiting for transfers between devices, all_to_all(): lax.all_to_all(x, axis, split_axis=0, concat_axis=0, tiled=True, axis_ind...  176 us
    all_to_all x3, starting transfers between devices, all_to_all(): lax.all_to_all(x, axis, split_axis=0, concat_axis=0, tiled=True, axis_ind...  39.4 us
    ppermute x21, waiting for transfers between devices, shifted(): return lax.ppermute(x, 'tm', [(i, (i + by) % n) for i in range(n)])  23.7 us
    ppermute x21, starting transfers between devices, shifted(): return lax.ppermute(x, 'tm', [(i, (i + by) % n) for i in range(n)])  17.9 us
    pallas_call x2, Pallas kernels, backward(): pl.pallas_call(backward_kernel, grid=(width // NCHUNK,), in_specs=[pl.Blo...  17.7 us
    unnamed x25, local copies, waits for them, and re-layouts  14.7 us
    pallas_call x1, Pallas kernels, forward(): pl.pallas_call(forward_kernel, grid=(2, nb), in_specs=[pl.BlockSpec((per,...  12.6 us
    ppermute x3, starting transfers between devices, across(): return lax.ppermute(x, 'grid', [(g, g ^ 1) for g in range(Y * Z * C)])  8.94 us
  transfers between devices with their start and end apart: 27, of which 14 were waited for; matrix products, arithmetic and copies ran while one was open for 6% of the time, Pallas kernels for 0%

profile of v2, /device:TPU:1, one launch (start us, length us, event | category | flops | bytes accessed | tf_op | source)
XLA Modules:
  0.0 347.7 jit_solution(9708461396768008152)
XLA Ops:
  0.6 2.8 copy-done.2
  3.4 2.8 copy-done.3
  6.2 2.3 pack.1
  8.6 4.5 %copy-done = bf16[32,2,32,3072]{3,2,1,0:T(8,128)(2,1)} copy-done((bf16[32,2,32,3072]{3,2,1,0:T(8,128)(2,1)}, bf16[32,2,32,3072]{3,2,1,0:T(8,128)(2,1)S(1)}, u32[]{:S(2)}) %copy-start) | copy-done | bytes 12582936
  13.1 9.8 %all-to-all-start = ((bf16[32,2,32,3072]{3,2,1,0:T(8,128)(2,1)}), bf16[32,2,32,3072]{3,2,1,0:T(8,128)(2,1)}, u32[]{:S(2)}, u32[]{:S(2)}) async-start(bf16[32,2,32,3072]{3,2,1,0:T(8,128)(2,1)} %copy-done), calls=%async_computation | async-start | bytes 25165824 | tf_op jit(solution)/shard_map/all_to_all | solution.py:178
  22.9 2.4 reduce-window.6
  31.0 166.9 %all-to-all-done.x_ref = bf16[32,2,32,3072]{3,2,1,0:T(8,128)(2,1)} async-done(((bf16[32,2,32,3072]{3,2,1,0:T(8,128)(2,1)}), bf16[32,2,32,3072]{3,2,1,0:T(8,128)(2,1)}, u32[]{:S(2)}, u32[]{:S(2)}) %all-to-all-start) | async-done | bytes 12582944 | tf_op jit(solution)/shard_map/all_to_all | solution.py:178
  199.9 12.6 %forward.1 = (f32[2,1024,256]{2,1,0:T(8,128)S(1)}, f32[2,8,256]{2,1,0:T(8,128)S(1)}) custom-call(bf16[32,2,32,3072]{3,2,1,0:T(8,128)(2,1)} %all-to-all-done.x_ref, bf16[2,3072,256]{2,1,0:T(8,128)(2,1)S(1)} %copy-done.1, f32[2,4,264,384]{3,2,1,0:T(8,128)S(1)} %fusion.block_ref), custom_call_target="tpu_custom_call" | custom-call | flops 3221225472 | bytes 12582912 | tf_op jit(solution)/shard_map/forward/pallas_call | solution.py:83
  213.8 2.5 collective-permute-start.2
  217.8 2.5 collective-permute-done.1
  224.9 4.2 %collective-permute-start.3 = (f32[2,512,256]{2,1,0:T(8,128)}, f32[2,512,256]{2,1,0:T(8,128)}, u32[]{:S(2)}, u32[]{:S(2)}) collective-permute-start(f32[2,512,256]{2,1,0:T(8,128)} %dynamic-slice_bitcast_fusion), channel_id=1, source_target_pairs={{0,1},{1,0},{2,3},{3,2},{4,5},{5,4},{6,7},{7,6},{8,9},{9,8},{10,11... | collective-permute-start | bytes 3145736 | tf_op jit(solution)/shard_map/ppermute | solution.py:202
  234.2 24.8 %all-to-all-start.1 = ((bf16[16,2,32,256]{3,2,1,0:T(8,128)(2,1)}), bf16[16,2,32,256]{3,2,1,0:T(8,128)(2,1)}, u32[]{:S(2)}, u32[]{:S(2)}) async-start(bf16[16,2,32,256]{3,2,1,0:T(8,128)(2,1)} %copy.35), calls=%async_computation.1 | async-start | bytes 1048576 | tf_op jit(solution)/shard_map/all_to_all | solution.py:178
  259.0 8.5 %multiply_reduce_fusion = f32[2,3072]{1,0:T(2,128)S(1)} fusion(bf16[32,2,32,3072]{3,2,1,0:T(8,128)(2,1)} %all-to-all-done.x_ref, f32[32,2,32]{2,1,0:T(2,128)S(1)} %copy.38), kind=kLoop, calls=%fused_computation | loop fusion | flops 18868224 | bytes 12615680 | tf_op jit(solution)/shard_map/reduce_sum | solution.py:265
  271.4 4.8 %all-to-all-start.2 = ((bf16[16,2,32,256]{3,2,1,0:T(8,128)(2,1)}), bf16[16,2,32,256]{3,2,1,0:T(8,128)(2,1)}, u32[]{:S(2)}, u32[]{:S(2)}) async-start(bf16[16,2,32,256]{3,2,1,0:T(8,128)(2,1)} %broadcast_in_dim.121), calls=%async_computation.2 | async-start | bytes 1048576 | tf_op jit(solution)/shard_map/all_to_all | solution.py:178
  278.5 6.8 %all-to-all-done.2 = bf16[16,2,32,256]{3,2,1,0:T(8,128)(2,1)} async-done(((bf16[16,2,32,256]{3,2,1,0:T(8,128)(2,1)}), bf16[16,2,32,256]{3,2,1,0:T(8,128)(2,1)}, u32[]{:S(2)}, u32[]{:S(2)}) %all-to-all-start.2) | async-done | bytes 524320 | tf_op jit(solution)/shard_map/all_to_all | solution.py:178
  286.3 3.6 %collective-permute-start.4 = (bf16[2,512,256]{2,1,0:T(8,128)(2,1)S(1)}, bf16[2,512,256]{2,1,0:T(8,128)(2,1)S(1)}, u32[]{:S(2)}, u32[]{:S(2)}) collective-permute-start(bf16[2,512,256]{2,1,0:T(8,128)(2,1)S(1)} %bitcast.80), channel_id=1, source_target_pairs={{0,1},{1,0},{2,3},{3,2},{4,5},{5,4},{6,7},{7,6},{8,9},{9,8},{10,11... | collective-permute-start | bytes 1572872 | tf_op jit(solution)/shard_map/ppermute | solution.py:202
  291.7 8.9 %backward.2 = bf16[256,3072]{1,0:T(8,128)(2,1)S(1)} custom-call(bf16[2,1024,256]{2,1,0:T(8,128)(2,1)S(1)} %bitcast.69, f32[2,4,264,384]{3,2,1,0:T(8,128)S(1)} %fusion.block_ref, bf16[32,2,32,3072]{3,2,1,0:T(8,128)(2,1)} %all-to-all-done.x_ref, f32[2,8,3072]{2,1,0:T(8,128)S(1)} %broadcast_in_dim.127.enter_ref), custom_call_target="tpu_custom_call" | custom-call | flops 3221225472 | bytes 6291456 | tf_op jit(solution)/shard_map/backward/pallas_call | solution.py:135
  300.6 8.9 %backward.3 = bf16[256,3072]{1,0:T(8,128)(2,1)S(1)} custom-call(bf16[2,1024,256]{2,1,0:T(8,128)(2,1)S(1)} %bitcast.70, f32[2,4,264,384]{3,2,1,0:T(8,128)S(1)} %fusion.block_ref, bf16[32,2,32,3072]{3,2,1,0:T(8,128)(2,1)} %all-to-all-done.x_ref, f32[2,8,3072]{2,1,0:T(8,128)S(1)} %broadcast_in_dim.127.enter_ref), custom_call_target="tpu_custom_call" | custom-call | flops 3221225472 | bytes 6291456 | tf_op jit(solution)/shard_map/backward/pallas_call | solution.py:135
  316.9 4.1 %collective-permute-done.9 = bf16[64,1536]{1,0:T(8,128)(2,1)S(1)} collective-permute-done((bf16[64,1536]{1,0:T(8,128)(2,1)S(1)}, bf16[64,1536]{1,0:T(8,128)(2,1)S(1)}, u32[]{:S(2)}, u32[]{:S(2)}) %collective-permute-start.9) | collective-permute-done | bytes 196640 | tf_op jit(solution)/shard_map/ppermute | solution.py:187
  323.0 2.5 collective-permute-start.18
  325.5 3.7 %collective-permute-done.15 = bf16[64,1536]{1,0:T(8,128)(2,1)S(1)} collective-permute-done((bf16[64,1536]{1,0:T(8,128)(2,1)S(1)}, bf16[64,1536]{1,0:T(8,128)(2,1)S(1)}, u32[]{:S(2)}, u32[]{:S(2)}) %collective-permute-start.15) | collective-permute-done | bytes 196640 | tf_op jit(solution)/shard_map/ppermute | solution.py:187
  335.7 2.4 collective-permute-done.10
  339.5 3.0 collective-permute-done.17
  342.4 4.2 %collective-permute-done.16 = bf16[64,1536]{1,0:T(8,128)(2,1)S(1)} collective-permute-done((bf16[64,1536]{1,0:T(8,128)(2,1)S(1)}, bf16[64,1536]{1,0:T(8,128)(2,1)S(1)}, u32[]{:S(2)}, u32[]{:S(2)}) %collective-permute-start.16) | collective-permute-done | bytes 196640 | tf_op jit(solution)/shard_map/ppermute | solution.py:187
  (143 shorter events, 47.3 us)
Async XLA Ops:
  13.1 184.9 %all-to-all-start = ((bf16[32,2,32,3072]{3,2,1,0:T(8,128)(2,1)}), bf16[32,2,32,3072]{3,2,1,0:T(8,128)(2,1)}, u32[]{:S(2)}, u32[]{:S(2)}) async-start(bf16[32,2,32,3072]{3,2,1,0:T(8,128)(2,1)} %copy-done), calls=%async_computation | async-start | bytes 25165824 | tf_op jit(solution)/shard_map/all_to_all | solution.py:178
  216.3 4.0 %collective-permute-start.1 = (f32[8,256]{1,0:T(8,128)S(1)}, f32[8,256]{1,0:T(8,128)S(1)}, u32[]{:S(2)}, u32[]{:S(2)}) collective-permute-start(f32[8,256]{1,0:T(8,128)S(1)} %maximum_maximum_fusion.2), channel_id=1, source_target_pairs={{0,64},{32,96},{64,0},{96,32},{1,65},{33,97},{65,1},{97,33},{2,66}... | collective-permute-start | bytes 24584 | tf_op jit(solution)/shard_map/ppermute | solution.py:187
  224.9 6.8 %collective-permute-start.3 = (f32[2,512,256]{2,1,0:T(8,128)}, f32[2,512,256]{2,1,0:T(8,128)}, u32[]{:S(2)}, u32[]{:S(2)}) collective-permute-start(f32[2,512,256]{2,1,0:T(8,128)} %dynamic-slice_bitcast_fusion), channel_id=1, source_target_pairs={{0,1},{1,0},{2,3},{3,2},{4,5},{5,4},{6,7},{7,6},{8,9},{9,8},{10,11... | collective-permute-start | bytes 3145736 | tf_op jit(solution)/shard_map/ppermute | solution.py:202
  234.2 35.3 %all-to-all-start.1 = ((bf16[16,2,32,256]{3,2,1,0:T(8,128)(2,1)}), bf16[16,2,32,256]{3,2,1,0:T(8,128)(2,1)}, u32[]{:S(2)}, u32[]{:S(2)}) async-start(bf16[16,2,32,256]{3,2,1,0:T(8,128)(2,1)} %copy.35), calls=%async_computation.1 | async-start | bytes 1048576 | tf_op jit(solution)/shard_map/all_to_all | solution.py:178
  271.4 13.8 %all-to-all-start.2 = ((bf16[16,2,32,256]{3,2,1,0:T(8,128)(2,1)}), bf16[16,2,32,256]{3,2,1,0:T(8,128)(2,1)}, u32[]{:S(2)}, u32[]{:S(2)}) async-start(bf16[16,2,32,256]{3,2,1,0:T(8,128)(2,1)} %broadcast_in_dim.121), calls=%async_computation.2 | async-start | bytes 1048576 | tf_op jit(solution)/shard_map/all_to_all | solution.py:178
  276.3 13.6 %collective-permute-start.7 = (f32[8,3072]{1,0:T(8,128)S(1)}, f32[8,3072]{1,0:T(8,128)S(1)}, u32[]{:S(2)}, u32[]{:S(2)}) collective-permute-start(f32[8,3072]{1,0:T(8,128)S(1)} %maximum_maximum_fusion), channel_id=1, source_target_pairs={{0,96},{32,0},{64,32},{96,64},{1,97},{33,1},{65,33},{97,65},{2,98}... | collective-permute-start | bytes 294920 | tf_op jit(solution)/shard_map/ppermute | solution.py:187
  276.4 13.5 %collective-permute-start.6 = (f32[8,3072]{1,0:T(8,128)S(1)}, f32[8,3072]{1,0:T(8,128)}, u32[]{:S(2)}, u32[]{:S(2)}) collective-permute-start(f32[8,3072]{1,0:T(8,128)S(1)} %maximum_maximum_fusion), channel_id=1, source_target_pairs={{0,64},{32,96},{64,0},{96,32},{1,65},{33,97},{65,1},{97,33},{2,66}... | collective-permute-start | bytes 294920 | tf_op jit(solution)/shard_map/ppermute | solution.py:187
  277.9 12.0 %collective-permute-start.5 = (f32[8,3072]{1,0:T(8,128)S(1)}, f32[8,3072]{1,0:T(8,128)}, u32[]{:S(2)}, u32[]{:S(2)}) collective-permute-start(f32[8,3072]{1,0:T(8,128)S(1)} %maximum_maximum_fusion), channel_id=1, source_target_pairs={{0,32},{32,64},{64,96},{96,0},{1,33},{33,65},{65,97},{97,1},{2,34}... | collective-permute-start | bytes 294920 | tf_op jit(solution)/shard_map/ppermute | solution.py:187
  286.3 5.1 %collective-permute-start.4 = (bf16[2,512,256]{2,1,0:T(8,128)(2,1)S(1)}, bf16[2,512,256]{2,1,0:T(8,128)(2,1)S(1)}, u32[]{:S(2)}, u32[]{:S(2)}) collective-permute-start(bf16[2,512,256]{2,1,0:T(8,128)(2,1)S(1)} %bitcast.80), channel_id=1, source_target_pairs={{0,1},{1,0},{2,3},{3,2},{4,5},{5,4},{6,7},{7,6},{8,9},{9,8},{10,11... | collective-permute-start | bytes 1572872 | tf_op jit(solution)/shard_map/ppermute | solution.py:202
  309.9 5.4 %collective-permute-start.22 = (bf16[128,256]{1,0:T(8,128)(2,1)S(1)}, bf16[128,256]{1,0:T(8,128)(2,1)S(1)}, u32[]{:S(2)}, u32[]{:S(2)}) collective-permute-start(bf16[128,256]{1,0:T(8,128)(2,1)S(1)} %fusion.3), channel_id=1, source_target_pairs={{0,96},{32,0},{64,32},{96,64},{1,97},{33,1},{65,33},{97,65},{2,98}... | collective-permute-start | bytes 196616 | tf_op jit(solution)/shard_map/ppermute | solution.py:187
  310.0 6.0 %collective-permute-start.21 = (bf16[128,256]{1,0:T(8,128)(2,1)S(1)}, bf16[128,256]{1,0:T(8,128)(2,1)S(1)}, u32[]{:S(2)}, u32[]{:S(2)}) collective-permute-start(bf16[128,256]{1,0:T(8,128)(2,1)S(1)} %fusion.3), channel_id=1, source_target_pairs={{0,64},{32,96},{64,0},{96,32},{1,65},{33,97},{65,1},{97,33},{2,66}... | collective-permute-start | bytes 196616 | tf_op jit(solution)/shard_map/ppermute | solution.py:187
  311.3 5.5 %collective-permute-start.20 = (bf16[128,256]{1,0:T(8,128)(2,1)S(1)}, bf16[128,256]{1,0:T(8,128)(2,1)S(1)}, u32[]{:S(2)}, u32[]{:S(2)}) collective-permute-start(bf16[128,256]{1,0:T(8,128)(2,1)S(1)} %fusion.3), channel_id=1, source_target_pairs={{0,32},{32,64},{64,96},{96,0},{1,33},{33,65},{65,97},{97,1},{2,34}... | collective-permute-start | bytes 196616 | tf_op jit(solution)/shard_map/ppermute | solution.py:187
  312.2 8.8 %collective-permute-start.9 = (bf16[64,1536]{1,0:T(8,128)(2,1)S(1)}, bf16[64,1536]{1,0:T(8,128)(2,1)S(1)}, u32[]{:S(2)}, u32[]{:S(2)}) collective-permute-start(bf16[64,1536]{1,0:T(8,128)(2,1)S(1)} %get-tuple-element.27), channel_id=1, source_target_pairs={{0,32},{32,64},{64,96},{96,0},{1,33},{33,65},{65,97},{97,1},{2,34}... | collective-permute-start | bytes 589832 | tf_op jit(solution)/shard_map/ppermute | solution.py:187
  312.9 22.7 %collective-permute-start.8 = (bf16[64,1536]{1,0:T(8,128)(2,1)S(1)}, bf16[64,1536]{1,0:T(8,128)(2,1)S(1)}, u32[]{:S(2)}, u32[]{:S(2)}) collective-permute-start(bf16[64,1536]{1,0:T(8,128)(2,1)S(1)} %slice.158), channel_id=1, source_target_pairs={{0,96},{32,0},{64,32},{96,64},{1,97},{33,1},{65,33},{97,65},{2,98}... | collective-permute-start | bytes 589832 | tf_op jit(solution)/shard_map/ppermute | solution.py:187
  315.3 7.7 %collective-permute-start.12 = (bf16[64,1536]{1,0:T(8,128)(2,1)S(1)}, bf16[64,1536]{1,0:T(8,128)(2,1)S(1)}, u32[]{:S(2)}, u32[]{:S(2)}) collective-permute-start(bf16[64,1536]{1,0:T(8,128)(2,1)S(1)} %get-tuple-element.28), channel_id=1, source_target_pairs={{0,96},{32,0},{64,32},{96,64},{1,97},{33,1},{65,33},{97,65},{2,98}... | collective-permute-start | bytes 589832 | tf_op jit(solution)/shard_map/ppermute | solution.py:187
  316.0 19.6 %collective-permute-start.11 = (bf16[64,1536]{1,0:T(8,128)(2,1)S(1)}, bf16[64,1536]{1,0:T(8,128)(2,1)S(1)}, u32[]{:S(2)}, u32[]{:S(2)}) collective-permute-start(bf16[64,1536]{1,0:T(8,128)(2,1)S(1)} %slice.162), channel_id=1, source_target_pairs={{0,32},{32,64},{64,96},{96,0},{1,33},{33,65},{65,97},{97,1},{2,34}... | collective-permute-start | bytes 589832 | tf_op jit(solution)/shard_map/ppermute | solution.py:187
  316.8 12.4 %collective-permute-start.15 = (bf16[64,1536]{1,0:T(8,128)(2,1)S(1)}, bf16[64,1536]{1,0:T(8,128)(2,1)S(1)}, u32[]{:S(2)}, u32[]{:S(2)}) collective-permute-start(bf16[64,1536]{1,0:T(8,128)(2,1)S(1)} %get-tuple-element.23), channel_id=1, source_target_pairs={{0,32},{32,64},{64,96},{96,0},{1,33},{33,65},{65,97},{97,1},{2,34}... | collective-permute-start | bytes 589832 | tf_op jit(solution)/shard_map/ppermute | solution.py:187
  321.0 18.5 %collective-permute-start.14 = (bf16[64,1536]{1,0:T(8,128)(2,1)S(1)}, bf16[64,1536]{1,0:T(8,128)(2,1)S(1)}, u32[]{:S(2)}, u32[]{:S(2)}) collective-permute-start(bf16[64,1536]{1,0:T(8,128)(2,1)S(1)} %slice.166), channel_id=1, source_target_pairs={{0,96},{32,0},{64,32},{96,64},{1,97},{33,1},{65,33},{97,65},{2,98}... | collective-permute-start | bytes 589832 | tf_op jit(solution)/shard_map/ppermute | solution.py:187
  323.0 9.1 %collective-permute-start.18 = (bf16[64,1536]{1,0:T(8,128)(2,1)S(1)}, bf16[64,1536]{1,0:T(8,128)(2,1)S(1)}, u32[]{:S(2)}, u32[]{:S(2)}) collective-permute-start(bf16[64,1536]{1,0:T(8,128)(2,1)S(1)} %get-tuple-element.24), channel_id=1, source_target_pairs={{0,96},{32,0},{64,32},{96,64},{1,97},{33,1},{65,33},{97,65},{2,98}... | collective-permute-start | bytes 589832 | tf_op jit(solution)/shard_map/ppermute | solution.py:187
  332.1 6.1 %collective-permute-start.10 = (bf16[64,1536]{1,0:T(8,128)(2,1)S(1)}, bf16[64,1536]{1,0:T(8,128)(2,1)S(1)}, u32[]{:S(2)}, u32[]{:S(2)}) collective-permute-start(bf16[64,1536]{1,0:T(8,128)(2,1)S(1)} %add_convert_fusion.3), channel_id=1, source_target_pairs={{0,32},{32,64},{64,96},{96,0},{1,33},{33,65},{65,97},{97,1},{2,34}... | collective-permute-start | bytes 589832 | tf_op jit(solution)/shard_map/ppermute | solution.py:187
  332.6 5.7 %collective-permute-start.13 = (bf16[64,1536]{1,0:T(8,128)(2,1)S(1)}, bf16[64,1536]{1,0:T(8,128)(2,1)S(1)}, u32[]{:S(2)}, u32[]{:S(2)}) collective-permute-start(bf16[64,1536]{1,0:T(8,128)(2,1)S(1)} %add_convert_fusion.2), channel_id=1, source_target_pairs={{0,96},{32,0},{64,32},{96,64},{1,97},{33,1},{65,33},{97,65},{2,98}... | collective-permute-start | bytes 589832 | tf_op jit(solution)/shard_map/ppermute | solution.py:187
  335.6 6.8 %collective-permute-start.17 = (bf16[64,1536]{1,0:T(8,128)(2,1)S(1)}, bf16[64,1536]{1,0:T(8,128)(2,1)S(1)}, u32[]{:S(2)}, u32[]{:S(2)}) collective-permute-start(bf16[64,1536]{1,0:T(8,128)(2,1)S(1)} %slice.170), channel_id=1, source_target_pairs={{0,32},{32,64},{64,96},{96,0},{1,33},{33,65},{65,97},{97,1},{2,34}... | collective-permute-start | bytes 589832 | tf_op jit(solution)/shard_map/ppermute | solution.py:187
  335.6 11.0 %collective-permute-start.16 = (bf16[64,1536]{1,0:T(8,128)(2,1)S(1)}, bf16[64,1536]{1,0:T(8,128)(2,1)S(1)}, u32[]{:S(2)}, u32[]{:S(2)}) collective-permute-start(bf16[64,1536]{1,0:T(8,128)(2,1)S(1)} %add_convert_fusion.1), channel_id=1, source_target_pairs={{0,32},{32,64},{64,96},{96,0},{1,33},{33,65},{65,97},{97,1},{2,34}... | collective-permute-start | bytes 589832 | tf_op jit(solution)/shard_map/ppermute | solution.py:187
  338.1 8.5 %collective-permute-start.19 = (bf16[64,1536]{1,0:T(8,128)(2,1)S(1)}, bf16[64,1536]{1,0:T(8,128)(2,1)S(1)}, u32[]{:S(2)}, u32[]{:S(2)}) collective-permute-start(bf16[64,1536]{1,0:T(8,128)(2,1)S(1)} %add_convert_fusion), channel_id=1, source_target_pairs={{0,96},{32,0},{64,32},{96,64},{1,97},{33,1},{65,33},{97,65},{2,98}... | collective-permute-start | bytes 589832 | tf_op jit(solution)/shard_map/ppermute | solution.py:187
  (14 other events, 85.9 us)

commit v3 on v2

--- a/solution.py
+++ b/solution.py
@@ -188,7 +188,7 @@
 
 
 def entering(end, gain, start):
-    message = jnp.concatenate([end, jnp.broadcast_to(gain[:, None], end.shape), jnp.zeros((4, end.shape[1]), F32)])
+    message = jnp.concatenate([end, jnp.broadcast_to(gain[:, None], end.shape)])
     i = lax.axis_index("tm")
     total, so_far = jnp.zeros_like(end), jnp.ones_like(end)
     for d in range(1, lax.axis_size("tm")):
@@ -247,7 +247,6 @@
     rows, points = x0.shape
     width, hours = points // grid, rows * grid
     scale = (hours * lax.axis_size("tm")) ** -0.5
-    x = all_to_all(pack(x0, x1, grid), "grid")
     block, since_start, to_end, gain = decay_blocks(fading)
     operators = jnp.stack([operator0, operator1])
     start = []
@@ -258,10 +257,15 @@
             rest = rest - parts[-1].astype(F32)
         start.append(jnp.dot(jnp.stack(parts), operators[f], preferred_element_type=F32).sum(axis=0))
     start = jnp.stack(start)
+    weight = to_end.reshape(2, grid, rows).transpose(1, 0, 2)[..., None]
+    ready = (block, since_start, weight, gain, start, operators)
+    packed, ready = lax.optimization_barrier((pack(x0, x1, grid), ready))
+    x = all_to_all(packed, "grid")
+    x, ready = lax.optimization_barrier((x, ready))
+    block, since_start, weight, gain, start, operators = ready
     p, end = forward(x, operators, block)
     p = p - since_start[:, :, None] * entering(end[:, 0], gain, start)[:, None]
     q, x = summed_over_grid(p, x)
-    weight = to_end.reshape(2, grid, rows).transpose(1, 0, 2)[..., None]
     mean = entering((x.astype(F32) * weight).sum(axis=(0, 2)), gain, starting)
     mean = jnp.broadcast_to(mean[:, None], (2, 8, width))
     w1 = backward(1, q, block, x, mean)

time: 350 us -> 294 us (0.84)
  waiting for transfers between devices: 202 us -> 26.2 us
  blocking collectives: 0 us -> 150 us
  starting transfers between devices: 66.2 us -> 40.5 us
  Pallas kernels: 33 us -> 28.2 us
    all_to_all x3 -> x2, waiting for transfers between devices: 176 us -> 6.98 us  [all_to_all(): lax.all_to_all(x, axis, split_axis=0, concat_axis=0, tiled=True, axis_ind...]
    all_to_all x0 -> x1, blocking collectives: none -> 150 us  [all_to_all(): lax.all_to_all(x, axis, split_axis=0, concat_axis=0, tiled=True, axis_ind...]
    all_to_all x3 -> x2, starting transfers between devices: 39.4 us -> 9.17 us  [all_to_all(): lax.all_to_all(x, axis, split_axis=0, concat_axis=0, tiled=True, axis_ind...]
    ppermute x21, waiting for transfers between devices: 23.7 us -> 15.2 us  [shifted(): return lax.ppermute(x, 'tm', [(i, (i + by) % n) for i in range(n)])]
    ppermute x21, starting transfers between devices: 17.9 us -> 24.3 us  [shifted(): return lax.ppermute(x, 'tm', [(i, (i + by) % n) for i in range(n)])]
    pallas_call x2, Pallas kernels: 17.7 us -> 13.8 us  [backward(): pl.pallas_call(backward_kernel, grid=(width // NCHUNK,), in_specs=[pl.Blo...]
    unnamed x25 -> x21, local copies, waits for them, and re-layouts: 14.7 us -> 12.9 us
  transfers between devices with their start and end apart: 27 -> 26, of which waited for: 14 -> 10; matrix products, arithmetic and copies ran while one was open for 6% -> 4% of each run, Pallas kernels for 0% -> 5%
where the time goes in v3:
time: 294 us; the launch traced here: 292 us
  blocking collectives  150 us (51%)
  starting transfers between devices  40.5 us (14%)
  Pallas kernels  28.2 us (10%)
  waiting for transfers between devices  26.2 us (9%)
  other arithmetic  23.5 us (8%)
  local copies, waits for them, and re-layouts  19 us (6%)
  matrix products  3.48 us (1%)
    all_to_all x1, blocking collectives, all_to_all(): lax.all_to_all(x, axis, split_axis=0, concat_axis=0, tiled=True, axis_ind...  150 us
    ppermute x21, starting transfers between devices, shifted(): return lax.ppermute(x, 'tm', [(i, (i + by) % n) for i in range(n)])  24.3 us
    ppermute x21, waiting for transfers between devices, shifted(): return lax.ppermute(x, 'tm', [(i, (i + by) % n) for i in range(n)])  15.2 us
    pallas_call x2, Pallas kernels, backward(): pl.pallas_call(backward_kernel, grid=(width // NCHUNK,), in_specs=[pl.Blo...  13.8 us
    unnamed x21, local copies, waits for them, and re-layouts  12.9 us
    pallas_call x1, Pallas kernels, forward(): pl.pallas_call(forward_kernel, grid=(2, nb), in_specs=[pl.BlockSpec((per,...  11.7 us
    all_to_all x2, starting transfers between devices, all_to_all(): lax.all_to_all(x, axis, split_axis=0, concat_axis=0, tiled=True, axis_ind...  9.17 us
    reduce_sum x1, other arithmetic, per_device(): mean = entering((x.astype(F32) * weight).sum(axis=(0, 2)), gain, starting)  8.51 us
  transfers between devices with their start and end apart: 26, of which 10 were waited for; matrix products, arithmetic and copies ran while one was open for 4% of the time, Pallas kernels for 5%

profile of v3, /device:TPU:1, one launch (start us, length us, event | category | flops | bytes accessed | tf_op | source)
XLA Modules:
  0.0 291.9 jit_solution(6424267594527559595)
XLA Ops:
  1.4 2.4 reduce-window.6
  11.2 2.8 copy-done.2
  14.0 2.8 copy-done.3
  16.8 2.3 pack.1
  20.8 149.9 %all_to_all.15.x_ref = bf16[32,2,32,3072]{3,2,1,0:T(8,128)(2,1)S(1)} all-to-all(bf16[32,2,32,3072]{3,2,1,0:T(8,128)(2,1)S(1)} %pack.1), channel_id=1, replica_groups=mesh['tm'=4,'grid'=32] {'grid'}, dimensions={0} | all-to-all | bytes 25165824 | tf_op jit(solution)/shard_map/all_to_all | solution.py:178
  170.7 11.7 %forward.1 = (f32[2,1024,256]{2,1,0:T(8,128)S(1)}, f32[2,8,256]{2,1,0:T(8,128)S(1)}) custom-call(bf16[32,2,32,3072]{3,2,1,0:T(8,128)(2,1)S(1)} %all_to_all.15.x_ref, bf16[2,3072,256]{2,1,0:T(8,128)(2,1)S(1)} %pad_maximum_fusion.op_ref, f32[2,4,264,384]{3,2,1,0:T(8,128)S(1)} %fusion.block_ref), custom_call_target="tpu_custom_call" | custom-call | flops 3221225472 | bytes 12582912 | tf_op jit(solution)/shard_map/forward/pallas_call | solution.py:83
  185.1 2.4 collective-permute-start.1
  190.2 1.9 multiply_subtract_fusion
  196.2 2.6 collective-permute-done.3
  201.3 4.2 %all-to-all-start.1 = ((bf16[16,2,32,256]{3,2,1,0:T(8,128)(2,1)}), bf16[16,2,32,256]{3,2,1,0:T(8,128)(2,1)}, u32[]{:S(2)}, u32[]{:S(2)}) async-start(bf16[16,2,32,256]{3,2,1,0:T(8,128)(2,1)} %copy.35), calls=%async_computation.1 | async-start | bytes 1048576 | tf_op jit(solution)/shard_map/all_to_all | solution.py:178
  205.5 8.5 %multiply_reduce_fusion = f32[2,3072]{1,0:T(2,128)S(1)} fusion(bf16[32,2,32,3072]{3,2,1,0:T(8,128)(2,1)} %copy-done, f32[32,2,32]{2,1,0:T(2,128)S(1)} %copy.38), kind=kLoop, calls=%fused_computation | loop fusion | flops 18868224 | bytes 12615680 | tf_op jit(solution)/shard_map/reduce_sum | solution.py:269
  217.7 4.9 %all-to-all-start.2 = ((bf16[16,2,32,256]{3,2,1,0:T(8,128)(2,1)}), bf16[16,2,32,256]{3,2,1,0:T(8,128)(2,1)}, u32[]{:S(2)}, u32[]{:S(2)}) async-start(bf16[16,2,32,256]{3,2,1,0:T(8,128)(2,1)} %broadcast_in_dim.119), calls=%async_computation.2 | async-start | bytes 1048576 | tf_op jit(solution)/shard_map/all_to_all | solution.py:178
  222.7 3.5 %collective-permute-start.6 = (f32[4,3072]{1,0:T(4,128)S(1)}, f32[4,3072]{1,0:T(4,128)S(1)}, u32[]{:S(2)}, u32[]{:S(2)}) collective-permute-start(f32[4,3072]{1,0:T(4,128)S(1)} %pad_maximum_fusion.2), channel_id=1, source_target_pairs={{0,64},{32,96},{64,0},{96,32},{1,65},{33,97},{65,1},{97,33},{2,66}... | collective-permute-start | bytes 147464 | tf_op jit(solution)/shard_map/ppermute | solution.py:187
  226.3 5.3 %all-to-all-done.2 = bf16[16,2,32,256]{3,2,1,0:T(8,128)(2,1)} async-done(((bf16[16,2,32,256]{3,2,1,0:T(8,128)(2,1)}), bf16[16,2,32,256]{3,2,1,0:T(8,128)(2,1)}, u32[]{:S(2)}, u32[]{:S(2)}) %all-to-all-start.2) | async-done | bytes 524320 | tf_op jit(solution)/shard_map/all_to_all | solution.py:178
  232.7 3.6 %collective-permute-start.4 = (bf16[2,512,256]{2,1,0:T(8,128)(2,1)S(1)}, bf16[2,512,256]{2,1,0:T(8,128)(2,1)S(1)}, u32[]{:S(2)}, u32[]{:S(2)}) collective-permute-start(bf16[2,512,256]{2,1,0:T(8,128)(2,1)S(1)} %bitcast.83), channel_id=1, source_target_pairs={{0,1},{1,0},{2,3},{3,2},{4,5},{5,4},{6,7},{7,6},{8,9},{9,8},{10,11... | collective-permute-start | bytes 1572872 | tf_op jit(solution)/shard_map/ppermute | solution.py:202
  238.6 3.5 %collective-permute-start.21 = (bf16[128,256]{1,0:T(8,128)(2,1)S(1)}, bf16[128,256]{1,0:T(8,128)(2,1)S(1)}, u32[]{:S(2)}, u32[]{:S(2)}) collective-permute-start(bf16[128,256]{1,0:T(8,128)(2,1)S(1)} %fusion.3), channel_id=1, source_target_pairs={{0,64},{32,96},{64,0},{96,32},{1,65},{33,97},{65,1},{97,33},{2,66}... | collective-permute-start | bytes 196616 | tf_op jit(solution)/shard_map/ppermute | solution.py:187
  242.1 4.6 %copy-done.1 = bf16[32,2,32,3072]{3,2,1,0:T(8,128)(2,1)S(1)} copy-done((bf16[32,2,32,3072]{3,2,1,0:T(8,128)(2,1)S(1)}, bf16[32,2,32,3072]{3,2,1,0:T(8,128)(2,1)}, u32[]{:S(2)}) %copy-start.1) | copy-done | bytes 12582936
  246.7 6.9 %backward.3 = bf16[256,3072]{1,0:T(8,128)(2,1)S(1)} custom-call(bf16[2,1024,256]{2,1,0:T(8,128)(2,1)S(1)} %bitcast.73, f32[2,4,264,384]{3,2,1,0:T(8,128)S(1)} %fusion.block_ref, bf16[32,2,32,3072]{3,2,1,0:T(8,128)(2,1)S(1)} %copy-done.1, f32[2,8,3072]{2,1,0:T(8,128)S(1)} %broadcast_in_dim.123.enter_ref), custom_call_target="tpu_custom_call" | custom-call | flops 3221225472 | bytes 6291456 | tf_op jit(solution)/shard_map/backward/pallas_call | solution.py:135
  253.6 6.9 %backward.2 = bf16[256,3072]{1,0:T(8,128)(2,1)S(1)} custom-call(bf16[2,1024,256]{2,1,0:T(8,128)(2,1)S(1)} %bitcast.74, f32[2,4,264,384]{3,2,1,0:T(8,128)S(1)} %fusion.block_ref, bf16[32,2,32,3072]{3,2,1,0:T(8,128)(2,1)S(1)} %copy-done.1, f32[2,8,3072]{2,1,0:T(8,128)S(1)} %broadcast_in_dim.123.enter_ref), custom_call_target="tpu_custom_call" | custom-call | flops 3221225472 | bytes 6291456 | tf_op jit(solution)/shard_map/backward/pallas_call | solution.py:135
  264.1 2.6 collective-permute-start.12
  267.6 7.0 %collective-permute-done.12 = bf16[64,1536]{1,0:T(8,128)(2,1)S(1)} collective-permute-done((bf16[64,1536]{1,0:T(8,128)(2,1)S(1)}, bf16[64,1536]{1,0:T(8,128)(2,1)S(1)}, u32[]{:S(2)}, u32[]{:S(2)}) %collective-permute-start.12) | collective-permute-done | bytes 196640 | tf_op jit(solution)/shard_map/ppermute | solution.py:187
  274.7 1.8 collective-permute-start.23
  279.7 2.0 collective-permute-start.8
  286.6 4.2 %collective-permute-done.13 = bf16[64,1536]{1,0:T(8,128)(2,1)S(1)} collective-permute-done((bf16[64,1536]{1,0:T(8,128)(2,1)S(1)}, bf16[64,1536]{1,0:T(8,128)(2,1)S(1)}, u32[]{:S(2)}, u32[]{:S(2)}) %collective-permute-start.13) | collective-permute-done | bytes 196640 | tf_op jit(solution)/shard_map/ppermute | solution.py:187
  (137 shorter events, 42.2 us)
Async XLA Ops:
  183.9 4.8 %collective-permute-start = (f32[4,256]{1,0:T(4,128)S(1)}, f32[4,256]{1,0:T(4,128)S(1)}, u32[]{:S(2)}, u32[]{:S(2)}) collective-permute-start(f32[4,256]{1,0:T(4,128)S(1)} %pad_maximum_fusion.3), channel_id=1, source_target_pairs={{0,32},{32,64},{64,96},{96,0},{1,33},{33,65},{65,97},{97,1},{2,34}... | collective-permute-start | bytes 12296 | tf_op jit(solution)/shard_map/ppermute | solution.py:187
  185.1 4.0 %collective-permute-start.1 = (f32[4,256]{1,0:T(4,128)S(1)}, f32[4,256]{1,0:T(4,128)S(1)}, u32[]{:S(2)}, u32[]{:S(2)}) collective-permute-start(f32[4,256]{1,0:T(4,128)S(1)} %pad_maximum_fusion.3), channel_id=1, source_target_pairs={{0,64},{32,96},{64,0},{96,32},{1,65},{33,97},{65,1},{97,33},{2,66}... | collective-permute-start | bytes 12296 | tf_op jit(solution)/shard_map/ppermute | solution.py:187
  194.5 4.2 %collective-permute-start.3 = (f32[2,512,256]{2,1,0:T(8,128)}, f32[2,512,256]{2,1,0:T(8,128)}, u32[]{:S(2)}, u32[]{:S(2)}) collective-permute-start(f32[2,512,256]{2,1,0:T(8,128)} %dynamic-slice_bitcast_fusion), channel_id=1, source_target_pairs={{0,1},{1,0},{2,3},{3,2},{4,5},{5,4},{6,7},{7,6},{8,9},{9,8},{10,11... | collective-permute-start | bytes 3145736 | tf_op jit(solution)/shard_map/ppermute | solution.py:202
  201.3 14.5 %all-to-all-start.1 = ((bf16[16,2,32,256]{3,2,1,0:T(8,128)(2,1)}), bf16[16,2,32,256]{3,2,1,0:T(8,128)(2,1)}, u32[]{:S(2)}, u32[]{:S(2)}) async-start(bf16[16,2,32,256]{3,2,1,0:T(8,128)(2,1)} %copy.35), calls=%async_computation.1 | async-start | bytes 1048576 | tf_op jit(solution)/shard_map/all_to_all | solution.py:178
  217.7 13.9 %all-to-all-start.2 = ((bf16[16,2,32,256]{3,2,1,0:T(8,128)(2,1)}), bf16[16,2,32,256]{3,2,1,0:T(8,128)(2,1)}, u32[]{:S(2)}, u32[]{:S(2)}) async-start(bf16[16,2,32,256]{3,2,1,0:T(8,128)(2,1)} %broadcast_in_dim.119), calls=%async_computation.2 | async-start | bytes 1048576 | tf_op jit(solution)/shard_map/all_to_all | solution.py:178
  222.7 13.6 %collective-permute-start.5 = (f32[4,3072]{1,0:T(4,128)S(1)}, f32[4,3072]{1,0:T(4,128)S(1)}, u32[]{:S(2)}, u32[]{:S(2)}) collective-permute-start(f32[4,3072]{1,0:T(4,128)S(1)} %pad_maximum_fusion.2), channel_id=1, source_target_pairs={{0,32},{32,64},{64,96},{96,0},{1,33},{33,65},{65,97},{97,1},{2,34}... | collective-permute-start | bytes 147464 | tf_op jit(solution)/shard_map/ppermute | solution.py:187
  222.7 13.5 %collective-permute-start.6 = (f32[4,3072]{1,0:T(4,128)S(1)}, f32[4,3072]{1,0:T(4,128)S(1)}, u32[]{:S(2)}, u32[]{:S(2)}) collective-permute-start(f32[4,3072]{1,0:T(4,128)S(1)} %pad_maximum_fusion.2), channel_id=1, source_target_pairs={{0,64},{32,96},{64,0},{96,32},{1,65},{33,97},{65,1},{97,33},{2,66}... | collective-permute-start | bytes 147464 | tf_op jit(solution)/shard_map/ppermute | solution.py:187
  226.3 10.0 %collective-permute-start.7 = (f32[4,3072]{1,0:T(4,128)S(1)}, f32[4,3072]{1,0:T(4,128)S(1)}, u32[]{:S(2)}, u32[]{:S(2)}) collective-permute-start(f32[4,3072]{1,0:T(4,128)S(1)} %pad_maximum_fusion.2), channel_id=1, source_target_pairs={{0,96},{32,0},{64,32},{96,64},{1,97},{33,1},{65,33},{97,65},{2,98}... | collective-permute-start | bytes 147464 | tf_op jit(solution)/shard_map/ppermute | solution.py:187
  232.7 5.1 %collective-permute-start.4 = (bf16[2,512,256]{2,1,0:T(8,128)(2,1)S(1)}, bf16[2,512,256]{2,1,0:T(8,128)(2,1)S(1)}, u32[]{:S(2)}, u32[]{:S(2)}) collective-permute-start(bf16[2,512,256]{2,1,0:T(8,128)(2,1)S(1)} %bitcast.83), channel_id=1, source_target_pairs={{0,1},{1,0},{2,3},{3,2},{4,5},{5,4},{6,7},{7,6},{8,9},{9,8},{10,11... | collective-permute-start | bytes 1572872 | tf_op jit(solution)/shard_map/ppermute | solution.py:202
  238.5 24.0 %collective-permute-start.20 = (bf16[128,256]{1,0:T(8,128)(2,1)S(1)}, bf16[128,256]{1,0:T(8,128)(2,1)S(1)}, u32[]{:S(2)}, u32[]{:S(2)}) collective-permute-start(bf16[128,256]{1,0:T(8,128)(2,1)S(1)} %fusion.3), channel_id=1, source_target_pairs={{0,32},{32,64},{64,96},{96,0},{1,33},{33,65},{65,97},{97,1},{2,34}... | collective-permute-start | bytes 196616 | tf_op jit(solution)/shard_map/ppermute | solution.py:187
  238.6 25.4 %collective-permute-start.21 = (bf16[128,256]{1,0:T(8,128)(2,1)S(1)}, bf16[128,256]{1,0:T(8,128)(2,1)S(1)}, u32[]{:S(2)}, u32[]{:S(2)}) collective-permute-start(bf16[128,256]{1,0:T(8,128)(2,1)S(1)} %fusion.3), channel_id=1, source_target_pairs={{0,64},{32,96},{64,0},{96,32},{1,65},{33,97},{65,1},{97,33},{2,66}... | collective-permute-start | bytes 196616 | tf_op jit(solution)/shard_map/ppermute | solution.py:187
  242.1 21.9 %collective-permute-start.22 = (bf16[128,256]{1,0:T(8,128)(2,1)S(1)}, bf16[128,256]{1,0:T(8,128)(2,1)S(1)}, u32[]{:S(2)}, u32[]{:S(2)}) collective-permute-start(bf16[128,256]{1,0:T(8,128)(2,1)S(1)} %fusion.3), channel_id=1, source_target_pairs={{0,96},{32,0},{64,32},{96,64},{1,97},{33,1},{65,33},{97,65},{2,98}... | collective-permute-start | bytes 196616 | tf_op jit(solution)/shard_map/ppermute | solution.py:187
  260.6 6.1 %collective-permute-start.18 = (bf16[64,1536]{1,0:T(8,128)(2,1)S(1)}, bf16[64,1536]{1,0:T(8,128)(2,1)S(1)}, u32[]{:S(2)}, u32[]{:S(2)}) collective-permute-start(bf16[64,1536]{1,0:T(8,128)(2,1)S(1)} %get-tuple-element.52), channel_id=1, source_target_pairs={{0,96},{32,0},{64,32},{96,64},{1,97},{33,1},{65,33},{97,65},{2,98}... | collective-permute-start | bytes 589832 | tf_op jit(solution)/shard_map/ppermute | solution.py:187
  261.0 6.5 %collective-permute-start.15 = (bf16[64,1536]{1,0:T(8,128)(2,1)S(1)}, bf16[64,1536]{1,0:T(8,128)(2,1)S(1)}, u32[]{:S(2)}, u32[]{:S(2)}) collective-permute-start(bf16[64,1536]{1,0:T(8,128)(2,1)S(1)} %get-tuple-element.51), channel_id=1, source_target_pairs={{0,32},{32,64},{64,96},{96,0},{1,33},{33,65},{65,97},{97,1},{2,34}... | collective-permute-start | bytes 589832 | tf_op jit(solution)/shard_map/ppermute | solution.py:187
  262.5 17.2 %collective-permute-start.14 = (bf16[64,1536]{1,0:T(8,128)(2,1)S(1)}, bf16[64,1536]{1,0:T(8,128)(2,1)S(1)}, u32[]{:S(2)}, u32[]{:S(2)}) collective-permute-start(bf16[64,1536]{1,0:T(8,128)(2,1)S(1)} %slice.166), channel_id=1, source_target_pairs={{0,96},{32,0},{64,32},{96,64},{1,97},{33,1},{65,33},{97,65},{2,98}... | collective-permute-start | bytes 589832 | tf_op jit(solution)/shard_map/ppermute | solution.py:187
  264.0 17.7 %collective-permute-start.17 = (bf16[64,1536]{1,0:T(8,128)(2,1)S(1)}, bf16[64,1536]{1,0:T(8,128)(2,1)S(1)}, u32[]{:S(2)}, u32[]{:S(2)}) collective-permute-start(bf16[64,1536]{1,0:T(8,128)(2,1)S(1)} %slice.170), channel_id=1, source_target_pairs={{0,32},{32,64},{64,96},{96,0},{1,33},{33,65},{65,97},{97,1},{2,34}... | collective-permute-start | bytes 589832 | tf_op jit(solution)/shard_map/ppermute | solution.py:187
  264.1 10.6 %collective-permute-start.12 = (bf16[64,1536]{1,0:T(8,128)(2,1)S(1)}, bf16[64,1536]{1,0:T(8,128)(2,1)S(1)}, u32[]{:S(2)}, u32[]{:S(2)}) collective-permute-start(bf16[64,1536]{1,0:T(8,128)(2,1)S(1)} %get-tuple-element.56), channel_id=1, source_target_pairs={{0,96},{32,0},{64,32},{96,64},{1,97},{33,1},{65,33},{97,65},{2,98}... | collective-permute-start | bytes 589832 | tf_op jit(solution)/shard_map/ppermute | solution.py:187
  266.7 9.8 %collective-permute-start.9 = (bf16[64,1536]{1,0:T(8,128)(2,1)S(1)}, bf16[64,1536]{1,0:T(8,128)(2,1)S(1)}, u32[]{:S(2)}, u32[]{:S(2)}) collective-permute-start(bf16[64,1536]{1,0:T(8,128)(2,1)S(1)} %get-tuple-element.55), channel_id=1, source_target_pairs={{0,32},{32,64},{64,96},{96,0},{1,33},{33,65},{65,97},{97,1},{2,34}... | collective-permute-start | bytes 589832 | tf_op jit(solution)/shard_map/ppermute | solution.py:187
  267.5 17.6 %collective-permute-start.11 = (bf16[64,1536]{1,0:T(8,128)(2,1)S(1)}, bf16[64,1536]{1,0:T(8,128)(2,1)S(1)}, u32[]{:S(2)}, u32[]{:S(2)}) collective-permute-start(bf16[64,1536]{1,0:T(8,128)(2,1)S(1)} %slice.162), channel_id=1, source_target_pairs={{0,32},{32,64},{64,96},{96,0},{1,33},{33,65},{65,97},{97,1},{2,34}... | collective-permute-start | bytes 589832 | tf_op jit(solution)/shard_map/ppermute | solution.py:187
  276.5 5.2 %collective-permute-start.19 = (bf16[64,1536]{1,0:T(8,128)(2,1)S(1)}, bf16[64,1536]{1,0:T(8,128)(2,1)S(1)}, u32[]{:S(2)}, u32[]{:S(2)}) collective-permute-start(bf16[64,1536]{1,0:T(8,128)(2,1)S(1)} %add_convert_fusion), channel_id=1, source_target_pairs={{0,96},{32,0},{64,32},{96,64},{1,97},{33,1},{65,33},{97,65},{2,98}... | collective-permute-start | bytes 589832 | tf_op jit(solution)/shard_map/ppermute | solution.py:187
  278.2 5.8 %collective-permute-start.16 = (bf16[64,1536]{1,0:T(8,128)(2,1)S(1)}, bf16[64,1536]{1,0:T(8,128)(2,1)S(1)}, u32[]{:S(2)}, u32[]{:S(2)}) collective-permute-start(bf16[64,1536]{1,0:T(8,128)(2,1)S(1)} %add_convert_fusion.1), channel_id=1, source_target_pairs={{0,32},{32,64},{64,96},{96,0},{1,33},{33,65},{65,97},{97,1},{2,34}... | collective-permute-start | bytes 589832 | tf_op jit(solution)/shard_map/ppermute | solution.py:187
  279.7 6.9 %collective-permute-start.8 = (bf16[64,1536]{1,0:T(8,128)(2,1)S(1)}, bf16[64,1536]{1,0:T(8,128)(2,1)S(1)}, u32[]{:S(2)}, u32[]{:S(2)}) collective-permute-start(bf16[64,1536]{1,0:T(8,128)(2,1)S(1)} %slice.158), channel_id=1, source_target_pairs={{0,96},{32,0},{64,32},{96,64},{1,97},{33,1},{65,33},{97,65},{2,98}... | collective-permute-start | bytes 589832 | tf_op jit(solution)/shard_map/ppermute | solution.py:187
  281.7 9.1 %collective-permute-start.13 = (bf16[64,1536]{1,0:T(8,128)(2,1)S(1)}, bf16[64,1536]{1,0:T(8,128)(2,1)S(1)}, u32[]{:S(2)}, u32[]{:S(2)}) collective-permute-start(bf16[64,1536]{1,0:T(8,128)(2,1)S(1)} %add_convert_fusion.2), channel_id=1, source_target_pairs={{0,96},{32,0},{64,32},{96,64},{1,97},{33,1},{65,33},{97,65},{2,98}... | collective-permute-start | bytes 589832 | tf_op jit(solution)/shard_map/ppermute | solution.py:187
  281.7 9.1 %collective-permute-start.10 = (bf16[64,1536]{1,0:T(8,128)(2,1)S(1)}, bf16[64,1536]{1,0:T(8,128)(2,1)S(1)}, u32[]{:S(2)}, u32[]{:S(2)}) collective-permute-start(bf16[64,1536]{1,0:T(8,128)(2,1)S(1)} %add_convert_fusion.3), channel_id=1, source_target_pairs={{0,32},{32,64},{64,96},{96,0},{1,33},{33,65},{65,97},{97,1},{2,34}... | collective-permute-start | bytes 589832 | tf_op jit(solution)/shard_map/ppermute | solution.py:187
  (11 other events, 57.6 us)

commit v4 on v2

v4 whole, which is shorter than its diff:
```python
import jax
import jax.numpy as jnp
from jax import lax
from jax.experimental import pallas as pl
from jax.experimental.pallas import tpu as pltpu
from jax.sharding import PartitionSpec as P


BLK = 256
NCHUNK = 512
Y, Z, C = 4, 4, 2
F32, BF16 = jnp.float32, jnp.bfloat16
HIGHEST = lax.Precision.HIGHEST
MIB = 1 << 20


def thirds(v):
    high = v.astype(BF16)
    v = v - high.astype(F32)
    middle = v.astype(BF16)
    return high, middle, (v - middle.astype(F32)).astype(BF16)


def prepare_kernel(x0_ref, x1_ref, fading_ref, out_ref, block_ref, since_ref, to_end_ref, gain_ref, sems):
    n, _, _, width = out_ref.shape

    def copies():
        for i in range(n):
            for f, x_ref in enumerate((x0_ref, x1_ref)):
                yield pltpu.make_async_copy(x_ref.at[:, pl.ds(i * width, width)], out_ref.at[i, f], sems.at[2 * i + f])

    for copy in copies():
        copy.start()
    a = fading_ref[...]
    log_a = jnp.log(a)
    r = lax.broadcasted_iota(jnp.int32, (BLK, BLK), 0)
    c = lax.broadcasted_iota(jnp.int32, (BLK, BLK), 1)
    upto = jnp.where(r <= c, 1.0, 0.0)
    inclusive = jnp.dot(log_a, upto, precision=HIGHEST, preferred_element_type=F32)
    exclusive = jnp.where(lax.broadcasted_iota(jnp.int32, a.shape, 1) == 0, 0.0, pltpu.roll(inclusive, 1, 1))
    column = exclusive.T
    fresh = 1.0 - a
    total = inclusive[:, BLK - 1 : BLK]
    nb = a.shape[0] // 2
    for f in range(2):
        sums = [total[f * nb + b : f * nb + b + 1] for b in range(nb)]
        ahead = jnp.zeros_like(sums[0])
        for b in range(nb):
            k = f * nb + b
            row = slice(k, k + 1)
            weight = jnp.exp(jnp.minimum(column[:, k : k + 1] - inclusive[row], 0.0)) * fresh[row]
            block_ref[k, :BLK, :BLK] = jnp.where(r == c, 1.0, jnp.where(c < r, -weight, 0.0))
            block_ref[k, :BLK, BLK:] = jnp.broadcast_to(jnp.exp(column[:, k : k + 1]), (BLK, 128))
            last = jnp.exp(sums[b] - inclusive[row]) * fresh[row]
            block_ref[k, BLK:, :BLK] = jnp.broadcast_to(last, (8, BLK))
            block_ref[k, BLK:, BLK:] = jnp.broadcast_to(-jnp.exp(sums[b]), (8, 128))
            behind = sum(sums[b + 1 :], jnp.zeros_like(ahead))
            since_ref[row] = jnp.exp(ahead + exclusive[row])
            to_end_ref[row] = jnp.exp(behind + (sums[b] - inclusive[row])) * fresh[row]
            ahead = ahead + sums[b]
        gain_ref[f : f + 1] = jnp.broadcast_to(jnp.exp(ahead), (1, BLK))
    for copy in copies():
        copy.wait()


def prepare(x0, x1, fading, n):
    rows, points = x0.shape
    width = points // n
    count = fading.size // BLK
    whole = pl.BlockSpec(memory_space=pltpu.VMEM)
    return pl.pallas_call(
        prepare_kernel,
        in_specs=[pl.BlockSpec(memory_space=pl.ANY), pl.BlockSpec(memory_space=pl.ANY), whole],
        out_specs=[pl.BlockSpec(memory_space=pl.ANY), whole, whole, whole, whole],
        out_shape=[
            jax.ShapeDtypeStruct((n, 2, rows, width), x0.dtype),
            jax.ShapeDtypeStruct((count, BLK + 8, BLK + 128), F32),
            jax.ShapeDtypeStruct((count, BLK), F32),
            jax.ShapeDtypeStruct((count, BLK), F32),
            jax.ShapeDtypeStruct((2, BLK), F32),
        ],
        scratch_shapes=[pltpu.SemaphoreType.DMA((2 * n,))],
        compiler_params=pltpu.CompilerParams(vmem_limit_bytes=24 * MIB),
        cost_estimate=pl.CostEstimate(flops=0, bytes_accessed=8 * x0.size, transcendentals=0),
        name="prepare",
    )(x0, x1, fading.reshape(count, BLK))


def forward_kernel(place_ref, x_ref, op_ref, block_ref, start_ref, own_ref, other_ref, end_ref, begin_ref, y_ref):
    f = pl.program_id(0)
    n, _, rows, width = x_ref.shape
    hours = n * rows
    nb = hours // BLK
    y_ref[...] = jnp.dot(x_ref[:, 0].reshape(hours, width), op_ref[0], preferred_element_type=F32)
    state = jnp.zeros((1, op_ref.shape[2]), F32)
    gain = jnp.ones((1, 1), F32)
    per = BLK // rows
    for b in range(nb):
        block = block_ref[b]
        out = jnp.dot(block[:, :BLK], y_ref[b * BLK : (b + 1) * BLK], precision=HIGHEST, preferred_element_type=F32)
        out = out - block[:, BLK : BLK + 1] * state
        part = out[:BLK].reshape(per, rows, out.shape[1])
        half, at = divmod(b, nb // 2)

        @pl.when(place_ref[0] == half)
        def _():
            own_ref[at * per : (at + 1) * per, 0] = part

        @pl.when(place_ref[0] != half)
        def _():
            other_ref[at * per : (at + 1) * per, 0] = part

        state = out[BLK : BLK + 1]
    start = jnp.concatenate([part.astype(F32) for part in thirds(start_ref[0])] + [jnp.zeros((5, width), F32)])
    begin = jnp.dot(start.astype(BF16), op_ref[0], preferred_element_type=F32)
    begin = begin[0:1] + begin[1:2] + begin[2:3]
    for k in range(2):

        @pl.when(f == k)
        def _():
            end_ref[k : k + 1] = state
            begin_ref[k : k + 1] = begin


def forward(place, x, operators, block, starting):
    n, _, rows, width = x.shape
    rank = operators.shape[2]
    hours = n * rows
    nb = hours // BLK
    half = jax.ShapeDtypeStruct((n // 2, 2, rows, rank), F32)
    half_spec = pl.BlockSpec((n // 2, 1, rows, rank), lambda f: (0, f, 0, 0))
    pair, pair_spec = jax.ShapeDtypeStruct((2, rank), F32), pl.BlockSpec((2, rank), lambda f: (0, 0))
    return pl.pallas_call(
        forward_kernel,
        grid=(2,),
        in_specs=[
            pl.BlockSpec(memory_space=pltpu.SMEM),
            pl.BlockSpec((n, 1, rows, width), lambda f: (0, f, 0, 0)),
            pl.BlockSpec((1, width, rank), lambda f: (f, 0, 0)),
            pl.BlockSpec((nb, BLK + 8, BLK + 128), lambda f: (f, 0, 0)),
            pl.BlockSpec((1, 1, width), lambda f: (f, 0, 0)),
        ],
        out_specs=[half_spec, half_spec, pair_spec, pair_spec],
        out_shape=[half, half, pair, pair],
        scratch_shapes=[pltpu.VMEM((hours, rank), F32)],
        compiler_params=pltpu.CompilerParams(vmem_limit_bytes=36 * MIB),
        cost_estimate=pl.CostEstimate(
            flops=4 * hours * width * rank, bytes_accessed=4 * hours * width, transcendentals=0
        ),
        name="forward",
    )(place, x, operators, block, starting)


def backward_kernel(
    place_ref, own_ref, other_ref, block_ref, x_ref, enter_ref, send0_ref, keep0_ref, send1_ref, keep1_ref, z_high, z_low, carried
):
    step = pl.program_id(0)
    rank = own_ref.shape[3]
    quarter = rank // 4

    @pl.when(step == 0)
    def _():
        nb = block_ref.shape[0]
        rows = own_ref.shape[2]
        per = BLK // rows
        swap = place_ref[1]
        reverse = jnp.zeros((rank, 1), F32)

        def placed(ref, value, cols):
            for d in range(4):
                at = pl.multiple_of(jnp.bitwise_xor(d, swap) * quarter, quarter)
                ref[pl.ds(at, quarter), cols] = value[d * quarter : (d + 1) * quarter]

        for b in reversed(range(nb)):
            half, at = divmod(b, nb // 2)
            own = own_ref[at * per : (at + 1) * per, 0].reshape(BLK, rank)
            other = other_ref[at * per : (at + 1) * per, 0].reshape(BLK, rank)
            q = jnp.where(place_ref[0] == half, own.astype(F32), other.astype(F32)).T.astype(BF16)
            out = jnp.zeros((rank, BLK + 128), F32)
            for part in reversed(thirds(block_ref[b, :BLK])):
                out = out + jnp.dot(q, part, preferred_element_type=F32)
            out = out - reverse * block_ref[b, BLK : BLK + 1, :]
            z = out[:, :BLK]
            high = z.astype(BF16)
            cols = slice(b * BLK, (b + 1) * BLK)
            placed(z_high, high, cols)
            placed(z_low, (z - high.astype(F32)).astype(BF16), cols)
            reverse = out[:, BLK : BLK + 1]
        placed(carried, jnp.broadcast_to(reverse, carried.shape), slice(0, carried.shape[1]))

    x = x_ref[:, 0].reshape(z_high.shape[1], x_ref.shape[3])
    w = jnp.dot(z_high[...], x, preferred_element_type=F32)
    w = w + jnp.dot(z_low[...], x, preferred_element_type=F32)
    w = w - carried[:, 0:1] * enter_ref[0]
    w = [w[k * quarter : (k + 1) * quarter].astype(BF16) for k in range(4)]

    @pl.when(step < pl.num_programs(0) // 2)
    def _():
        send0_ref[:quarter], send0_ref[quarter:] = w[1], w[2]
        keep0_ref[:quarter], keep0_ref[quarter:] = w[0], w[3]

    @pl.when(step >= pl.num_programs(0) // 2)
    def _():
        send1_ref[:quarter], send1_ref[quarter:] = w[2], w[3]
        keep1_ref[:quarter], keep1_ref[quarter:] = w[0], w[1]


def backward(f, place, own, other, block, x, enter):
    n, _, rows, width = x.shape
    hours, rank = n * rows, own.shape[3]
    nb = hours // BLK
    steps = width // NCHUNK // 2
    q_spec = pl.BlockSpec((n // 2, 1, rows, rank), lambda i: (0, 1 - f, 0, 0))
    left = pl.BlockSpec((rank // 2, NCHUNK), lambda i: (0, jnp.minimum(i, steps - 1)))
    right = pl.BlockSpec((rank // 2, NCHUNK), lambda i: (0, jnp.maximum(i - steps, 0)))
    piece = jax.ShapeDtypeStruct((rank // 2, width // 2), BF16)
    return pl.pallas_call(
        backward_kernel,
        grid=(2 * steps,),
        in_specs=[
            pl.BlockSpec(memory_space=pltpu.SMEM),
            q_spec,
            q_spec,
            pl.BlockSpec((nb, BLK + 8, BLK + 128), lambda i: (f, 0, 0)),
            pl.BlockSpec((n, 1, rows, NCHUNK), lambda i: (0, f, 0, i)),
            pl.BlockSpec((1, 1, NCHUNK), lambda i: (f, 0, i)),
        ],
        out_specs=[left, left, right, right],
        out_shape=[piece] * 4,
        scratch_shapes=[
            pltpu.VMEM((rank, hours), BF16),
            pltpu.VMEM((rank, hours), BF16),
            pltpu.VMEM((rank, 128), F32),
        ],
        compiler_params=pltpu.CompilerParams(vmem_limit_bytes=54 * MIB),
        cost_estimate=pl.CostEstimate(
            flops=4 * hours * width * rank, bytes_accessed=2 * hours * width, transcendentals=0
        ),
        name="backward",
    )(place, own, other, block, x, enter[:, None])


def cross_kernel(place_ref, own_ref, other_ref, out_ref):
    n, _, rows, rank = own_ref.shape
    out = jnp.zeros(out_ref.shape, F32)
    for ref in (own_ref, other_ref):
        left = ref[:, 0].reshape(n * rows, rank).astype(F32).T.astype(BF16)
        out = out + jnp.dot(left, ref[:, 1].reshape(n * rows, rank), preferred_element_type=F32)
    out_ref[...] = out


def cross(place, own, other):
    rank = own.shape[3]
    whole = pl.BlockSpec(memory_space=pltpu.VMEM)
    return pl.pallas_call(
        cross_kernel,
        out_shape=jax.ShapeDtypeStruct((rank, rank), F32),
        in_specs=[pl.BlockSpec(memory_space=pltpu.SMEM), whole, whole],
        out_specs=whole,
        compiler_params=pltpu.CompilerParams(vmem_limit_bytes=8 * MIB),
        cost_estimate=pl.CostEstimate(flops=2 * own.size * rank, bytes_accessed=4 * own.size, transcendentals=0),
        name="cross",
    )(place, own, other)


def all_to_all(x, axis, groups=None):
    return lax.all_to_all(x, axis, split_axis=0, concat_axis=0, tiled=True, axis_index_groups=groups)


def shifted(x, by):
    n = lax.axis_size("tm")
    return lax.ppermute(x, "tm", [(i, (i + by) % n) for i in range(n)])


def paired(x, by):
    return lax.ppermute(x, "tm", [(i, i ^ by) for i in range(lax.axis_size("tm"))])


def across(x):
    return lax.ppermute(x, "grid", [(g, g ^ 1) for g in range(Y * Z * C)])


def entering(end, gain, start):
    message = jnp.concatenate([end, jnp.broadcast_to(gain, end.shape)])
    i = lax.axis_index("tm")
    total, so_far = jnp.zeros_like(end), jnp.ones_like(end)
    for d in range(1, lax.axis_size("tm")):
        got = shifted(message, d)
        total = total + jnp.where(i >= d, so_far * got[:2], 0.0)
        so_far = so_far * jnp.where(i >= d, got[2:4], 1.0)
    return total + so_far * start


def summed_over_hours(pieces):
    send0, keep0, send1, keep1 = pieces
    q = send0.shape[0] // 2
    wide = lambda v: v.astype(F32)
    got0 = paired(send0, 1)
    got1 = paired(send1, 3)
    last0 = paired((wide(keep0[q:]) + wide(got0[q:])).astype(BF16), 3)
    last1 = paired((wide(keep1[q:]) + wide(got1[:q])).astype(BF16), 1)
    left = wide(keep0[:q]) + wide(got0[:q]) + wide(last0)
    right = wide(keep1[:q]) + wide(got1[q:]) + wide(last1)
    return jnp.concatenate([left, right], axis=1)


def per_device(x0, x1, fading, starting, operator0, operator1):
    grid = lax.axis_size("grid")
    rows, _ = x0.shape
    hours = rows * grid
    scale = (hours * lax.axis_size("tm")) ** -0.5
    core = lax.axis_index("grid") % C
    place = jnp.stack([core, lax.axis_index("tm")]).astype(jnp.int32)
    n = grid // C
    groups = [[k * C + c for k in range(n)] for c in range(C)]
    packed, *tables = prepare(x0, x1, fading, grid)
    operators = jnp.stack([operator0, operator1])
    rest = (tables, operators, place, starting, starting[:, None])
    packed, rest = lax.optimization_barrier((packed, rest))
    x = all_to_all(packed, "grid")
    x, (tables, operators, place, starting, start_rows) = lax.optimization_barrier((x, rest))
    block, since, to_end, gain = tables
    own, other, end, begin = forward(place, x, operators, block, start_rows)
    enter = entering(end, gain[:, :1], begin)
    enter = enter + across(enter)
    since = lax.dynamic_index_in_dim(since.reshape(2, C, n, rows), core, 1, keepdims=False).transpose(1, 0, 2)
    p = own + across(other) - since[..., None] * enter[None, :, None]
    p, x = lax.optimization_barrier((p.astype(BF16), x))
    p = all_to_all(p, "grid", groups)
    q = p.astype(F32).sum(axis=0).astype(BF16)
    q_own = all_to_all(jnp.broadcast_to(q, p.shape), "grid", groups)
    q_other = across(q_own)
    weight = to_end.reshape(2, grid, rows).transpose(1, 0, 2)[..., None]
    mean = entering((x.astype(F32) * weight).sum(axis=(0, 2)), gain[:, :1], starting)
    w1 = backward(1, place, q_own, q_other, block, x, mean)
    wetness = summed_over_hours(w1) * scale
    sent = lax.dynamic_index_in_dim(cross(place, q_own, q_other).reshape(C, -1, q.shape[2]), core, 0, keepdims=False)
    sent = sent.astype(BF16)
    half = sent.astype(F32)
    for d in range(1, lax.axis_size("tm")):
        half = half + shifted(sent, d).astype(F32)
    partner = across(half)
    middle = jnp.concatenate([jnp.where(core == 0, half, partner), jnp.where(core == 0, partner, half)])
    w0 = backward(0, place, q_own, q_other, block, x, mean)
    warmth = summed_over_hours(w0) * scale
    return warmth, wetness, middle * scale


def solution(mesh):
    return jax.shard_map(
        per_device,
        mesh=mesh,
        in_specs=(
            P(("tm", "grid"), None),
            P(("tm", "grid"), None),
            P(None, "tm"),
            P(None, "grid"),
            P("grid", None),
            P("grid", None),
        ),
        out_specs=(P("tm", "grid"), P("tm", "grid"), P()),
        check_vma=False,
    )
```

time: 350 us -> 277 us (0.79)
  waiting for transfers between devices: 202 us -> 22.4 us
  blocking collectives: 0 us -> 150 us
  starting transfers between devices: 66.2 us -> 34.5 us
  local copies, waits for them, and re-layouts: 20.1 us -> 8.46 us
  Pallas kernels: 33 us -> 41.3 us
  other arithmetic: 24.7 us -> 18.5 us
    all_to_all x3 -> x2, waiting for transfers between devices: 176 us -> 8.09 us  [all_to_all(): lax.all_to_all(x, axis, split_axis=0, concat_axis=0, tiled=True, axis_ind...]
    all_to_all x0 -> x1, blocking collectives: none -> 150 us  [all_to_all(): lax.all_to_all(x, axis, split_axis=0, concat_axis=0, tiled=True, axis_ind...]
    all_to_all x3 -> x2, starting transfers between devices: 39.4 us -> 8.8 us  [all_to_all(): lax.all_to_all(x, axis, split_axis=0, concat_axis=0, tiled=True, axis_ind...]
    ppermute x21 -> x9, waiting for transfers between devices: 23.7 us -> 1.54 us  [shifted(): return lax.ppermute(x, 'tm', [(i, (i + by) % n) for i in range(n)])]
    ppermute x0 -> x8, waiting for transfers between devices: none -> 11.3 us  [paired(): lax.ppermute(x, 'tm', [(i, i ^ by) for i in range(lax.axis_size('tm'))])]
    unnamed x25 -> x24, local copies, waits for them, and re-layouts: 14.7 us -> 5.12 us
    pallas_call x5, Pallas kernels: 33 us -> 41.3 us  [the longest x2 19.9 us: backward(): pl.pallas_call(backward_kernel, grid=(2 * steps,), in_specs=[pl.BlockSpec...]
    ppermute x0 -> x8, starting transfers between devices: none -> 7.77 us  [paired(): lax.ppermute(x, 'tm', [(i, i ^ by) for i in range(lax.axis_size('tm'))])]
  transfers between devices with their start and end apart: 27 -> 23, of which waited for: 14 -> 9; matrix products, arithmetic and copies ran while one was open for 6% -> 5% of each run, Pallas kernels for 0% -> 7%
where the time goes in v4:
time: 277 us; the launch traced here: 276 us
  blocking collectives  150 us (54%)
  Pallas kernels  41.3 us (15%)
  starting transfers between devices  34.5 us (12%)
  waiting for transfers between devices  22.4 us (8%)
  other arithmetic  18.5 us (7%)
  local copies, waits for them, and re-layouts  8.46 us (3%)
    all_to_all x1, blocking collectives, all_to_all(): lax.all_to_all(x, axis, split_axis=0, concat_axis=0, tiled=True, axis_ind...  150 us
    pallas_call x2, Pallas kernels, backward(): pl.pallas_call(backward_kernel, grid=(2 * steps,), in_specs=[pl.BlockSpec...  19.9 us
    pallas_call x1, Pallas kernels, forward(): pl.pallas_call(forward_kernel, grid=(2,), in_specs=[pl.BlockSpec(memory_s...  14.6 us
    ppermute x9, starting transfers between devices, shifted(): return lax.ppermute(x, 'tm', [(i, (i + by) % n) for i in range(n)])  12 us
    ppermute x8, waiting for transfers between devices, paired(): lax.ppermute(x, 'tm', [(i, i ^ by) for i in range(lax.axis_size('tm'))])  11.3 us
    all_to_all x2, starting transfers between devices, all_to_all(): lax.all_to_all(x, axis, split_axis=0, concat_axis=0, tiled=True, axis_ind...  8.8 us
    reduce_sum x1, other arithmetic, per_device(): (x.astype(F32) * weight).sum(axis=(0, 2))  8.54 us
    all_to_all x2, waiting for transfers between devices, all_to_all(): lax.all_to_all(x, axis, split_axis=0, concat_axis=0, tiled=True, axis_ind...  8.09 us
  transfers between devices with their start and end apart: 23, of which 9 were waited for; matrix products, arithmetic and copies ran while one was open for 5% of the time, Pallas kernels for 7%

profile of v4, /device:TPU:1, one launch (start us, length us, event | category | flops | bytes accessed | tf_op | source)
XLA Modules:
  0.0 276.0 jit_solution(2558099100454644295)
XLA Ops:
  2.2 2.3 pad_maximum_fusion.op_ref
  5.8 2.8 %copy-done.3 = bf16[32,98304]{1,0:T(8,128)(2,1)S(1)} copy-done((bf16[32,98304]{1,0:T(8,128)(2,1)S(1)}, bf16[32,98304]{1,0:T(8,128)(2,1)}, u32[]{:S(2)}) %copy-start.3) | copy-done | bytes 6291480
  8.6 5.9 %prepare.1 = (bf16[32,2,32,3072]{3,2,1,0:T(8,128)(2,1)S(1)}, f32[8,264,384]{2,1,0:T(8,128)S(1)}, f32[8,256]{1,0:T(8,128)S(1)}, f32[8,256]{1,0:T(8,128)S(1)}, f32[2,256]{1,0:T(2,128)S(1)}) custom-call(bf16[32,98304]{1,0:T(8,128)(2,1)S(1)} %copy-done.2, bf16[32,98304]{1,0:T(8,128)(2,1)S(1)} %copy-done.3, f32[8,256]{1,0:T(8,128)S(1)} %reshape.22.fading_ref), custom_call_target="tpu_custom_call" | custom-call | bytes 25165824 | tf_op jit(solution)/shard_map/prepare/pallas_call | solution.py:71
  14.6 150.0 %all_to_all.15.x_ref = bf16[32,2,32,3072]{3,2,1,0:T(8,128)(2,1)} all-to-all(bf16[32,2,32,3072]{3,2,1,0:T(8,128)(2,1)S(1)} %get-tuple-element.45), channel_id=1, replica_groups=mesh['tm'=4,'grid'=32] {'grid'}, dimensions={0} | all-to-all | bytes 25165824 | tf_op jit(solution)/shard_map/all_to_all | solution.py:267
  164.5 14.6 %forward.1 = (f32[16,2,32,256]{3,2,1,0:T(8,128)S(1)}, f32[16,2,32,256]{3,2,1,0:T(8,128)}, f32[2,256]{1,0:T(2,128)S(1)}, f32[2,256]{1,0:T(2,128)S(1)}) custom-call(s32[2]{0:T(128)S(1)} %pad_add_fusion.place_ref, bf16[32,2,32,3072]{3,2,1,0:T(8,128)(2,1)} %all_to_all.15.x_ref, bf16[2,3072,256]{2,1,0:T(8,128)(2,1)S(1)} %pad_maximum_fusion.op_ref, ...), custom_call_target="tpu_custom_call" | custom-call | flops 3221225472 | bytes 12582912 | tf_op jit(solution)/shard_map/forward/pallas_call | solution.py:133
  181.7 2.4 collective-permute-start.2
  186.9 1.9 collective-permute-start.4
  189.6 2.2 subtract_convert_fusion
  191.9 3.8 %all-to-all-start.1 = ((bf16[16,2,32,256]{3,2,1,0:T(8,128)(2,1)}), bf16[16,2,32,256]{3,2,1,0:T(8,128)(2,1)S(1)}, u32[]{:S(2)}, u32[]{:S(2)}) async-start(bf16[16,2,32,256]{3,2,1,0:T(8,128)(2,1)} %subtract_convert_fusion), calls=%async_computation.1 | async-start | bytes 1048576 | tf_op jit(solution)/shard_map/all_to_all | solution.py:267
  195.6 8.5 %multiply_reduce_fusion = f32[2,3072]{1,0:T(2,128)S(1)} fusion(bf16[32,2,32,3072]{3,2,1,0:T(8,128)(2,1)} %all_to_all.15.x_ref, f32[32,2,32]{2,1,0:T(2,128)S(1)} %bitcast.21), kind=kLoop, calls=%fused_computation | loop fusion | flops 18868224 | bytes 12615680 | tf_op jit(solution)/shard_map/reduce_sum | solution.py:334
  204.2 1.4 all-to-all-done.1
  206.5 5.0 %all-to-all-start.2 = ((bf16[16,2,32,256]{3,2,1,0:T(8,128)(2,1)}), bf16[16,2,32,256]{3,2,1,0:T(8,128)(2,1)S(1)}, u32[]{:S(2)}, u32[]{:S(2)}) async-start(bf16[16,2,32,256]{3,2,1,0:T(8,128)(2,1)} %broadcast_in_dim.52), calls=%async_computation.2 | async-start | bytes 1048576 | tf_op jit(solution)/shard_map/all_to_all | solution.py:267
  211.7 3.5 %collective-permute-start.7 = (f32[4,3072]{1,0:T(4,128)S(1)}, f32[4,3072]{1,0:T(4,128)S(1)}, u32[]{:S(2)}, u32[]{:S(2)}) collective-permute-start(f32[4,3072]{1,0:T(4,128)S(1)} %pad_maximum_fusion.1), channel_id=1, source_target_pairs={{0,64},{32,96},{64,0},{96,32},{1,65},{33,97},{65,1},{97,33},{2,66}... | collective-permute-start | bytes 147464 | tf_op jit(solution)/shard_map/ppermute | solution.py:272
  215.2 6.7 %all-to-all-done.2.own_ref = bf16[16,2,32,256]{3,2,1,0:T(8,128)(2,1)S(1)} async-done(((bf16[16,2,32,256]{3,2,1,0:T(8,128)(2,1)}), bf16[16,2,32,256]{3,2,1,0:T(8,128)(2,1)S(1)}, u32[]{:S(2)}, u32[]{:S(2)}) %all-to-all-start.2) | async-done | bytes 524320 | tf_op jit(solution)/shard_map/all_to_all | solution.py:267
  221.9 2.1 collective-permute-start.5
  226.6 3.5 %collective-permute-start.18 = (bf16[128,256]{1,0:T(8,128)(2,1)S(1)}, bf16[128,256]{1,0:T(8,128)(2,1)S(1)}, u32[]{:S(2)}, u32[]{:S(2)}) collective-permute-start(bf16[128,256]{1,0:T(8,128)(2,1)S(1)} %fusion), channel_id=1, source_target_pairs={{0,64},{32,96},{64,0},{96,32},{1,65},{33,97},{65,1},{97,33},{2,66}... | collective-permute-start | bytes 196616 | tf_op jit(solution)/shard_map/ppermute | solution.py:272
  230.1 10.0 %backward.3 = (bf16[128,1536]{1,0:T(8,128)(2,1)}, bf16[128,1536]{1,0:T(8,128)(2,1)}, bf16[128,1536]{1,0:T(8,128)(2,1)}, bf16[128,1536]{1,0:T(8,128)(2,1)}) custom-call(s32[2]{0:T(128)} %copy-done.6, bf16[16,2,32,256]{3,2,1,0:T(8,128)(2,1)} %copy-done.1, bf16[16,2,32,256]{3,2,1,0:T(8,128)(2,1)} %copy-done.4, f32[8,264,384]{2,1,0:T(8,128)} %copy-done, ...), custom_call_target="tpu_custom_call" | custom-call | flops 3221225472 | bytes 6291456 | tf_op jit(solution)/shard_map/backward/pallas_call | solution.py:217
  240.1 1.4 collective-permute-start.13
  242.0 1.9 collective-permute-start.20
  243.8 9.9 %backward.2 = (bf16[128,1536]{1,0:T(8,128)(2,1)}, bf16[128,1536]{1,0:T(8,128)(2,1)}, bf16[128,1536]{1,0:T(8,128)(2,1)}, bf16[128,1536]{1,0:T(8,128)(2,1)}) custom-call(s32[2]{0:T(128)} %copy-done.6, bf16[16,2,32,256]{3,2,1,0:T(8,128)(2,1)} %copy-done.1, bf16[16,2,32,256]{3,2,1,0:T(8,128)(2,1)} %copy-done.4, f32[8,264,384]{2,1,0:T(8,128)} %copy-done, ...), custom_call_target="tpu_custom_call" | custom-call | flops 3221225472 | bytes 6291456 | tf_op jit(solution)/shard_map/backward/pallas_call | solution.py:217
  253.8 2.4 collective-permute-start.11
  258.1 6.5 %collective-permute-done.9 = bf16[128,1536]{1,0:T(8,128)(2,1)S(1)} collective-permute-done((bf16[128,1536]{1,0:T(8,128)(2,1)}, bf16[128,1536]{1,0:T(8,128)(2,1)S(1)}, u32[]{:S(2)}, u32[]{:S(2)}) %collective-permute-start.9) | collective-permute-done | bytes 393248 | tf_op jit(solution)/shard_map/ppermute | solution.py:276
  265.6 2.4 collective-permute-start.10
  270.2 3.7 %collective-permute-done.10 = bf16[64,1536]{1,0:T(8,128)(2,1)S(1)} collective-permute-done((bf16[64,1536]{1,0:T(8,128)(2,1)S(1)}, bf16[64,1536]{1,0:T(8,128)(2,1)S(1)}, u32[]{:S(2)}, u32[]{:S(2)}) %collective-permute-start.10) | collective-permute-done | bytes 196640 | tf_op jit(solution)/shard_map/ppermute | solution.py:276
  (87 shorter events, 20.1 us)
Async XLA Ops:
  2.2 223.3 %copy-start.6 = (s32[2]{0:T(128)}, s32[2]{0:T(128)S(1)}, u32[]{:S(2)}) copy-start(s32[2]{0:T(128)S(1)} %pad_add_fusion.place_ref) | copy-start | bytes 28
  180.1 9.5 %collective-permute-start = (f32[16,2,32,256]{3,2,1,0:T(8,128)}, f32[16,2,32,256]{3,2,1,0:T(8,128)S(1)}, u32[]{:S(2)}, u32[]{:S(2)}) collective-permute-start(f32[16,2,32,256]{3,2,1,0:T(8,128)} %get-tuple-element.60), channel_id=1, source_target_pairs={{0,1},{1,0},{2,3},{3,2},{4,5},{5,4},{6,7},{7,6},{8,9},{9,8},{10,11... | collective-permute-start | bytes 3145736 | tf_op jit(solution)/shard_map/ppermute | solution.py:280
  180.5 4.9 %collective-permute-start.1 = (f32[4,256]{1,0:T(4,128)S(1)}, f32[4,256]{1,0:T(4,128)S(1)}, u32[]{:S(2)}, u32[]{:S(2)}) collective-permute-start(f32[4,256]{1,0:T(4,128)S(1)} %pad_maximum_fusion.2), channel_id=1, source_target_pairs={{0,32},{32,64},{64,96},{96,0},{1,33},{33,65},{65,97},{97,1},{2,34}... | collective-permute-start | bytes 12296 | tf_op jit(solution)/shard_map/ppermute | solution.py:272
  181.7 4.0 %collective-permute-start.2 = (f32[4,256]{1,0:T(4,128)S(1)}, f32[4,256]{1,0:T(4,128)S(1)}, u32[]{:S(2)}, u32[]{:S(2)}) collective-permute-start(f32[4,256]{1,0:T(4,128)S(1)} %pad_maximum_fusion.2), channel_id=1, source_target_pairs={{0,64},{32,96},{64,0},{96,32},{1,65},{33,97},{65,1},{97,33},{2,66}... | collective-permute-start | bytes 12296 | tf_op jit(solution)/shard_map/ppermute | solution.py:272
  184.1 2.8 collective-permute-start.3
  186.9 2.7 collective-permute-start.4
  191.9 13.7 %all-to-all-start.1 = ((bf16[16,2,32,256]{3,2,1,0:T(8,128)(2,1)}), bf16[16,2,32,256]{3,2,1,0:T(8,128)(2,1)S(1)}, u32[]{:S(2)}, u32[]{:S(2)}) async-start(bf16[16,2,32,256]{3,2,1,0:T(8,128)(2,1)} %subtract_convert_fusion), calls=%async_computation.1 | async-start | bytes 1048576 | tf_op jit(solution)/shard_map/all_to_all | solution.py:267
  206.5 15.4 %all-to-all-start.2 = ((bf16[16,2,32,256]{3,2,1,0:T(8,128)(2,1)}), bf16[16,2,32,256]{3,2,1,0:T(8,128)(2,1)S(1)}, u32[]{:S(2)}, u32[]{:S(2)}) async-start(bf16[16,2,32,256]{3,2,1,0:T(8,128)(2,1)} %broadcast_in_dim.52), calls=%async_computation.2 | async-start | bytes 1048576 | tf_op jit(solution)/shard_map/all_to_all | solution.py:267
  211.6 12.4 %collective-permute-start.6 = (f32[4,3072]{1,0:T(4,128)S(1)}, f32[4,3072]{1,0:T(4,128)S(1)}, u32[]{:S(2)}, u32[]{:S(2)}) collective-permute-start(f32[4,3072]{1,0:T(4,128)S(1)} %pad_maximum_fusion.1), channel_id=1, source_target_pairs={{0,32},{32,64},{64,96},{96,0},{1,33},{33,65},{65,97},{97,1},{2,34}... | collective-permute-start | bytes 147464 | tf_op jit(solution)/shard_map/ppermute | solution.py:272
  211.7 12.3 %collective-permute-start.7 = (f32[4,3072]{1,0:T(4,128)S(1)}, f32[4,3072]{1,0:T(4,128)S(1)}, u32[]{:S(2)}, u32[]{:S(2)}) collective-permute-start(f32[4,3072]{1,0:T(4,128)S(1)} %pad_maximum_fusion.1), channel_id=1, source_target_pairs={{0,64},{32,96},{64,0},{96,32},{1,65},{33,97},{65,1},{97,33},{2,66}... | collective-permute-start | bytes 147464 | tf_op jit(solution)/shard_map/ppermute | solution.py:272
  215.2 8.8 %collective-permute-start.8 = (f32[4,3072]{1,0:T(4,128)S(1)}, f32[4,3072]{1,0:T(4,128)S(1)}, u32[]{:S(2)}, u32[]{:S(2)}) collective-permute-start(f32[4,3072]{1,0:T(4,128)S(1)} %pad_maximum_fusion.1), channel_id=1, source_target_pairs={{0,96},{32,0},{64,32},{96,64},{1,97},{33,1},{65,33},{97,65},{2,98}... | collective-permute-start | bytes 147464 | tf_op jit(solution)/shard_map/ppermute | solution.py:272
  221.9 3.6 %collective-permute-start.5 = (bf16[16,2,32,256]{3,2,1,0:T(8,128)(2,1)S(1)}, bf16[16,2,32,256]{3,2,1,0:T(8,128)(2,1)S(1)}, u32[]{:S(2)}, u32[]{:S(2)}) collective-permute-start(bf16[16,2,32,256]{3,2,1,0:T(8,128)(2,1)S(1)} %all-to-all-done.2.own_ref), channel_id=1, source_target_pairs={{0,1},{1,0},{2,3},{3,2},{4,5},{5,4},{6,7},{7,6},{8,9},{9,8},{10,11... | collective-permute-start | bytes 1572872 | tf_op jit(solution)/shard_map/ppermute | solution.py:280
  226.5 15.4 %collective-permute-start.17 = (bf16[128,256]{1,0:T(8,128)(2,1)S(1)}, bf16[128,256]{1,0:T(8,128)(2,1)S(1)}, u32[]{:S(2)}, u32[]{:S(2)}) collective-permute-start(bf16[128,256]{1,0:T(8,128)(2,1)S(1)} %fusion), channel_id=1, source_target_pairs={{0,32},{32,64},{64,96},{96,0},{1,33},{33,65},{65,97},{97,1},{2,34}... | collective-permute-start | bytes 196616 | tf_op jit(solution)/shard_map/ppermute | solution.py:272
  226.6 15.3 %collective-permute-start.18 = (bf16[128,256]{1,0:T(8,128)(2,1)S(1)}, bf16[128,256]{1,0:T(8,128)(2,1)S(1)}, u32[]{:S(2)}, u32[]{:S(2)}) collective-permute-start(bf16[128,256]{1,0:T(8,128)(2,1)S(1)} %fusion), channel_id=1, source_target_pairs={{0,64},{32,96},{64,0},{96,32},{1,65},{33,97},{65,1},{97,33},{2,66}... | collective-permute-start | bytes 196616 | tf_op jit(solution)/shard_map/ppermute | solution.py:272
  230.1 11.8 %collective-permute-start.19 = (bf16[128,256]{1,0:T(8,128)(2,1)S(1)}, bf16[128,256]{1,0:T(8,128)(2,1)S(1)}, u32[]{:S(2)}, u32[]{:S(2)}) collective-permute-start(bf16[128,256]{1,0:T(8,128)(2,1)S(1)} %fusion), channel_id=1, source_target_pairs={{0,96},{32,0},{64,32},{96,64},{1,97},{33,1},{65,33},{97,65},{2,98}... | collective-permute-start | bytes 196616 | tf_op jit(solution)/shard_map/ppermute | solution.py:272
  240.1 16.9 %collective-permute-start.13 = (bf16[128,1536]{1,0:T(8,128)(2,1)}, bf16[128,1536]{1,0:T(8,128)(2,1)S(1)}, u32[]{:S(2)}, u32[]{:S(2)}) collective-permute-start(bf16[128,1536]{1,0:T(8,128)(2,1)} %get-tuple-element.74), channel_id=1, source_target_pairs={{0,32},{32,0},{64,96},{96,64},{1,33},{33,1},{65,97},{97,65},{2,34}... | collective-permute-start | bytes 1179656 | tf_op jit(solution)/shard_map/ppermute | solution.py:276
  241.6 15.9 %collective-permute-start.15 = (bf16[128,1536]{1,0:T(8,128)(2,1)}, bf16[128,1536]{1,0:T(8,128)(2,1)S(1)}, u32[]{:S(2)}, u32[]{:S(2)}) collective-permute-start(bf16[128,1536]{1,0:T(8,128)(2,1)} %get-tuple-element.76), channel_id=1, source_target_pairs={{0,96},{32,64},{64,32},{96,0},{1,97},{33,65},{65,33},{97,1},{2,98}... | collective-permute-start | bytes 1179656 | tf_op jit(solution)/shard_map/ppermute | solution.py:276
  242.0 14.3 %collective-permute-start.20 = (f32[128,256]{1,0:T(8,128)S(1)}, f32[128,256]{1,0:T(8,128)S(1)}, u32[]{:S(2)}, u32[]{:S(2)}) collective-permute-start(f32[128,256]{1,0:T(8,128)S(1)} %convert_add_fusion.4), channel_id=1, source_target_pairs={{0,1},{1,0},{2,3},{3,2},{4,5},{5,4},{6,7},{7,6},{8,9},{9,8},{10,11... | collective-permute-start | bytes 393224 | tf_op jit(solution)/shard_map/ppermute | solution.py:280
  253.7 10.9 %collective-permute-start.9 = (bf16[128,1536]{1,0:T(8,128)(2,1)}, bf16[128,1536]{1,0:T(8,128)(2,1)S(1)}, u32[]{:S(2)}, u32[]{:S(2)}) collective-permute-start(bf16[128,1536]{1,0:T(8,128)(2,1)} %get-tuple-element.70), channel_id=1, source_target_pairs={{0,32},{32,0},{64,96},{96,64},{1,33},{33,1},{65,97},{97,65},{2,34}... | collective-permute-start | bytes 1179656 | tf_op jit(solution)/shard_map/ppermute | solution.py:276
  253.8 14.2 %collective-permute-start.11 = (bf16[128,1536]{1,0:T(8,128)(2,1)}, bf16[128,1536]{1,0:T(8,128)(2,1)S(1)}, u32[]{:S(2)}, u32[]{:S(2)}) collective-permute-start(bf16[128,1536]{1,0:T(8,128)(2,1)} %get-tuple-element.72), channel_id=1, source_target_pairs={{0,96},{32,64},{64,32},{96,0},{1,97},{33,65},{65,33},{97,1},{2,98}... | collective-permute-start | bytes 1179656 | tf_op jit(solution)/shard_map/ppermute | solution.py:276
  257.1 13.0 %collective-permute-start.14 = (bf16[64,1536]{1,0:T(8,128)(2,1)S(1)}, bf16[64,1536]{1,0:T(8,128)(2,1)S(1)}, u32[]{:S(2)}, u32[]{:S(2)}) collective-permute-start(bf16[64,1536]{1,0:T(8,128)(2,1)S(1)} %add_convert_fusion.1), channel_id=1, source_target_pairs={{0,96},{32,64},{64,32},{96,0},{1,97},{33,65},{65,33},{97,1},{2,98}... | collective-permute-start | bytes 589832 | tf_op jit(solution)/shard_map/ppermute | solution.py:276
  257.5 12.6 %collective-permute-start.16 = (bf16[64,1536]{1,0:T(8,128)(2,1)S(1)}, bf16[64,1536]{1,0:T(8,128)(2,1)S(1)}, u32[]{:S(2)}, u32[]{:S(2)}) collective-permute-start(bf16[64,1536]{1,0:T(8,128)(2,1)S(1)} %add_convert_fusion), channel_id=1, source_target_pairs={{0,32},{32,0},{64,96},{96,64},{1,33},{33,1},{65,97},{97,65},{2,34}... | collective-permute-start | bytes 589832 | tf_op jit(solution)/shard_map/ppermute | solution.py:276
  265.6 8.4 %collective-permute-start.10 = (bf16[64,1536]{1,0:T(8,128)(2,1)S(1)}, bf16[64,1536]{1,0:T(8,128)(2,1)S(1)}, u32[]{:S(2)}, u32[]{:S(2)}) collective-permute-start(bf16[64,1536]{1,0:T(8,128)(2,1)S(1)} %add_convert_fusion.3), channel_id=1, source_target_pairs={{0,96},{32,64},{64,32},{96,0},{1,97},{33,65},{65,33},{97,1},{2,98}... | collective-permute-start | bytes 589832 | tf_op jit(solution)/shard_map/ppermute | solution.py:276
  269.0 6.0 %collective-permute-start.12 = (bf16[64,1536]{1,0:T(8,128)(2,1)S(1)}, bf16[64,1536]{1,0:T(8,128)(2,1)S(1)}, u32[]{:S(2)}, u32[]{:S(2)}) collective-permute-start(bf16[64,1536]{1,0:T(8,128)(2,1)S(1)} %add_convert_fusion.2), channel_id=1, source_target_pairs={{0,32},{32,0},{64,96},{96,64},{1,33},{33,1},{65,97},{97,65},{2,34}... | collective-permute-start | bytes 589832 | tf_op jit(solution)/shard_map/ppermute | solution.py:276
  (11 other events, 267.4 us)

commit v5 on v4

v5 whole, which is shorter than its diff:
```python
import functools

import jax
import jax.numpy as jnp
from jax import lax
from jax.experimental import pallas as pl
from jax.experimental.pallas import tpu as pltpu
from jax.sharding import PartitionSpec as P


BLK = 256
NCHUNK = 512
Y, Z, C = 4, 4, 2
F32, BF16 = jnp.float32, jnp.bfloat16
HIGHEST = lax.Precision.HIGHEST
MIB = 1 << 20


def thirds(v):
    high = v.astype(BF16)
    v = v - high.astype(F32)
    middle = v.astype(BF16)
    return high, middle, (v - middle.astype(F32)).astype(BF16)


def prepare_kernel(x0_ref, x1_ref, fading_ref, out_ref, block_ref, since_ref, to_end_ref, sems):
    n, _, _, width = out_ref.shape

    def copies():
        for i in range(n):
            for f, x_ref in enumerate((x0_ref, x1_ref)):
                yield pltpu.make_async_copy(x_ref.at[:, pl.ds(i * width, width)], out_ref.at[i, f], sems.at[2 * i + f])

    for copy in copies():
        copy.start()
    nb = fading_ref.shape[1] // BLK
    a = jnp.concatenate([fading_ref[f : f + 1, b * BLK : (b + 1) * BLK] for f in range(2) for b in range(nb)])
    log_a = jnp.log(a)
    r = lax.broadcasted_iota(jnp.int32, (BLK, BLK), 0)
    c = lax.broadcasted_iota(jnp.int32, (BLK, BLK), 1)
    upto = jnp.where(r <= c, 1.0, 0.0)
    inclusive = jnp.dot(log_a, upto, precision=HIGHEST, preferred_element_type=F32)
    exclusive = jnp.where(lax.broadcasted_iota(jnp.int32, a.shape, 1) == 0, 0.0, pltpu.roll(inclusive, 1, 1))
    column = exclusive.T
    fresh = 1.0 - a
    total = inclusive[:, BLK - 1 : BLK]
    ends = []
    for f in range(2):
        sums = [total[f * nb + b : f * nb + b + 1] for b in range(nb)]
        ahead = jnp.zeros_like(sums[0])
        for b in range(nb):
            k = f * nb + b
            row = slice(k, k + 1)
            weight = jnp.exp(jnp.minimum(column[:, k : k + 1] - inclusive[row], 0.0)) * fresh[row]
            block_ref[k, :BLK, :BLK] = jnp.where(r == c, 1.0, jnp.where(c < r, -weight, 0.0))
            block_ref[k, :BLK, BLK:] = jnp.broadcast_to(jnp.exp(column[:, k : k + 1]), (BLK, 128))
            last = jnp.exp(sums[b] - inclusive[row]) * fresh[row]
            block_ref[k, BLK:, :BLK] = jnp.broadcast_to(last, (8, BLK))
            block_ref[k, BLK:, BLK:] = jnp.broadcast_to(-jnp.exp(sums[b]), (8, 128))
            behind = sum(sums[b + 1 :], jnp.zeros_like(ahead))
            since_ref[row] = jnp.exp(ahead + exclusive[row])
            ends.append(jnp.exp(behind + (sums[b] - inclusive[row])) * fresh[row])
            ahead = ahead + sums[b]
    to_end_ref[...] = jnp.concatenate(ends).T
    for copy in copies():
        copy.wait()


def prepare(x0, x1, fading, n):
    rows, points = x0.shape
    width = points // n
    count = fading.size // BLK
    whole = pl.BlockSpec(memory_space=pltpu.VMEM)
    return pl.pallas_call(
        prepare_kernel,
        in_specs=[pl.BlockSpec(memory_space=pl.ANY), pl.BlockSpec(memory_space=pl.ANY), whole],
        out_specs=[pl.BlockSpec(memory_space=pl.ANY), whole, whole, whole],
        out_shape=[
            jax.ShapeDtypeStruct((n, 2, rows, width), x0.dtype),
            jax.ShapeDtypeStruct((count, BLK + 8, BLK + 128), F32),
            jax.ShapeDtypeStruct((count, BLK), F32),
            jax.ShapeDtypeStruct((BLK, count), F32),
        ],
        scratch_shapes=[pltpu.SemaphoreType.DMA((2 * n,))],
        compiler_params=pltpu.CompilerParams(vmem_limit_bytes=24 * MIB),
        cost_estimate=pl.CostEstimate(flops=0, bytes_accessed=8 * x0.size, transcendentals=0),
        name="prepare",
    )(x0, x1, fading)


def forward_kernel(
    field, place_ref, x_ref, op_ref, block_ref, to_end_ref, start_ref, own_ref, other_ref, end_ref, begin_ref, y_ref, s_ref
):
    step = pl.program_id(0)
    _, _, rows, chunk = x_ref.shape
    hours, rank = y_ref.shape
    nb = hours // BLK
    x = x_ref[:, 0].reshape(hours, chunk)
    y = jnp.dot(x, op_ref[...], preferred_element_type=F32)
    start = jnp.concatenate([part.astype(F32) for part in thirds(start_ref[field : field + 1])] + [jnp.zeros((5, chunk), F32)])
    begin = jnp.dot(start.astype(BF16), op_ref[...], preferred_element_type=F32)

    @pl.when(step == 0)
    def _():
        y_ref[...] = y
        s_ref[...] = begin

    @pl.when(step > 0)
    def _():
        y_ref[...] += y
        s_ref[...] += begin

    end = jnp.zeros((1, chunk), F32)
    for b in range(nb):
        part = x_ref[b * (BLK // rows) : (b + 1) * (BLK // rows), 0].reshape(BLK, chunk).astype(F32)
        k = field * nb + b
        end = end + (part * to_end_ref[:, k : k + 1]).sum(axis=0, keepdims=True)
    last = pl.num_programs(0) - 1
    for i in range(begin_ref.shape[1] // chunk):

        @pl.when(step == i)
        def _():
            end_ref[0:1, i * chunk : (i + 1) * chunk] = end
            begin_ref[:, i * chunk : (i + 1) * chunk] = start_ref[field : field + 1]

    @pl.when(step == last)
    def _():
        width = begin_ref.shape[1] - rank
        state = jnp.zeros((1, rank), F32)
        gain = jnp.ones((1, 1), F32)
        per = BLK // rows
        for b in range(nb):
            block = block_ref[b]
            out = jnp.dot(block[:, :BLK], y_ref[b * BLK : (b + 1) * BLK], precision=HIGHEST, preferred_element_type=F32)
            out = out - block[:, BLK : BLK + 1] * state
            part = out[:BLK].reshape(per, rows, rank)
            half, at = divmod(b, nb // 2)

            @pl.when(place_ref[0] == half)
            def _():
                own_ref[at * per : (at + 1) * per] = part

            @pl.when(place_ref[0] != half)
            def _():
                other_ref[at * per : (at + 1) * per] = part

            state = out[BLK : BLK + 1]
            gain = gain * -block[BLK : BLK + 1, BLK : BLK + 1]
        end_ref[0:1, width:] = state
        end_ref[1:2] = jnp.broadcast_to(gain, (1, width + rank))
        begin_ref[:, width:] = s_ref[0:1] + s_ref[1:2] + s_ref[2:3]


def forward(field, place, x, operator, tables, starting):
    block, _, to_end = tables
    n, _, rows, width = x.shape
    rank = operator.shape[1]
    hours, chunk = n * rows, 2 * NCHUNK
    nb = hours // BLK
    half = jax.ShapeDtypeStruct((n // 2, rows, rank), F32)
    fixed = lambda *shape: pl.BlockSpec(shape, lambda i: (0,) * len(shape))
    return pl.pallas_call(
        functools.partial(forward_kernel, field),
        grid=(width // chunk,),
        in_specs=[
            pl.BlockSpec(memory_space=pltpu.SMEM),
            pl.BlockSpec((n, 1, rows, chunk), lambda i: (0, field, 0, i)),
            pl.BlockSpec((chunk, rank), lambda i: (i, 0)),
            pl.BlockSpec((nb, BLK + 8, BLK + 128), lambda i: (field, 0, 0)),
            fixed(BLK, 2 * nb),
            pl.BlockSpec((2, chunk), lambda i: (0, i)),
        ],
        out_specs=[fixed(n // 2, rows, rank), fixed(n // 2, rows, rank), fixed(2, width + rank), fixed(1, width + rank)],
        out_shape=[half, half, jax.ShapeDtypeStruct((2, width + rank), F32), jax.ShapeDtypeStruct((1, width + rank), F32)],
        scratch_shapes=[pltpu.VMEM((hours, rank), F32), pltpu.VMEM((8, rank), F32)],
        compiler_params=pltpu.CompilerParams(vmem_limit_bytes=54 * MIB),
        cost_estimate=pl.CostEstimate(
            flops=2 * hours * width * rank, bytes_accessed=2 * hours * width, transcendentals=0
        ),
        name="forward",
    )(place, x, operator, block, to_end, starting)


def backward_kernel(
    place_ref, own_ref, other_ref, block_ref, x_ref, enter_ref, send0_ref, keep0_ref, send1_ref, keep1_ref, z_ref, carried
):
    step = pl.program_id(0)
    rank = own_ref.shape[2]
    quarter = rank // 4

    @pl.when(step == 0)
    def _():
        nb = block_ref.shape[0]
        rows = own_ref.shape[1]
        per = BLK // rows
        swap = place_ref[1]
        reverse = jnp.zeros((rank, 1), F32)

        def placed(ref, value, cols, base=0):
            for d in range(4):
                at = pl.multiple_of(base + jnp.bitwise_xor(d, swap) * quarter, quarter)
                ref[pl.ds(at, quarter), cols] = value[d * quarter : (d + 1) * quarter]

        for b in reversed(range(nb)):
            half, at = divmod(b, nb // 2)
            own = own_ref[at * per : (at + 1) * per].reshape(BLK, rank)
            other = other_ref[at * per : (at + 1) * per].reshape(BLK, rank)
            q = jnp.where(place_ref[0] == half, own.astype(F32), other.astype(F32)).T.astype(BF16)
            out = jnp.zeros((rank, BLK + 128), F32)
            for part in reversed(thirds(block_ref[b, :BLK])):
                out = out + jnp.dot(q, part, preferred_element_type=F32)
            out = out - reverse * block_ref[b, BLK : BLK + 1, :]
            z = out[:, :BLK]
            high = z.astype(BF16)
            cols = slice(b * BLK, (b + 1) * BLK)
            placed(z_ref, high, cols)
            placed(z_ref, (z - high.astype(F32)).astype(BF16), cols, rank)
            reverse = out[:, BLK : BLK + 1]
        placed(carried, jnp.broadcast_to(reverse, carried.shape), slice(0, carried.shape[1]))

    x = x_ref[:, 0].reshape(z_ref.shape[1], x_ref.shape[3])
    w = jnp.dot(z_ref[...], x, preferred_element_type=F32)
    w = w[:rank] + w[rank:] - carried[:, 0:1] * enter_ref[...]
    w = [w[k * quarter : (k + 1) * quarter].astype(BF16) for k in range(4)]

    @pl.when(step < pl.num_programs(0) // 2)
    def _():
        send0_ref[:quarter], send0_ref[quarter:] = w[1], w[2]
        keep0_ref[:quarter], keep0_ref[quarter:] = w[0], w[3]

    @pl.when(step >= pl.num_programs(0) // 2)
    def _():
        send1_ref[:quarter], send1_ref[quarter:] = w[2], w[3]
        keep1_ref[:quarter], keep1_ref[quarter:] = w[0], w[1]


def backward(f, place, own, other, block, x, enter):
    n, _, rows, width = x.shape
    hours, rank = n * rows, own.shape[2]
    nb = hours // BLK
    steps = width // NCHUNK // 2
    q_spec = pl.BlockSpec((n // 2, rows, rank), lambda i: (0, 0, 0))
    left = pl.BlockSpec((rank // 2, NCHUNK), lambda i: (0, jnp.minimum(i, steps - 1)))
    right = pl.BlockSpec((rank // 2, NCHUNK), lambda i: (0, jnp.maximum(i - steps, 0)))
    piece = jax.ShapeDtypeStruct((rank // 2, width // 2), BF16)
    return pl.pallas_call(
        backward_kernel,
        grid=(2 * steps,),
        in_specs=[
            pl.BlockSpec(memory_space=pltpu.SMEM),
            q_spec,
            q_spec,
            pl.BlockSpec((nb, BLK + 8, BLK + 128), lambda i: (f, 0, 0)),
            pl.BlockSpec((n, 1, rows, NCHUNK), lambda i: (0, f, 0, i)),
            pl.BlockSpec((1, NCHUNK), lambda i: (0, i)),
        ],
        out_specs=[left, left, right, right],
        out_shape=[piece] * 4,
        scratch_shapes=[
            pltpu.VMEM((2 * rank, hours), BF16),
            pltpu.VMEM((rank, 128), F32),
        ],
        compiler_params=pltpu.CompilerParams(vmem_limit_bytes=54 * MIB),
        cost_estimate=pl.CostEstimate(
            flops=4 * hours * width * rank, bytes_accessed=2 * hours * width, transcendentals=0
        ),
        name="backward",
    )(place, own, other, block, x, enter)


def cross_kernel(own0_ref, other0_ref, own1_ref, other1_ref, out_ref):
    n, rows, rank = own0_ref.shape
    out = jnp.zeros(out_ref.shape, F32)
    for ref0, ref1 in ((own0_ref, own1_ref), (other0_ref, other1_ref)):
        left = ref0[...].reshape(n * rows, rank).astype(F32).T.astype(BF16)
        out = out + jnp.dot(left, ref1[...].reshape(n * rows, rank), preferred_element_type=F32)
    out_ref[...] = out.astype(out_ref.dtype)


def cross(q0, q1):
    rank, size = q0[0].shape[2], q0[0].size
    whole = pl.BlockSpec(memory_space=pltpu.VMEM)
    return pl.pallas_call(
        cross_kernel,
        out_shape=jax.ShapeDtypeStruct((rank, rank), BF16),
        in_specs=[whole] * 4,
        out_specs=whole,
        compiler_params=pltpu.CompilerParams(vmem_limit_bytes=8 * MIB),
        cost_estimate=pl.CostEstimate(flops=4 * size * rank, bytes_accessed=8 * size, transcendentals=0),
        name="cross",
    )(*q0, *q1)


def all_to_all(x, axis, groups=None):
    return lax.all_to_all(x, axis, split_axis=0, concat_axis=0, tiled=True, axis_index_groups=groups)


def shifted(x, by):
    n = lax.axis_size("tm")
    return lax.ppermute(x, "tm", [(i, (i + by) % n) for i in range(n)])


def paired(x, by):
    return lax.ppermute(x, "tm", [(i, i ^ by) for i in range(lax.axis_size("tm"))])


def across(x):
    return lax.ppermute(x, "grid", [(g, g ^ 1) for g in range(Y * Z * C)])


def entering(end, start, i):
    total, so_far = jnp.zeros_like(start), jnp.ones_like(start)
    for d in range(1, lax.axis_size("tm")):
        got = shifted(end, d)
        total = total + jnp.where(i >= d, so_far * got[:1], 0.0)
        so_far = so_far * jnp.where(i >= d, got[1:], 1.0)
    return total + so_far * start


def summed_over_hours(pieces):
    send0, keep0, send1, keep1 = pieces
    q = send0.shape[0] // 2
    wide = lambda v: v.astype(F32)
    got0 = paired(send0, 1)
    got1 = paired(send1, 3)
    last0 = paired((wide(keep0[q:]) + wide(got0[q:])).astype(BF16), 3)
    last1 = paired((wide(keep1[q:]) + wide(got1[:q])).astype(BF16), 1)
    left = wide(keep0[:q]) + wide(got0[:q]) + wide(last0)
    right = wide(keep1[:q]) + wide(got1[q:]) + wide(last1)
    return jnp.concatenate([left, right], axis=1)


def per_device(x0, x1, fading, starting, operator0, operator1):
    grid = lax.axis_size("grid")
    rows, points = x0.shape
    width, hours = points // grid, rows * grid
    scale = (hours * lax.axis_size("tm")) ** -0.5
    core, shard = lax.axis_index("grid") & (C - 1), lax.axis_index("tm")
    place = jnp.stack([core, shard]).astype(jnp.int32)
    n = grid // C
    groups = [[k * C + c for k in range(n)] for c in range(C)]
    barrier = lax.optimization_barrier

    def lead(f, x, core, shard):
        own, other, end, start = forward(f, place, x, operators[f], tables, starting)
        enter = entering(end, start, shard)
        mean, part = enter[:, :width], enter[:, width:]
        part = part + across(part)
        since = lax.dynamic_index_in_dim(tables[1].reshape(2, C, n, rows)[f], core, 0, keepdims=False)
        p = own + across(other) - since[..., None] * part[None]
        return p.astype(BF16), mean

    def there(p):
        return all_to_all(p, "grid", groups).astype(F32).sum(axis=0).astype(BF16)

    def back(q):
        own = all_to_all(jnp.broadcast_to(q, (n, *q.shape)), "grid", groups)
        return own, across(own)

    packed, *tables = prepare(x0, x1, fading, grid)
    packed, rest = barrier((packed, (tables, place, core, shard, starting, operator0, operator1)))
    x = all_to_all(packed, "grid")
    x, (tables, place, core, shard, starting, *operators) = barrier((x, rest))
    p0, mean0 = lead(0, x, core, shard)
    r0 = there(p0)
    p1, mean1 = lead(1, x, core, shard)
    q0 = back(r0)
    p1, q0 = barrier((p1, q0))
    r1 = there(p1)
    w1 = backward(1, place, *q0, tables[0], x, mean1)
    q1 = back(r1)
    wetness = summed_over_hours(w1) * scale
    w0 = backward(0, place, *q1, tables[0], x, mean0)
    warmth = summed_over_hours(w0) * scale
    sent = lax.dynamic_index_in_dim(cross(q0, q1).reshape(C, -1, operator0.shape[1]), core, 0, keepdims=False)
    half = sent.astype(F32)
    for d in range(1, lax.axis_size("tm")):
        half = half + shifted(sent, d).astype(F32)
    partner = across(half)
    middle = jnp.concatenate([jnp.where(core == 0, half, partner), jnp.where(core == 0, partner, half)])
    return warmth, wetness, middle * scale


def solution(mesh):
    return jax.shard_map(
        per_device,
        mesh=mesh,
        in_specs=(
            P(("tm", "grid"), None),
            P(("tm", "grid"), None),
            P(None, "tm"),
            P(None, "grid"),
            P("grid", None),
            P("grid", None),
        ),
        out_specs=(P("tm", "grid"), P("tm", "grid"), P()),
        check_vma=False,
    )
```

time: 277 us -> 306 us (1.10)
  starting transfers between devices: 34.5 us -> 47.1 us
  waiting for transfers between devices: 22.4 us -> 29.4 us
  local copies, waits for them, and re-layouts: 8.46 us -> 14 us
  Pallas kernels: 41.3 us -> 46.1 us
    all_to_all x2 -> x4, starting transfers between devices: 8.8 us -> 18 us  [all_to_all(): lax.all_to_all(x, axis, split_axis=0, concat_axis=0, tiled=True, axis_ind...]
    reduce_sum x2, other arithmetic: 8.62 us -> 0.09 us  [there(): return all_to_all(p, 'grid', groups).astype(F32).sum(axis=0).astype(BF16)]
    unnamed x24 -> x22, local copies, waits for them, and re-layouts: 5.12 us -> 11.2 us
    pallas_call x1 -> x2, Pallas kernels: 14.6 us -> 20.1 us  [forward(): pl.pallas_call(functools.partial(forward_kernel, field), grid=(width // c...]
    all_to_all x2 -> x4, waiting for transfers between devices: 8.09 us -> 12.9 us  [all_to_all(): lax.all_to_all(x, axis, split_axis=0, concat_axis=0, tiled=True, axis_ind...]
    ppermute x4 -> x7, starting transfers between devices: 5.93 us -> 10.1 us  [across(): return lax.ppermute(x, 'grid', [(g, g ^ 1) for g in range(Y * Z * C)])]
  transfers between devices with their start and end apart: 23 -> 28, of which waited for: 9 -> 10; matrix products, arithmetic and copies ran while one was open for 5% -> 5% of each run, Pallas kernels for 7% -> 7%
where the time goes in v5:
time: 306 us; the launch traced here: 304 us
  blocking collectives  150 us (49%)
  starting transfers between devices  47.1 us (15%)
  Pallas kernels  46.1 us (15%)
  waiting for transfers between devices  29.4 us (10%)
  other arithmetic  16.6 us (5%)
  local copies, waits for them, and re-layouts  14 us (5%)
    all_to_all x1, blocking collectives, all_to_all(): lax.all_to_all(x, axis, split_axis=0, concat_axis=0, tiled=True, axis_ind...  150 us
    pallas_call x2, Pallas kernels, forward(): pl.pallas_call(functools.partial(forward_kernel, field), grid=(width // c...  20.1 us
    pallas_call x2, Pallas kernels, backward(): pl.pallas_call(backward_kernel, grid=(2 * steps,), in_specs=[pl.BlockSpec...  19.7 us
    all_to_all x4, starting transfers between devices, all_to_all(): lax.all_to_all(x, axis, split_axis=0, concat_axis=0, tiled=True, axis_ind...  18 us
    ppermute x8, waiting for transfers between devices, paired(): lax.ppermute(x, 'tm', [(i, i ^ by) for i in range(lax.axis_size('tm'))])  13.1 us
    all_to_all x4, waiting for transfers between devices, all_to_all(): lax.all_to_all(x, axis, split_axis=0, concat_axis=0, tiled=True, axis_ind...  12.9 us
    unnamed x22, local copies, waits for them, and re-layouts  11.2 us
    ppermute x9, starting transfers between devices, shifted(): return lax.ppermute(x, 'tm', [(i, (i + by) % n) for i in range(n)])  10.9 us
  transfers between devices with their start and end apart: 28, of which 10 were waited for; matrix products, arithmetic and copies ran while one was open for 5% of the time, Pallas kernels for 7%

profile of v5, /device:TPU:1, one launch (start us, length us, event | category | flops | bytes accessed | tf_op | source)
XLA Modules:
  0.0 304.0 jit_solution(5170289069868880337)
XLA Ops:
  1.3 2.8 copy-done.1
  4.1 2.8 copy-done.2
  7.6 5.9 %prepare.1 = (bf16[32,2,32,3072]{3,2,1,0:T(8,128)(2,1)S(1)}, f32[8,264,384]{2,1,0:T(8,128)S(1)}, f32[8,256]{1,0:T(8,128)S(1)}, f32[256,8]{1,0:T(8,128)S(1)}) custom-call(bf16[32,98304]{1,0:T(8,128)(2,1)S(1)} %copy-done.1, bf16[32,98304]{1,0:T(8,128)(2,1)S(1)} %copy-done.2, f32[2,1024]{1,0:T(2,128)S(1)} %copy-done.10), custom_call_target="tpu_custom_call" | custom-call | bytes 25165824 | tf_op jit(solution)/shard_map/prepare/pallas_call | solution.py:74
  15.8 150.0 %all_to_all.25.x_ref = bf16[32,2,32,3072]{3,2,1,0:T(8,128)(2,1)} all-to-all(bf16[32,2,32,3072]{3,2,1,0:T(8,128)(2,1)S(1)} %get-tuple-element.50), channel_id=1, replica_groups=mesh['tm'=4,'grid'=32] {'grid'}, dimensions={0} | all-to-all | bytes 25165824 | tf_op jit(solution)/shard_map/all_to_all | solution.py:295
  165.8 10.0 %forward.3 = (f32[16,32,256]{2,1,0:T(8,128)}, f32[16,32,256]{2,1,0:T(8,128)}, f32[2,3328]{1,0:T(2,128)}, f32[1,3328]{1,0:T(1,128)}) custom-call(s32[2]{0:T(128)} %pad_add_fusion.place_ref, bf16[32,2,32,3072]{3,2,1,0:T(8,128)(2,1)} %all_to_all.25.x_ref, bf16[3072,256]{1,0:T(8,128)(2,1)} %op_ref.1, f32[8,264,384]{2,1,0:T(8,128)} %copy-done, ...), custom_call_target="tpu_custom_call" | custom-call | flops 1610612736 | bytes 6291456 | tf_op jit(solution)/shard_map/forward/pallas_call | solution.py:162
  175.8 2.5 collective-permute-start.8
  180.5 2.2 collective-permute-done.7
  188.4 3.5 %all-to-all-start.1 = ((bf16[16,32,256]{2,1,0:T(8,128)(2,1)}), bf16[16,32,256]{2,1,0:T(8,128)(2,1)S(1)}, u32[]{:S(2)}, u32[]{:S(2)}) async-start(bf16[16,32,256]{2,1,0:T(8,128)(2,1)} %subtract_convert_fusion), calls=%async_computation.1 | async-start | bytes 524288 | tf_op jit(solution)/shard_map/all_to_all | solution.py:295
  192.0 10.1 %forward.2 = (f32[16,32,256]{2,1,0:T(8,128)}, f32[16,32,256]{2,1,0:T(8,128)}, f32[2,3328]{1,0:T(2,128)}, f32[1,3328]{1,0:T(1,128)}) custom-call(s32[2]{0:T(128)} %pad_add_fusion.place_ref, bf16[32,2,32,3072]{3,2,1,0:T(8,128)(2,1)} %all_to_all.25.x_ref, bf16[3072,256]{1,0:T(8,128)(2,1)} %op_ref, f32[8,264,384]{2,1,0:T(8,128)} %copy-done, f32[256,8]{1,0:T(8,128)} %copy-done.9, ...), custom_call_target="tpu_custom_call" | custom-call | flops 1610612736 | bytes 6291456 | tf_op jit(solution)/shard_map/forward/pallas_call | solution.py:162
  206.5 7.1 %all-to-all-start.2 = ((bf16[16,32,256]{2,1,0:T(8,128)(2,1)}), bf16[16,32,256]{2,1,0:T(8,128)(2,1)S(1)}, u32[]{:S(2)}, u32[]{:S(2)}) async-start(bf16[16,32,256]{2,1,0:T(8,128)(2,1)} %broadcast_in_dim.29), calls=%async_computation.2 | async-start | bytes 524288 | tf_op jit(solution)/shard_map/all_to_all | solution.py:295
  215.4 6.0 %all-to-all-done.2.own_ref.own0_ref = bf16[16,32,256]{2,1,0:T(8,128)(2,1)S(1)} async-done(((bf16[16,32,256]{2,1,0:T(8,128)(2,1)}), bf16[16,32,256]{2,1,0:T(8,128)(2,1)S(1)}, u32[]{:S(2)}, u32[]{:S(2)}) %all-to-all-start.2) | async-done | bytes 262176 | tf_op jit(solution)/shard_map/all_to_all | solution.py:295
  225.6 9.8 %backward.3 = (bf16[128,1536]{1,0:T(8,128)(2,1)}, bf16[128,1536]{1,0:T(8,128)(2,1)}, bf16[128,1536]{1,0:T(8,128)(2,1)}, bf16[128,1536]{1,0:T(8,128)(2,1)}) custom-call(s32[2]{0:T(128)} %pad_add_fusion.place_ref, bf16[16,32,256]{2,1,0:T(8,128)(2,1)} %copy-done.3, bf16[16,32,256]{2,1,0:T(8,128)(2,1)} %copy-done.6, f32[8,264,384]{2,1,0:T(8,128)} %copy-done, ...), custom_call_target="tpu_custom_call" | custom-call | flops 3221225472 | bytes 6291456 | tf_op jit(solution)/shard_map/backward/pallas_call | solution.py:246
  236.1 3.5 %all-to-all-start.3 = ((bf16[16,32,256]{2,1,0:T(8,128)(2,1)}), bf16[16,32,256]{2,1,0:T(8,128)(2,1)S(1)}, u32[]{:S(2)}, u32[]{:S(2)}) async-start(bf16[16,32,256]{2,1,0:T(8,128)(2,1)} %subtract_convert_fusion.1), calls=%async_computation.3 | async-start | bytes 524288 | tf_op jit(solution)/shard_map/all_to_all | solution.py:295
  240.2 2.6 collective-permute-start.18
  242.8 4.4 %all-to-all-done.3 = bf16[16,32,256]{2,1,0:T(8,128)(2,1)S(1)} async-done(((bf16[16,32,256]{2,1,0:T(8,128)(2,1)}), bf16[16,32,256]{2,1,0:T(8,128)(2,1)S(1)}, u32[]{:S(2)}, u32[]{:S(2)}) %all-to-all-start.3) | async-done | bytes 262176 | tf_op jit(solution)/shard_map/all_to_all | solution.py:295
  248.0 3.8 %all-to-all-start.4 = ((bf16[16,32,256]{2,1,0:T(8,128)(2,1)}), bf16[16,32,256]{2,1,0:T(8,128)(2,1)S(1)}, u32[]{:S(2)}, u32[]{:S(2)}) async-start(bf16[16,32,256]{2,1,0:T(8,128)(2,1)} %broadcast_in_dim.30), calls=%async_computation.4 | async-start | bytes 524288 | tf_op jit(solution)/shard_map/all_to_all | solution.py:295
  252.8 2.7 collective-permute-start.17
  256.6 2.6 all-to-all-done.4.own_ref.own1_ref
  259.1 2.8 collective-permute-start.11
  266.3 2.4 collective-permute-start.21
  271.4 9.9 %backward.2 = (bf16[128,1536]{1,0:T(8,128)(2,1)}, bf16[128,1536]{1,0:T(8,128)(2,1)}, bf16[128,1536]{1,0:T(8,128)(2,1)}, bf16[128,1536]{1,0:T(8,128)(2,1)}) custom-call(s32[2]{0:T(128)} %pad_add_fusion.place_ref, bf16[16,32,256]{2,1,0:T(8,128)(2,1)} %copy-done.5, bf16[16,32,256]{2,1,0:T(8,128)(2,1)} %copy-done.8, f32[8,264,384]{2,1,0:T(8,128)} %copy-done, ...), custom_call_target="tpu_custom_call" | custom-call | flops 3221225472 | bytes 6291456 | tf_op jit(solution)/shard_map/backward/pallas_call | solution.py:246
  285.1 6.1 %collective-permute-done.12 = bf16[128,1536]{1,0:T(8,128)(2,1)S(1)} collective-permute-done((bf16[128,1536]{1,0:T(8,128)(2,1)}, bf16[128,1536]{1,0:T(8,128)(2,1)S(1)}, u32[]{:S(2)}, u32[]{:S(2)}) %collective-permute-start.12) | collective-permute-done | bytes 393248 | tf_op jit(solution)/shard_map/ppermute | solution.py:304
  292.6 2.8 collective-permute-done.14
  299.0 3.1 %collective-permute-done.15 = bf16[64,1536]{1,0:T(8,128)(2,1)S(1)} collective-permute-done((bf16[64,1536]{1,0:T(8,128)(2,1)S(1)}, bf16[64,1536]{1,0:T(8,128)(2,1)S(1)}, u32[]{:S(2)}, u32[]{:S(2)}) %collective-permute-start.15) | collective-permute-done | bytes 196640 | tf_op jit(solution)/shard_map/ppermute | solution.py:304
  (95 shorter events, 43.6 us)
Async XLA Ops:
  175.8 4.7 %collective-permute-start.8 = (f32[2,3328]{1,0:T(2,128)}, f32[2,3328]{1,0:T(2,128)S(1)}, u32[]{:S(2)}, u32[]{:S(2)}) collective-permute-start(f32[2,3328]{1,0:T(2,128)} %get-tuple-element.76), channel_id=1, source_target_pairs={{0,96},{32,0},{64,32},{96,64},{1,97},{33,1},{65,33},{97,65},{2,98}... | collective-permute-start | bytes 79880 | tf_op jit(solution)/shard_map/ppermute | solution.py:300
  178.4 4.4 %collective-permute-start.7 = (f32[2,3328]{1,0:T(2,128)}, f32[2,3328]{1,0:T(2,128)S(1)}, u32[]{:S(2)}, u32[]{:S(2)}) collective-permute-start(f32[2,3328]{1,0:T(2,128)} %get-tuple-element.76), channel_id=1, source_target_pairs={{0,64},{32,96},{64,0},{96,32},{1,65},{33,97},{65,1},{97,33},{2,66}... | collective-permute-start | bytes 79880 | tf_op jit(solution)/shard_map/ppermute | solution.py:300
  179.6 7.0 %collective-permute-start.5 = (f32[16,32,256]{2,1,0:T(8,128)}, f32[16,32,256]{2,1,0:T(8,128)S(1)}, u32[]{:S(2)}, u32[]{:S(2)}) collective-permute-start(f32[16,32,256]{2,1,0:T(8,128)} %get-tuple-element.75), channel_id=1, source_target_pairs={{0,1},{1,0},{2,3},{3,2},{4,5},{5,4},{6,7},{7,6},{8,9},{9,8},{10,11... | collective-permute-start | bytes 1572872 | tf_op jit(solution)/shard_map/ppermute | solution.py:308
  188.4 17.3 %all-to-all-start.1 = ((bf16[16,32,256]{2,1,0:T(8,128)(2,1)}), bf16[16,32,256]{2,1,0:T(8,128)(2,1)S(1)}, u32[]{:S(2)}, u32[]{:S(2)}) async-start(bf16[16,32,256]{2,1,0:T(8,128)(2,1)} %subtract_convert_fusion), calls=%async_computation.1 | async-start | bytes 524288 | tf_op jit(solution)/shard_map/all_to_all | solution.py:295
  202.0 11.5 %collective-permute-start.3 = (f32[2,3328]{1,0:T(2,128)}, f32[2,3328]{1,0:T(2,128)S(1)}, u32[]{:S(2)}, u32[]{:S(2)}) collective-permute-start(f32[2,3328]{1,0:T(2,128)} %get-tuple-element.71), channel_id=1, source_target_pairs={{0,96},{32,0},{64,32},{96,64},{1,97},{33,1},{65,33},{97,65},{2,98}... | collective-permute-start | bytes 79880 | tf_op jit(solution)/shard_map/ppermute | solution.py:300
  202.2 11.4 %collective-permute-start.2 = (f32[2,3328]{1,0:T(2,128)}, f32[2,3328]{1,0:T(2,128)S(1)}, u32[]{:S(2)}, u32[]{:S(2)}) collective-permute-start(f32[2,3328]{1,0:T(2,128)} %get-tuple-element.71), channel_id=1, source_target_pairs={{0,64},{32,96},{64,0},{96,32},{1,65},{33,97},{65,1},{97,33},{2,66}... | collective-permute-start | bytes 79880 | tf_op jit(solution)/shard_map/ppermute | solution.py:300
  203.4 10.2 %collective-permute-start.1 = (f32[2,3328]{1,0:T(2,128)}, f32[2,3328]{1,0:T(2,128)S(1)}, u32[]{:S(2)}, u32[]{:S(2)}) collective-permute-start(f32[2,3328]{1,0:T(2,128)} %get-tuple-element.71), channel_id=1, source_target_pairs={{0,32},{32,64},{64,96},{96,0},{1,33},{33,65},{65,97},{97,1},{2,34}... | collective-permute-start | bytes 79880 | tf_op jit(solution)/shard_map/ppermute | solution.py:300
  204.3 18.8 %collective-permute-start = (f32[16,32,256]{2,1,0:T(8,128)}, f32[16,32,256]{2,1,0:T(8,128)S(1)}, u32[]{:S(2)}, u32[]{:S(2)}) collective-permute-start(f32[16,32,256]{2,1,0:T(8,128)} %get-tuple-element.67), channel_id=1, source_target_pairs={{0,1},{1,0},{2,3},{3,2},{4,5},{5,4},{6,7},{7,6},{8,9},{9,8},{10,11... | collective-permute-start | bytes 1572872 | tf_op jit(solution)/shard_map/ppermute | solution.py:308
  206.5 14.9 %all-to-all-start.2 = ((bf16[16,32,256]{2,1,0:T(8,128)(2,1)}), bf16[16,32,256]{2,1,0:T(8,128)(2,1)S(1)}, u32[]{:S(2)}, u32[]{:S(2)}) async-start(bf16[16,32,256]{2,1,0:T(8,128)(2,1)} %broadcast_in_dim.29), calls=%async_computation.2 | async-start | bytes 524288 | tf_op jit(solution)/shard_map/all_to_all | solution.py:295
  214.4 8.6 %collective-permute-start.4 = (f32[1,256]{1,0:T(1,128)S(1)}, f32[1,256]{1,0:T(1,128)S(1)}, u32[]{:S(2)}, u32[]{:S(2)}) collective-permute-start(f32[1,256]{1,0:T(1,128)S(1)} %slice.144), channel_id=1, source_target_pairs={{0,1},{1,0},{2,3},{3,2},{4,5},{5,4},{6,7},{7,6},{8,9},{9,8},{10,11... | collective-permute-start | bytes 3080 | tf_op jit(solution)/shard_map/ppermute | solution.py:308
  235.4 16.4 %collective-permute-start.16 = (bf16[128,1536]{1,0:T(8,128)(2,1)}, bf16[128,1536]{1,0:T(8,128)(2,1)S(1)}, u32[]{:S(2)}, u32[]{:S(2)}) collective-permute-start(bf16[128,1536]{1,0:T(8,128)(2,1)} %get-tuple-element.86), channel_id=1, source_target_pairs={{0,32},{32,0},{64,96},{96,64},{1,33},{33,1},{65,97},{97,65},{2,34}... | collective-permute-start | bytes 1179656 | tf_op jit(solution)/shard_map/ppermute | solution.py:304
  236.1 11.1 %all-to-all-start.3 = ((bf16[16,32,256]{2,1,0:T(8,128)(2,1)}), bf16[16,32,256]{2,1,0:T(8,128)(2,1)S(1)}, u32[]{:S(2)}, u32[]{:S(2)}) async-start(bf16[16,32,256]{2,1,0:T(8,128)(2,1)} %subtract_convert_fusion.1), calls=%async_computation.3 | async-start | bytes 524288 | tf_op jit(solution)/shard_map/all_to_all | solution.py:295
  240.2 15.3 %collective-permute-start.18 = (bf16[128,1536]{1,0:T(8,128)(2,1)}, bf16[128,1536]{1,0:T(8,128)(2,1)S(1)}, u32[]{:S(2)}, u32[]{:S(2)}) collective-permute-start(bf16[128,1536]{1,0:T(8,128)(2,1)} %get-tuple-element.88), channel_id=1, source_target_pairs={{0,96},{32,64},{64,32},{96,0},{1,97},{33,65},{65,33},{97,1},{2,98}... | collective-permute-start | bytes 1179656 | tf_op jit(solution)/shard_map/ppermute | solution.py:304
  248.0 11.2 %all-to-all-start.4 = ((bf16[16,32,256]{2,1,0:T(8,128)(2,1)}), bf16[16,32,256]{2,1,0:T(8,128)(2,1)S(1)}, u32[]{:S(2)}, u32[]{:S(2)}) async-start(bf16[16,32,256]{2,1,0:T(8,128)(2,1)} %broadcast_in_dim.30), calls=%async_computation.4 | async-start | bytes 524288 | tf_op jit(solution)/shard_map/all_to_all | solution.py:295
  252.8 9.2 %collective-permute-start.17 = (bf16[64,1536]{1,0:T(8,128)(2,1)S(1)}, bf16[64,1536]{1,0:T(8,128)(2,1)S(1)}, u32[]{:S(2)}, u32[]{:S(2)}) collective-permute-start(bf16[64,1536]{1,0:T(8,128)(2,1)S(1)} %add_convert_fusion.1), channel_id=1, source_target_pairs={{0,96},{32,64},{64,32},{96,0},{1,97},{33,65},{65,33},{97,1},{2,98}... | collective-permute-start | bytes 589832 | tf_op jit(solution)/shard_map/ppermute | solution.py:304
  256.5 6.5 %collective-permute-start.19 = (bf16[64,1536]{1,0:T(8,128)(2,1)S(1)}, bf16[64,1536]{1,0:T(8,128)(2,1)S(1)}, u32[]{:S(2)}, u32[]{:S(2)}) collective-permute-start(bf16[64,1536]{1,0:T(8,128)(2,1)S(1)} %add_convert_fusion), channel_id=1, source_target_pairs={{0,32},{32,0},{64,96},{96,64},{1,33},{33,1},{65,97},{97,65},{2,34}... | collective-permute-start | bytes 589832 | tf_op jit(solution)/shard_map/ppermute | solution.py:304
  259.1 4.8 %collective-permute-start.11 = (bf16[16,32,256]{2,1,0:T(8,128)(2,1)S(1)}, bf16[16,32,256]{2,1,0:T(8,128)(2,1)S(1)}, u32[]{:S(2)}, u32[]{:S(2)}) collective-permute-start(bf16[16,32,256]{2,1,0:T(8,128)(2,1)S(1)} %all-to-all-done.4.own_ref.own1_ref), channel_id=1, source_target_pairs={{0,1},{1,0},{2,3},{3,2},{4,5},{5,4},{6,7},{7,6},{8,9},{9,8},{10,11... | collective-permute-start | bytes 786440 | tf_op jit(solution)/shard_map/ppermute | solution.py:308
  266.3 15.1 %collective-permute-start.21 = (bf16[128,256]{1,0:T(8,128)(2,1)S(1)}, bf16[128,256]{1,0:T(8,128)(2,1)S(1)}, u32[]{:S(2)}, u32[]{:S(2)}) collective-permute-start(bf16[128,256]{1,0:T(8,128)(2,1)S(1)} %dynamic-slice_bitcast_fusion), channel_id=1, source_target_pairs={{0,64},{32,96},{64,0},{96,32},{1,65},{33,97},{65,1},{97,33},{2,66}... | collective-permute-start | bytes 196616 | tf_op jit(solution)/shard_map/ppermute | solution.py:300
  268.7 12.6 %collective-permute-start.20 = (bf16[128,256]{1,0:T(8,128)(2,1)S(1)}, bf16[128,256]{1,0:T(8,128)(2,1)S(1)}, u32[]{:S(2)}, u32[]{:S(2)}) collective-permute-start(bf16[128,256]{1,0:T(8,128)(2,1)S(1)} %dynamic-slice_bitcast_fusion), channel_id=1, source_target_pairs={{0,32},{32,64},{64,96},{96,0},{1,33},{33,65},{65,97},{97,1},{2,34}... | collective-permute-start | bytes 196616 | tf_op jit(solution)/shard_map/ppermute | solution.py:300
  269.5 11.8 %collective-permute-start.22 = (bf16[128,256]{1,0:T(8,128)(2,1)S(1)}, bf16[128,256]{1,0:T(8,128)(2,1)S(1)}, u32[]{:S(2)}, u32[]{:S(2)}) collective-permute-start(bf16[128,256]{1,0:T(8,128)(2,1)S(1)} %dynamic-slice_bitcast_fusion), channel_id=1, source_target_pairs={{0,96},{32,0},{64,32},{96,64},{1,97},{33,1},{65,33},{97,65},{2,98}... | collective-permute-start | bytes 196616 | tf_op jit(solution)/shard_map/ppermute | solution.py:300
  281.3 10.0 %collective-permute-start.12 = (bf16[128,1536]{1,0:T(8,128)(2,1)}, bf16[128,1536]{1,0:T(8,128)(2,1)S(1)}, u32[]{:S(2)}, u32[]{:S(2)}) collective-permute-start(bf16[128,1536]{1,0:T(8,128)(2,1)} %get-tuple-element.80), channel_id=1, source_target_pairs={{0,32},{32,0},{64,96},{96,64},{1,33},{33,1},{65,97},{97,65},{2,34}... | collective-permute-start | bytes 1179656 | tf_op jit(solution)/shard_map/ppermute | solution.py:304
  283.4 12.1 %collective-permute-start.14 = (bf16[128,1536]{1,0:T(8,128)(2,1)}, bf16[128,1536]{1,0:T(8,128)(2,1)S(1)}, u32[]{:S(2)}, u32[]{:S(2)}) collective-permute-start(bf16[128,1536]{1,0:T(8,128)(2,1)} %get-tuple-element.82), channel_id=1, source_target_pairs={{0,96},{32,64},{64,32},{96,0},{1,97},{33,65},{65,33},{97,1},{2,98}... | collective-permute-start | bytes 1179656 | tf_op jit(solution)/shard_map/ppermute | solution.py:304
  292.2 5.8 %collective-permute-start.13 = (bf16[64,1536]{1,0:T(8,128)(2,1)S(1)}, bf16[64,1536]{1,0:T(8,128)(2,1)S(1)}, u32[]{:S(2)}, u32[]{:S(2)}) collective-permute-start(bf16[64,1536]{1,0:T(8,128)(2,1)S(1)} %add_convert_fusion.3), channel_id=1, source_target_pairs={{0,96},{32,64},{64,32},{96,0},{1,97},{33,65},{65,33},{97,1},{2,98}... | collective-permute-start | bytes 589832 | tf_op jit(solution)/shard_map/ppermute | solution.py:304
  296.4 5.7 %collective-permute-start.15 = (bf16[64,1536]{1,0:T(8,128)(2,1)S(1)}, bf16[64,1536]{1,0:T(8,128)(2,1)S(1)}, u32[]{:S(2)}, u32[]{:S(2)}) collective-permute-start(bf16[64,1536]{1,0:T(8,128)(2,1)S(1)} %add_convert_fusion.2), channel_id=1, source_target_pairs={{0,32},{32,0},{64,96},{96,64},{1,33},{33,1},{65,97},{97,65},{2,34}... | collective-permute-start | bytes 589832 | tf_op jit(solution)/shard_map/ppermute | solution.py:304
  (15 other events, 45.9 us)

commit v6 on v4

--- a/solution.py
+++ b/solution.py
@@ -7,7 +7,8 @@
 
 
 BLK = 256
-NCHUNK = 512
+NCHUNK = 768
+TILE = 256
 Y, Z, C = 4, 4, 2
 F32, BF16 = jnp.float32, jnp.bfloat16
 HIGHEST = lax.Precision.HIGHEST
@@ -31,7 +32,8 @@
 
     for copy in copies():
         copy.start()
-    a = fading_ref[...]
+    nb = fading_ref.shape[1] // BLK
+    a = jnp.concatenate([fading_ref[f : f + 1, b * BLK : (b + 1) * BLK] for f in range(2) for b in range(nb)])
     log_a = jnp.log(a)
     r = lax.broadcasted_iota(jnp.int32, (BLK, BLK), 0)
     c = lax.broadcasted_iota(jnp.int32, (BLK, BLK), 1)
@@ -41,7 +43,6 @@
     column = exclusive.T
     fresh = 1.0 - a
     total = inclusive[:, BLK - 1 : BLK]
-    nb = a.shape[0] // 2
     for f in range(2):
         sums = [total[f * nb + b : f * nb + b + 1] for b in range(nb)]
         ahead = jnp.zeros_like(sums[0])
@@ -80,80 +81,95 @@
             jax.ShapeDtypeStruct((2, BLK), F32),
         ],
         scratch_shapes=[pltpu.SemaphoreType.DMA((2 * n,))],
-        compiler_params=pltpu.CompilerParams(vmem_limit_bytes=24 * MIB),
+        compiler_params=pltpu.CompilerParams(vmem_limit_bytes=20 * MIB),
         cost_estimate=pl.CostEstimate(flops=0, bytes_accessed=8 * x0.size, transcendentals=0),
         name="prepare",
-    )(x0, x1, fading.reshape(count, BLK))
-
-
-def forward_kernel(place_ref, x_ref, op_ref, block_ref, start_ref, own_ref, other_ref, end_ref, begin_ref, y_ref):
-    f = pl.program_id(0)
-    n, _, rows, width = x_ref.shape
-    hours = n * rows
+    )(x0, x1, fading)
+
+
+def exact_dot(left, right):
+    lh, lm, ll = thirds(left)
+    rh, rm, rl = thirds(right)
+    return jnp.dot(
+        jnp.concatenate([ll, lm, lh, lm, lh, lh], axis=1),
+        jnp.concatenate([rh, rm, rl, rh, rm, rh], axis=0),
+        preferred_element_type=F32,
+    )
+
+
+def forward_kernel(
+    place_ref, x_ref, op0_ref, op1_ref, block_ref, start_ref, p_ref, end_ref, begin_ref, y_ref
+):
+    f, step = pl.program_id(0), pl.program_id(1)
+    count, _, rows, width = x_ref.shape
+    hours, rank = y_ref.shape
     nb = hours // BLK
-    y_ref[...] = jnp.dot(x_ref[:, 0].reshape(hours, width), op_ref[0], preferred_element_type=F32)
-    state = jnp.zeros((1, op_ref.shape[2]), F32)
-    gain = jnp.ones((1, 1), F32)
-    per = BLK // rows
-    for b in range(nb):
-        block = block_ref[b]
-        out = jnp.dot(block[:, :BLK], y_ref[b * BLK : (b + 1) * BLK], precision=HIGHEST, preferred_element_type=F32)
-        out = out - block[:, BLK : BLK + 1] * state
-        part = out[:BLK].reshape(per, rows, out.shape[1])
-        half, at = divmod(b, nb // 2)
-
-        @pl.when(place_ref[0] == half)
+    at = pl.multiple_of(step * (count * rows), count * rows)
+
+    def products(k, op_ref):
+        y_ref[pl.ds(at, count * rows)] = jnp.dot(
+            x_ref[:, 0].reshape(count * rows, width), op_ref[...], preferred_element_type=F32
+        )
+
+        @pl.when(step == 0)
         def _():
-            own_ref[at * per : (at + 1) * per, 0] = part
-
-        @pl.when(place_ref[0] != half)
-        def _():
-            other_ref[at * per : (at + 1) * per, 0] = part
-
-        state = out[BLK : BLK + 1]
-    start = jnp.concatenate([part.astype(F32) for part in thirds(start_ref[0])] + [jnp.zeros((5, width), F32)])
-    begin = jnp.dot(start.astype(BF16), op_ref[0], preferred_element_type=F32)
-    begin = begin[0:1] + begin[1:2] + begin[2:3]
-    for k in range(2):
+            parts = thirds(start_ref[k : k + 1])
+            start = jnp.concatenate([part.astype(F32) for part in parts] + [jnp.zeros((5, width), F32)])
+            begin = jnp.dot(start.astype(BF16), op_ref[...], preferred_element_type=F32)
+            begin_ref[k : k + 1] = begin[0:1] + begin[1:2] + begin[2:3]
+
+    for k, op_ref in enumerate((op0_ref, op1_ref)):
 
         @pl.when(f == k)
         def _():
-            end_ref[k : k + 1] = state
-            begin_ref[k : k + 1] = begin
+            products(k, op_ref)
+
+    @pl.when(step == pl.num_programs(1) - 1)
+    def _():
+        state = jnp.zeros((1, rank), F32)
+        per = BLK // rows
+        outs = [exact_dot(block_ref[b, :, :BLK], y_ref[b * BLK : (b + 1) * BLK]) for b in range(nb)]
+        for b, out in enumerate(outs):
+            out = out - block_ref[b, :, BLK : BLK + 1] * state
+            half, at = divmod(b, nb // 2)
+            slot = jnp.bitwise_xor(half, place_ref[0])
+            p_ref[slot, at * per : (at + 1) * per, 0] = out[:BLK].reshape(per, rows, rank)
+            state = out[BLK : BLK + 1]
+        end_ref[pl.ds(f, 1)] = state
 
 
 def forward(place, x, operators, block, starting):
     n, _, rows, width = x.shape
-    rank = operators.shape[2]
-    hours = n * rows
+    rank = operators[0].shape[1]
+    hours, steps = n * rows, 2
     nb = hours // BLK
-    half = jax.ShapeDtypeStruct((n // 2, 2, rows, rank), F32)
-    half_spec = pl.BlockSpec((n // 2, 1, rows, rank), lambda f: (0, f, 0, 0))
-    pair, pair_spec = jax.ShapeDtypeStruct((2, rank), F32), pl.BlockSpec((2, rank), lambda f: (0, 0))
+    halves = jax.ShapeDtypeStruct((2, n // 2, 2, rows, rank), F32)
+    halves_spec = pl.BlockSpec((2, n // 2, 1, rows, rank), lambda f, i: (0, 0, f, 0, 0))
+    pair, pair_spec = jax.ShapeDtypeStruct((2, rank), F32), pl.BlockSpec((2, rank), lambda f, i: (0, 0))
+    op_spec = pl.BlockSpec((width, rank), lambda f, i: (0, 0))
     return pl.pallas_call(
         forward_kernel,
-        grid=(2,),
+        grid=(2, steps),
         in_specs=[
             pl.BlockSpec(memory_space=pltpu.SMEM),
-            pl.BlockSpec((n, 1, rows, width), lambda f: (0, f, 0, 0)),
-            pl.BlockSpec((1, width, rank), lambda f: (f, 0, 0)),
-            pl.BlockSpec((nb, BLK + 8, BLK + 128), lambda f: (f, 0, 0)),
-            pl.BlockSpec((1, 1, width), lambda f: (f, 0, 0)),
+            pl.BlockSpec((n // steps, 1, rows, width), lambda f, i: (i, f, 0, 0)),
+            op_spec,
+            op_spec,
+            pl.BlockSpec((nb, BLK + 8, BLK + 128), lambda f, i: (f, 0, 0)),
+            pl.BlockSpec((2, width), lambda f, i: (0, 0)),
         ],
-        out_specs=[half_spec, half_spec, pair_spec, pair_spec],
-        out_shape=[half, half, pair, pair],
+        out_specs=[halves_spec, pair_spec, pair_spec],
+        out_shape=[halves, pair, pair],
         scratch_shapes=[pltpu.VMEM((hours, rank), F32)],
-        compiler_params=pltpu.CompilerParams(vmem_limit_bytes=36 * MIB),
+        compiler_params=pltpu.CompilerParams(vmem_limit_bytes=24 * MIB),
         cost_estimate=pl.CostEstimate(
             flops=4 * hours * width * rank, bytes_accessed=4 * hours * width, transcendentals=0
         ),
         name="forward",
-    )(place, x, operators, block, starting)
-
-
-def backward_kernel(
-    place_ref, own_ref, other_ref, block_ref, x_ref, enter_ref, send0_ref, keep0_ref, send1_ref, keep1_ref, z_high, z_low, carried
-):
+    )(place, x, *operators, block, starting)
+
+
+def backward_kernel(place_ref, own_ref, other_ref, block_ref, x_ref, enter_ref, keep_ref, send_ref, z_ref, carried):
     step = pl.program_id(0)
     rank = own_ref.shape[3]
     quarter = rank // 4
@@ -163,46 +179,50 @@
         nb = block_ref.shape[0]
         rows = own_ref.shape[2]
         per = BLK // rows
-        swap = place_ref[1]
         reverse = jnp.zeros((rank, 1), F32)
 
-        def placed(ref, value, cols):
-            for d in range(4):
-                at = pl.multiple_of(jnp.bitwise_xor(d, swap) * quarter, quarter)
-                ref[pl.ds(at, quarter), cols] = value[d * quarter : (d + 1) * quarter]
-
-        for b in reversed(range(nb)):
+        def placed(ref, value, cols, base=0):
+            for order in range(2):
+                for d in range(4):
+                    to = jnp.bitwise_xor(d, place_ref[1])
+                    if order == 0:
+                        to = jnp.where(to == 0, 0, to % 3 + 1)
+                    at = pl.multiple_of(base + to * quarter, quarter)
+                    ref[order, pl.ds(at, quarter), cols] = value[d * quarter : (d + 1) * quarter]
+
+        parts = []
+        for b in range(nb):
             half, at = divmod(b, nb // 2)
             own = own_ref[at * per : (at + 1) * per, 0].reshape(BLK, rank)
             other = other_ref[at * per : (at + 1) * per, 0].reshape(BLK, rank)
             q = jnp.where(place_ref[0] == half, own.astype(F32), other.astype(F32)).T.astype(BF16)
-            out = jnp.zeros((rank, BLK + 128), F32)
-            for part in reversed(thirds(block_ref[b, :BLK])):
-                out = out + jnp.dot(q, part, preferred_element_type=F32)
-            out = out - reverse * block_ref[b, BLK : BLK + 1, :]
+            high, middle, low = thirds(block_ref[b, :BLK])
+            parts.append(
+                jnp.dot(
+                    jnp.concatenate([q, q, q], axis=1),
+                    jnp.concatenate([low, middle, high], axis=0),
+                    preferred_element_type=F32,
+                )
+            )
+        for b in reversed(range(nb)):
+            out = parts[b] - reverse * block_ref[b, BLK : BLK + 1, :]
             z = out[:, :BLK]
             high = z.astype(BF16)
             cols = slice(b * BLK, (b + 1) * BLK)
-            placed(z_high, high, cols)
-            placed(z_low, (z - high.astype(F32)).astype(BF16), cols)
+            placed(z_ref, high, cols)
+            placed(z_ref, (z - high.astype(F32)).astype(BF16), cols, rank)
             reverse = out[:, BLK : BLK + 1]
-        placed(carried, jnp.broadcast_to(reverse, carried.shape), slice(0, carried.shape[1]))
-
-    x = x_ref[:, 0].reshape(z_high.shape[1], x_ref.shape[3])
-    w = jnp.dot(z_high[...], x, preferred_element_type=F32)
-    w = w + jnp.dot(z_low[...], x, preferred_element_type=F32)
-    w = w - carried[:, 0:1] * enter_ref[0]
-    w = [w[k * quarter : (k + 1) * quarter].astype(BF16) for k in range(4)]
-
-    @pl.when(step < pl.num_programs(0) // 2)
-    def _():
-        send0_ref[:quarter], send0_ref[quarter:] = w[1], w[2]
-        keep0_ref[:quarter], keep0_ref[quarter:] = w[0], w[3]
-
-    @pl.when(step >= pl.num_programs(0) // 2)
-    def _():
-        send1_ref[:quarter], send1_ref[quarter:] = w[2], w[3]
-        keep1_ref[:quarter], keep1_ref[quarter:] = w[0], w[1]
+        placed(carried, jnp.broadcast_to(reverse, carried.shape[1:]), slice(0, carried.shape[2]))
+
+    hours = z_ref.shape[2]
+    order = step // (pl.num_programs(0) // 2)
+    for t in range(x_ref.shape[3] // TILE):
+        cols = slice(t * TILE, (t + 1) * TILE)
+        w = jnp.dot(z_ref[order], x_ref[:, 0, :, cols].reshape(hours, TILE), preferred_element_type=F32)
+        w = w[:rank] + w[rank:] - carried[order][:, 0:1] * enter_ref[0, :, cols]
+        w = w.astype(BF16)
+        keep_ref[0, :, cols] = w[: rank // 2]
+        send_ref[0, :, cols] = w[rank // 2 :]
 
 
 def backward(f, place, own, other, block, x, enter):
@@ -211,9 +231,8 @@
     nb = hours // BLK
     steps = width // NCHUNK // 2
     q_spec = pl.BlockSpec((n // 2, 1, rows, rank), lambda i: (0, 1 - f, 0, 0))
-    left = pl.BlockSpec((rank // 2, NCHUNK), lambda i: (0, jnp.minimum(i, steps - 1)))
-    right = pl.BlockSpec((rank // 2, NCHUNK), lambda i: (0, jnp.maximum(i - steps, 0)))
-    piece = jax.ShapeDtypeStruct((rank // 2, width // 2), BF16)
+    out_spec = pl.BlockSpec((1, rank // 2, NCHUNK), lambda i: (i // steps, 0, i % steps))
+    piece = jax.ShapeDtypeStruct((2, rank // 2, width // 2), BF16)
     return pl.pallas_call(
         backward_kernel,
         grid=(2 * steps,),
@@ -225,12 +244,11 @@
             pl.BlockSpec((n, 1, rows, NCHUNK), lambda i: (0, f, 0, i)),
             pl.BlockSpec((1, 1, NCHUNK), lambda i: (f, 0, i)),
         ],
-        out_specs=[left, left, right, right],
-        out_shape=[piece] * 4,
+        out_specs=[out_spec, out_spec],
+        out_shape=[piece, piece],
         scratch_shapes=[
-            pltpu.VMEM((rank, hours), BF16),
-            pltpu.VMEM((rank, hours), BF16),
-            pltpu.VMEM((rank, 128), F32),
+            pltpu.VMEM((2, 2 * rank, hours), BF16),
+            pltpu.VMEM((2, rank, 128), F32),
         ],
         compiler_params=pltpu.CompilerParams(vmem_limit_bytes=54 * MIB),
         cost_estimate=pl.CostEstimate(
@@ -280,9 +298,8 @@
     return lax.ppermute(x, "grid", [(g, g ^ 1) for g in range(Y * Z * C)])
 
 
-def entering(end, gain, start):
+def entering(end, gain, start, i):
     message = jnp.concatenate([end, jnp.broadcast_to(gain, end.shape)])
-    i = lax.axis_index("tm")
     total, so_far = jnp.zeros_like(end), jnp.ones_like(end)
     for d in range(1, lax.axis_size("tm")):
         got = shifted(message, d)
@@ -292,7 +309,7 @@
 
 
 def summed_over_hours(pieces):
-    send0, keep0, send1, keep1 = pieces
+    (keep0, keep1), (send0, send1) = pieces
     q = send0.shape[0] // 2
     wide = lambda v: v.astype(F32)
     got0 = paired(send0, 1)
@@ -309,19 +326,18 @@
     rows, _ = x0.shape
     hours = rows * grid
     scale = (hours * lax.axis_size("tm")) ** -0.5
-    core = lax.axis_index("grid") % C
-    place = jnp.stack([core, lax.axis_index("tm")]).astype(jnp.int32)
+    core, shard = lax.axis_index("grid") & (C - 1), lax.axis_index("tm")
+    place = jnp.stack([core, shard]).astype(jnp.int32)
     n = grid // C
     groups = [[k * C + c for k in range(n)] for c in range(C)]
     packed, *tables = prepare(x0, x1, fading, grid)
-    operators = jnp.stack([operator0, operator1])
-    rest = (tables, operators, place, starting, starting[:, None])
+    rest = (tables, operator0, operator1, place, core, shard, starting)
     packed, rest = lax.optimization_barrier((packed, rest))
     x = all_to_all(packed, "grid")
-    x, (tables, operators, place, starting, start_rows) = lax.optimization_barrier((x, rest))
+    x, (tables, *operators, place, core, shard, starting) = lax.optimization_barrier((x, rest))
     block, since, to_end, gain = tables
-    own, other, end, begin = forward(place, x, operators, block, start_rows)
-    enter = entering(end, gain[:, :1], begin)
+    (own, other), end, begin = forward(place, x, operators, block, starting)
+    enter = entering(end, gain[:, :1], begin, shard)
     enter = enter + across(enter)
     since = lax.dynamic_index_in_dim(since.reshape(2, C, n, rows), core, 1, keepdims=False).transpose(1, 0, 2)
     p = own + across(other) - since[..., None] * enter[None, :, None]
@@ -331,7 +347,7 @@
     q_own = all_to_all(jnp.broadcast_to(q, p.shape), "grid", groups)
     q_other = across(q_own)
     weight = to_end.reshape(2, grid, rows).transpose(1, 0, 2)[..., None]
-    mean = entering((x.astype(F32) * weight).sum(axis=(0, 2)), gain[:, :1], starting)
+    mean = entering((x.astype(F32) * weight).sum(axis=(0, 2)), gain[:, :1], starting, shard)
     w1 = backward(1, place, q_own, q_other, block, x, mean)
     wetness = summed_over_hours(w1) * scale
     sent = lax.dynamic_index_in_dim(cross(place, q_own, q_other).reshape(C, -1, q.shape[2]), core, 0, keepdims=False)

time: 277 us -> 283 us (1.022)
  waiting for transfers between devices: 22.4 us -> 38.5 us
  Pallas kernels: 41.3 us -> 33.3 us
  local copies, waits for them, and re-layouts: 8.46 us -> 11.6 us
  starting transfers between devices: 34.5 us -> 31.4 us
    ppermute x8, waiting for transfers between devices: 11.3 us -> 24.2 us  [paired(): lax.ppermute(x, 'tm', [(i, i ^ by) for i in range(lax.axis_size('tm'))])]
    pallas_call x1, Pallas kernels: 14.6 us -> 8.32 us  [forward(): pl.pallas_call(forward_kernel, grid=(2, steps), in_specs=[pl.BlockSpec(me...]
    another operation x0 -> x3, local copies, waits for them, and re-layouts: none -> 3.39 us  [the longest x2 2.33 us: summed_over_hours(): (keep0, keep1), (send0, send1) = pieces]
  transfers between devices with their start and end apart: 23 -> 23, of which waited for: 9 -> 10; matrix products, arithmetic and copies ran while one was open for 5% -> 6% of each run, Pallas kernels for 7% -> 6%
where the time goes in v6:
time: 283 us; the launch traced here: 282 us
  blocking collectives  150 us (53%)
  waiting for transfers between devices  38.5 us (14%)
  Pallas kernels  33.3 us (12%)
  starting transfers between devices  31.4 us (11%)
  other arithmetic  15.9 us (6%)
  local copies, waits for them, and re-layouts  11.6 us (4%)
    all_to_all x1, blocking collectives, all_to_all(): lax.all_to_all(x, axis, split_axis=0, concat_axis=0, tiled=True, axis_ind...  150 us
    ppermute x8, waiting for transfers between devices, paired(): lax.ppermute(x, 'tm', [(i, i ^ by) for i in range(lax.axis_size('tm'))])  24.2 us
    pallas_call x2, Pallas kernels, backward(): pl.pallas_call(backward_kernel, grid=(2 * steps,), in_specs=[pl.BlockSpec...  18.2 us
    all_to_all x2, waiting for transfers between devices, all_to_all(): lax.all_to_all(x, axis, split_axis=0, concat_axis=0, tiled=True, axis_ind...  9.75 us
    ppermute x9, starting transfers between devices, shifted(): return lax.ppermute(x, 'tm', [(i, (i + by) % n) for i in range(n)])  9.74 us
    all_to_all x2, starting transfers between devices, all_to_all(): lax.all_to_all(x, axis, split_axis=0, concat_axis=0, tiled=True, axis_ind...  8.59 us
    reduce_sum x1, other arithmetic, per_device(): (x.astype(F32) * weight).sum(axis=(0, 2))  8.51 us
    pallas_call x1, Pallas kernels, forward(): pl.pallas_call(forward_kernel, grid=(2, steps), in_specs=[pl.BlockSpec(me...  8.32 us
  transfers between devices with their start and end apart: 23, of which 10 were waited for; matrix products, arithmetic and copies ran while one was open for 6% of the time, Pallas kernels for 6%

profile of v6, /device:TPU:1, one launch (start us, length us, event | category | flops | bytes accessed | tf_op | source)
XLA Modules:
  0.0 281.7 jit_solution(2779815633884925999)
XLA Ops:
  0.7 2.8 copy-done.3
  3.5 2.8 copy-done.4
  7.0 5.9 %prepare.1 = (bf16[32,2,32,3072]{3,2,1,0:T(8,128)(2,1)S(1)}, f32[8,264,384]{2,1,0:T(8,128)S(1)}, f32[8,256]{1,0:T(8,128)S(1)}, f32[8,256]{1,0:T(8,128)S(1)}, f32[2,256]{1,0:T(2,128)S(1)}) custom-call(bf16[32,98304]{1,0:T(8,128)(2,1)S(1)} %copy-done.3, bf16[32,98304]{1,0:T(8,128)(2,1)S(1)} %copy-done.4, f32[2,1024]{1,0:T(2,128)S(1)} %copy-done.10), custom_call_target="tpu_custom_call" | custom-call | bytes 25165824 | tf_op jit(solution)/shard_map/prepare/pallas_call | solution.py:72
  12.9 150.2 %all_to_all.15.x_ref = bf16[32,2,32,3072]{3,2,1,0:T(8,128)(2,1)S(1)} all-to-all(bf16[32,2,32,3072]{3,2,1,0:T(8,128)(2,1)S(1)} %get-tuple-element.44), channel_id=1, replica_groups=mesh['tm'=4,'grid'=32] {'grid'}, dimensions={0} | all-to-all | bytes 25165824 | tf_op jit(solution)/shard_map/all_to_all | solution.py:285
  163.1 8.3 %forward.1 = (f32[2,16,2,32,256]{4,3,2,1,0:T(8,128)S(1)}, f32[2,256]{1,0:T(2,128)S(1)}, f32[2,256]{1,0:T(2,128)S(1)}) custom-call(s32[2]{0:T(128)S(1)} %pad_add_fusion.place_ref, bf16[32,2,32,3072]{3,2,1,0:T(8,128)(2,1)S(1)} %all_to_all.15.x_ref, bf16[3072,256]{1,0:T(8,128)(2,1)S(1)} %copy-done.6, bf16[3072,256]{1,0:T(8,128)(2,1)S(1)} %copy-done.7, ...), custom_call_target="tpu_custom_call" | custom-call | flops 3221225472 | bytes 12582912 | tf_op jit(solution)/shard_map/forward/pallas_call | solution.py:150
  172.9 2.5 collective-permute-start.3
  176.6 2.8 collective-permute-done.2
  179.6 2.2 collective-permute-start.4
  183.6 3.6 %all-to-all-start.1 = ((bf16[16,2,32,256]{3,2,1,0:T(8,128)(2,1)}), bf16[16,2,32,256]{3,2,1,0:T(8,128)(2,1)S(1)}, u32[]{:S(2)}, u32[]{:S(2)}) async-start(bf16[16,2,32,256]{3,2,1,0:T(8,128)(2,1)} %fusion.1), calls=%async_computation.1 | async-start | bytes 1048576 | tf_op jit(solution)/shard_map/all_to_all | solution.py:285
  187.2 8.5 %multiply_reduce_fusion = f32[2,3072]{1,0:T(2,128)S(1)} fusion(bf16[32,2,32,3072]{3,2,1,0:T(8,128)(2,1)} %copy-done, f32[32,2,32]{2,1,0:T(2,128)S(1)} %bitcast.57), kind=kLoop, calls=%fused_computation | loop fusion | flops 18868224 | bytes 12615680 | tf_op jit(solution)/shard_map/reduce_sum | solution.py:350
  195.7 1.6 all-to-all-done.1
  198.2 5.0 %all-to-all-start.2 = ((bf16[16,2,32,256]{3,2,1,0:T(8,128)(2,1)}), bf16[16,2,32,256]{3,2,1,0:T(8,128)(2,1)S(1)}, u32[]{:S(2)}, u32[]{:S(2)}) async-start(bf16[16,2,32,256]{3,2,1,0:T(8,128)(2,1)} %broadcast_in_dim.48), calls=%async_computation.2 | async-start | bytes 1048576 | tf_op jit(solution)/shard_map/all_to_all | solution.py:285
  205.5 8.1 %all-to-all-done.2.own_ref = bf16[16,2,32,256]{3,2,1,0:T(8,128)(2,1)S(1)} async-done(((bf16[16,2,32,256]{3,2,1,0:T(8,128)(2,1)}), bf16[16,2,32,256]{3,2,1,0:T(8,128)(2,1)S(1)}, u32[]{:S(2)}, u32[]{:S(2)}) %all-to-all-start.2) | async-done | bytes 524320 | tf_op jit(solution)/shard_map/all_to_all | solution.py:285
  213.6 2.1 collective-permute-start.5
  218.2 1.3 collective-permute-start.18
  219.5 2.7 collective-permute-start.19
  222.2 9.0 %backward.2 = (bf16[2,128,1536]{2,1,0:T(8,128)(2,1)}, bf16[2,128,1536]{2,1,0:T(8,128)(2,1)}) custom-call(s32[2]{0:T(128)} %copy-done.9, bf16[16,2,32,256]{3,2,1,0:T(8,128)(2,1)} %copy-done.2, bf16[16,2,32,256]{3,2,1,0:T(8,128)(2,1)} %copy-done.5, f32[8,264,384]{2,1,0:T(8,128)} %copy-done.1, bf16[32,2,32,3072]{3,2,1,0:T(8,128)(2,1)} %copy-done, ...), custom_call_target="tpu_custom_call" | custom-call | flops 3221225472 | bytes 6291456 | tf_op jit(solution)/shard_map/backward/pallas_call | solution.py:236
  232.5 9.1 %backward.3 = (bf16[2,128,1536]{2,1,0:T(8,128)(2,1)}, bf16[2,128,1536]{2,1,0:T(8,128)(2,1)}) custom-call(s32[2]{0:T(128)} %copy-done.9, bf16[16,2,32,256]{3,2,1,0:T(8,128)(2,1)} %copy-done.2, bf16[16,2,32,256]{3,2,1,0:T(8,128)(2,1)} %copy-done.5, f32[8,264,384]{2,1,0:T(8,128)} %copy-done.1, bf16[32,2,32,3072]{3,2,1,0:T(8,128)(2,1)} %copy-done, ...), custom_call_target="tpu_custom_call" | custom-call | flops 3221225472 | bytes 6291456 | tf_op jit(solution)/shard_map/backward/pallas_call | solution.py:236
  246.0 2.0 collective-permute-start.15
  249.5 6.0 %collective-permute-done.13 = bf16[128,1536]{1,0:T(8,128)(2,1)S(1)} collective-permute-done((bf16[128,1536]{1,0:T(8,128)(2,1)S(1)}, bf16[128,1536]{1,0:T(8,128)(2,1)S(1)}, u32[]{:S(2)}, u32[]{:S(2)}) %collective-permute-start.13) | collective-permute-done | bytes 393248 | tf_op jit(solution)/shard_map/ppermute | solution.py:294
  256.5 1.8 collective-permute-start.14
  258.4 10.4 %collective-permute-done.10 = bf16[64,1536]{1,0:T(8,128)(2,1)S(1)} collective-permute-done((bf16[64,1536]{1,0:T(8,128)(2,1)S(1)}, bf16[64,1536]{1,0:T(8,128)(2,1)S(1)}, u32[]{:S(2)}, u32[]{:S(2)}) %collective-permute-start.10) | collective-permute-done | bytes 196640 | tf_op jit(solution)/shard_map/ppermute | solution.py:294
  269.4 3.6 %collective-permute-done.14 = bf16[64,1536]{1,0:T(8,128)(2,1)S(1)} collective-permute-done((bf16[64,1536]{1,0:T(8,128)(2,1)S(1)}, bf16[64,1536]{1,0:T(8,128)(2,1)S(1)}, u32[]{:S(2)}, u32[]{:S(2)}) %collective-permute-start.14) | collective-permute-done | bytes 196640 | tf_op jit(solution)/shard_map/ppermute | solution.py:294
  275.6 4.2 %collective-permute-done.16 = bf16[64,1536]{1,0:T(8,128)(2,1)S(1)} collective-permute-done((bf16[64,1536]{1,0:T(8,128)(2,1)S(1)}, bf16[64,1536]{1,0:T(8,128)(2,1)S(1)}, u32[]{:S(2)}, u32[]{:S(2)}) %collective-permute-start.16) | collective-permute-done | bytes 196640 | tf_op jit(solution)/shard_map/ppermute | solution.py:294
  (85 shorter events, 24.3 us)
Async XLA Ops:
  7.0 210.3 %copy-start.9 = (s32[2]{0:T(128)}, s32[2]{0:T(128)S(1)}, u32[]{:S(2)}) copy-start(s32[2]{0:T(128)S(1)} %pad_add_fusion.place_ref) | copy-start | bytes 28
  172.5 10.1 %collective-permute-start = (f32[16,2,32,256]{3,2,1,0:T(8,128)}, f32[16,2,32,256]{3,2,1,0:T(8,128)S(1)}, u32[]{:S(2)}, u32[]{:S(2)}) collective-permute-start(f32[16,2,32,256]{3,2,1,0:T(8,128)} %slice_bitcast_fusion), channel_id=1, source_target_pairs={{0,1},{1,0},{2,3},{3,2},{4,5},{5,4},{6,7},{7,6},{8,9},{9,8},{10,11... | collective-permute-start | bytes 3145736 | tf_op jit(solution)/shard_map/ppermute | solution.py:298
  172.9 3.7 %collective-permute-start.3 = (f32[4,256]{1,0:T(4,128)S(1)}, f32[4,256]{1,0:T(4,128)S(1)}, u32[]{:S(2)}, u32[]{:S(2)}) collective-permute-start(f32[4,256]{1,0:T(4,128)S(1)} %pad_maximum_fusion.1), channel_id=1, source_target_pairs={{0,96},{32,0},{64,32},{96,64},{1,97},{33,1},{65,33},{97,65},{2,98}... | collective-permute-start | bytes 12296 | tf_op jit(solution)/shard_map/ppermute | solution.py:290
  175.4 4.0 %collective-permute-start.2 = (f32[4,256]{1,0:T(4,128)S(1)}, f32[4,256]{1,0:T(4,128)S(1)}, u32[]{:S(2)}, u32[]{:S(2)}) collective-permute-start(f32[4,256]{1,0:T(4,128)S(1)} %pad_maximum_fusion.1), channel_id=1, source_target_pairs={{0,64},{32,96},{64,0},{96,32},{1,65},{33,97},{65,1},{97,33},{2,66}... | collective-permute-start | bytes 12296 | tf_op jit(solution)/shard_map/ppermute | solution.py:290
  175.9 3.7 %collective-permute-start.1 = (f32[4,256]{1,0:T(4,128)S(1)}, f32[4,256]{1,0:T(4,128)S(1)}, u32[]{:S(2)}, u32[]{:S(2)}) collective-permute-start(f32[4,256]{1,0:T(4,128)S(1)} %pad_maximum_fusion.1), channel_id=1, source_target_pairs={{0,32},{32,64},{64,96},{96,0},{1,33},{33,65},{65,97},{97,1},{2,34}... | collective-permute-start | bytes 12296 | tf_op jit(solution)/shard_map/ppermute | solution.py:290
  179.6 3.0 %collective-permute-start.4 = (f32[2,256]{1,0:T(2,128)S(1)}, f32[2,256]{1,0:T(2,128)S(1)}, u32[]{:S(2)}, u32[]{:S(2)}) collective-permute-start(f32[2,256]{1,0:T(2,128)S(1)} %fusion.21), channel_id=1, source_target_pairs={{0,1},{1,0},{2,3},{3,2},{4,5},{5,4},{6,7},{7,6},{8,9},{9,8},{10,11... | collective-permute-start | bytes 6152 | tf_op jit(solution)/shard_map/ppermute | solution.py:298
  183.6 13.7 %all-to-all-start.1 = ((bf16[16,2,32,256]{3,2,1,0:T(8,128)(2,1)}), bf16[16,2,32,256]{3,2,1,0:T(8,128)(2,1)S(1)}, u32[]{:S(2)}, u32[]{:S(2)}) async-start(bf16[16,2,32,256]{3,2,1,0:T(8,128)(2,1)} %fusion.1), calls=%async_computation.1 | async-start | bytes 1048576 | tf_op jit(solution)/shard_map/all_to_all | solution.py:285
  198.2 15.4 %all-to-all-start.2 = ((bf16[16,2,32,256]{3,2,1,0:T(8,128)(2,1)}), bf16[16,2,32,256]{3,2,1,0:T(8,128)(2,1)S(1)}, u32[]{:S(2)}, u32[]{:S(2)}) async-start(bf16[16,2,32,256]{3,2,1,0:T(8,128)(2,1)} %broadcast_in_dim.48), calls=%async_computation.2 | async-start | bytes 1048576 | tf_op jit(solution)/shard_map/all_to_all | solution.py:285
  203.3 12.4 %collective-permute-start.8 = (f32[4,3072]{1,0:T(4,128)S(1)}, f32[4,3072]{1,0:T(4,128)S(1)}, u32[]{:S(2)}, u32[]{:S(2)}) collective-permute-start(f32[4,3072]{1,0:T(4,128)S(1)} %pad_maximum_fusion), channel_id=1, source_target_pairs={{0,96},{32,0},{64,32},{96,64},{1,97},{33,1},{65,33},{97,65},{2,98}... | collective-permute-start | bytes 147464 | tf_op jit(solution)/shard_map/ppermute | solution.py:290
  203.4 12.3 %collective-permute-start.7 = (f32[4,3072]{1,0:T(4,128)S(1)}, f32[4,3072]{1,0:T(4,128)S(1)}, u32[]{:S(2)}, u32[]{:S(2)}) collective-permute-start(f32[4,3072]{1,0:T(4,128)S(1)} %pad_maximum_fusion), channel_id=1, source_target_pairs={{0,64},{32,96},{64,0},{96,32},{1,65},{33,97},{65,1},{97,33},{2,66}... | collective-permute-start | bytes 147464 | tf_op jit(solution)/shard_map/ppermute | solution.py:290
  204.7 11.0 %collective-permute-start.6 = (f32[4,3072]{1,0:T(4,128)S(1)}, f32[4,3072]{1,0:T(4,128)S(1)}, u32[]{:S(2)}, u32[]{:S(2)}) collective-permute-start(f32[4,3072]{1,0:T(4,128)S(1)} %pad_maximum_fusion), channel_id=1, source_target_pairs={{0,32},{32,64},{64,96},{96,0},{1,33},{33,65},{65,97},{97,1},{2,34}... | collective-permute-start | bytes 147464 | tf_op jit(solution)/shard_map/ppermute | solution.py:290
  213.6 3.6 %collective-permute-start.5 = (bf16[16,2,32,256]{3,2,1,0:T(8,128)(2,1)S(1)}, bf16[16,2,32,256]{3,2,1,0:T(8,128)(2,1)S(1)}, u32[]{:S(2)}, u32[]{:S(2)}) collective-permute-start(bf16[16,2,32,256]{3,2,1,0:T(8,128)(2,1)S(1)} %all-to-all-done.2.own_ref), channel_id=1, source_target_pairs={{0,1},{1,0},{2,3},{3,2},{4,5},{5,4},{6,7},{7,6},{8,9},{9,8},{10,11... | collective-permute-start | bytes 1572872 | tf_op jit(solution)/shard_map/ppermute | solution.py:298
  218.2 23.5 %collective-permute-start.18 = (bf16[128,256]{1,0:T(8,128)(2,1)S(1)}, bf16[128,256]{1,0:T(8,128)(2,1)S(1)}, u32[]{:S(2)}, u32[]{:S(2)}) collective-permute-start(bf16[128,256]{1,0:T(8,128)(2,1)S(1)} %fusion.10), channel_id=1, source_target_pairs={{0,64},{32,96},{64,0},{96,32},{1,65},{33,97},{65,1},{97,33},{2,66}... | collective-permute-start | bytes 196616 | tf_op jit(solution)/shard_map/ppermute | solution.py:290
  219.5 22.1 %collective-permute-start.17 = (bf16[128,256]{1,0:T(8,128)(2,1)S(1)}, bf16[128,256]{1,0:T(8,128)(2,1)S(1)}, u32[]{:S(2)}, u32[]{:S(2)}) collective-permute-start(bf16[128,256]{1,0:T(8,128)(2,1)S(1)} %fusion.10), channel_id=1, source_target_pairs={{0,32},{32,64},{64,96},{96,0},{1,33},{33,65},{65,97},{97,1},{2,34}... | collective-permute-start | bytes 196616 | tf_op jit(solution)/shard_map/ppermute | solution.py:290
  219.5 22.1 %collective-permute-start.19 = (bf16[128,256]{1,0:T(8,128)(2,1)S(1)}, bf16[128,256]{1,0:T(8,128)(2,1)S(1)}, u32[]{:S(2)}, u32[]{:S(2)}) collective-permute-start(bf16[128,256]{1,0:T(8,128)(2,1)S(1)} %fusion.10), channel_id=1, source_target_pairs={{0,96},{32,0},{64,32},{96,64},{1,97},{33,1},{65,33},{97,65},{2,98}... | collective-permute-start | bytes 196616 | tf_op jit(solution)/shard_map/ppermute | solution.py:290
  232.4 16.3 %collective-permute-start.9 = (bf16[128,1536]{1,0:T(8,128)(2,1)S(1)}, bf16[128,1536]{1,0:T(8,128)(2,1)S(1)}, u32[]{:S(2)}, u32[]{:S(2)}) collective-permute-start(bf16[128,1536]{1,0:T(8,128)(2,1)S(1)} %get-tuple-element.81), channel_id=1, source_target_pairs={{0,32},{32,0},{64,96},{96,64},{1,33},{33,1},{65,97},{97,65},{2,34}... | collective-permute-start | bytes 1179656 | tf_op jit(solution)/shard_map/ppermute | solution.py:294
  241.7 6.2 %collective-permute-start.20 = (f32[128,256]{1,0:T(8,128)S(1)}, f32[128,256]{1,0:T(8,128)S(1)}, u32[]{:S(2)}, u32[]{:S(2)}) collective-permute-start(f32[128,256]{1,0:T(8,128)S(1)} %convert_add_fusion.8), channel_id=1, source_target_pairs={{0,1},{1,0},{2,3},{3,2},{4,5},{5,4},{6,7},{7,6},{8,9},{9,8},{10,11... | collective-permute-start | bytes 393224 | tf_op jit(solution)/shard_map/ppermute | solution.py:298
  244.2 14.2 %collective-permute-start.11 = (bf16[128,1536]{1,0:T(8,128)(2,1)S(1)}, bf16[128,1536]{1,0:T(8,128)(2,1)S(1)}, u32[]{:S(2)}, u32[]{:S(2)}) collective-permute-start(bf16[128,1536]{1,0:T(8,128)(2,1)S(1)} %get-tuple-element.82), channel_id=1, source_target_pairs={{0,96},{32,64},{64,32},{96,0},{1,97},{33,65},{65,33},{97,1},{2,98}... | collective-permute-start | bytes 1179656 | tf_op jit(solution)/shard_map/ppermute | solution.py:294
  245.2 10.4 %collective-permute-start.13 = (bf16[128,1536]{1,0:T(8,128)(2,1)S(1)}, bf16[128,1536]{1,0:T(8,128)(2,1)S(1)}, u32[]{:S(2)}, u32[]{:S(2)}) collective-permute-start(bf16[128,1536]{1,0:T(8,128)(2,1)S(1)} %get-tuple-element.77), channel_id=1, source_target_pairs={{0,32},{32,0},{64,96},{96,64},{1,33},{33,1},{65,97},{97,65},{2,34}... | collective-permute-start | bytes 1179656 | tf_op jit(solution)/shard_map/ppermute | solution.py:294
  246.0 23.4 %collective-permute-start.15 = (bf16[128,1536]{1,0:T(8,128)(2,1)S(1)}, bf16[128,1536]{1,0:T(8,128)(2,1)S(1)}, u32[]{:S(2)}, u32[]{:S(2)}) collective-permute-start(bf16[128,1536]{1,0:T(8,128)(2,1)S(1)} %get-tuple-element.78), channel_id=1, source_target_pairs={{0,96},{32,64},{64,32},{96,0},{1,97},{33,65},{65,33},{97,1},{2,98}... | collective-permute-start | bytes 1179656 | tf_op jit(solution)/shard_map/ppermute | solution.py:294
  248.7 20.0 %collective-permute-start.10 = (bf16[64,1536]{1,0:T(8,128)(2,1)S(1)}, bf16[64,1536]{1,0:T(8,128)(2,1)S(1)}, u32[]{:S(2)}, u32[]{:S(2)}) collective-permute-start(bf16[64,1536]{1,0:T(8,128)(2,1)S(1)} %fusion.8), channel_id=1, source_target_pairs={{0,96},{32,64},{64,32},{96,0},{1,97},{33,65},{65,33},{97,1},{2,98}... | collective-permute-start | bytes 589832 | tf_op jit(solution)/shard_map/ppermute | solution.py:294
  256.5 16.4 %collective-permute-start.14 = (bf16[64,1536]{1,0:T(8,128)(2,1)S(1)}, bf16[64,1536]{1,0:T(8,128)(2,1)S(1)}, u32[]{:S(2)}, u32[]{:S(2)}) collective-permute-start(bf16[64,1536]{1,0:T(8,128)(2,1)S(1)} %fusion.4), channel_id=1, source_target_pairs={{0,96},{32,64},{64,32},{96,0},{1,97},{33,65},{65,33},{97,1},{2,98}... | collective-permute-start | bytes 589832 | tf_op jit(solution)/shard_map/ppermute | solution.py:294
  268.9 5.7 %collective-permute-start.12 = (bf16[64,1536]{1,0:T(8,128)(2,1)S(1)}, bf16[64,1536]{1,0:T(8,128)(2,1)S(1)}, u32[]{:S(2)}, u32[]{:S(2)}) collective-permute-start(bf16[64,1536]{1,0:T(8,128)(2,1)S(1)} %get-tuple-element.80), channel_id=1, source_target_pairs={{0,32},{32,0},{64,96},{96,64},{1,33},{33,1},{65,97},{97,65},{2,34}... | collective-permute-start | bytes 589832 | tf_op jit(solution)/shard_map/ppermute | solution.py:294
  274.1 5.7 %collective-permute-start.16 = (bf16[64,1536]{1,0:T(8,128)(2,1)S(1)}, bf16[64,1536]{1,0:T(8,128)(2,1)S(1)}, u32[]{:S(2)}, u32[]{:S(2)}) collective-permute-start(bf16[64,1536]{1,0:T(8,128)(2,1)S(1)} %get-tuple-element.76), channel_id=1, source_target_pairs={{0,32},{32,0},{64,96},{96,64},{1,33},{33,1},{65,97},{97,65},{2,34}... | collective-permute-start | bytes 589832 | tf_op jit(solution)/shard_map/ppermute | solution.py:294
  (11 other events, 645.1 us)

commit v7 on v6

--- a/solution.py
+++ b/solution.py
@@ -98,7 +98,7 @@
 
 
 def forward_kernel(
-    place_ref, x_ref, op0_ref, op1_ref, block_ref, start_ref, p_ref, end_ref, begin_ref, y_ref
+    place_ref, x_ref, op0_ref, op1_ref, block_ref, start_ref, own_ref, other_ref, end_ref, begin_ref, y_ref, p_ref
 ):
     f, step = pl.program_id(0), pl.program_id(1)
     count, _, rows, width = x_ref.shape
@@ -132,10 +132,11 @@
         for b, out in enumerate(outs):
             out = out - block_ref[b, :, BLK : BLK + 1] * state
             half, at = divmod(b, nb // 2)
-            slot = jnp.bitwise_xor(half, place_ref[0])
-            p_ref[slot, at * per : (at + 1) * per, 0] = out[:BLK].reshape(per, rows, rank)
+            p_ref[half, at * per : (at + 1) * per] = out[:BLK].reshape(per, rows, rank)
             state = out[BLK : BLK + 1]
         end_ref[pl.ds(f, 1)] = state
+        own_ref[:, 0] = p_ref[place_ref[0]]
+        other_ref[:, 0] = p_ref[1 - place_ref[0]]
 
 
 def forward(place, x, operators, block, starting):
@@ -143,8 +144,8 @@
     rank = operators[0].shape[1]
     hours, steps = n * rows, 2
     nb = hours // BLK
-    halves = jax.ShapeDtypeStruct((2, n // 2, 2, rows, rank), F32)
-    halves_spec = pl.BlockSpec((2, n // 2, 1, rows, rank), lambda f, i: (0, 0, f, 0, 0))
+    half = jax.ShapeDtypeStruct((n // 2, 2, rows, rank), F32)
+    half_spec = pl.BlockSpec((n // 2, 1, rows, rank), lambda f, i: (0, f, 0, 0))
     pair, pair_spec = jax.ShapeDtypeStruct((2, rank), F32), pl.BlockSpec((2, rank), lambda f, i: (0, 0))
     op_spec = pl.BlockSpec((width, rank), lambda f, i: (0, 0))
     return pl.pallas_call(
@@ -158,9 +159,9 @@
             pl.BlockSpec((nb, BLK + 8, BLK + 128), lambda f, i: (f, 0, 0)),
             pl.BlockSpec((2, width), lambda f, i: (0, 0)),
         ],
-        out_specs=[halves_spec, pair_spec, pair_spec],
-        out_shape=[halves, pair, pair],
-        scratch_shapes=[pltpu.VMEM((hours, rank), F32)],
+        out_specs=[half_spec, half_spec, pair_spec, pair_spec],
+        out_shape=[half, half, pair, pair],
+        scratch_shapes=[pltpu.VMEM((hours, rank), F32), pltpu.VMEM((2, n // 2, rows, rank), F32)],
         compiler_params=pltpu.CompilerParams(vmem_limit_bytes=24 * MIB),
         cost_estimate=pl.CostEstimate(
             flops=4 * hours * width * rank, bytes_accessed=4 * hours * width, transcendentals=0
@@ -169,7 +170,9 @@
     )(place, x, *operators, block, starting)
 
 
-def backward_kernel(place_ref, own_ref, other_ref, block_ref, x_ref, enter_ref, keep_ref, send_ref, z_ref, carried):
+def backward_kernel(
+    place_ref, own_ref, other_ref, block_ref, x_ref, enter_ref, keep0_ref, send0_ref, keep1_ref, send1_ref, z_ref, carried, w_ref
+):
     step = pl.program_id(0)
     rank = own_ref.shape[3]
     quarter = rank // 4
@@ -220,9 +223,13 @@
         cols = slice(t * TILE, (t + 1) * TILE)
         w = jnp.dot(z_ref[order], x_ref[:, 0, :, cols].reshape(hours, TILE), preferred_element_type=F32)
         w = w[:rank] + w[rank:] - carried[order][:, 0:1] * enter_ref[0, :, cols]
-        w = w.astype(BF16)
-        keep_ref[0, :, cols] = w[: rank // 2]
-        send_ref[0, :, cols] = w[rank // 2 :]
+        w_ref[:, cols] = w.astype(BF16)
+    for k, (keep_ref, send_ref) in enumerate(((keep0_ref, send0_ref), (keep1_ref, send1_ref))):
+
+        @pl.when(order == k)
+        def _():
+            keep_ref[...] = w_ref[: rank // 2]
+            send_ref[...] = w_ref[rank // 2 :]
 
 
 def backward(f, place, own, other, block, x, enter):
@@ -231,8 +238,9 @@
     nb = hours // BLK
     steps = width // NCHUNK // 2
     q_spec = pl.BlockSpec((n // 2, 1, rows, rank), lambda i: (0, 1 - f, 0, 0))
-    out_spec = pl.BlockSpec((1, rank // 2, NCHUNK), lambda i: (i // steps, 0, i % steps))
-    piece = jax.ShapeDtypeStruct((2, rank // 2, width // 2), BF16)
+    left = pl.BlockSpec((rank // 2, NCHUNK), lambda i: (0, jnp.minimum(i, steps - 1)))
+    right = pl.BlockSpec((rank // 2, NCHUNK), lambda i: (0, jnp.maximum(i - steps, 0)))
+    piece = jax.ShapeDtypeStruct((rank // 2, width // 2), BF16)
     return pl.pallas_call(
         backward_kernel,
         grid=(2 * steps,),
@@ -244,11 +252,12 @@
             pl.BlockSpec((n, 1, rows, NCHUNK), lambda i: (0, f, 0, i)),
             pl.BlockSpec((1, 1, NCHUNK), lambda i: (f, 0, i)),
         ],
-        out_specs=[out_spec, out_spec],
-        out_shape=[piece, piece],
+        out_specs=[left, left, right, right],
+        out_shape=[piece] * 4,
         scratch_shapes=[
             pltpu.VMEM((2, 2 * rank, hours), BF16),
             pltpu.VMEM((2, rank, 128), F32),
+            pltpu.VMEM((rank, NCHUNK), BF16),
         ],
         compiler_params=pltpu.CompilerParams(vmem_limit_bytes=54 * MIB),
         cost_estimate=pl.CostEstimate(
@@ -309,7 +318,7 @@
 
 
 def summed_over_hours(pieces):
-    (keep0, keep1), (send0, send1) = pieces
+    keep0, send0, keep1, send1 = pieces
     q = send0.shape[0] // 2
     wide = lambda v: v.astype(F32)
     got0 = paired(send0, 1)
@@ -336,7 +345,7 @@
     x = all_to_all(packed, "grid")
     x, (tables, *operators, place, core, shard, starting) = lax.optimization_barrier((x, rest))
     block, since, to_end, gain = tables
-    (own, other), end, begin = forward(place, x, operators, block, starting)
+    own, other, end, begin = forward(place, x, operators, block, starting)
     enter = entering(end, gain[:, :1], begin, shard)
     enter = enter + across(enter)
     since = lax.dynamic_index_in_dim(since.reshape(2, C, n, rows), core, 1, keepdims=False).transpose(1, 0, 2)

time: 283 us -> 275 us (0.972)
  waiting for transfers between devices: 38.5 us -> 26.4 us
    ppermute x8, waiting for transfers between devices: 24.2 us -> 12.1 us  [paired(): lax.ppermute(x, 'tm', [(i, i ^ by) for i in range(lax.axis_size('tm'))])]
    unnamed x24 -> x28, local copies, waits for them, and re-layouts: 6.31 us -> 11.8 us
    another operation x3 -> x0, local copies, waits for them, and re-layouts: 3.39 us -> none  [the longest x2 2.33 us: summed_over_hours(): (keep0, keep1), (send0, send1) = pieces]
  transfers between devices with their start and end apart: 23 -> 23, of which waited for: 10 -> 9; matrix products, arithmetic and copies ran while one was open for 6% -> 5% of each run, Pallas kernels for 6% -> 7%
where the time goes in v7:
time: 275 us
  blocking collectives  150 us (55%)
  Pallas kernels  34.7 us (13%)
  starting transfers between devices  30.9 us (11%)
  waiting for transfers between devices  26.4 us (10%)
  other arithmetic  18 us (7%)
  local copies, waits for them, and re-layouts  13.7 us (5%)
    all_to_all x1, blocking collectives, all_to_all(): lax.all_to_all(x, axis, split_axis=0, concat_axis=0, tiled=True, axis_ind...  150 us
    pallas_call x2, Pallas kernels, backward(): pl.pallas_call(backward_kernel, grid=(2 * steps,), in_specs=[pl.BlockSpec...  18.7 us
    ppermute x8, waiting for transfers between devices, paired(): lax.ppermute(x, 'tm', [(i, i ^ by) for i in range(lax.axis_size('tm'))])  12.1 us
    unnamed x28, local copies, waits for them, and re-layouts  11.8 us
    all_to_all x2, waiting for transfers between devices, all_to_all(): lax.all_to_all(x, axis, split_axis=0, concat_axis=0, tiled=True, axis_ind...  9.75 us
    ppermute x9, starting transfers between devices, shifted(): return lax.ppermute(x, 'tm', [(i, (i + by) % n) for i in range(n)])  9.74 us
    pallas_call x1, Pallas kernels, forward(): pl.pallas_call(forward_kernel, grid=(2, steps), in_specs=[pl.BlockSpec(me...  9.19 us
    all_to_all x2, starting transfers between devices, all_to_all(): lax.all_to_all(x, axis, split_axis=0, concat_axis=0, tiled=True, axis_ind...  8.59 us
  transfers between devices with their start and end apart: 23, of which 9 were waited for; matrix products, arithmetic and copies ran while one was open for 5% of the time, Pallas kernels for 7%

profile of v7, /device:TPU:1, one launch (start us, length us, event | category | flops | bytes accessed | tf_op | source)
XLA Modules:
  0.0 274.6 jit_solution(522672407966288323)
XLA Ops:
  0.7 2.8 %copy-done.3 = bf16[32,98304]{1,0:T(8,128)(2,1)S(1)} copy-done((bf16[32,98304]{1,0:T(8,128)(2,1)S(1)}, bf16[32,98304]{1,0:T(8,128)(2,1)}, u32[]{:S(2)}) %copy-start.3) | copy-done | bytes 6291480
  3.5 2.8 %copy-done.4 = bf16[32,98304]{1,0:T(8,128)(2,1)S(1)} copy-done((bf16[32,98304]{1,0:T(8,128)(2,1)S(1)}, bf16[32,98304]{1,0:T(8,128)(2,1)}, u32[]{:S(2)}) %copy-start.4) | copy-done | bytes 6291480
  7.0 5.9 %prepare.1 = (bf16[32,2,32,3072]{3,2,1,0:T(8,128)(2,1)S(1)}, f32[8,264,384]{2,1,0:T(8,128)S(1)}, f32[8,256]{1,0:T(8,128)S(1)}, f32[8,256]{1,0:T(8,128)S(1)}, f32[2,256]{1,0:T(2,128)S(1)}) custom-call(bf16[32,98304]{1,0:T(8,128)(2,1)S(1)} %copy-done.3, bf16[32,98304]{1,0:T(8,128)(2,1)S(1)} %copy-done.4, f32[2,1024]{1,0:T(2,128)S(1)} %copy-done.11), custom_call_target="tpu_custom_call" | custom-call | bytes 25165824 | tf_op jit(solution)/shard_map/prepare/pallas_call | solution.py:72
  12.9 150.2 %all_to_all.15.x_ref = bf16[32,2,32,3072]{3,2,1,0:T(8,128)(2,1)S(1)} all-to-all(bf16[32,2,32,3072]{3,2,1,0:T(8,128)(2,1)S(1)} %get-tuple-element.49), channel_id=1, replica_groups=mesh['tm'=4,'grid'=32] {'grid'}, dimensions={0} | all-to-all | bytes 25165824 | tf_op jit(solution)/shard_map/all_to_all | solution.py:294
  163.1 9.2 %forward.1 = (f32[16,2,32,256]{3,2,1,0:T(8,128)S(1)}, f32[16,2,32,256]{3,2,1,0:T(8,128)}, f32[2,256]{1,0:T(2,128)S(1)}, f32[2,256]{1,0:T(2,128)S(1)}) custom-call(s32[2]{0:T(128)S(1)} %pad_add_fusion.place_ref, bf16[32,2,32,3072]{3,2,1,0:T(8,128)(2,1)S(1)} %all_to_all.15.x_ref, bf16[3072,256]{1,0:T(8,128)(2,1)S(1)} %copy-done.6, ...), custom_call_target="tpu_custom_call" | custom-call | flops 3221225472 | bytes 12582912 | tf_op jit(solution)/shard_map/forward/pallas_call | solution.py:151
  172.3 4.5 %copy-done = bf16[32,2,32,3072]{3,2,1,0:T(8,128)(2,1)} copy-done((bf16[32,2,32,3072]{3,2,1,0:T(8,128)(2,1)}, bf16[32,2,32,3072]{3,2,1,0:T(8,128)(2,1)S(1)}, u32[]{:S(2)}) %copy-start) | copy-done | bytes 12582936
  178.2 2.5 collective-permute-start.3
  181.9 2.8 %collective-permute-done.2 = f32[4,256]{1,0:T(4,128)S(1)} collective-permute-done((f32[4,256]{1,0:T(4,128)S(1)}, f32[4,256]{1,0:T(4,128)S(1)}, u32[]{:S(2)}, u32[]{:S(2)}) %collective-permute-start.2) | collective-permute-done | bytes 4128 | tf_op jit(solution)/shard_map/ppermute | solution.py:299
  184.9 2.2 collective-permute-start.4
  187.9 2.2 subtract_convert_fusion
  190.1 3.6 %all-to-all-start.1 = ((bf16[16,2,32,256]{3,2,1,0:T(8,128)(2,1)}), bf16[16,2,32,256]{3,2,1,0:T(8,128)(2,1)S(1)}, u32[]{:S(2)}, u32[]{:S(2)}) async-start(bf16[16,2,32,256]{3,2,1,0:T(8,128)(2,1)} %subtract_convert_fusion), calls=%async_computation.1 | async-start | bytes 1048576 | tf_op jit(solution)/shard_map/all_to_all | solution.py:294
  193.7 8.5 %multiply_reduce_fusion = f32[2,3072]{1,0:T(2,128)S(1)} fusion(bf16[32,2,32,3072]{3,2,1,0:T(8,128)(2,1)} %copy-done, f32[32,2,32]{2,1,0:T(2,128)S(1)} %bitcast.17), kind=kLoop, calls=%fused_computation | loop fusion | flops 18868224 | bytes 12615680 | tf_op jit(solution)/shard_map/reduce_sum | solution.py:359
  202.2 1.6 all-to-all-done.1
  204.7 5.0 %all-to-all-start.2 = ((bf16[16,2,32,256]{3,2,1,0:T(8,128)(2,1)}), bf16[16,2,32,256]{3,2,1,0:T(8,128)(2,1)S(1)}, u32[]{:S(2)}, u32[]{:S(2)}) async-start(bf16[16,2,32,256]{3,2,1,0:T(8,128)(2,1)} %broadcast_in_dim.48), calls=%async_computation.2 | async-start | bytes 1048576 | tf_op jit(solution)/shard_map/all_to_all | solution.py:294
  212.0 8.1 %all-to-all-done.2.own_ref = bf16[16,2,32,256]{3,2,1,0:T(8,128)(2,1)S(1)} async-done(((bf16[16,2,32,256]{3,2,1,0:T(8,128)(2,1)}), bf16[16,2,32,256]{3,2,1,0:T(8,128)(2,1)S(1)}, u32[]{:S(2)}, u32[]{:S(2)}) %all-to-all-start.2) | async-done | bytes 524320 | tf_op jit(solution)/shard_map/all_to_all | solution.py:294
  220.1 2.1 collective-permute-start.5
  226.0 2.7 collective-permute-start.19
  228.7 9.4 %backward.3 = (bf16[128,1536]{1,0:T(8,128)(2,1)}, bf16[128,1536]{1,0:T(8,128)(2,1)}, bf16[128,1536]{1,0:T(8,128)(2,1)}, bf16[128,1536]{1,0:T(8,128)(2,1)}) custom-call(s32[2]{0:T(128)} %copy-done.10, bf16[16,2,32,256]{3,2,1,0:T(8,128)(2,1)} %copy-done.2, bf16[16,2,32,256]{3,2,1,0:T(8,128)(2,1)} %copy-done.5, f32[8,264,384]{2,1,0:T(8,128)} %copy-done.1, ...), custom_call_target="tpu_custom_call" | custom-call | flops 3221225472 | bytes 6291456 | tf_op jit(solution)/shard_map/backward/pallas_call | solution.py:244
  239.0 1.9 collective-permute-start.20
  240.9 9.3 %backward.2 = (bf16[128,1536]{1,0:T(8,128)(2,1)}, bf16[128,1536]{1,0:T(8,128)(2,1)}, bf16[128,1536]{1,0:T(8,128)(2,1)}, bf16[128,1536]{1,0:T(8,128)(2,1)}) custom-call(s32[2]{0:T(128)} %copy-done.10, bf16[16,2,32,256]{3,2,1,0:T(8,128)(2,1)} %copy-done.2, bf16[16,2,32,256]{3,2,1,0:T(8,128)(2,1)} %copy-done.5, f32[8,264,384]{2,1,0:T(8,128)} %copy-done.1, ...), custom_call_target="tpu_custom_call" | custom-call | flops 3221225472 | bytes 6291456 | tf_op jit(solution)/shard_map/backward/pallas_call | solution.py:244
  250.6 2.3 collective-permute-start.11
  254.3 6.7 %collective-permute-done.9 = bf16[128,1536]{1,0:T(8,128)(2,1)S(1)} collective-permute-done((bf16[128,1536]{1,0:T(8,128)(2,1)}, bf16[128,1536]{1,0:T(8,128)(2,1)S(1)}, u32[]{:S(2)}, u32[]{:S(2)}) %collective-permute-start.9) | collective-permute-done | bytes 393248 | tf_op jit(solution)/shard_map/ppermute | solution.py:303
  262.0 1.8 collective-permute-start.10
  266.7 4.1 %collective-permute-done.10 = bf16[64,1536]{1,0:T(8,128)(2,1)S(1)} collective-permute-done((bf16[64,1536]{1,0:T(8,128)(2,1)S(1)}, bf16[64,1536]{1,0:T(8,128)(2,1)S(1)}, u32[]{:S(2)}, u32[]{:S(2)}) %collective-permute-start.10) | collective-permute-done | bytes 196640 | tf_op jit(solution)/shard_map/ppermute | solution.py:303
  (88 shorter events, 21.8 us)
Async XLA Ops:
  7.0 216.8 %copy-start.10 = (s32[2]{0:T(128)}, s32[2]{0:T(128)S(1)}, u32[]{:S(2)}) copy-start(s32[2]{0:T(128)S(1)} %pad_add_fusion.place_ref) | copy-start | bytes 28
  177.8 10.1 %collective-permute-start = (f32[16,2,32,256]{3,2,1,0:T(8,128)}, f32[16,2,32,256]{3,2,1,0:T(8,128)S(1)}, u32[]{:S(2)}, u32[]{:S(2)}) collective-permute-start(f32[16,2,32,256]{3,2,1,0:T(8,128)} %get-tuple-element.67), channel_id=1, source_target_pairs={{0,1},{1,0},{2,3},{3,2},{4,5},{5,4},{6,7},{7,6},{8,9},{9,8},{10,11... | collective-permute-start | bytes 3145736 | tf_op jit(solution)/shard_map/ppermute | solution.py:307
  178.2 3.7 %collective-permute-start.3 = (f32[4,256]{1,0:T(4,128)S(1)}, f32[4,256]{1,0:T(4,128)S(1)}, u32[]{:S(2)}, u32[]{:S(2)}) collective-permute-start(f32[4,256]{1,0:T(4,128)S(1)} %pad_maximum_fusion.1), channel_id=1, source_target_pairs={{0,96},{32,0},{64,32},{96,64},{1,97},{33,1},{65,33},{97,65},{2,98}... | collective-permute-start | bytes 12296 | tf_op jit(solution)/shard_map/ppermute | solution.py:299
  180.7 4.0 %collective-permute-start.2 = (f32[4,256]{1,0:T(4,128)S(1)}, f32[4,256]{1,0:T(4,128)S(1)}, u32[]{:S(2)}, u32[]{:S(2)}) collective-permute-start(f32[4,256]{1,0:T(4,128)S(1)} %pad_maximum_fusion.1), channel_id=1, source_target_pairs={{0,64},{32,96},{64,0},{96,32},{1,65},{33,97},{65,1},{97,33},{2,66}... | collective-permute-start | bytes 12296 | tf_op jit(solution)/shard_map/ppermute | solution.py:299
  181.2 3.7 %collective-permute-start.1 = (f32[4,256]{1,0:T(4,128)S(1)}, f32[4,256]{1,0:T(4,128)S(1)}, u32[]{:S(2)}, u32[]{:S(2)}) collective-permute-start(f32[4,256]{1,0:T(4,128)S(1)} %pad_maximum_fusion.1), channel_id=1, source_target_pairs={{0,32},{32,64},{64,96},{96,0},{1,33},{33,65},{65,97},{97,1},{2,34}... | collective-permute-start | bytes 12296 | tf_op jit(solution)/shard_map/ppermute | solution.py:299
  184.9 3.0 %collective-permute-start.4 = (f32[2,256]{1,0:T(2,128)S(1)}, f32[2,256]{1,0:T(2,128)S(1)}, u32[]{:S(2)}, u32[]{:S(2)}) collective-permute-start(f32[2,256]{1,0:T(2,128)S(1)} %fusion.11), channel_id=1, source_target_pairs={{0,1},{1,0},{2,3},{3,2},{4,5},{5,4},{6,7},{7,6},{8,9},{9,8},{10,11... | collective-permute-start | bytes 6152 | tf_op jit(solution)/shard_map/ppermute | solution.py:307
  190.1 13.7 %all-to-all-start.1 = ((bf16[16,2,32,256]{3,2,1,0:T(8,128)(2,1)}), bf16[16,2,32,256]{3,2,1,0:T(8,128)(2,1)S(1)}, u32[]{:S(2)}, u32[]{:S(2)}) async-start(bf16[16,2,32,256]{3,2,1,0:T(8,128)(2,1)} %subtract_convert_fusion), calls=%async_computation.1 | async-start | bytes 1048576 | tf_op jit(solution)/shard_map/all_to_all | solution.py:294
  204.7 15.4 %all-to-all-start.2 = ((bf16[16,2,32,256]{3,2,1,0:T(8,128)(2,1)}), bf16[16,2,32,256]{3,2,1,0:T(8,128)(2,1)S(1)}, u32[]{:S(2)}, u32[]{:S(2)}) async-start(bf16[16,2,32,256]{3,2,1,0:T(8,128)(2,1)} %broadcast_in_dim.48), calls=%async_computation.2 | async-start | bytes 1048576 | tf_op jit(solution)/shard_map/all_to_all | solution.py:294
  209.8 12.4 %collective-permute-start.8 = (f32[4,3072]{1,0:T(4,128)S(1)}, f32[4,3072]{1,0:T(4,128)S(1)}, u32[]{:S(2)}, u32[]{:S(2)}) collective-permute-start(f32[4,3072]{1,0:T(4,128)S(1)} %pad_maximum_fusion), channel_id=1, source_target_pairs={{0,96},{32,0},{64,32},{96,64},{1,97},{33,1},{65,33},{97,65},{2,98}... | collective-permute-start | bytes 147464 | tf_op jit(solution)/shard_map/ppermute | solution.py:299
  209.9 12.3 %collective-permute-start.7 = (f32[4,3072]{1,0:T(4,128)S(1)}, f32[4,3072]{1,0:T(4,128)S(1)}, u32[]{:S(2)}, u32[]{:S(2)}) collective-permute-start(f32[4,3072]{1,0:T(4,128)S(1)} %pad_maximum_fusion), channel_id=1, source_target_pairs={{0,64},{32,96},{64,0},{96,32},{1,65},{33,97},{65,1},{97,33},{2,66}... | collective-permute-start | bytes 147464 | tf_op jit(solution)/shard_map/ppermute | solution.py:299
  211.2 11.0 %collective-permute-start.6 = (f32[4,3072]{1,0:T(4,128)S(1)}, f32[4,3072]{1,0:T(4,128)S(1)}, u32[]{:S(2)}, u32[]{:S(2)}) collective-permute-start(f32[4,3072]{1,0:T(4,128)S(1)} %pad_maximum_fusion), channel_id=1, source_target_pairs={{0,32},{32,64},{64,96},{96,0},{1,33},{33,65},{65,97},{97,1},{2,34}... | collective-permute-start | bytes 147464 | tf_op jit(solution)/shard_map/ppermute | solution.py:299
  220.1 3.6 %collective-permute-start.5 = (bf16[16,2,32,256]{3,2,1,0:T(8,128)(2,1)S(1)}, bf16[16,2,32,256]{3,2,1,0:T(8,128)(2,1)S(1)}, u32[]{:S(2)}, u32[]{:S(2)}) collective-permute-start(bf16[16,2,32,256]{3,2,1,0:T(8,128)(2,1)S(1)} %all-to-all-done.2.own_ref), channel_id=1, source_target_pairs={{0,1},{1,0},{2,3},{3,2},{4,5},{5,4},{6,7},{7,6},{8,9},{9,8},{10,11... | collective-permute-start | bytes 1572872 | tf_op jit(solution)/shard_map/ppermute | solution.py:307
  224.7 14.3 %collective-permute-start.18 = (bf16[128,256]{1,0:T(8,128)(2,1)S(1)}, bf16[128,256]{1,0:T(8,128)(2,1)S(1)}, u32[]{:S(2)}, u32[]{:S(2)}) collective-permute-start(bf16[128,256]{1,0:T(8,128)(2,1)S(1)} %fusion), channel_id=1, source_target_pairs={{0,64},{32,96},{64,0},{96,32},{1,65},{33,97},{65,1},{97,33},{2,66}... | collective-permute-start | bytes 196616 | tf_op jit(solution)/shard_map/ppermute | solution.py:299
  226.0 12.9 %collective-permute-start.17 = (bf16[128,256]{1,0:T(8,128)(2,1)S(1)}, bf16[128,256]{1,0:T(8,128)(2,1)S(1)}, u32[]{:S(2)}, u32[]{:S(2)}) collective-permute-start(bf16[128,256]{1,0:T(8,128)(2,1)S(1)} %fusion), channel_id=1, source_target_pairs={{0,32},{32,64},{64,96},{96,0},{1,33},{33,65},{65,97},{97,1},{2,34}... | collective-permute-start | bytes 196616 | tf_op jit(solution)/shard_map/ppermute | solution.py:299
  226.0 12.9 %collective-permute-start.19 = (bf16[128,256]{1,0:T(8,128)(2,1)S(1)}, bf16[128,256]{1,0:T(8,128)(2,1)S(1)}, u32[]{:S(2)}, u32[]{:S(2)}) collective-permute-start(bf16[128,256]{1,0:T(8,128)(2,1)S(1)} %fusion), channel_id=1, source_target_pairs={{0,96},{32,0},{64,32},{96,64},{1,97},{33,1},{65,33},{97,65},{2,98}... | collective-permute-start | bytes 196616 | tf_op jit(solution)/shard_map/ppermute | solution.py:299
  238.1 15.6 %collective-permute-start.13 = (bf16[128,1536]{1,0:T(8,128)(2,1)}, bf16[128,1536]{1,0:T(8,128)(2,1)S(1)}, u32[]{:S(2)}, u32[]{:S(2)}) collective-permute-start(bf16[128,1536]{1,0:T(8,128)(2,1)} %get-tuple-element.82), channel_id=1, source_target_pairs={{0,32},{32,0},{64,96},{96,64},{1,33},{33,1},{65,97},{97,65},{2,34}... | collective-permute-start | bytes 1179656 | tf_op jit(solution)/shard_map/ppermute | solution.py:303
  238.2 16.0 %collective-permute-start.15 = (bf16[128,1536]{1,0:T(8,128)(2,1)}, bf16[128,1536]{1,0:T(8,128)(2,1)S(1)}, u32[]{:S(2)}, u32[]{:S(2)}) collective-permute-start(bf16[128,1536]{1,0:T(8,128)(2,1)} %get-tuple-element.84), channel_id=1, source_target_pairs={{0,96},{32,64},{64,32},{96,0},{1,97},{33,65},{65,33},{97,1},{2,98}... | collective-permute-start | bytes 1179656 | tf_op jit(solution)/shard_map/ppermute | solution.py:303
  239.0 13.9 %collective-permute-start.20 = (f32[128,256]{1,0:T(8,128)S(1)}, f32[128,256]{1,0:T(8,128)S(1)}, u32[]{:S(2)}, u32[]{:S(2)}) collective-permute-start(f32[128,256]{1,0:T(8,128)S(1)} %convert_add_fusion.4), channel_id=1, source_target_pairs={{0,1},{1,0},{2,3},{3,2},{4,5},{5,4},{6,7},{7,6},{8,9},{9,8},{10,11... | collective-permute-start | bytes 393224 | tf_op jit(solution)/shard_map/ppermute | solution.py:307
  250.2 10.8 %collective-permute-start.9 = (bf16[128,1536]{1,0:T(8,128)(2,1)}, bf16[128,1536]{1,0:T(8,128)(2,1)S(1)}, u32[]{:S(2)}, u32[]{:S(2)}) collective-permute-start(bf16[128,1536]{1,0:T(8,128)(2,1)} %get-tuple-element.78), channel_id=1, source_target_pairs={{0,32},{32,0},{64,96},{96,64},{1,33},{33,1},{65,97},{97,65},{2,34}... | collective-permute-start | bytes 1179656 | tf_op jit(solution)/shard_map/ppermute | solution.py:303
  250.6 13.2 %collective-permute-start.11 = (bf16[128,1536]{1,0:T(8,128)(2,1)}, bf16[128,1536]{1,0:T(8,128)(2,1)S(1)}, u32[]{:S(2)}, u32[]{:S(2)}) collective-permute-start(bf16[128,1536]{1,0:T(8,128)(2,1)} %get-tuple-element.80), channel_id=1, source_target_pairs={{0,96},{32,64},{64,32},{96,0},{1,97},{33,65},{65,33},{97,1},{2,98}... | collective-permute-start | bytes 1179656 | tf_op jit(solution)/shard_map/ppermute | solution.py:303
  253.7 12.8 %collective-permute-start.14 = (bf16[64,1536]{1,0:T(8,128)(2,1)S(1)}, bf16[64,1536]{1,0:T(8,128)(2,1)S(1)}, u32[]{:S(2)}, u32[]{:S(2)}) collective-permute-start(bf16[64,1536]{1,0:T(8,128)(2,1)S(1)} %add_convert_fusion.1), channel_id=1, source_target_pairs={{0,96},{32,64},{64,32},{96,0},{1,97},{33,65},{65,33},{97,1},{2,98}... | collective-permute-start | bytes 589832 | tf_op jit(solution)/shard_map/ppermute | solution.py:303
  254.2 12.4 %collective-permute-start.16 = (bf16[64,1536]{1,0:T(8,128)(2,1)S(1)}, bf16[64,1536]{1,0:T(8,128)(2,1)S(1)}, u32[]{:S(2)}, u32[]{:S(2)}) collective-permute-start(bf16[64,1536]{1,0:T(8,128)(2,1)S(1)} %add_convert_fusion), channel_id=1, source_target_pairs={{0,32},{32,0},{64,96},{96,64},{1,33},{33,1},{65,97},{97,65},{2,34}... | collective-permute-start | bytes 589832 | tf_op jit(solution)/shard_map/ppermute | solution.py:303
  262.0 8.8 %collective-permute-start.10 = (bf16[64,1536]{1,0:T(8,128)(2,1)S(1)}, bf16[64,1536]{1,0:T(8,128)(2,1)S(1)}, u32[]{:S(2)}, u32[]{:S(2)}) collective-permute-start(bf16[64,1536]{1,0:T(8,128)(2,1)S(1)} %add_convert_fusion.3), channel_id=1, source_target_pairs={{0,96},{32,64},{64,32},{96,0},{1,97},{33,65},{65,33},{97,1},{2,98}... | collective-permute-start | bytes 589832 | tf_op jit(solution)/shard_map/ppermute | solution.py:303
  264.7 8.0 %collective-permute-start.12 = (bf16[64,1536]{1,0:T(8,128)(2,1)S(1)}, bf16[64,1536]{1,0:T(8,128)(2,1)S(1)}, u32[]{:S(2)}, u32[]{:S(2)}) collective-permute-start(bf16[64,1536]{1,0:T(8,128)(2,1)S(1)} %add_convert_fusion.2), channel_id=1, source_target_pairs={{0,32},{32,0},{64,96},{96,64},{1,33},{33,1},{65,97},{97,65},{2,34}... | collective-permute-start | bytes 589832 | tf_op jit(solution)/shard_map/ppermute | solution.py:303
  (13 other events, 657.7 us)

commit v8 on v7

--- a/solution.py
+++ b/solution.py
@@ -98,7 +98,7 @@
 
 
 def forward_kernel(
-    place_ref, x_ref, op0_ref, op1_ref, block_ref, start_ref, own_ref, other_ref, end_ref, begin_ref, y_ref, p_ref
+    place_ref, x_ref, op0_ref, op1_ref, block_ref, start_ref, p_ref, end_ref, begin_ref, y_ref
 ):
     f, step = pl.program_id(0), pl.program_id(1)
     count, _, rows, width = x_ref.shape
@@ -132,11 +132,10 @@
         for b, out in enumerate(outs):
             out = out - block_ref[b, :, BLK : BLK + 1] * state
             half, at = divmod(b, nb // 2)
-            p_ref[half, at * per : (at + 1) * per] = out[:BLK].reshape(per, rows, rank)
+            slot = jnp.bitwise_xor(half, place_ref[0])
+            p_ref[slot, at * per : (at + 1) * per, 0] = out[:BLK].reshape(per, rows, rank)
             state = out[BLK : BLK + 1]
         end_ref[pl.ds(f, 1)] = state
-        own_ref[:, 0] = p_ref[place_ref[0]]
-        other_ref[:, 0] = p_ref[1 - place_ref[0]]
 
 
 def forward(place, x, operators, block, starting):
@@ -144,8 +143,8 @@
     rank = operators[0].shape[1]
     hours, steps = n * rows, 2
     nb = hours // BLK
-    half = jax.ShapeDtypeStruct((n // 2, 2, rows, rank), F32)
-    half_spec = pl.BlockSpec((n // 2, 1, rows, rank), lambda f, i: (0, f, 0, 0))
+    halves = jax.ShapeDtypeStruct((2, n // 2, 2, rows, rank), F32)
+    halves_spec = pl.BlockSpec((2, n // 2, 1, rows, rank), lambda f, i: (0, 0, f, 0, 0))
     pair, pair_spec = jax.ShapeDtypeStruct((2, rank), F32), pl.BlockSpec((2, rank), lambda f, i: (0, 0))
     op_spec = pl.BlockSpec((width, rank), lambda f, i: (0, 0))
     return pl.pallas_call(
@@ -159,9 +158,9 @@
             pl.BlockSpec((nb, BLK + 8, BLK + 128), lambda f, i: (f, 0, 0)),
             pl.BlockSpec((2, width), lambda f, i: (0, 0)),
         ],
-        out_specs=[half_spec, half_spec, pair_spec, pair_spec],
-        out_shape=[half, half, pair, pair],
-        scratch_shapes=[pltpu.VMEM((hours, rank), F32), pltpu.VMEM((2, n // 2, rows, rank), F32)],
+        out_specs=[halves_spec, pair_spec, pair_spec],
+        out_shape=[halves, pair, pair],
+        scratch_shapes=[pltpu.VMEM((hours, rank), F32)],
         compiler_params=pltpu.CompilerParams(vmem_limit_bytes=24 * MIB),
         cost_estimate=pl.CostEstimate(
             flops=4 * hours * width * rank, bytes_accessed=4 * hours * width, transcendentals=0
@@ -323,11 +322,12 @@
     wide = lambda v: v.astype(F32)
     got0 = paired(send0, 1)
     got1 = paired(send1, 3)
-    last0 = paired((wide(keep0[q:]) + wide(got0[q:])).astype(BF16), 3)
-    last1 = paired((wide(keep1[q:]) + wide(got1[:q])).astype(BF16), 1)
+    sent0 = (wide(keep0[q:]) + wide(got0[q:])).astype(BF16)
+    sent1 = (wide(keep1[q:]) + wide(got1[:q])).astype(BF16)
+    last0, last1 = paired(sent0, 3), paired(sent1, 1)
     left = wide(keep0[:q]) + wide(got0[:q]) + wide(last0)
     right = wide(keep1[:q]) + wide(got1[q:]) + wide(last1)
-    return jnp.concatenate([left, right], axis=1)
+    return jnp.concatenate([left, right], axis=1), (sent0, sent1)
 
 
 def per_device(x0, x1, fading, starting, operator0, operator1):
@@ -345,7 +345,7 @@
     x = all_to_all(packed, "grid")
     x, (tables, *operators, place, core, shard, starting) = lax.optimization_barrier((x, rest))
     block, since, to_end, gain = tables
-    own, other, end, begin = forward(place, x, operators, block, starting)
+    (own, other), end, begin = forward(place, x, operators, block, starting)
     enter = entering(end, gain[:, :1], begin, shard)
     enter = enter + across(enter)
     since = lax.dynamic_index_in_dim(since.reshape(2, C, n, rows), core, 1, keepdims=False).transpose(1, 0, 2)
@@ -358,16 +358,17 @@
     weight = to_end.reshape(2, grid, rows).transpose(1, 0, 2)[..., None]
     mean = entering((x.astype(F32) * weight).sum(axis=(0, 2)), gain[:, :1], starting, shard)
     w1 = backward(1, place, q_own, q_other, block, x, mean)
-    wetness = summed_over_hours(w1) * scale
-    sent = lax.dynamic_index_in_dim(cross(place, q_own, q_other).reshape(C, -1, q.shape[2]), core, 0, keepdims=False)
-    sent = sent.astype(BF16)
-    half = sent.astype(F32)
-    for d in range(1, lax.axis_size("tm")):
-        half = half + shifted(sent, d).astype(F32)
+    wetness = summed_over_hours(w1)[0] * scale
+    w0 = backward(0, place, q_own, q_other, block, x, mean)
+    warmth, last = summed_over_hours(w0)
+    warmth = warmth * scale
+    sent = cross(place, q_own, q_other).reshape(C, -1, q.shape[2])
+    sent = lax.dynamic_index_in_dim(sent, core, 0, keepdims=False).astype(BF16)
+    got = [shifted(sent, d) for d in range(1, lax.axis_size("tm"))]
+    got, _ = lax.optimization_barrier((got, last))
+    half = sum((part.astype(F32) for part in got), sent.astype(F32))
     partner = across(half)
     middle = jnp.concatenate([jnp.where(core == 0, half, partner), jnp.where(core == 0, partner, half)])
-    w0 = backward(0, place, q_own, q_other, block, x, mean)
-    warmth = summed_over_hours(w0) * scale
     return warmth, wetness, middle * scale
 
 

time: 275 us -> 284 us (1.033)
  waiting for transfers between devices: 26.4 us -> 35.1 us
  starting transfers between devices: 30.9 us -> 34.2 us
    ppermute x8, waiting for transfers between devices: 12.1 us -> 20.8 us  [paired(): lax.ppermute(x, 'tm', [(i, i ^ by) for i in range(lax.axis_size('tm'))])]
    unnamed x28 -> x34, local copies, waits for them, and re-layouts: 11.8 us -> 9.19 us
  transfers between devices with their start and end apart: 23 -> 23, of which waited for: 9 -> 9; matrix products, arithmetic and copies ran while one was open for 5% -> 5% of each run, Pallas kernels for 7% -> 4%
where the time goes in v8:
time: 284 us; the launch traced here: 282 us
  blocking collectives  150 us (53%)
  waiting for transfers between devices  35.1 us (12%)
  starting transfers between devices  34.2 us (12%)
  Pallas kernels  33.8 us (12%)
  other arithmetic  15.8 us (6%)
  local copies, waits for them, and re-layouts  12.1 us (4%)
    all_to_all x1, blocking collectives, all_to_all(): lax.all_to_all(x, axis, split_axis=0, concat_axis=0, tiled=True, axis_ind...  150 us
    ppermute x8, waiting for transfers between devices, paired(): lax.ppermute(x, 'tm', [(i, i ^ by) for i in range(lax.axis_size('tm'))])  20.8 us
    pallas_call x2, Pallas kernels, backward(): pl.pallas_call(backward_kernel, grid=(2 * steps,), in_specs=[pl.BlockSpec...  18.6 us
    all_to_all x2, waiting for transfers between devices, all_to_all(): lax.all_to_all(x, axis, split_axis=0, concat_axis=0, tiled=True, axis_ind...  9.75 us
    ppermute x9, starting transfers between devices, shifted(): return lax.ppermute(x, 'tm', [(i, (i + by) % n) for i in range(n)])  9.74 us
    unnamed x34, local copies, waits for them, and re-layouts  9.19 us
    all_to_all x2, starting transfers between devices, all_to_all(): lax.all_to_all(x, axis, split_axis=0, concat_axis=0, tiled=True, axis_ind...  8.59 us
    reduce_sum x1, other arithmetic, per_device(): (x.astype(F32) * weight).sum(axis=(0, 2))  8.51 us
  transfers between devices with their start and end apart: 23, of which 9 were waited for; matrix products, arithmetic and copies ran while one was open for 5% of the time, Pallas kernels for 4%

profile of v8, /device:TPU:1, one launch (start us, length us, event | category | flops | bytes accessed | tf_op | source)
XLA Modules:
  0.0 282.1 jit_solution(7843586709905739834)
XLA Ops:
  0.7 2.8 copy-done.4
  3.5 2.8 copy-done.5
  7.0 5.9 %prepare.1 = (bf16[32,2,32,3072]{3,2,1,0:T(8,128)(2,1)S(1)}, f32[8,264,384]{2,1,0:T(8,128)S(1)}, f32[8,256]{1,0:T(8,128)S(1)}, f32[8,256]{1,0:T(8,128)S(1)}, f32[2,256]{1,0:T(2,128)S(1)}) custom-call(bf16[32,98304]{1,0:T(8,128)(2,1)S(1)} %copy-done.4, bf16[32,98304]{1,0:T(8,128)(2,1)S(1)} %copy-done.5, f32[2,1024]{1,0:T(2,128)S(1)} %copy-done.13), custom_call_target="tpu_custom_call" | custom-call | bytes 25165824 | tf_op jit(solution)/shard_map/prepare/pallas_call | solution.py:72
  12.9 150.2 %all_to_all.15.x_ref = bf16[32,2,32,3072]{3,2,1,0:T(8,128)(2,1)S(1)} all-to-all(bf16[32,2,32,3072]{3,2,1,0:T(8,128)(2,1)S(1)} %get-tuple-element.51), channel_id=1, replica_groups=mesh['tm'=4,'grid'=32] {'grid'}, dimensions={0} | all-to-all | bytes 25165824 | tf_op jit(solution)/shard_map/all_to_all | solution.py:293
  163.1 8.3 %forward.1 = (f32[2,16,2,32,256]{4,3,2,1,0:T(8,128)S(1)}, f32[2,256]{1,0:T(2,128)S(1)}, f32[2,256]{1,0:T(2,128)S(1)}) custom-call(s32[2]{0:T(128)S(1)} %pad_add_fusion.place_ref, bf16[32,2,32,3072]{3,2,1,0:T(8,128)(2,1)S(1)} %all_to_all.15.x_ref, bf16[3072,256]{1,0:T(8,128)(2,1)S(1)} %copy-done.8, bf16[3072,256]{1,0:T(8,128)(2,1)S(1)} %copy-done.9, ...), custom_call_target="tpu_custom_call" | custom-call | flops 3221225472 | bytes 12582912 | tf_op jit(solution)/shard_map/forward/pallas_call | solution.py:150
  172.9 2.5 collective-permute-start.3
  176.6 2.8 collective-permute-done.2
  179.6 2.2 collective-permute-start.4
  183.6 3.6 %all-to-all-start.1 = ((bf16[16,2,32,256]{3,2,1,0:T(8,128)(2,1)}), bf16[16,2,32,256]{3,2,1,0:T(8,128)(2,1)S(1)}, u32[]{:S(2)}, u32[]{:S(2)}) async-start(bf16[16,2,32,256]{3,2,1,0:T(8,128)(2,1)} %fusion.1), calls=%async_computation.1 | async-start | bytes 1048576 | tf_op jit(solution)/shard_map/all_to_all | solution.py:293
  187.2 8.5 %multiply_reduce_fusion = f32[2,3072]{1,0:T(2,128)S(1)} fusion(bf16[32,2,32,3072]{3,2,1,0:T(8,128)(2,1)} %copy-done, f32[32,2,32]{2,1,0:T(2,128)S(1)} %bitcast.25), kind=kLoop, calls=%fused_computation | loop fusion | flops 18868224 | bytes 12615680 | tf_op jit(solution)/shard_map/reduce_sum | solution.py:359
  195.7 1.6 all-to-all-done.1
  198.2 5.0 %all-to-all-start.2 = ((bf16[16,2,32,256]{3,2,1,0:T(8,128)(2,1)}), bf16[16,2,32,256]{3,2,1,0:T(8,128)(2,1)S(1)}, u32[]{:S(2)}, u32[]{:S(2)}) async-start(bf16[16,2,32,256]{3,2,1,0:T(8,128)(2,1)} %broadcast_in_dim.48), calls=%async_computation.2 | async-start | bytes 1048576 | tf_op jit(solution)/shard_map/all_to_all | solution.py:293
  205.5 8.1 %all-to-all-done.2.own_ref = bf16[16,2,32,256]{3,2,1,0:T(8,128)(2,1)S(1)} async-done(((bf16[16,2,32,256]{3,2,1,0:T(8,128)(2,1)}), bf16[16,2,32,256]{3,2,1,0:T(8,128)(2,1)S(1)}, u32[]{:S(2)}, u32[]{:S(2)}) %all-to-all-start.2) | async-done | bytes 524320 | tf_op jit(solution)/shard_map/all_to_all | solution.py:293
  213.6 2.1 collective-permute-start.5
  218.0 9.3 %backward.3 = (bf16[128,1536]{1,0:T(8,128)(2,1)}, bf16[128,1536]{1,0:T(8,128)(2,1)}, bf16[128,1536]{1,0:T(8,128)(2,1)}, bf16[128,1536]{1,0:T(8,128)(2,1)}) custom-call(s32[2]{0:T(128)} %copy-done.11, bf16[16,2,32,256]{3,2,1,0:T(8,128)(2,1)} %copy-done.2, bf16[16,2,32,256]{3,2,1,0:T(8,128)(2,1)} %copy-done.6, f32[8,264,384]{2,1,0:T(8,128)} %copy-done.1, ...), custom_call_target="tpu_custom_call" | custom-call | flops 3221225472 | bytes 6291456 | tf_op jit(solution)/shard_map/backward/pallas_call | solution.py:243
  232.6 1.8 collective-permute-start.19
  234.4 1.4 collective-permute-start.15
  235.8 9.3 %backward.2 = (bf16[128,1536]{1,0:T(8,128)(2,1)}, bf16[128,1536]{1,0:T(8,128)(2,1)}, bf16[128,1536]{1,0:T(8,128)(2,1)}, bf16[128,1536]{1,0:T(8,128)(2,1)}) custom-call(s32[2]{0:T(128)} %copy-done.11, bf16[16,2,32,256]{3,2,1,0:T(8,128)(2,1)} %copy-done.2, bf16[16,2,32,256]{3,2,1,0:T(8,128)(2,1)} %copy-done.6, f32[8,264,384]{2,1,0:T(8,128)} %copy-done.1, ...), custom_call_target="tpu_custom_call" | custom-call | flops 3221225472 | bytes 6291456 | tf_op jit(solution)/shard_map/backward/pallas_call | solution.py:243
  245.3 9.0 %collective-permute-done.9 = bf16[128,1536]{1,0:T(8,128)(2,1)S(1)} collective-permute-done((bf16[128,1536]{1,0:T(8,128)(2,1)}, bf16[128,1536]{1,0:T(8,128)(2,1)S(1)}, u32[]{:S(2)}, u32[]{:S(2)}) %collective-permute-start.9) | collective-permute-done | bytes 393248 | tf_op jit(solution)/shard_map/ppermute | solution.py:302
  256.6 7.1 %collective-permute-done.11 = bf16[128,1536]{1,0:T(8,128)(2,1)S(1)} collective-permute-done((bf16[128,1536]{1,0:T(8,128)(2,1)}, bf16[128,1536]{1,0:T(8,128)(2,1)S(1)}, u32[]{:S(2)}, u32[]{:S(2)}) %collective-permute-start.11) | collective-permute-done | bytes 393248 | tf_op jit(solution)/shard_map/ppermute | solution.py:302
  263.8 1.4 collective-permute-start.14
  267.6 4.1 %collective-permute-start.20 = (f32[128,256]{1,0:T(8,128)S(1)}, f32[128,256]{1,0:T(8,128)S(1)}, u32[]{:S(2)}, u32[]{:S(2)}) collective-permute-start(f32[128,256]{1,0:T(8,128)S(1)} %convert_add_fusion.4), channel_id=1, source_target_pairs={{0,1},{1,0},{2,3},{3,2},{4,5},{5,4},{6,7},{7,6},{8,9},{9,8},{10,11... | collective-permute-start | bytes 393224 | tf_op jit(solution)/shard_map/ppermute | solution.py:306
  271.7 1.8 collective-permute-start.16
  274.4 4.6 %collective-permute-done.16 = bf16[64,1536]{1,0:T(8,128)(2,1)S(1)} collective-permute-done((bf16[64,1536]{1,0:T(8,128)(2,1)S(1)}, bf16[64,1536]{1,0:T(8,128)(2,1)S(1)}, u32[]{:S(2)}, u32[]{:S(2)}) %collective-permute-start.16) | collective-permute-done | bytes 196640 | tf_op jit(solution)/shard_map/ppermute | solution.py:302
  (95 shorter events, 24.9 us)
Async XLA Ops:
  7.0 156.1 %copy-start.11 = (s32[2]{0:T(128)}, s32[2]{0:T(128)S(1)}, u32[]{:S(2)}) copy-start(s32[2]{0:T(128)S(1)} %pad_add_fusion.place_ref) | copy-start | bytes 28
  172.5 10.1 %collective-permute-start = (f32[16,2,32,256]{3,2,1,0:T(8,128)}, f32[16,2,32,256]{3,2,1,0:T(8,128)S(1)}, u32[]{:S(2)}, u32[]{:S(2)}) collective-permute-start(f32[16,2,32,256]{3,2,1,0:T(8,128)} %slice_bitcast_fusion), channel_id=1, source_target_pairs={{0,1},{1,0},{2,3},{3,2},{4,5},{5,4},{6,7},{7,6},{8,9},{9,8},{10,11... | collective-permute-start | bytes 3145736 | tf_op jit(solution)/shard_map/ppermute | solution.py:306
  172.9 3.7 %collective-permute-start.3 = (f32[4,256]{1,0:T(4,128)S(1)}, f32[4,256]{1,0:T(4,128)S(1)}, u32[]{:S(2)}, u32[]{:S(2)}) collective-permute-start(f32[4,256]{1,0:T(4,128)S(1)} %pad_maximum_fusion.1), channel_id=1, source_target_pairs={{0,96},{32,0},{64,32},{96,64},{1,97},{33,1},{65,33},{97,65},{2,98}... | collective-permute-start | bytes 12296 | tf_op jit(solution)/shard_map/ppermute | solution.py:298
  175.4 4.0 %collective-permute-start.2 = (f32[4,256]{1,0:T(4,128)S(1)}, f32[4,256]{1,0:T(4,128)S(1)}, u32[]{:S(2)}, u32[]{:S(2)}) collective-permute-start(f32[4,256]{1,0:T(4,128)S(1)} %pad_maximum_fusion.1), channel_id=1, source_target_pairs={{0,64},{32,96},{64,0},{96,32},{1,65},{33,97},{65,1},{97,33},{2,66}... | collective-permute-start | bytes 12296 | tf_op jit(solution)/shard_map/ppermute | solution.py:298
  175.9 3.7 %collective-permute-start.1 = (f32[4,256]{1,0:T(4,128)S(1)}, f32[4,256]{1,0:T(4,128)S(1)}, u32[]{:S(2)}, u32[]{:S(2)}) collective-permute-start(f32[4,256]{1,0:T(4,128)S(1)} %pad_maximum_fusion.1), channel_id=1, source_target_pairs={{0,32},{32,64},{64,96},{96,0},{1,33},{33,65},{65,97},{97,1},{2,34}... | collective-permute-start | bytes 12296 | tf_op jit(solution)/shard_map/ppermute | solution.py:298
  179.6 3.0 %collective-permute-start.4 = (f32[2,256]{1,0:T(2,128)S(1)}, f32[2,256]{1,0:T(2,128)S(1)}, u32[]{:S(2)}, u32[]{:S(2)}) collective-permute-start(f32[2,256]{1,0:T(2,128)S(1)} %fusion.13), channel_id=1, source_target_pairs={{0,1},{1,0},{2,3},{3,2},{4,5},{5,4},{6,7},{7,6},{8,9},{9,8},{10,11... | collective-permute-start | bytes 6152 | tf_op jit(solution)/shard_map/ppermute | solution.py:306
  183.6 13.7 %all-to-all-start.1 = ((bf16[16,2,32,256]{3,2,1,0:T(8,128)(2,1)}), bf16[16,2,32,256]{3,2,1,0:T(8,128)(2,1)S(1)}, u32[]{:S(2)}, u32[]{:S(2)}) async-start(bf16[16,2,32,256]{3,2,1,0:T(8,128)(2,1)} %fusion.1), calls=%async_computation.1 | async-start | bytes 1048576 | tf_op jit(solution)/shard_map/all_to_all | solution.py:293
  198.2 15.4 %all-to-all-start.2 = ((bf16[16,2,32,256]{3,2,1,0:T(8,128)(2,1)}), bf16[16,2,32,256]{3,2,1,0:T(8,128)(2,1)S(1)}, u32[]{:S(2)}, u32[]{:S(2)}) async-start(bf16[16,2,32,256]{3,2,1,0:T(8,128)(2,1)} %broadcast_in_dim.48), calls=%async_computation.2 | async-start | bytes 1048576 | tf_op jit(solution)/shard_map/all_to_all | solution.py:293
  203.4 12.4 %collective-permute-start.8 = (f32[4,3072]{1,0:T(4,128)S(1)}, f32[4,3072]{1,0:T(4,128)S(1)}, u32[]{:S(2)}, u32[]{:S(2)}) collective-permute-start(f32[4,3072]{1,0:T(4,128)S(1)} %pad_maximum_fusion), channel_id=1, source_target_pairs={{0,96},{32,0},{64,32},{96,64},{1,97},{33,1},{65,33},{97,65},{2,98}... | collective-permute-start | bytes 147464 | tf_op jit(solution)/shard_map/ppermute | solution.py:298
  203.4 12.3 %collective-permute-start.7 = (f32[4,3072]{1,0:T(4,128)S(1)}, f32[4,3072]{1,0:T(4,128)S(1)}, u32[]{:S(2)}, u32[]{:S(2)}) collective-permute-start(f32[4,3072]{1,0:T(4,128)S(1)} %pad_maximum_fusion), channel_id=1, source_target_pairs={{0,64},{32,96},{64,0},{96,32},{1,65},{33,97},{65,1},{97,33},{2,66}... | collective-permute-start | bytes 147464 | tf_op jit(solution)/shard_map/ppermute | solution.py:298
  204.7 11.0 %collective-permute-start.6 = (f32[4,3072]{1,0:T(4,128)S(1)}, f32[4,3072]{1,0:T(4,128)S(1)}, u32[]{:S(2)}, u32[]{:S(2)}) collective-permute-start(f32[4,3072]{1,0:T(4,128)S(1)} %pad_maximum_fusion), channel_id=1, source_target_pairs={{0,32},{32,64},{64,96},{96,0},{1,33},{33,65},{65,97},{97,1},{2,34}... | collective-permute-start | bytes 147464 | tf_op jit(solution)/shard_map/ppermute | solution.py:298
  213.6 3.6 %collective-permute-start.5 = (bf16[16,2,32,256]{3,2,1,0:T(8,128)(2,1)S(1)}, bf16[16,2,32,256]{3,2,1,0:T(8,128)(2,1)S(1)}, u32[]{:S(2)}, u32[]{:S(2)}) collective-permute-start(bf16[16,2,32,256]{3,2,1,0:T(8,128)(2,1)S(1)} %all-to-all-done.2.own_ref), channel_id=1, source_target_pairs={{0,1},{1,0},{2,3},{3,2},{4,5},{5,4},{6,7},{7,6},{8,9},{9,8},{10,11... | collective-permute-start | bytes 1572872 | tf_op jit(solution)/shard_map/ppermute | solution.py:306
  227.4 17.7 %collective-permute-start.13 = (bf16[128,1536]{1,0:T(8,128)(2,1)}, bf16[128,1536]{1,0:T(8,128)(2,1)S(1)}, u32[]{:S(2)}, u32[]{:S(2)}) collective-permute-start(bf16[128,1536]{1,0:T(8,128)(2,1)} %get-tuple-element.83), channel_id=1, source_target_pairs={{0,32},{32,0},{64,96},{96,64},{1,33},{33,1},{65,97},{97,65},{2,34}... | collective-permute-start | bytes 1179656 | tf_op jit(solution)/shard_map/ppermute | solution.py:302
  230.4 35.7 %collective-permute-start.18 = (bf16[128,256]{1,0:T(8,128)(2,1)S(1)}, bf16[128,256]{1,0:T(8,128)(2,1)S(1)}, u32[]{:S(2)}, u32[]{:S(2)}) collective-permute-start(bf16[128,256]{1,0:T(8,128)(2,1)S(1)} %fusion.2), channel_id=1, source_target_pairs={{0,64},{32,96},{64,0},{96,32},{1,65},{33,97},{65,1},{97,33},{2,66}... | collective-permute-start | bytes 196616 | tf_op jit(solution)/shard_map/ppermute | solution.py:298
  231.7 35.8 %collective-permute-start.17 = (bf16[128,256]{1,0:T(8,128)(2,1)S(1)}, bf16[128,256]{1,0:T(8,128)(2,1)S(1)}, u32[]{:S(2)}, u32[]{:S(2)}) collective-permute-start(bf16[128,256]{1,0:T(8,128)(2,1)S(1)} %fusion.2), channel_id=1, source_target_pairs={{0,32},{32,64},{64,96},{96,0},{1,33},{33,65},{65,97},{97,1},{2,34}... | collective-permute-start | bytes 196616 | tf_op jit(solution)/shard_map/ppermute | solution.py:298
  232.6 35.0 %collective-permute-start.19 = (bf16[128,256]{1,0:T(8,128)(2,1)S(1)}, bf16[128,256]{1,0:T(8,128)(2,1)S(1)}, u32[]{:S(2)}, u32[]{:S(2)}) collective-permute-start(bf16[128,256]{1,0:T(8,128)(2,1)S(1)} %fusion.2), channel_id=1, source_target_pairs={{0,96},{32,0},{64,32},{96,64},{1,97},{33,1},{65,33},{97,65},{2,98}... | collective-permute-start | bytes 196616 | tf_op jit(solution)/shard_map/ppermute | solution.py:298
  234.4 37.3 %collective-permute-start.15 = (bf16[128,1536]{1,0:T(8,128)(2,1)}, bf16[128,1536]{1,0:T(8,128)(2,1)S(1)}, u32[]{:S(2)}, u32[]{:S(2)}) collective-permute-start(bf16[128,1536]{1,0:T(8,128)(2,1)} %get-tuple-element.85), channel_id=1, source_target_pairs={{0,96},{32,64},{64,32},{96,0},{1,97},{33,65},{65,33},{97,1},{2,98}... | collective-permute-start | bytes 1179656 | tf_op jit(solution)/shard_map/ppermute | solution.py:302
  245.1 9.2 %collective-permute-start.9 = (bf16[128,1536]{1,0:T(8,128)(2,1)}, bf16[128,1536]{1,0:T(8,128)(2,1)S(1)}, u32[]{:S(2)}, u32[]{:S(2)}) collective-permute-start(bf16[128,1536]{1,0:T(8,128)(2,1)} %get-tuple-element.79), channel_id=1, source_target_pairs={{0,32},{32,0},{64,96},{96,64},{1,33},{33,1},{65,97},{97,65},{2,34}... | collective-permute-start | bytes 1179656 | tf_op jit(solution)/shard_map/ppermute | solution.py:302
  254.3 9.5 %collective-permute-start.11 = (bf16[128,1536]{1,0:T(8,128)(2,1)}, bf16[128,1536]{1,0:T(8,128)(2,1)S(1)}, u32[]{:S(2)}, u32[]{:S(2)}) collective-permute-start(bf16[128,1536]{1,0:T(8,128)(2,1)} %get-tuple-element.81), channel_id=1, source_target_pairs={{0,96},{32,64},{64,32},{96,0},{1,97},{33,65},{65,33},{97,1},{2,98}... | collective-permute-start | bytes 1179656 | tf_op jit(solution)/shard_map/ppermute | solution.py:302
  263.8 10.6 %collective-permute-start.14 = (bf16[64,1536]{1,0:T(8,128)(2,1)S(1)}, bf16[64,1536]{1,0:T(8,128)(2,1)S(1)}, u32[]{:S(2)}, u32[]{:S(2)}) collective-permute-start(bf16[64,1536]{1,0:T(8,128)(2,1)S(1)} %add_convert_fusion.1), channel_id=1, source_target_pairs={{0,96},{32,64},{64,32},{96,0},{1,97},{33,65},{65,33},{97,1},{2,98}... | collective-permute-start | bytes 589832 | tf_op jit(solution)/shard_map/ppermute | solution.py:302
  266.1 12.9 %collective-permute-start.10 = (bf16[64,1536]{1,0:T(8,128)(2,1)S(1)}, bf16[64,1536]{1,0:T(8,128)(2,1)S(1)}, u32[]{:S(2)}, u32[]{:S(2)}) collective-permute-start(bf16[64,1536]{1,0:T(8,128)(2,1)S(1)} %add_convert_fusion.3), channel_id=1, source_target_pairs={{0,96},{32,64},{64,32},{96,0},{1,97},{33,65},{65,33},{97,1},{2,98}... | collective-permute-start | bytes 589832 | tf_op jit(solution)/shard_map/ppermute | solution.py:302
  267.5 13.5 %collective-permute-start.12 = (bf16[64,1536]{1,0:T(8,128)(2,1)S(1)}, bf16[64,1536]{1,0:T(8,128)(2,1)S(1)}, u32[]{:S(2)}, u32[]{:S(2)}) collective-permute-start(bf16[64,1536]{1,0:T(8,128)(2,1)S(1)} %add_convert_fusion.2), channel_id=1, source_target_pairs={{0,32},{32,0},{64,96},{96,64},{1,33},{33,1},{65,97},{97,65},{2,34}... | collective-permute-start | bytes 589832 | tf_op jit(solution)/shard_map/ppermute | solution.py:302
  267.6 6.0 %collective-permute-start.20 = (f32[128,256]{1,0:T(8,128)S(1)}, f32[128,256]{1,0:T(8,128)S(1)}, u32[]{:S(2)}, u32[]{:S(2)}) collective-permute-start(f32[128,256]{1,0:T(8,128)S(1)} %convert_add_fusion.4), channel_id=1, source_target_pairs={{0,1},{1,0},{2,3},{3,2},{4,5},{5,4},{6,7},{7,6},{8,9},{9,8},{10,11... | collective-permute-start | bytes 393224 | tf_op jit(solution)/shard_map/ppermute | solution.py:306
  271.7 7.3 %collective-permute-start.16 = (bf16[64,1536]{1,0:T(8,128)(2,1)S(1)}, bf16[64,1536]{1,0:T(8,128)(2,1)S(1)}, u32[]{:S(2)}, u32[]{:S(2)}) collective-permute-start(bf16[64,1536]{1,0:T(8,128)(2,1)S(1)} %add_convert_fusion), channel_id=1, source_target_pairs={{0,32},{32,0},{64,96},{96,64},{1,33},{33,1},{65,97},{97,65},{2,34}... | collective-permute-start | bytes 589832 | tf_op jit(solution)/shard_map/ppermute | solution.py:302
  (16 other events, 716.9 us)

commit v9 on v8

--- a/solution.py
+++ b/solution.py
@@ -1,3 +1,5 @@
+import functools
+
 import jax
 import jax.numpy as jnp
 from jax import lax
@@ -170,14 +172,22 @@
 
 
 def backward_kernel(
-    place_ref, own_ref, other_ref, block_ref, x_ref, enter_ref, keep0_ref, send0_ref, keep1_ref, send1_ref, z_ref, carried, w_ref
+    f, place_ref, own_ref, other_ref, block_ref, x_ref, enter_ref, keep0_ref, send0_ref, keep1_ref, send1_ref, z_ref, carried, w_ref,
+    held, sems,
 ):
     step = pl.program_id(0)
     rank = own_ref.shape[3]
     quarter = rank // 4
 
+    count, _, _, chunk = held.shape
+
+    def load(i):
+        return pltpu.make_async_copy(x_ref.at[:, f, :, pl.ds(i * chunk, chunk)], held.at[i], sems.at[i])
+
     @pl.when(step == 0)
     def _():
+        for i in range(count):
+            load(i).start()
         nb = block_ref.shape[0]
         rows = own_ref.shape[2]
         per = BLK // rows
@@ -216,11 +226,12 @@
             reverse = out[:, BLK : BLK + 1]
         placed(carried, jnp.broadcast_to(reverse, carried.shape[1:]), slice(0, carried.shape[2]))
 
+    load(step).wait()
     hours = z_ref.shape[2]
     order = step // (pl.num_programs(0) // 2)
-    for t in range(x_ref.shape[3] // TILE):
+    for t in range(chunk // TILE):
         cols = slice(t * TILE, (t + 1) * TILE)
-        w = jnp.dot(z_ref[order], x_ref[:, 0, :, cols].reshape(hours, TILE), preferred_element_type=F32)
+        w = jnp.dot(z_ref[order], held[step, :, :, cols].reshape(hours, TILE), preferred_element_type=F32)
         w = w[:rank] + w[rank:] - carried[order][:, 0:1] * enter_ref[0, :, cols]
         w_ref[:, cols] = w.astype(BF16)
     for k, (keep_ref, send_ref) in enumerate(((keep0_ref, send0_ref), (keep1_ref, send1_ref))):
@@ -241,14 +252,14 @@
     right = pl.BlockSpec((rank // 2, NCHUNK), lambda i: (0, jnp.maximum(i - steps, 0)))
     piece = jax.ShapeDtypeStruct((rank // 2, width // 2), BF16)
     return pl.pallas_call(
-        backward_kernel,
+        functools.partial(backward_kernel, f),
         grid=(2 * steps,),
         in_specs=[
             pl.BlockSpec(memory_space=pltpu.SMEM),
             q_spec,
             q_spec,
             pl.BlockSpec((nb, BLK + 8, BLK + 128), lambda i: (f, 0, 0)),
-            pl.BlockSpec((n, 1, rows, NCHUNK), lambda i: (0, f, 0, i)),
+            pl.BlockSpec(memory_space=pl.ANY),
             pl.BlockSpec((1, 1, NCHUNK), lambda i: (f, 0, i)),
         ],
         out_specs=[left, left, right, right],
@@ -257,8 +268,10 @@
             pltpu.VMEM((2, 2 * rank, hours), BF16),
             pltpu.VMEM((2, rank, 128), F32),
             pltpu.VMEM((rank, NCHUNK), BF16),
+            pltpu.VMEM((2 * steps, n, rows, NCHUNK), BF16),
+            pltpu.SemaphoreType.DMA((2 * steps,)),
         ],
-        compiler_params=pltpu.CompilerParams(vmem_limit_bytes=54 * MIB),
+        compiler_params=pltpu.CompilerParams(vmem_limit_bytes=51 * MIB),
         cost_estimate=pl.CostEstimate(
             flops=4 * hours * width * rank, bytes_accessed=2 * hours * width, transcendentals=0
         ),

time: 284 us -> 275 us (0.968)
  Pallas kernels: 33.8 us -> 30 us
  local copies, waits for them, and re-layouts: 12.1 us -> 8.61 us
    pallas_call x2, Pallas kernels: 18.6 us -> 14.9 us  [backward(): pl.pallas_call(functools.partial(backward_kernel, f), grid=(2 * steps,),...]
    unnamed x34 -> x16, local copies, waits for them, and re-layouts: 9.19 us -> 6.29 us
  transfers between devices with their start and end apart: 23 -> 23, of which waited for: 9 -> 9; matrix products, arithmetic and copies ran while one was open for 5% -> 4% of each run, Pallas kernels for 4% -> 3%
where the time goes in v9:
time: 275 us; the launch traced here: 273 us
  blocking collectives  150 us (55%)
  waiting for transfers between devices  36.2 us (13%)
  starting transfers between devices  34.3 us (12%)
  Pallas kernels  30 us (11%)
  other arithmetic  13 us (5%)
  local copies, waits for them, and re-layouts  8.61 us (3%)
    all_to_all x1, blocking collectives, all_to_all(): lax.all_to_all(x, axis, split_axis=0, concat_axis=0, tiled=True, axis_ind...  150 us
    ppermute x8, waiting for transfers between devices, paired(): lax.ppermute(x, 'tm', [(i, i ^ by) for i in range(lax.axis_size('tm'))])  21.3 us
    pallas_call x2, Pallas kernels, backward(): pl.pallas_call(functools.partial(backward_kernel, f), grid=(2 * steps,),...  14.9 us
    all_to_all x2, waiting for transfers between devices, all_to_all(): lax.all_to_all(x, axis, split_axis=0, concat_axis=0, tiled=True, axis_ind...  9.75 us
    ppermute x9, starting transfers between devices, shifted(): return lax.ppermute(x, 'tm', [(i, (i + by) % n) for i in range(n)])  9.74 us
    all_to_all x2, starting transfers between devices, all_to_all(): lax.all_to_all(x, axis, split_axis=0, concat_axis=0, tiled=True, axis_ind...  8.59 us
    reduce_sum x1, other arithmetic, per_device(): (x.astype(F32) * weight).sum(axis=(0, 2))  8.51 us
    ppermute x4, starting transfers between devices, across(): return lax.ppermute(x, 'grid', [(g, g ^ 1) for g in range(Y * Z * C)])  8.51 us
  transfers between devices with their start and end apart: 23, of which 9 were waited for; matrix products, arithmetic and copies ran while one was open for 4% of the time, Pallas kernels for 3%

profile of v9, /device:TPU:1, one launch (start us, length us, event | category | flops | bytes accessed | tf_op | source)
XLA Modules:
  0.0 273.3 jit_solution(11028927345881074495)
XLA Ops:
  0.7 2.8 %copy-done.2 = bf16[32,98304]{1,0:T(8,128)(2,1)S(1)} copy-done((bf16[32,98304]{1,0:T(8,128)(2,1)S(1)}, bf16[32,98304]{1,0:T(8,128)(2,1)}, u32[]{:S(2)}) %copy-start.2) | copy-done | bytes 6291480
  3.5 2.8 %copy-done.3 = bf16[32,98304]{1,0:T(8,128)(2,1)S(1)} copy-done((bf16[32,98304]{1,0:T(8,128)(2,1)S(1)}, bf16[32,98304]{1,0:T(8,128)(2,1)}, u32[]{:S(2)}) %copy-start.3) | copy-done | bytes 6291480
  7.0 5.9 %prepare.1 = (bf16[32,2,32,3072]{3,2,1,0:T(8,128)(2,1)S(1)}, f32[8,264,384]{2,1,0:T(8,128)S(1)}, f32[8,256]{1,0:T(8,128)S(1)}, f32[8,256]{1,0:T(8,128)S(1)}, f32[2,256]{1,0:T(2,128)S(1)}) custom-call(bf16[32,98304]{1,0:T(8,128)(2,1)S(1)} %copy-done.2, bf16[32,98304]{1,0:T(8,128)(2,1)S(1)} %copy-done.3, f32[2,1024]{1,0:T(2,128)S(1)} %copy-done.7), custom_call_target="tpu_custom_call" | custom-call | bytes 25165824 | tf_op jit(solution)/shard_map/prepare/pallas_call | solution.py:74
  12.9 150.2 %all_to_all.15.x_ref = bf16[32,2,32,3072]{3,2,1,0:T(8,128)(2,1)S(1)} all-to-all(bf16[32,2,32,3072]{3,2,1,0:T(8,128)(2,1)S(1)} %get-tuple-element.51), channel_id=1, replica_groups=mesh['tm'=4,'grid'=32] {'grid'}, dimensions={0} | all-to-all | bytes 25165824 | tf_op jit(solution)/shard_map/all_to_all | solution.py:306
  163.1 8.3 %forward.1 = (f32[2,16,2,32,256]{4,3,2,1,0:T(8,128)S(1)}, f32[2,256]{1,0:T(2,128)S(1)}, f32[2,256]{1,0:T(2,128)S(1)}) custom-call(s32[2]{0:T(128)S(1)} %pad_add_fusion.place_ref, bf16[32,2,32,3072]{3,2,1,0:T(8,128)(2,1)S(1)} %all_to_all.15.x_ref, bf16[3072,256]{1,0:T(8,128)(2,1)S(1)} %copy-done.4, bf16[3072,256]{1,0:T(8,128)(2,1)S(1)} %copy-done.5, ...), custom_call_target="tpu_custom_call" | custom-call | flops 3221225472 | bytes 12582912 | tf_op jit(solution)/shard_map/forward/pallas_call | solution.py:152
  172.9 2.5 collective-permute-start.3
  176.6 2.8 %collective-permute-done.2 = f32[4,256]{1,0:T(4,128)S(1)} collective-permute-done((f32[4,256]{1,0:T(4,128)S(1)}, f32[4,256]{1,0:T(4,128)S(1)}, u32[]{:S(2)}, u32[]{:S(2)}) %collective-permute-start.2) | collective-permute-done | bytes 4128 | tf_op jit(solution)/shard_map/ppermute | solution.py:311
  179.6 2.2 collective-permute-start.4
  183.6 3.6 %all-to-all-start.1 = ((bf16[16,2,32,256]{3,2,1,0:T(8,128)(2,1)}), bf16[16,2,32,256]{3,2,1,0:T(8,128)(2,1)S(1)}, u32[]{:S(2)}, u32[]{:S(2)}) async-start(bf16[16,2,32,256]{3,2,1,0:T(8,128)(2,1)} %fusion.1), calls=%async_computation.1 | async-start | bytes 1048576 | tf_op jit(solution)/shard_map/all_to_all | solution.py:306
  187.2 8.5 %multiply_reduce_fusion = f32[2,3072]{1,0:T(2,128)S(1)} fusion(bf16[32,2,32,3072]{3,2,1,0:T(8,128)(2,1)} %copy-done, f32[32,2,32]{2,1,0:T(2,128)S(1)} %bitcast.25), kind=kLoop, calls=%fused_computation | loop fusion | flops 18868224 | bytes 12615680 | tf_op jit(solution)/shard_map/reduce_sum | solution.py:372
  195.7 1.6 all-to-all-done.1
  198.2 5.0 %all-to-all-start.2 = ((bf16[16,2,32,256]{3,2,1,0:T(8,128)(2,1)}), bf16[16,2,32,256]{3,2,1,0:T(8,128)(2,1)S(1)}, u32[]{:S(2)}, u32[]{:S(2)}) async-start(bf16[16,2,32,256]{3,2,1,0:T(8,128)(2,1)} %broadcast_in_dim.48), calls=%async_computation.2 | async-start | bytes 1048576 | tf_op jit(solution)/shard_map/all_to_all | solution.py:306
  205.5 8.2 %all-to-all-done.2.own_ref = bf16[16,2,32,256]{3,2,1,0:T(8,128)(2,1)S(1)} async-done(((bf16[16,2,32,256]{3,2,1,0:T(8,128)(2,1)}), bf16[16,2,32,256]{3,2,1,0:T(8,128)(2,1)S(1)}, u32[]{:S(2)}, u32[]{:S(2)}) %all-to-all-start.2) | async-done | bytes 524320 | tf_op jit(solution)/shard_map/all_to_all | solution.py:306
  213.6 2.1 collective-permute-start.5
  215.8 1.4 collective-permute-done.5.other_ref
  217.2 7.5 %backward.3 = (bf16[128,1536]{1,0:T(8,128)(2,1)S(1)}, bf16[128,1536]{1,0:T(8,128)(2,1)S(1)}, bf16[128,1536]{1,0:T(8,128)(2,1)S(1)}, bf16[128,1536]{1,0:T(8,128)(2,1)S(1)}) custom-call(s32[2]{0:T(128)S(1)} %pad_add_fusion.place_ref, bf16[16,2,32,256]{3,2,1,0:T(8,128)(2,1)S(1)} %all-to-all-done.2.own_ref, ...), custom_call_target="tpu_custom_call" | custom-call | flops 3221225472 | bytes 6291456 | tf_op jit(solution)/shard_map/backward/pallas_call | solution.py:254
  227.9 1.8 collective-permute-start.19
  231.1 7.4 %backward.2 = (bf16[128,1536]{1,0:T(8,128)(2,1)S(1)}, bf16[128,1536]{1,0:T(8,128)(2,1)S(1)}, bf16[128,1536]{1,0:T(8,128)(2,1)S(1)}, bf16[128,1536]{1,0:T(8,128)(2,1)S(1)}) custom-call(s32[2]{0:T(128)S(1)} %pad_add_fusion.place_ref, bf16[16,2,32,256]{3,2,1,0:T(8,128)(2,1)S(1)} %all-to-all-done.2.own_ref, ...), custom_call_target="tpu_custom_call" | custom-call | flops 3221225472 | bytes 6291456 | tf_op jit(solution)/shard_map/backward/pallas_call | solution.py:254
  238.7 8.8 %collective-permute-done.9 = bf16[128,1536]{1,0:T(8,128)(2,1)S(1)} collective-permute-done((bf16[128,1536]{1,0:T(8,128)(2,1)S(1)}, bf16[128,1536]{1,0:T(8,128)(2,1)S(1)}, u32[]{:S(2)}, u32[]{:S(2)}) %collective-permute-start.9) | collective-permute-done | bytes 393248 | tf_op jit(solution)/shard_map/ppermute | solution.py:315
  248.9 7.9 %collective-permute-done.11 = bf16[128,1536]{1,0:T(8,128)(2,1)S(1)} collective-permute-done((bf16[128,1536]{1,0:T(8,128)(2,1)S(1)}, bf16[128,1536]{1,0:T(8,128)(2,1)S(1)}, u32[]{:S(2)}, u32[]{:S(2)}) %collective-permute-start.11) | collective-permute-done | bytes 393248 | tf_op jit(solution)/shard_map/ppermute | solution.py:315
  258.2 1.4 collective-permute-start.10
  259.7 4.1 %collective-permute-start.20 = (f32[128,256]{1,0:T(8,128)S(1)}, f32[128,256]{1,0:T(8,128)S(1)}, u32[]{:S(2)}, u32[]{:S(2)}) collective-permute-start(f32[128,256]{1,0:T(8,128)S(1)} %convert_add_fusion.4), channel_id=1, source_target_pairs={{0,1},{1,0},{2,3},{3,2},{4,5},{5,4},{6,7},{7,6},{8,9},{9,8},{10,11... | collective-permute-start | bytes 393224 | tf_op jit(solution)/shard_map/ppermute | solution.py:319
  263.9 1.8 collective-permute-start.16
  266.5 4.6 %collective-permute-done.16 = bf16[64,1536]{1,0:T(8,128)(2,1)S(1)} collective-permute-done((bf16[64,1536]{1,0:T(8,128)(2,1)S(1)}, bf16[64,1536]{1,0:T(8,128)(2,1)S(1)}, u32[]{:S(2)}, u32[]{:S(2)}) %collective-permute-start.16) | collective-permute-done | bytes 196640 | tf_op jit(solution)/shard_map/ppermute | solution.py:315
  (77 shorter events, 19.2 us)
Async XLA Ops:
  12.9 150.2 %copy-start.1 = (f32[8,264,384]{2,1,0:T(8,128)}, f32[8,264,384]{2,1,0:T(8,128)S(1)}, u32[]{:S(2)}) copy-start(f32[8,264,384]{2,1,0:T(8,128)S(1)} %get-tuple-element.66.block_ref) | copy-start | bytes 9732100
  172.5 10.1 %collective-permute-start = (f32[16,2,32,256]{3,2,1,0:T(8,128)}, f32[16,2,32,256]{3,2,1,0:T(8,128)S(1)}, u32[]{:S(2)}, u32[]{:S(2)}) collective-permute-start(f32[16,2,32,256]{3,2,1,0:T(8,128)} %slice_bitcast_fusion), channel_id=1, source_target_pairs={{0,1},{1,0},{2,3},{3,2},{4,5},{5,4},{6,7},{7,6},{8,9},{9,8},{10,11... | collective-permute-start | bytes 3145736 | tf_op jit(solution)/shard_map/ppermute | solution.py:319
  172.9 3.7 %collective-permute-start.3 = (f32[4,256]{1,0:T(4,128)S(1)}, f32[4,256]{1,0:T(4,128)S(1)}, u32[]{:S(2)}, u32[]{:S(2)}) collective-permute-start(f32[4,256]{1,0:T(4,128)S(1)} %pad_maximum_fusion.1), channel_id=1, source_target_pairs={{0,96},{32,0},{64,32},{96,64},{1,97},{33,1},{65,33},{97,65},{2,98}... | collective-permute-start | bytes 12296 | tf_op jit(solution)/shard_map/ppermute | solution.py:311
  175.4 4.0 %collective-permute-start.2 = (f32[4,256]{1,0:T(4,128)S(1)}, f32[4,256]{1,0:T(4,128)S(1)}, u32[]{:S(2)}, u32[]{:S(2)}) collective-permute-start(f32[4,256]{1,0:T(4,128)S(1)} %pad_maximum_fusion.1), channel_id=1, source_target_pairs={{0,64},{32,96},{64,0},{96,32},{1,65},{33,97},{65,1},{97,33},{2,66}... | collective-permute-start | bytes 12296 | tf_op jit(solution)/shard_map/ppermute | solution.py:311
  175.9 3.7 %collective-permute-start.1 = (f32[4,256]{1,0:T(4,128)S(1)}, f32[4,256]{1,0:T(4,128)S(1)}, u32[]{:S(2)}, u32[]{:S(2)}) collective-permute-start(f32[4,256]{1,0:T(4,128)S(1)} %pad_maximum_fusion.1), channel_id=1, source_target_pairs={{0,32},{32,64},{64,96},{96,0},{1,33},{33,65},{65,97},{97,1},{2,34}... | collective-permute-start | bytes 12296 | tf_op jit(solution)/shard_map/ppermute | solution.py:311
  179.6 3.0 %collective-permute-start.4 = (f32[2,256]{1,0:T(2,128)S(1)}, f32[2,256]{1,0:T(2,128)S(1)}, u32[]{:S(2)}, u32[]{:S(2)}) collective-permute-start(f32[2,256]{1,0:T(2,128)S(1)} %fusion.13), channel_id=1, source_target_pairs={{0,1},{1,0},{2,3},{3,2},{4,5},{5,4},{6,7},{7,6},{8,9},{9,8},{10,11... | collective-permute-start | bytes 6152 | tf_op jit(solution)/shard_map/ppermute | solution.py:319
  183.6 13.7 %all-to-all-start.1 = ((bf16[16,2,32,256]{3,2,1,0:T(8,128)(2,1)}), bf16[16,2,32,256]{3,2,1,0:T(8,128)(2,1)S(1)}, u32[]{:S(2)}, u32[]{:S(2)}) async-start(bf16[16,2,32,256]{3,2,1,0:T(8,128)(2,1)} %fusion.1), calls=%async_computation.1 | async-start | bytes 1048576 | tf_op jit(solution)/shard_map/all_to_all | solution.py:306
  198.2 15.4 %all-to-all-start.2 = ((bf16[16,2,32,256]{3,2,1,0:T(8,128)(2,1)}), bf16[16,2,32,256]{3,2,1,0:T(8,128)(2,1)S(1)}, u32[]{:S(2)}, u32[]{:S(2)}) async-start(bf16[16,2,32,256]{3,2,1,0:T(8,128)(2,1)} %broadcast_in_dim.48), calls=%async_computation.2 | async-start | bytes 1048576 | tf_op jit(solution)/shard_map/all_to_all | solution.py:306
  203.3 12.4 %collective-permute-start.8 = (f32[4,3072]{1,0:T(4,128)S(1)}, f32[4,3072]{1,0:T(4,128)S(1)}, u32[]{:S(2)}, u32[]{:S(2)}) collective-permute-start(f32[4,3072]{1,0:T(4,128)S(1)} %pad_maximum_fusion), channel_id=1, source_target_pairs={{0,96},{32,0},{64,32},{96,64},{1,97},{33,1},{65,33},{97,65},{2,98}... | collective-permute-start | bytes 147464 | tf_op jit(solution)/shard_map/ppermute | solution.py:311
  203.4 12.3 %collective-permute-start.7 = (f32[4,3072]{1,0:T(4,128)S(1)}, f32[4,3072]{1,0:T(4,128)S(1)}, u32[]{:S(2)}, u32[]{:S(2)}) collective-permute-start(f32[4,3072]{1,0:T(4,128)S(1)} %pad_maximum_fusion), channel_id=1, source_target_pairs={{0,64},{32,96},{64,0},{96,32},{1,65},{33,97},{65,1},{97,33},{2,66}... | collective-permute-start | bytes 147464 | tf_op jit(solution)/shard_map/ppermute | solution.py:311
  204.7 11.0 %collective-permute-start.6 = (f32[4,3072]{1,0:T(4,128)S(1)}, f32[4,3072]{1,0:T(4,128)S(1)}, u32[]{:S(2)}, u32[]{:S(2)}) collective-permute-start(f32[4,3072]{1,0:T(4,128)S(1)} %pad_maximum_fusion), channel_id=1, source_target_pairs={{0,32},{32,64},{64,96},{96,0},{1,33},{33,65},{65,97},{97,1},{2,34}... | collective-permute-start | bytes 147464 | tf_op jit(solution)/shard_map/ppermute | solution.py:311
  213.6 3.6 %collective-permute-start.5 = (bf16[16,2,32,256]{3,2,1,0:T(8,128)(2,1)S(1)}, bf16[16,2,32,256]{3,2,1,0:T(8,128)(2,1)S(1)}, u32[]{:S(2)}, u32[]{:S(2)}) collective-permute-start(bf16[16,2,32,256]{3,2,1,0:T(8,128)(2,1)S(1)} %all-to-all-done.2.own_ref), channel_id=1, source_target_pairs={{0,1},{1,0},{2,3},{3,2},{4,5},{5,4},{6,7},{7,6},{8,9},{9,8},{10,11... | collective-permute-start | bytes 1572872 | tf_op jit(solution)/shard_map/ppermute | solution.py:319
  224.7 13.9 %collective-permute-start.13 = (bf16[128,1536]{1,0:T(8,128)(2,1)S(1)}, bf16[128,1536]{1,0:T(8,128)(2,1)S(1)}, u32[]{:S(2)}, u32[]{:S(2)}) collective-permute-start(bf16[128,1536]{1,0:T(8,128)(2,1)S(1)} %get-tuple-element.83), channel_id=1, source_target_pairs={{0,32},{32,0},{64,96},{96,64},{1,33},{33,1},{65,97},{97,65},{2,34}... | collective-permute-start | bytes 1179656 | tf_op jit(solution)/shard_map/ppermute | solution.py:315
  225.7 32.5 %collective-permute-start.18 = (bf16[128,256]{1,0:T(8,128)(2,1)S(1)}, bf16[128,256]{1,0:T(8,128)(2,1)S(1)}, u32[]{:S(2)}, u32[]{:S(2)}) collective-permute-start(bf16[128,256]{1,0:T(8,128)(2,1)S(1)} %fusion.2), channel_id=1, source_target_pairs={{0,64},{32,96},{64,0},{96,32},{1,65},{33,97},{65,1},{97,33},{2,66}... | collective-permute-start | bytes 196616 | tf_op jit(solution)/shard_map/ppermute | solution.py:311
  227.0 32.6 %collective-permute-start.17 = (bf16[128,256]{1,0:T(8,128)(2,1)S(1)}, bf16[128,256]{1,0:T(8,128)(2,1)S(1)}, u32[]{:S(2)}, u32[]{:S(2)}) collective-permute-start(bf16[128,256]{1,0:T(8,128)(2,1)S(1)} %fusion.2), channel_id=1, source_target_pairs={{0,32},{32,64},{64,96},{96,0},{1,33},{33,65},{65,97},{97,1},{2,34}... | collective-permute-start | bytes 196616 | tf_op jit(solution)/shard_map/ppermute | solution.py:311
  227.9 31.7 %collective-permute-start.19 = (bf16[128,256]{1,0:T(8,128)(2,1)S(1)}, bf16[128,256]{1,0:T(8,128)(2,1)S(1)}, u32[]{:S(2)}, u32[]{:S(2)}) collective-permute-start(bf16[128,256]{1,0:T(8,128)(2,1)S(1)} %fusion.2), channel_id=1, source_target_pairs={{0,96},{32,0},{64,32},{96,64},{1,97},{33,1},{65,33},{97,65},{2,98}... | collective-permute-start | bytes 196616 | tf_op jit(solution)/shard_map/ppermute | solution.py:311
  229.7 34.1 %collective-permute-start.15 = (bf16[128,1536]{1,0:T(8,128)(2,1)S(1)}, bf16[128,1536]{1,0:T(8,128)(2,1)S(1)}, u32[]{:S(2)}, u32[]{:S(2)}) collective-permute-start(bf16[128,1536]{1,0:T(8,128)(2,1)S(1)} %get-tuple-element.85), channel_id=1, source_target_pairs={{0,96},{32,64},{64,32},{96,0},{1,97},{33,65},{65,33},{97,1},{2,98}... | collective-permute-start | bytes 1179656 | tf_op jit(solution)/shard_map/ppermute | solution.py:315
  238.6 9.0 %collective-permute-start.9 = (bf16[128,1536]{1,0:T(8,128)(2,1)S(1)}, bf16[128,1536]{1,0:T(8,128)(2,1)S(1)}, u32[]{:S(2)}, u32[]{:S(2)}) collective-permute-start(bf16[128,1536]{1,0:T(8,128)(2,1)S(1)} %get-tuple-element.79), channel_id=1, source_target_pairs={{0,32},{32,0},{64,96},{96,64},{1,33},{33,1},{65,97},{97,65},{2,34}... | collective-permute-start | bytes 1179656 | tf_op jit(solution)/shard_map/ppermute | solution.py:315
  247.5 9.3 %collective-permute-start.11 = (bf16[128,1536]{1,0:T(8,128)(2,1)S(1)}, bf16[128,1536]{1,0:T(8,128)(2,1)S(1)}, u32[]{:S(2)}, u32[]{:S(2)}) collective-permute-start(bf16[128,1536]{1,0:T(8,128)(2,1)S(1)} %get-tuple-element.81), channel_id=1, source_target_pairs={{0,96},{32,64},{64,32},{96,0},{1,97},{33,65},{65,33},{97,1},{2,98}... | collective-permute-start | bytes 1179656 | tf_op jit(solution)/shard_map/ppermute | solution.py:315
  256.8 9.6 %collective-permute-start.14 = (bf16[64,1536]{1,0:T(8,128)(2,1)S(1)}, bf16[64,1536]{1,0:T(8,128)(2,1)S(1)}, u32[]{:S(2)}, u32[]{:S(2)}) collective-permute-start(bf16[64,1536]{1,0:T(8,128)(2,1)S(1)} %add_convert_fusion.1), channel_id=1, source_target_pairs={{0,96},{32,64},{64,32},{96,0},{1,97},{33,65},{65,33},{97,1},{2,98}... | collective-permute-start | bytes 589832 | tf_op jit(solution)/shard_map/ppermute | solution.py:315
  258.2 13.0 %collective-permute-start.10 = (bf16[64,1536]{1,0:T(8,128)(2,1)S(1)}, bf16[64,1536]{1,0:T(8,128)(2,1)S(1)}, u32[]{:S(2)}, u32[]{:S(2)}) collective-permute-start(bf16[64,1536]{1,0:T(8,128)(2,1)S(1)} %add_convert_fusion.3), channel_id=1, source_target_pairs={{0,96},{32,64},{64,32},{96,0},{1,97},{33,65},{65,33},{97,1},{2,98}... | collective-permute-start | bytes 589832 | tf_op jit(solution)/shard_map/ppermute | solution.py:315
  259.6 12.6 %collective-permute-start.12 = (bf16[64,1536]{1,0:T(8,128)(2,1)S(1)}, bf16[64,1536]{1,0:T(8,128)(2,1)S(1)}, u32[]{:S(2)}, u32[]{:S(2)}) collective-permute-start(bf16[64,1536]{1,0:T(8,128)(2,1)S(1)} %add_convert_fusion.2), channel_id=1, source_target_pairs={{0,32},{32,0},{64,96},{96,64},{1,33},{33,1},{65,97},{97,65},{2,34}... | collective-permute-start | bytes 589832 | tf_op jit(solution)/shard_map/ppermute | solution.py:315
  259.7 6.0 %collective-permute-start.20 = (f32[128,256]{1,0:T(8,128)S(1)}, f32[128,256]{1,0:T(8,128)S(1)}, u32[]{:S(2)}, u32[]{:S(2)}) collective-permute-start(f32[128,256]{1,0:T(8,128)S(1)} %convert_add_fusion.4), channel_id=1, source_target_pairs={{0,1},{1,0},{2,3},{3,2},{4,5},{5,4},{6,7},{7,6},{8,9},{9,8},{10,11... | collective-permute-start | bytes 393224 | tf_op jit(solution)/shard_map/ppermute | solution.py:319
  263.9 7.3 %collective-permute-start.16 = (bf16[64,1536]{1,0:T(8,128)(2,1)S(1)}, bf16[64,1536]{1,0:T(8,128)(2,1)S(1)}, u32[]{:S(2)}, u32[]{:S(2)}) collective-permute-start(bf16[64,1536]{1,0:T(8,128)(2,1)S(1)} %add_convert_fusion), channel_id=1, source_target_pairs={{0,32},{32,0},{64,96},{96,64},{1,33},{33,1},{65,97},{97,65},{2,34}... | collective-permute-start | bytes 589832 | tf_op jit(solution)/shard_map/ppermute | solution.py:315
  (7 other events, 465.2 us)

commit v10 on v9

--- a/solution.py
+++ b/solution.py
@@ -9,6 +9,7 @@
 
 
 BLK = 256
+HALF = BLK // 2
 NCHUNK = 768
 TILE = 256
 Y, Z, C = 4, 4, 2
@@ -40,6 +41,7 @@
     r = lax.broadcasted_iota(jnp.int32, (BLK, BLK), 0)
     c = lax.broadcasted_iota(jnp.int32, (BLK, BLK), 1)
     upto = jnp.where(r <= c, 1.0, 0.0)
+    r, c = r[:HALF, :HALF], c[:HALF, :HALF]
     inclusive = jnp.dot(log_a, upto, precision=HIGHEST, preferred_element_type=F32)
     exclusive = jnp.where(lax.broadcasted_iota(jnp.int32, a.shape, 1) == 0, 0.0, pltpu.roll(inclusive, 1, 1))
     column = exclusive.T
@@ -51,8 +53,15 @@
         for b in range(nb):
             k = f * nb + b
             row = slice(k, k + 1)
-            weight = jnp.exp(jnp.minimum(column[:, k : k + 1] - inclusive[row], 0.0)) * fresh[row]
-            block_ref[k, :BLK, :BLK] = jnp.where(r == c, 1.0, jnp.where(c < r, -weight, 0.0))
+            for i in range(2):
+                for j in range(2):
+                    down, over = slice(i * HALF, (i + 1) * HALF), slice(j * HALF, (j + 1) * HALF)
+                    if i < j:
+                        block_ref[k, down, over] = jnp.zeros((HALF, HALF), F32)
+                        continue
+                    spread = column[down, k : k + 1] - inclusive[row, over]
+                    weight = jnp.exp(jnp.minimum(spread, 0.0)) * -fresh[row, over]
+                    block_ref[k, down, over] = jnp.where(r == c, 1.0, jnp.where(c < r, weight, 0.0)) if i == j else weight
             block_ref[k, :BLK, BLK:] = jnp.broadcast_to(jnp.exp(column[:, k : k + 1]), (BLK, 128))
             last = jnp.exp(sums[b] - inclusive[row]) * fresh[row]
             block_ref[k, BLK:, :BLK] = jnp.broadcast_to(last, (8, BLK))

time: 275 us -> 275 us (level)
  no operation moved by 1% of the time
where the time goes in v10:
time: 275 us; the launch traced here: 273 us
  blocking collectives  150 us (55%)
  waiting for transfers between devices  36.1 us (13%)
  starting transfers between devices  34.4 us (13%)
  Pallas kernels  30 us (11%)
  other arithmetic  13 us (5%)
  local copies, waits for them, and re-layouts  8.61 us (3%)
    all_to_all x1, blocking collectives, all_to_all(): lax.all_to_all(x, axis, split_axis=0, concat_axis=0, tiled=True, axis_ind...  150 us
    ppermute x8, waiting for transfers between devices, paired(): lax.ppermute(x, 'tm', [(i, i ^ by) for i in range(lax.axis_size('tm'))])  21.4 us
    pallas_call x2, Pallas kernels, backward(): pl.pallas_call(functools.partial(backward_kernel, f), grid=(2 * steps,),...  14.9 us
    ppermute x9, starting transfers between devices, shifted(): return lax.ppermute(x, 'tm', [(i, (i + by) % n) for i in range(n)])  9.91 us
    all_to_all x2, waiting for transfers between devices, all_to_all(): lax.all_to_all(x, axis, split_axis=0, concat_axis=0, tiled=True, axis_ind...  9.57 us
    all_to_all x2, starting transfers between devices, all_to_all(): lax.all_to_all(x, axis, split_axis=0, concat_axis=0, tiled=True, axis_ind...  8.59 us
    reduce_sum x1, other arithmetic, per_device(): (x.astype(F32) * weight).sum(axis=(0, 2))  8.51 us
    ppermute x4, starting transfers between devices, across(): return lax.ppermute(x, 'grid', [(g, g ^ 1) for g in range(Y * Z * C)])  8.51 us
  transfers between devices with their start and end apart: 23, of which 9 were waited for; matrix products, arithmetic and copies ran while one was open for 4% of the time, Pallas kernels for 3%

profile of v10, /device:TPU:1, one launch (start us, length us, event | category | flops | bytes accessed | tf_op | source)
XLA Modules:
  0.0 273.2 jit_solution(3630498333239499072)
XLA Ops:
  0.7 2.8 %copy-done.2 = bf16[32,98304]{1,0:T(8,128)(2,1)S(1)} copy-done((bf16[32,98304]{1,0:T(8,128)(2,1)S(1)}, bf16[32,98304]{1,0:T(8,128)(2,1)}, u32[]{:S(2)}) %copy-start.2) | copy-done | bytes 6291480
  3.5 2.8 %copy-done.3 = bf16[32,98304]{1,0:T(8,128)(2,1)S(1)} copy-done((bf16[32,98304]{1,0:T(8,128)(2,1)S(1)}, bf16[32,98304]{1,0:T(8,128)(2,1)}, u32[]{:S(2)}) %copy-start.3) | copy-done | bytes 6291480
  7.0 5.9 %prepare.1 = (bf16[32,2,32,3072]{3,2,1,0:T(8,128)(2,1)S(1)}, f32[8,264,384]{2,1,0:T(8,128)S(1)}, f32[8,256]{1,0:T(8,128)S(1)}, f32[8,256]{1,0:T(8,128)S(1)}, f32[2,256]{1,0:T(2,128)S(1)}) custom-call(bf16[32,98304]{1,0:T(8,128)(2,1)S(1)} %copy-done.2, bf16[32,98304]{1,0:T(8,128)(2,1)S(1)} %copy-done.3, f32[2,1024]{1,0:T(2,128)S(1)} %copy-done.7), custom_call_target="tpu_custom_call" | custom-call | bytes 25165824 | tf_op jit(solution)/shard_map/prepare/pallas_call | solution.py:83
  12.9 150.2 %all_to_all.15.x_ref = bf16[32,2,32,3072]{3,2,1,0:T(8,128)(2,1)S(1)} all-to-all(bf16[32,2,32,3072]{3,2,1,0:T(8,128)(2,1)S(1)} %get-tuple-element.51), channel_id=1, replica_groups=mesh['tm'=4,'grid'=32] {'grid'}, dimensions={0} | all-to-all | bytes 25165824 | tf_op jit(solution)/shard_map/all_to_all | solution.py:315
  163.1 8.3 %forward.1 = (f32[2,16,2,32,256]{4,3,2,1,0:T(8,128)S(1)}, f32[2,256]{1,0:T(2,128)S(1)}, f32[2,256]{1,0:T(2,128)S(1)}) custom-call(s32[2]{0:T(128)S(1)} %pad_add_fusion.place_ref, bf16[32,2,32,3072]{3,2,1,0:T(8,128)(2,1)S(1)} %all_to_all.15.x_ref, bf16[3072,256]{1,0:T(8,128)(2,1)S(1)} %copy-done.4, bf16[3072,256]{1,0:T(8,128)(2,1)S(1)} %copy-done.5, ...), custom_call_target="tpu_custom_call" | custom-call | flops 3221225472 | bytes 12582912 | tf_op jit(solution)/shard_map/forward/pallas_call | solution.py:161
  172.9 2.5 collective-permute-start.3
  176.6 2.8 %collective-permute-done.2 = f32[4,256]{1,0:T(4,128)S(1)} collective-permute-done((f32[4,256]{1,0:T(4,128)S(1)}, f32[4,256]{1,0:T(4,128)S(1)}, u32[]{:S(2)}, u32[]{:S(2)}) %collective-permute-start.2) | collective-permute-done | bytes 4128 | tf_op jit(solution)/shard_map/ppermute | solution.py:320
  179.6 2.2 collective-permute-start.4
  183.6 3.6 %all-to-all-start.1 = ((bf16[16,2,32,256]{3,2,1,0:T(8,128)(2,1)}), bf16[16,2,32,256]{3,2,1,0:T(8,128)(2,1)S(1)}, u32[]{:S(2)}, u32[]{:S(2)}) async-start(bf16[16,2,32,256]{3,2,1,0:T(8,128)(2,1)} %fusion.1), calls=%async_computation.1 | async-start | bytes 1048576 | tf_op jit(solution)/shard_map/all_to_all | solution.py:315
  187.1 8.5 %multiply_reduce_fusion = f32[2,3072]{1,0:T(2,128)S(1)} fusion(bf16[32,2,32,3072]{3,2,1,0:T(8,128)(2,1)} %copy-done, f32[32,2,32]{2,1,0:T(2,128)S(1)} %bitcast.25), kind=kLoop, calls=%fused_computation | loop fusion | flops 18868224 | bytes 12615680 | tf_op jit(solution)/shard_map/reduce_sum | solution.py:381
  195.7 1.6 all-to-all-done.1
  198.2 5.0 %all-to-all-start.2 = ((bf16[16,2,32,256]{3,2,1,0:T(8,128)(2,1)}), bf16[16,2,32,256]{3,2,1,0:T(8,128)(2,1)S(1)}, u32[]{:S(2)}, u32[]{:S(2)}) async-start(bf16[16,2,32,256]{3,2,1,0:T(8,128)(2,1)} %broadcast_in_dim.48), calls=%async_computation.2 | async-start | bytes 1048576 | tf_op jit(solution)/shard_map/all_to_all | solution.py:315
  205.6 8.0 %all-to-all-done.2.own_ref = bf16[16,2,32,256]{3,2,1,0:T(8,128)(2,1)S(1)} async-done(((bf16[16,2,32,256]{3,2,1,0:T(8,128)(2,1)}), bf16[16,2,32,256]{3,2,1,0:T(8,128)(2,1)S(1)}, u32[]{:S(2)}, u32[]{:S(2)}) %all-to-all-start.2) | async-done | bytes 524320 | tf_op jit(solution)/shard_map/all_to_all | solution.py:315
  213.6 2.1 collective-permute-start.5
  215.8 1.4 collective-permute-done.5.other_ref
  217.2 7.5 %backward.3 = (bf16[128,1536]{1,0:T(8,128)(2,1)S(1)}, bf16[128,1536]{1,0:T(8,128)(2,1)S(1)}, bf16[128,1536]{1,0:T(8,128)(2,1)S(1)}, bf16[128,1536]{1,0:T(8,128)(2,1)S(1)}) custom-call(s32[2]{0:T(128)S(1)} %pad_add_fusion.place_ref, bf16[16,2,32,256]{3,2,1,0:T(8,128)(2,1)S(1)} %all-to-all-done.2.own_ref, ...), custom_call_target="tpu_custom_call" | custom-call | flops 3221225472 | bytes 6291456 | tf_op jit(solution)/shard_map/backward/pallas_call | solution.py:263
  227.9 1.8 collective-permute-start.19
  231.1 7.4 %backward.2 = (bf16[128,1536]{1,0:T(8,128)(2,1)S(1)}, bf16[128,1536]{1,0:T(8,128)(2,1)S(1)}, bf16[128,1536]{1,0:T(8,128)(2,1)S(1)}, bf16[128,1536]{1,0:T(8,128)(2,1)S(1)}) custom-call(s32[2]{0:T(128)S(1)} %pad_add_fusion.place_ref, bf16[16,2,32,256]{3,2,1,0:T(8,128)(2,1)S(1)} %all-to-all-done.2.own_ref, ...), custom_call_target="tpu_custom_call" | custom-call | flops 3221225472 | bytes 6291456 | tf_op jit(solution)/shard_map/backward/pallas_call | solution.py:263
  238.7 8.8 %collective-permute-done.9 = bf16[128,1536]{1,0:T(8,128)(2,1)S(1)} collective-permute-done((bf16[128,1536]{1,0:T(8,128)(2,1)S(1)}, bf16[128,1536]{1,0:T(8,128)(2,1)S(1)}, u32[]{:S(2)}, u32[]{:S(2)}) %collective-permute-start.9) | collective-permute-done | bytes 393248 | tf_op jit(solution)/shard_map/ppermute | solution.py:324
  248.9 7.9 %collective-permute-done.11 = bf16[128,1536]{1,0:T(8,128)(2,1)S(1)} collective-permute-done((bf16[128,1536]{1,0:T(8,128)(2,1)S(1)}, bf16[128,1536]{1,0:T(8,128)(2,1)S(1)}, u32[]{:S(2)}, u32[]{:S(2)}) %collective-permute-start.11) | collective-permute-done | bytes 393248 | tf_op jit(solution)/shard_map/ppermute | solution.py:324
  258.2 1.4 collective-permute-start.10
  259.6 4.1 %collective-permute-start.20 = (f32[128,256]{1,0:T(8,128)S(1)}, f32[128,256]{1,0:T(8,128)S(1)}, u32[]{:S(2)}, u32[]{:S(2)}) collective-permute-start(f32[128,256]{1,0:T(8,128)S(1)} %convert_add_fusion.4), channel_id=1, source_target_pairs={{0,1},{1,0},{2,3},{3,2},{4,5},{5,4},{6,7},{7,6},{8,9},{9,8},{10,11... | collective-permute-start | bytes 393224 | tf_op jit(solution)/shard_map/ppermute | solution.py:328
  263.8 1.8 collective-permute-start.16
  266.5 4.6 %collective-permute-done.16 = bf16[64,1536]{1,0:T(8,128)(2,1)S(1)} collective-permute-done((bf16[64,1536]{1,0:T(8,128)(2,1)S(1)}, bf16[64,1536]{1,0:T(8,128)(2,1)S(1)}, u32[]{:S(2)}, u32[]{:S(2)}) %collective-permute-start.16) | collective-permute-done | bytes 196640 | tf_op jit(solution)/shard_map/ppermute | solution.py:324
  (77 shorter events, 19.4 us)
Async XLA Ops:
  12.9 150.2 %copy-start.1 = (f32[8,264,384]{2,1,0:T(8,128)}, f32[8,264,384]{2,1,0:T(8,128)S(1)}, u32[]{:S(2)}) copy-start(f32[8,264,384]{2,1,0:T(8,128)S(1)} %get-tuple-element.66.block_ref) | copy-start | bytes 9732100
  172.5 10.1 %collective-permute-start = (f32[16,2,32,256]{3,2,1,0:T(8,128)}, f32[16,2,32,256]{3,2,1,0:T(8,128)S(1)}, u32[]{:S(2)}, u32[]{:S(2)}) collective-permute-start(f32[16,2,32,256]{3,2,1,0:T(8,128)} %slice_bitcast_fusion), channel_id=1, source_target_pairs={{0,1},{1,0},{2,3},{3,2},{4,5},{5,4},{6,7},{7,6},{8,9},{9,8},{10,11... | collective-permute-start | bytes 3145736 | tf_op jit(solution)/shard_map/ppermute | solution.py:328
  172.9 3.7 %collective-permute-start.3 = (f32[4,256]{1,0:T(4,128)S(1)}, f32[4,256]{1,0:T(4,128)S(1)}, u32[]{:S(2)}, u32[]{:S(2)}) collective-permute-start(f32[4,256]{1,0:T(4,128)S(1)} %pad_maximum_fusion.1), channel_id=1, source_target_pairs={{0,96},{32,0},{64,32},{96,64},{1,97},{33,1},{65,33},{97,65},{2,98}... | collective-permute-start | bytes 12296 | tf_op jit(solution)/shard_map/ppermute | solution.py:320
  175.3 4.0 %collective-permute-start.2 = (f32[4,256]{1,0:T(4,128)S(1)}, f32[4,256]{1,0:T(4,128)S(1)}, u32[]{:S(2)}, u32[]{:S(2)}) collective-permute-start(f32[4,256]{1,0:T(4,128)S(1)} %pad_maximum_fusion.1), channel_id=1, source_target_pairs={{0,64},{32,96},{64,0},{96,32},{1,65},{33,97},{65,1},{97,33},{2,66}... | collective-permute-start | bytes 12296 | tf_op jit(solution)/shard_map/ppermute | solution.py:320
  175.9 3.7 %collective-permute-start.1 = (f32[4,256]{1,0:T(4,128)S(1)}, f32[4,256]{1,0:T(4,128)S(1)}, u32[]{:S(2)}, u32[]{:S(2)}) collective-permute-start(f32[4,256]{1,0:T(4,128)S(1)} %pad_maximum_fusion.1), channel_id=1, source_target_pairs={{0,32},{32,64},{64,96},{96,0},{1,33},{33,65},{65,97},{97,1},{2,34}... | collective-permute-start | bytes 12296 | tf_op jit(solution)/shard_map/ppermute | solution.py:320
  179.6 3.0 %collective-permute-start.4 = (f32[2,256]{1,0:T(2,128)S(1)}, f32[2,256]{1,0:T(2,128)S(1)}, u32[]{:S(2)}, u32[]{:S(2)}) collective-permute-start(f32[2,256]{1,0:T(2,128)S(1)} %fusion.13), channel_id=1, source_target_pairs={{0,1},{1,0},{2,3},{3,2},{4,5},{5,4},{6,7},{7,6},{8,9},{9,8},{10,11... | collective-permute-start | bytes 6152 | tf_op jit(solution)/shard_map/ppermute | solution.py:328
  183.6 13.7 %all-to-all-start.1 = ((bf16[16,2,32,256]{3,2,1,0:T(8,128)(2,1)}), bf16[16,2,32,256]{3,2,1,0:T(8,128)(2,1)S(1)}, u32[]{:S(2)}, u32[]{:S(2)}) async-start(bf16[16,2,32,256]{3,2,1,0:T(8,128)(2,1)} %fusion.1), calls=%async_computation.1 | async-start | bytes 1048576 | tf_op jit(solution)/shard_map/all_to_all | solution.py:315
  198.2 15.4 %all-to-all-start.2 = ((bf16[16,2,32,256]{3,2,1,0:T(8,128)(2,1)}), bf16[16,2,32,256]{3,2,1,0:T(8,128)(2,1)S(1)}, u32[]{:S(2)}, u32[]{:S(2)}) async-start(bf16[16,2,32,256]{3,2,1,0:T(8,128)(2,1)} %broadcast_in_dim.48), calls=%async_computation.2 | async-start | bytes 1048576 | tf_op jit(solution)/shard_map/all_to_all | solution.py:315
  203.3 12.4 %collective-permute-start.8 = (f32[4,3072]{1,0:T(4,128)S(1)}, f32[4,3072]{1,0:T(4,128)S(1)}, u32[]{:S(2)}, u32[]{:S(2)}) collective-permute-start(f32[4,3072]{1,0:T(4,128)S(1)} %pad_maximum_fusion), channel_id=1, source_target_pairs={{0,96},{32,0},{64,32},{96,64},{1,97},{33,1},{65,33},{97,65},{2,98}... | collective-permute-start | bytes 147464 | tf_op jit(solution)/shard_map/ppermute | solution.py:320
  203.6 12.1 %collective-permute-start.7 = (f32[4,3072]{1,0:T(4,128)S(1)}, f32[4,3072]{1,0:T(4,128)S(1)}, u32[]{:S(2)}, u32[]{:S(2)}) collective-permute-start(f32[4,3072]{1,0:T(4,128)S(1)} %pad_maximum_fusion), channel_id=1, source_target_pairs={{0,64},{32,96},{64,0},{96,32},{1,65},{33,97},{65,1},{97,33},{2,66}... | collective-permute-start | bytes 147464 | tf_op jit(solution)/shard_map/ppermute | solution.py:320
  204.8 10.8 %collective-permute-start.6 = (f32[4,3072]{1,0:T(4,128)S(1)}, f32[4,3072]{1,0:T(4,128)S(1)}, u32[]{:S(2)}, u32[]{:S(2)}) collective-permute-start(f32[4,3072]{1,0:T(4,128)S(1)} %pad_maximum_fusion), channel_id=1, source_target_pairs={{0,32},{32,64},{64,96},{96,0},{1,33},{33,65},{65,97},{97,1},{2,34}... | collective-permute-start | bytes 147464 | tf_op jit(solution)/shard_map/ppermute | solution.py:320
  213.6 3.6 %collective-permute-start.5 = (bf16[16,2,32,256]{3,2,1,0:T(8,128)(2,1)S(1)}, bf16[16,2,32,256]{3,2,1,0:T(8,128)(2,1)S(1)}, u32[]{:S(2)}, u32[]{:S(2)}) collective-permute-start(bf16[16,2,32,256]{3,2,1,0:T(8,128)(2,1)S(1)} %all-to-all-done.2.own_ref), channel_id=1, source_target_pairs={{0,1},{1,0},{2,3},{3,2},{4,5},{5,4},{6,7},{7,6},{8,9},{9,8},{10,11... | collective-permute-start | bytes 1572872 | tf_op jit(solution)/shard_map/ppermute | solution.py:328
  224.7 13.9 %collective-permute-start.13 = (bf16[128,1536]{1,0:T(8,128)(2,1)S(1)}, bf16[128,1536]{1,0:T(8,128)(2,1)S(1)}, u32[]{:S(2)}, u32[]{:S(2)}) collective-permute-start(bf16[128,1536]{1,0:T(8,128)(2,1)S(1)} %get-tuple-element.83), channel_id=1, source_target_pairs={{0,32},{32,0},{64,96},{96,64},{1,33},{33,1},{65,97},{97,65},{2,34}... | collective-permute-start | bytes 1179656 | tf_op jit(solution)/shard_map/ppermute | solution.py:324
  225.7 32.5 %collective-permute-start.18 = (bf16[128,256]{1,0:T(8,128)(2,1)S(1)}, bf16[128,256]{1,0:T(8,128)(2,1)S(1)}, u32[]{:S(2)}, u32[]{:S(2)}) collective-permute-start(bf16[128,256]{1,0:T(8,128)(2,1)S(1)} %fusion.2), channel_id=1, source_target_pairs={{0,64},{32,96},{64,0},{96,32},{1,65},{33,97},{65,1},{97,33},{2,66}... | collective-permute-start | bytes 196616 | tf_op jit(solution)/shard_map/ppermute | solution.py:320
  227.0 32.6 %collective-permute-start.17 = (bf16[128,256]{1,0:T(8,128)(2,1)S(1)}, bf16[128,256]{1,0:T(8,128)(2,1)S(1)}, u32[]{:S(2)}, u32[]{:S(2)}) collective-permute-start(bf16[128,256]{1,0:T(8,128)(2,1)S(1)} %fusion.2), channel_id=1, source_target_pairs={{0,32},{32,64},{64,96},{96,0},{1,33},{33,65},{65,97},{97,1},{2,34}... | collective-permute-start | bytes 196616 | tf_op jit(solution)/shard_map/ppermute | solution.py:320
  227.9 31.8 %collective-permute-start.19 = (bf16[128,256]{1,0:T(8,128)(2,1)S(1)}, bf16[128,256]{1,0:T(8,128)(2,1)S(1)}, u32[]{:S(2)}, u32[]{:S(2)}) collective-permute-start(bf16[128,256]{1,0:T(8,128)(2,1)S(1)} %fusion.2), channel_id=1, source_target_pairs={{0,96},{32,0},{64,32},{96,64},{1,97},{33,1},{65,33},{97,65},{2,98}... | collective-permute-start | bytes 196616 | tf_op jit(solution)/shard_map/ppermute | solution.py:320
  229.7 34.1 %collective-permute-start.15 = (bf16[128,1536]{1,0:T(8,128)(2,1)S(1)}, bf16[128,1536]{1,0:T(8,128)(2,1)S(1)}, u32[]{:S(2)}, u32[]{:S(2)}) collective-permute-start(bf16[128,1536]{1,0:T(8,128)(2,1)S(1)} %get-tuple-element.85), channel_id=1, source_target_pairs={{0,96},{32,64},{64,32},{96,0},{1,97},{33,65},{65,33},{97,1},{2,98}... | collective-permute-start | bytes 1179656 | tf_op jit(solution)/shard_map/ppermute | solution.py:324
  238.5 9.0 %collective-permute-start.9 = (bf16[128,1536]{1,0:T(8,128)(2,1)S(1)}, bf16[128,1536]{1,0:T(8,128)(2,1)S(1)}, u32[]{:S(2)}, u32[]{:S(2)}) collective-permute-start(bf16[128,1536]{1,0:T(8,128)(2,1)S(1)} %get-tuple-element.79), channel_id=1, source_target_pairs={{0,32},{32,0},{64,96},{96,64},{1,33},{33,1},{65,97},{97,65},{2,34}... | collective-permute-start | bytes 1179656 | tf_op jit(solution)/shard_map/ppermute | solution.py:324
  247.5 9.3 %collective-permute-start.11 = (bf16[128,1536]{1,0:T(8,128)(2,1)S(1)}, bf16[128,1536]{1,0:T(8,128)(2,1)S(1)}, u32[]{:S(2)}, u32[]{:S(2)}) collective-permute-start(bf16[128,1536]{1,0:T(8,128)(2,1)S(1)} %get-tuple-element.81), channel_id=1, source_target_pairs={{0,96},{32,64},{64,32},{96,0},{1,97},{33,65},{65,33},{97,1},{2,98}... | collective-permute-start | bytes 1179656 | tf_op jit(solution)/shard_map/ppermute | solution.py:324
  256.8 9.6 %collective-permute-start.14 = (bf16[64,1536]{1,0:T(8,128)(2,1)S(1)}, bf16[64,1536]{1,0:T(8,128)(2,1)S(1)}, u32[]{:S(2)}, u32[]{:S(2)}) collective-permute-start(bf16[64,1536]{1,0:T(8,128)(2,1)S(1)} %add_convert_fusion.1), channel_id=1, source_target_pairs={{0,96},{32,64},{64,32},{96,0},{1,97},{33,65},{65,33},{97,1},{2,98}... | collective-permute-start | bytes 589832 | tf_op jit(solution)/shard_map/ppermute | solution.py:324
  258.2 13.0 %collective-permute-start.10 = (bf16[64,1536]{1,0:T(8,128)(2,1)S(1)}, bf16[64,1536]{1,0:T(8,128)(2,1)S(1)}, u32[]{:S(2)}, u32[]{:S(2)}) collective-permute-start(bf16[64,1536]{1,0:T(8,128)(2,1)S(1)} %add_convert_fusion.3), channel_id=1, source_target_pairs={{0,96},{32,64},{64,32},{96,0},{1,97},{33,65},{65,33},{97,1},{2,98}... | collective-permute-start | bytes 589832 | tf_op jit(solution)/shard_map/ppermute | solution.py:324
  259.6 12.6 %collective-permute-start.12 = (bf16[64,1536]{1,0:T(8,128)(2,1)S(1)}, bf16[64,1536]{1,0:T(8,128)(2,1)S(1)}, u32[]{:S(2)}, u32[]{:S(2)}) collective-permute-start(bf16[64,1536]{1,0:T(8,128)(2,1)S(1)} %add_convert_fusion.2), channel_id=1, source_target_pairs={{0,32},{32,0},{64,96},{96,64},{1,33},{33,1},{65,97},{97,65},{2,34}... | collective-permute-start | bytes 589832 | tf_op jit(solution)/shard_map/ppermute | solution.py:324
  259.6 6.0 %collective-permute-start.20 = (f32[128,256]{1,0:T(8,128)S(1)}, f32[128,256]{1,0:T(8,128)S(1)}, u32[]{:S(2)}, u32[]{:S(2)}) collective-permute-start(f32[128,256]{1,0:T(8,128)S(1)} %convert_add_fusion.4), channel_id=1, source_target_pairs={{0,1},{1,0},{2,3},{3,2},{4,5},{5,4},{6,7},{7,6},{8,9},{9,8},{10,11... | collective-permute-start | bytes 393224 | tf_op jit(solution)/shard_map/ppermute | solution.py:328
  263.8 7.3 %collective-permute-start.16 = (bf16[64,1536]{1,0:T(8,128)(2,1)S(1)}, bf16[64,1536]{1,0:T(8,128)(2,1)S(1)}, u32[]{:S(2)}, u32[]{:S(2)}) collective-permute-start(bf16[64,1536]{1,0:T(8,128)(2,1)S(1)} %add_convert_fusion), channel_id=1, source_target_pairs={{0,32},{32,0},{64,96},{96,64},{1,33},{33,1},{65,97},{97,65},{2,34}... | collective-permute-start | bytes 589832 | tf_op jit(solution)/shard_map/ppermute | solution.py:324
  (7 other events, 465.2 us)

commit v11 on v10

--- a/solution.py
+++ b/solution.py
@@ -25,16 +25,9 @@
     return high, middle, (v - middle.astype(F32)).astype(BF16)
 
 
-def prepare_kernel(x0_ref, x1_ref, fading_ref, out_ref, block_ref, since_ref, to_end_ref, gain_ref, sems):
+def prepare_kernel(x0_ref, x1_ref, fading_ref, out_ref, block_ref, since_ref, to_end_ref, gain_ref):
     n, _, _, width = out_ref.shape
 
-    def copies():
-        for i in range(n):
-            for f, x_ref in enumerate((x0_ref, x1_ref)):
-                yield pltpu.make_async_copy(x_ref.at[:, pl.ds(i * width, width)], out_ref.at[i, f], sems.at[2 * i + f])
-
-    for copy in copies():
-        copy.start()
     nb = fading_ref.shape[1] // BLK
     a = jnp.concatenate([fading_ref[f : f + 1, b * BLK : (b + 1) * BLK] for f in range(2) for b in range(nb)])
     log_a = jnp.log(a)
@@ -71,8 +64,9 @@
             to_end_ref[row] = jnp.exp(behind + (sums[b] - inclusive[row])) * fresh[row]
             ahead = ahead + sums[b]
         gain_ref[f : f + 1] = jnp.broadcast_to(jnp.exp(ahead), (1, BLK))
-    for copy in copies():
-        copy.wait()
+    for i in range(n):
+        for f, x_ref in enumerate((x0_ref, x1_ref)):
+            out_ref[i, f] = x_ref[:, i * width : (i + 1) * width]
 
 
 def prepare(x0, x1, fading, n):
@@ -82,8 +76,8 @@
     whole = pl.BlockSpec(memory_space=pltpu.VMEM)
     return pl.pallas_call(
         prepare_kernel,
-        in_specs=[pl.BlockSpec(memory_space=pl.ANY), pl.BlockSpec(memory_space=pl.ANY), whole],
-        out_specs=[pl.BlockSpec(memory_space=pl.ANY), whole, whole, whole, whole],
+        in_specs=[whole, whole, whole],
+        out_specs=[whole, whole, whole, whole, whole],
         out_shape=[
             jax.ShapeDtypeStruct((n, 2, rows, width), x0.dtype),
             jax.ShapeDtypeStruct((count, BLK + 8, BLK + 128), F32),
@@ -91,7 +85,6 @@
             jax.ShapeDtypeStruct((count, BLK), F32),
             jax.ShapeDtypeStruct((2, BLK), F32),
         ],
-        scratch_shapes=[pltpu.SemaphoreType.DMA((2 * n,))],
         compiler_params=pltpu.CompilerParams(vmem_limit_bytes=20 * MIB),
         cost_estimate=pl.CostEstimate(flops=0, bytes_accessed=8 * x0.size, transcendentals=0),
         name="prepare",

time: 275 us -> 271 us (0.985)
  Pallas kernels: 30 us -> 26 us
    pallas_call x1, Pallas kernels: 5.89 us -> 1.88 us  [prepare(): pl.pallas_call(prepare_kernel, in_specs=[whole, whole, whole], out_specs=...]
where the time goes in v11:
time: 271 us; the launch traced here: 269 us
  blocking collectives  150 us (55%)
  waiting for transfers between devices  36.2 us (13%)
  starting transfers between devices  34.3 us (13%)
  Pallas kernels  26 us (10%)
  other arithmetic  13 us (5%)
  local copies, waits for them, and re-layouts  8.61 us (3%)
    all_to_all x1, blocking collectives, all_to_all(): lax.all_to_all(x, axis, split_axis=0, concat_axis=0, tiled=True, axis_ind...  150 us
    ppermute x8, waiting for transfers between devices, paired(): lax.ppermute(x, 'tm', [(i, i ^ by) for i in range(lax.axis_size('tm'))])  21.4 us
    pallas_call x2, Pallas kernels, backward(): pl.pallas_call(functools.partial(backward_kernel, f), grid=(2 * steps,),...  14.9 us
    all_to_all x2, waiting for transfers between devices, all_to_all(): lax.all_to_all(x, axis, split_axis=0, concat_axis=0, tiled=True, axis_ind...  9.74 us
    ppermute x9, starting transfers between devices, shifted(): return lax.ppermute(x, 'tm', [(i, (i + by) % n) for i in range(n)])  9.73 us
    all_to_all x2, starting transfers between devices, all_to_all(): lax.all_to_all(x, axis, split_axis=0, concat_axis=0, tiled=True, axis_ind...  8.59 us
    ppermute x4, starting transfers between devices, across(): return lax.ppermute(x, 'grid', [(g, g ^ 1) for g in range(Y * Z * C)])  8.52 us
    reduce_sum x1, other arithmetic, per_device(): (x.astype(F32) * weight).sum(axis=(0, 2))  8.51 us
  transfers between devices with their start and end apart: 23, of which 9 were waited for; matrix products, arithmetic and copies ran while one was open for 4% of the time, Pallas kernels for 3%

profile of v11, /device:TPU:1, one launch (start us, length us, event | category | flops | bytes accessed | tf_op | source)
XLA Modules:
  0.0 269.2 jit_solution(5815832941570327230)
XLA Ops:
  0.7 2.8 %copy-done.2 = bf16[32,98304]{1,0:T(8,128)(2,1)S(1)} copy-done((bf16[32,98304]{1,0:T(8,128)(2,1)S(1)}, bf16[32,98304]{1,0:T(8,128)(2,1)}, u32[]{:S(2)}) %copy-start.2) | copy-done | bytes 6291480
  3.5 2.8 %copy-done.3 = bf16[32,98304]{1,0:T(8,128)(2,1)S(1)} copy-done((bf16[32,98304]{1,0:T(8,128)(2,1)S(1)}, bf16[32,98304]{1,0:T(8,128)(2,1)}, u32[]{:S(2)}) %copy-start.3) | copy-done | bytes 6291480
  7.0 1.9 prepare.1
  8.9 150.2 %all_to_all.15.x_ref = bf16[32,2,32,3072]{3,2,1,0:T(8,128)(2,1)S(1)} all-to-all(bf16[32,2,32,3072]{3,2,1,0:T(8,128)(2,1)S(1)} %get-tuple-element.51), channel_id=1, replica_groups=mesh['tm'=4,'grid'=32] {'grid'}, dimensions={0} | all-to-all | bytes 25165824 | tf_op jit(solution)/shard_map/all_to_all | solution.py:308
  159.1 8.3 %forward.1 = (f32[2,16,2,32,256]{4,3,2,1,0:T(8,128)S(1)}, f32[2,256]{1,0:T(2,128)S(1)}, f32[2,256]{1,0:T(2,128)S(1)}) custom-call(s32[2]{0:T(128)S(1)} %pad_add_fusion.place_ref, bf16[32,2,32,3072]{3,2,1,0:T(8,128)(2,1)S(1)} %all_to_all.15.x_ref, bf16[3072,256]{1,0:T(8,128)(2,1)S(1)} %copy-done.4, bf16[3072,256]{1,0:T(8,128)(2,1)S(1)} %copy-done.5, ...), custom_call_target="tpu_custom_call" | custom-call | flops 3221225472 | bytes 12582912 | tf_op jit(solution)/shard_map/forward/pallas_call | solution.py:154
  168.9 2.5 collective-permute-start.3
  172.5 2.8 %collective-permute-done.2 = f32[4,256]{1,0:T(4,128)S(1)} collective-permute-done((f32[4,256]{1,0:T(4,128)S(1)}, f32[4,256]{1,0:T(4,128)S(1)}, u32[]{:S(2)}, u32[]{:S(2)}) %collective-permute-start.2) | collective-permute-done | bytes 4128 | tf_op jit(solution)/shard_map/ppermute | solution.py:313
  175.5 2.2 collective-permute-start.4
  179.6 3.6 %all-to-all-start.1 = ((bf16[16,2,32,256]{3,2,1,0:T(8,128)(2,1)}), bf16[16,2,32,256]{3,2,1,0:T(8,128)(2,1)S(1)}, u32[]{:S(2)}, u32[]{:S(2)}) async-start(bf16[16,2,32,256]{3,2,1,0:T(8,128)(2,1)} %fusion.1), calls=%async_computation.1 | async-start | bytes 1048576 | tf_op jit(solution)/shard_map/all_to_all | solution.py:308
  183.1 8.5 %multiply_reduce_fusion = f32[2,3072]{1,0:T(2,128)S(1)} fusion(bf16[32,2,32,3072]{3,2,1,0:T(8,128)(2,1)} %copy-done, f32[32,2,32]{2,1,0:T(2,128)S(1)} %bitcast.25), kind=kLoop, calls=%fused_computation | loop fusion | flops 18868224 | bytes 12615680 | tf_op jit(solution)/shard_map/reduce_sum | solution.py:374
  191.7 1.6 all-to-all-done.1
  194.2 5.0 %all-to-all-start.2 = ((bf16[16,2,32,256]{3,2,1,0:T(8,128)(2,1)}), bf16[16,2,32,256]{3,2,1,0:T(8,128)(2,1)S(1)}, u32[]{:S(2)}, u32[]{:S(2)}) async-start(bf16[16,2,32,256]{3,2,1,0:T(8,128)(2,1)} %broadcast_in_dim.48), calls=%async_computation.2 | async-start | bytes 1048576 | tf_op jit(solution)/shard_map/all_to_all | solution.py:308
  201.4 8.1 %all-to-all-done.2.own_ref = bf16[16,2,32,256]{3,2,1,0:T(8,128)(2,1)S(1)} async-done(((bf16[16,2,32,256]{3,2,1,0:T(8,128)(2,1)}), bf16[16,2,32,256]{3,2,1,0:T(8,128)(2,1)S(1)}, u32[]{:S(2)}, u32[]{:S(2)}) %all-to-all-start.2) | async-done | bytes 524320 | tf_op jit(solution)/shard_map/all_to_all | solution.py:308
  209.6 2.1 collective-permute-start.5
  211.8 1.4 collective-permute-done.5.other_ref
  213.2 7.5 %backward.3 = (bf16[128,1536]{1,0:T(8,128)(2,1)S(1)}, bf16[128,1536]{1,0:T(8,128)(2,1)S(1)}, bf16[128,1536]{1,0:T(8,128)(2,1)S(1)}, bf16[128,1536]{1,0:T(8,128)(2,1)S(1)}) custom-call(s32[2]{0:T(128)S(1)} %pad_add_fusion.place_ref, bf16[16,2,32,256]{3,2,1,0:T(8,128)(2,1)S(1)} %all-to-all-done.2.own_ref, ...), custom_call_target="tpu_custom_call" | custom-call | flops 3221225472 | bytes 6291456 | tf_op jit(solution)/shard_map/backward/pallas_call | solution.py:256
  223.8 1.8 collective-permute-start.19
  227.1 7.4 %backward.2 = (bf16[128,1536]{1,0:T(8,128)(2,1)S(1)}, bf16[128,1536]{1,0:T(8,128)(2,1)S(1)}, bf16[128,1536]{1,0:T(8,128)(2,1)S(1)}, bf16[128,1536]{1,0:T(8,128)(2,1)S(1)}) custom-call(s32[2]{0:T(128)S(1)} %pad_add_fusion.place_ref, bf16[16,2,32,256]{3,2,1,0:T(8,128)(2,1)S(1)} %all-to-all-done.2.own_ref, ...), custom_call_target="tpu_custom_call" | custom-call | flops 3221225472 | bytes 6291456 | tf_op jit(solution)/shard_map/backward/pallas_call | solution.py:256
  234.7 8.8 %collective-permute-done.9 = bf16[128,1536]{1,0:T(8,128)(2,1)S(1)} collective-permute-done((bf16[128,1536]{1,0:T(8,128)(2,1)S(1)}, bf16[128,1536]{1,0:T(8,128)(2,1)S(1)}, u32[]{:S(2)}, u32[]{:S(2)}) %collective-permute-start.9) | collective-permute-done | bytes 393248 | tf_op jit(solution)/shard_map/ppermute | solution.py:317
  244.9 7.9 %collective-permute-done.11 = bf16[128,1536]{1,0:T(8,128)(2,1)S(1)} collective-permute-done((bf16[128,1536]{1,0:T(8,128)(2,1)S(1)}, bf16[128,1536]{1,0:T(8,128)(2,1)S(1)}, u32[]{:S(2)}, u32[]{:S(2)}) %collective-permute-start.11) | collective-permute-done | bytes 393248 | tf_op jit(solution)/shard_map/ppermute | solution.py:317
  254.1 1.4 collective-permute-start.10
  255.6 4.1 %collective-permute-start.20 = (f32[128,256]{1,0:T(8,128)S(1)}, f32[128,256]{1,0:T(8,128)S(1)}, u32[]{:S(2)}, u32[]{:S(2)}) collective-permute-start(f32[128,256]{1,0:T(8,128)S(1)} %convert_add_fusion.4), channel_id=1, source_target_pairs={{0,1},{1,0},{2,3},{3,2},{4,5},{5,4},{6,7},{7,6},{8,9},{9,8},{10,11... | collective-permute-start | bytes 393224 | tf_op jit(solution)/shard_map/ppermute | solution.py:321
  259.8 1.8 collective-permute-start.16
  262.5 4.6 %collective-permute-done.16 = bf16[64,1536]{1,0:T(8,128)(2,1)S(1)} collective-permute-done((bf16[64,1536]{1,0:T(8,128)(2,1)S(1)}, bf16[64,1536]{1,0:T(8,128)(2,1)S(1)}, u32[]{:S(2)}, u32[]{:S(2)}) %collective-permute-start.16) | collective-permute-done | bytes 196640 | tf_op jit(solution)/shard_map/ppermute | solution.py:317
  (77 shorter events, 19.2 us)
Async XLA Ops:
  8.9 150.2 %copy-start.1 = (f32[8,264,384]{2,1,0:T(8,128)}, f32[8,264,384]{2,1,0:T(8,128)S(1)}, u32[]{:S(2)}) copy-start(f32[8,264,384]{2,1,0:T(8,128)S(1)} %get-tuple-element.66.block_ref) | copy-start | bytes 9732100
  168.5 10.1 %collective-permute-start = (f32[16,2,32,256]{3,2,1,0:T(8,128)}, f32[16,2,32,256]{3,2,1,0:T(8,128)S(1)}, u32[]{:S(2)}, u32[]{:S(2)}) collective-permute-start(f32[16,2,32,256]{3,2,1,0:T(8,128)} %slice_bitcast_fusion), channel_id=1, source_target_pairs={{0,1},{1,0},{2,3},{3,2},{4,5},{5,4},{6,7},{7,6},{8,9},{9,8},{10,11... | collective-permute-start | bytes 3145736 | tf_op jit(solution)/shard_map/ppermute | solution.py:321
  168.9 3.7 %collective-permute-start.3 = (f32[4,256]{1,0:T(4,128)S(1)}, f32[4,256]{1,0:T(4,128)S(1)}, u32[]{:S(2)}, u32[]{:S(2)}) collective-permute-start(f32[4,256]{1,0:T(4,128)S(1)} %pad_maximum_fusion.1), channel_id=1, source_target_pairs={{0,96},{32,0},{64,32},{96,64},{1,97},{33,1},{65,33},{97,65},{2,98}... | collective-permute-start | bytes 12296 | tf_op jit(solution)/shard_map/ppermute | solution.py:313
  171.3 4.0 %collective-permute-start.2 = (f32[4,256]{1,0:T(4,128)S(1)}, f32[4,256]{1,0:T(4,128)S(1)}, u32[]{:S(2)}, u32[]{:S(2)}) collective-permute-start(f32[4,256]{1,0:T(4,128)S(1)} %pad_maximum_fusion.1), channel_id=1, source_target_pairs={{0,64},{32,96},{64,0},{96,32},{1,65},{33,97},{65,1},{97,33},{2,66}... | collective-permute-start | bytes 12296 | tf_op jit(solution)/shard_map/ppermute | solution.py:313
  171.9 3.7 %collective-permute-start.1 = (f32[4,256]{1,0:T(4,128)S(1)}, f32[4,256]{1,0:T(4,128)S(1)}, u32[]{:S(2)}, u32[]{:S(2)}) collective-permute-start(f32[4,256]{1,0:T(4,128)S(1)} %pad_maximum_fusion.1), channel_id=1, source_target_pairs={{0,32},{32,64},{64,96},{96,0},{1,33},{33,65},{65,97},{97,1},{2,34}... | collective-permute-start | bytes 12296 | tf_op jit(solution)/shard_map/ppermute | solution.py:313
  175.5 3.0 %collective-permute-start.4 = (f32[2,256]{1,0:T(2,128)S(1)}, f32[2,256]{1,0:T(2,128)S(1)}, u32[]{:S(2)}, u32[]{:S(2)}) collective-permute-start(f32[2,256]{1,0:T(2,128)S(1)} %fusion.13), channel_id=1, source_target_pairs={{0,1},{1,0},{2,3},{3,2},{4,5},{5,4},{6,7},{7,6},{8,9},{9,8},{10,11... | collective-permute-start | bytes 6152 | tf_op jit(solution)/shard_map/ppermute | solution.py:321
  179.6 13.7 %all-to-all-start.1 = ((bf16[16,2,32,256]{3,2,1,0:T(8,128)(2,1)}), bf16[16,2,32,256]{3,2,1,0:T(8,128)(2,1)S(1)}, u32[]{:S(2)}, u32[]{:S(2)}) async-start(bf16[16,2,32,256]{3,2,1,0:T(8,128)(2,1)} %fusion.1), calls=%async_computation.1 | async-start | bytes 1048576 | tf_op jit(solution)/shard_map/all_to_all | solution.py:308
  194.2 15.4 %all-to-all-start.2 = ((bf16[16,2,32,256]{3,2,1,0:T(8,128)(2,1)}), bf16[16,2,32,256]{3,2,1,0:T(8,128)(2,1)S(1)}, u32[]{:S(2)}, u32[]{:S(2)}) async-start(bf16[16,2,32,256]{3,2,1,0:T(8,128)(2,1)} %broadcast_in_dim.48), calls=%async_computation.2 | async-start | bytes 1048576 | tf_op jit(solution)/shard_map/all_to_all | solution.py:308
  199.3 12.4 %collective-permute-start.8 = (f32[4,3072]{1,0:T(4,128)S(1)}, f32[4,3072]{1,0:T(4,128)S(1)}, u32[]{:S(2)}, u32[]{:S(2)}) collective-permute-start(f32[4,3072]{1,0:T(4,128)S(1)} %pad_maximum_fusion), channel_id=1, source_target_pairs={{0,96},{32,0},{64,32},{96,64},{1,97},{33,1},{65,33},{97,65},{2,98}... | collective-permute-start | bytes 147464 | tf_op jit(solution)/shard_map/ppermute | solution.py:313
  199.4 12.3 %collective-permute-start.7 = (f32[4,3072]{1,0:T(4,128)S(1)}, f32[4,3072]{1,0:T(4,128)S(1)}, u32[]{:S(2)}, u32[]{:S(2)}) collective-permute-start(f32[4,3072]{1,0:T(4,128)S(1)} %pad_maximum_fusion), channel_id=1, source_target_pairs={{0,64},{32,96},{64,0},{96,32},{1,65},{33,97},{65,1},{97,33},{2,66}... | collective-permute-start | bytes 147464 | tf_op jit(solution)/shard_map/ppermute | solution.py:313
  200.7 11.0 %collective-permute-start.6 = (f32[4,3072]{1,0:T(4,128)S(1)}, f32[4,3072]{1,0:T(4,128)S(1)}, u32[]{:S(2)}, u32[]{:S(2)}) collective-permute-start(f32[4,3072]{1,0:T(4,128)S(1)} %pad_maximum_fusion), channel_id=1, source_target_pairs={{0,32},{32,64},{64,96},{96,0},{1,33},{33,65},{65,97},{97,1},{2,34}... | collective-permute-start | bytes 147464 | tf_op jit(solution)/shard_map/ppermute | solution.py:313
  209.6 3.6 %collective-permute-start.5 = (bf16[16,2,32,256]{3,2,1,0:T(8,128)(2,1)S(1)}, bf16[16,2,32,256]{3,2,1,0:T(8,128)(2,1)S(1)}, u32[]{:S(2)}, u32[]{:S(2)}) collective-permute-start(bf16[16,2,32,256]{3,2,1,0:T(8,128)(2,1)S(1)} %all-to-all-done.2.own_ref), channel_id=1, source_target_pairs={{0,1},{1,0},{2,3},{3,2},{4,5},{5,4},{6,7},{7,6},{8,9},{9,8},{10,11... | collective-permute-start | bytes 1572872 | tf_op jit(solution)/shard_map/ppermute | solution.py:321
  220.7 13.9 %collective-permute-start.13 = (bf16[128,1536]{1,0:T(8,128)(2,1)S(1)}, bf16[128,1536]{1,0:T(8,128)(2,1)S(1)}, u32[]{:S(2)}, u32[]{:S(2)}) collective-permute-start(bf16[128,1536]{1,0:T(8,128)(2,1)S(1)} %get-tuple-element.83), channel_id=1, source_target_pairs={{0,32},{32,0},{64,96},{96,64},{1,33},{33,1},{65,97},{97,65},{2,34}... | collective-permute-start | bytes 1179656 | tf_op jit(solution)/shard_map/ppermute | solution.py:317
  221.7 32.5 %collective-permute-start.18 = (bf16[128,256]{1,0:T(8,128)(2,1)S(1)}, bf16[128,256]{1,0:T(8,128)(2,1)S(1)}, u32[]{:S(2)}, u32[]{:S(2)}) collective-permute-start(bf16[128,256]{1,0:T(8,128)(2,1)S(1)} %fusion.2), channel_id=1, source_target_pairs={{0,64},{32,96},{64,0},{96,32},{1,65},{33,97},{65,1},{97,33},{2,66}... | collective-permute-start | bytes 196616 | tf_op jit(solution)/shard_map/ppermute | solution.py:313
  223.0 32.6 %collective-permute-start.17 = (bf16[128,256]{1,0:T(8,128)(2,1)S(1)}, bf16[128,256]{1,0:T(8,128)(2,1)S(1)}, u32[]{:S(2)}, u32[]{:S(2)}) collective-permute-start(bf16[128,256]{1,0:T(8,128)(2,1)S(1)} %fusion.2), channel_id=1, source_target_pairs={{0,32},{32,64},{64,96},{96,0},{1,33},{33,65},{65,97},{97,1},{2,34}... | collective-permute-start | bytes 196616 | tf_op jit(solution)/shard_map/ppermute | solution.py:313
  223.8 31.8 %collective-permute-start.19 = (bf16[128,256]{1,0:T(8,128)(2,1)S(1)}, bf16[128,256]{1,0:T(8,128)(2,1)S(1)}, u32[]{:S(2)}, u32[]{:S(2)}) collective-permute-start(bf16[128,256]{1,0:T(8,128)(2,1)S(1)} %fusion.2), channel_id=1, source_target_pairs={{0,96},{32,0},{64,32},{96,64},{1,97},{33,1},{65,33},{97,65},{2,98}... | collective-permute-start | bytes 196616 | tf_op jit(solution)/shard_map/ppermute | solution.py:313
  225.7 34.1 %collective-permute-start.15 = (bf16[128,1536]{1,0:T(8,128)(2,1)S(1)}, bf16[128,1536]{1,0:T(8,128)(2,1)S(1)}, u32[]{:S(2)}, u32[]{:S(2)}) collective-permute-start(bf16[128,1536]{1,0:T(8,128)(2,1)S(1)} %get-tuple-element.85), channel_id=1, source_target_pairs={{0,96},{32,64},{64,32},{96,0},{1,97},{33,65},{65,33},{97,1},{2,98}... | collective-permute-start | bytes 1179656 | tf_op jit(solution)/shard_map/ppermute | solution.py:317
  234.5 9.0 %collective-permute-start.9 = (bf16[128,1536]{1,0:T(8,128)(2,1)S(1)}, bf16[128,1536]{1,0:T(8,128)(2,1)S(1)}, u32[]{:S(2)}, u32[]{:S(2)}) collective-permute-start(bf16[128,1536]{1,0:T(8,128)(2,1)S(1)} %get-tuple-element.79), channel_id=1, source_target_pairs={{0,32},{32,0},{64,96},{96,64},{1,33},{33,1},{65,97},{97,65},{2,34}... | collective-permute-start | bytes 1179656 | tf_op jit(solution)/shard_map/ppermute | solution.py:317
  243.5 9.3 %collective-permute-start.11 = (bf16[128,1536]{1,0:T(8,128)(2,1)S(1)}, bf16[128,1536]{1,0:T(8,128)(2,1)S(1)}, u32[]{:S(2)}, u32[]{:S(2)}) collective-permute-start(bf16[128,1536]{1,0:T(8,128)(2,1)S(1)} %get-tuple-element.81), channel_id=1, source_target_pairs={{0,96},{32,64},{64,32},{96,0},{1,97},{33,65},{65,33},{97,1},{2,98}... | collective-permute-start | bytes 1179656 | tf_op jit(solution)/shard_map/ppermute | solution.py:317
  252.8 9.6 %collective-permute-start.14 = (bf16[64,1536]{1,0:T(8,128)(2,1)S(1)}, bf16[64,1536]{1,0:T(8,128)(2,1)S(1)}, u32[]{:S(2)}, u32[]{:S(2)}) collective-permute-start(bf16[64,1536]{1,0:T(8,128)(2,1)S(1)} %add_convert_fusion.1), channel_id=1, source_target_pairs={{0,96},{32,64},{64,32},{96,0},{1,97},{33,65},{65,33},{97,1},{2,98}... | collective-permute-start | bytes 589832 | tf_op jit(solution)/shard_map/ppermute | solution.py:317
  254.1 13.0 %collective-permute-start.10 = (bf16[64,1536]{1,0:T(8,128)(2,1)S(1)}, bf16[64,1536]{1,0:T(8,128)(2,1)S(1)}, u32[]{:S(2)}, u32[]{:S(2)}) collective-permute-start(bf16[64,1536]{1,0:T(8,128)(2,1)S(1)} %add_convert_fusion.3), channel_id=1, source_target_pairs={{0,96},{32,64},{64,32},{96,0},{1,97},{33,65},{65,33},{97,1},{2,98}... | collective-permute-start | bytes 589832 | tf_op jit(solution)/shard_map/ppermute | solution.py:317
  255.6 12.6 %collective-permute-start.12 = (bf16[64,1536]{1,0:T(8,128)(2,1)S(1)}, bf16[64,1536]{1,0:T(8,128)(2,1)S(1)}, u32[]{:S(2)}, u32[]{:S(2)}) collective-permute-start(bf16[64,1536]{1,0:T(8,128)(2,1)S(1)} %add_convert_fusion.2), channel_id=1, source_target_pairs={{0,32},{32,0},{64,96},{96,64},{1,33},{33,1},{65,97},{97,65},{2,34}... | collective-permute-start | bytes 589832 | tf_op jit(solution)/shard_map/ppermute | solution.py:317
  255.6 6.0 %collective-permute-start.20 = (f32[128,256]{1,0:T(8,128)S(1)}, f32[128,256]{1,0:T(8,128)S(1)}, u32[]{:S(2)}, u32[]{:S(2)}) collective-permute-start(f32[128,256]{1,0:T(8,128)S(1)} %convert_add_fusion.4), channel_id=1, source_target_pairs={{0,1},{1,0},{2,3},{3,2},{4,5},{5,4},{6,7},{7,6},{8,9},{9,8},{10,11... | collective-permute-start | bytes 393224 | tf_op jit(solution)/shard_map/ppermute | solution.py:321
  259.8 7.3 %collective-permute-start.16 = (bf16[64,1536]{1,0:T(8,128)(2,1)S(1)}, bf16[64,1536]{1,0:T(8,128)(2,1)S(1)}, u32[]{:S(2)}, u32[]{:S(2)}) collective-permute-start(bf16[64,1536]{1,0:T(8,128)(2,1)S(1)} %add_convert_fusion), channel_id=1, source_target_pairs={{0,32},{32,0},{64,96},{96,64},{1,33},{33,1},{65,97},{97,65},{2,34}... | collective-permute-start | bytes 589832 | tf_op jit(solution)/shard_map/ppermute | solution.py:317
  (7 other events, 465.2 us)
